TPU v7x, 256 devices: a whole 4x4x8 slice. The times are simulated.
256 devices in a mesh: rcv: 4 (over z_lo), shot: 64 (over z_hi, y, x, core).
Axes of the slice: x: 4, y: 4, z: 8 (z_hi: 2, z_lo: 4; z = z_hi * 4 + z_lo), core: 2. Of those that a mesh axis runs over, the one named last changes fastest.
Arguments:
- traces: bfloat16 [16, 2000, 8192], P('rcv', None, 'shot'), may hold values from -6 to 6
- first_trace_taps: bfloat16 [8, 16], replicated, may hold values from -1.5 to 1.5
- first_time_taps: bfloat16 [8, 64], replicated, may hold values from -0.25 to 0.25
- second_trace_taps: bfloat16 [8, 16], replicated, may hold values from -1.5 to 1.5
- second_time_taps: bfloat16 [8, 64], replicated, may hold values from -0.25 to 0.25
- dest_row: int32 [16, 64], P('rcv', 'shot'), may hold values from 0 to 15, as said below
Outputs:
- filtered: float32 [16, 2000, 8192], P('rcv', None, 'shot')
Inputs may be any that keep to these rules, and one draw needn't show every extreme that they name: For each column c, dest_row[:, c] is a permutation of the gathers; the rows r * 4 to (r + 1) * 4 - 1 of a column send at most 2 blocks into the rows o * 4 to (o + 1) * 4 - 1 for any o, and exactly 2 into some such range.
All inputs are finite; a program needn't handle non-finite values.
Results may differ from a plain program's by a relative error of at most 0.005.
Values may be sent and summed in bfloat16 or wider, within the bound.
No kernel may reach another device: no remote copies, remote signals or barrier semaphores. Data moves between devices by JAX's collectives and lax.ppermute only.
A program may use at most 64 MiB of HBM per device.

v0:
```python
import jax
import jax.numpy as jnp
from jax import lax
from jax.sharding import PartitionSpec as P

segment_span = 128


def padded_2(block, sides, width):
    for axis, dim in sides:
        count = lax.axis_size(axis)
        forward = [(i, i + 1) for i in range(count - 1)]
        backward = [(target, source) for source, target in forward]
        low = lax.ppermute(
            lax.slice_in_dim(block, block.shape[dim] - width, None, axis=dim), axis, forward
        )
        high = lax.ppermute(lax.slice_in_dim(block, 0, width, axis=dim), axis, backward)
        block = jnp.concatenate([low, block, high], axis=dim)
    return block


def tap_table(taps, rows_in, cols_out):
    width = taps.shape[1]
    offset = (
        jnp.arange(rows_in, dtype=jnp.int32)[:, None]
        - jnp.arange(cols_out, dtype=jnp.int32)[None, :]
    )
    picker = (offset[:, :, None] == jnp.arange(width, dtype=jnp.int32)[None, None, :]).astype(
        jnp.float32
    )
    return jnp.einsum(
        "wak,fk->fwa", picker, taps.astype(jnp.float32), precision=lax.Precision.HIGHEST
    )


def filter_block(one_block, trace_mats, time_mats, lead_taps):
    fanned = jnp.einsum("tu,fux->ftx", one_block, trace_mats, preferred_element_type=jnp.float32)
    fanned = fanned.astype(jnp.bfloat16)
    fan_count, samples, block_width = fanned.shape
    segments = -(-samples // segment_span)
    padded = jnp.pad(
        fanned, ((0, 0), (lead_taps, (segments + 1) * segment_span - samples - lead_taps), (0, 0))
    )
    pieces = padded.reshape(fan_count, segments + 1, segment_span, block_width)
    upper = time_mats[:, :segment_span]
    lower = time_mats[:, segment_span:]
    result = jnp.einsum(
        "fwa,fiwx->iax", upper, pieces[:, :segments], preferred_element_type=jnp.float32
    )
    result = result + jnp.einsum(
        "fwa,fiwx->iax", lower, pieces[:, 1:], preferred_element_type=jnp.float32
    )
    return result.reshape(segments * segment_span, block_width)[:samples]


def per_device(
    traces, first_trace_taps, first_time_taps, second_trace_taps, second_time_taps, dest_row
):
    half_taps = first_trace_taps.shape[1] // 2
    lead_taps = first_time_taps.shape[1] // 2
    blocks, samples, block_width = traces.shape
    first_mats = tap_table(first_trace_taps, block_width + 2 * half_taps, block_width).astype(
        jnp.bfloat16
    )
    first_times = tap_table(first_time_taps, 2 * segment_span, segment_span).astype(jnp.bfloat16)
    widened = padded_2(traces, (("shot", 2),), half_taps)
    first_pass = lax.map(
        lambda one_block: filter_block(one_block, first_mats, first_times, lead_taps).astype(
            jnp.bfloat16
        ),
        widened,
    )
    owner_count = lax.axis_size("rcv")
    slot_cap = blocks // 2
    target = dest_row[:, 0]
    dest_owner = target // blocks
    dest_slot = target % blocks
    block_ids = jnp.arange(blocks, dtype=jnp.int32)
    before = (block_ids[:, None] > block_ids[None, :]) & (
        dest_owner[:, None] == dest_owner[None, :]
    )
    send_rank = jnp.sum(before.astype(jnp.int32), axis=1)
    send_key = dest_owner * slot_cap + send_rank
    pick_table = send_key[None, :] == jnp.arange(owner_count * slot_cap, dtype=jnp.int32)[:, None]
    buffer = jnp.einsum(
        "kj,jtx->ktx",
        pick_table.astype(jnp.bfloat16),
        first_pass,
        preferred_element_type=jnp.float32,
    ).astype(jnp.bfloat16)
    buffer = buffer.reshape(owner_count, slot_cap, samples, block_width)
    labels = (jnp.sum(pick_table.astype(jnp.int32) * (dest_slot + 1)[None, :], axis=1) - 1).reshape(
        owner_count, slot_cap
    )
    buffer, labels = (
        lax.all_to_all(buffer, "rcv", split_axis=0, concat_axis=0, tiled=True),
        lax.all_to_all(labels, "rcv", split_axis=0, concat_axis=0, tiled=True),
    )
    arrived = buffer.reshape(owner_count * slot_cap, samples, block_width)
    arrived_labels = labels.reshape(owner_count * slot_cap)
    placing = (arrived_labels[None, :] == block_ids[:, None]).astype(jnp.bfloat16)
    resorted = jnp.einsum(
        "gk,ktx->gtx", placing, arrived, preferred_element_type=jnp.float32
    ).astype(jnp.bfloat16)
    second_mats = tap_table(second_trace_taps, block_width + 2 * half_taps, block_width).astype(
        jnp.bfloat16
    )
    second_times = tap_table(second_time_taps, 2 * segment_span, segment_span).astype(jnp.bfloat16)
    widened_sorted = padded_2(resorted, (("shot", 2),), half_taps)
    return lax.map(
        lambda one_block: filter_block(one_block, second_mats, second_times, lead_taps),
        widened_sorted,
    )


def solution(mesh):
    in_specs = (P("rcv", None, "shot"), P(), P(), P(), P(), P("rcv", "shot"))
    out_specs = P("rcv", None, "shot")
    return jax.shard_map(
        per_device, mesh=mesh, in_specs=in_specs, out_specs=out_specs, check_vma=False
    )
```

profile of v0, /device:TPU:31, one launch (start us, length us, event | category | flops | bytes accessed | tf_op | source)
XLA Modules:
  0.0 217.1 jit_solution(3494526951230842162)
XLA Ops:
  0.0 2.9 %copy.54 = bf16[4,2000,128]{1,2,0:T(8,128)(2,1)S(1)} copy(bf16[4,2000,128]{2,1,0:T(8,128)(2,1)} %param.10) | data formatting | bytes 4096000 | tf_op args[0]
  3.0 0.8 fusion.71
  3.8 8.9 %collective-permute-start = (bf16[4,2000,8]{1,2,0:T(8,128)(2,1)}, bf16[4,2000,8]{1,2,0:T(8,128)(2,1)S(1)}, u32[]{:S(2)}, u32[]{:S(2)}) collective-permute-start(bf16[4,2000,8]{1,2,0:T(8,128)(2,1)} %get-tuple-element.187), channel_id=1, source_target_pairs={{0,1},{1,2},{2,3},{3,4},{4,5},{5,6},{6,7},{7,8},{8,9},{9,10},{10,1... | collective-permute-start | bytes 384008 | tf_op jit(solution)/shard_map/ppermute | solution.py:14
  12.7 1.9 collective-permute-start.1
  15.0 0.7 sub.74
  15.6 3.2 %all-to-all-start = ((s32[4,1,2]{2,1,0:T(1,128)}), s32[4,1,2]{2,1,0:T(1,128)S(1)}, u32[]{:S(2)}, u32[]{:S(2)}) async-start(s32[4,1,2]{2,1,0:T(1,128)} %bitcast.28), calls=%async_computation | async-start | bytes 4096 | tf_op jit(solution)/shard_map/all_to_all | solution.py:97
  18.9 0.6 copy-done.3
  19.5 1.3 fusion.53
  21.6 5.9 %collective-permute-done.1 = bf16[4,2000,8]{1,2,0:T(8,128)(2,1)S(1)} collective-permute-done((bf16[4,2000,8]{1,2,0:T(8,128)(2,1)}, bf16[4,2000,8]{1,2,0:T(8,128)(2,1)S(1)}, u32[]{:S(2)}, u32[]{:S(2)}) %collective-permute-start.1) | collective-permute-done | bytes 128032 | tf_op jit(solution)/shard_map/ppermute | solution.py:17
  27.4 1.8 pad_maximum_fusion.1
  29.2 15.9 %while.24 = (s32[]{:T(128)}, bf16[4,2000,128]{2,1,0:T(8,128)(2,1)}, bf16[4,2000,144]{1,2,0:T(8,128)(2,1)S(1)}, bf16[8,144,128]{2,1,0:T(8,128)(2,1)S(1)}, bf16[8,...) while((s32[]{:T(128)}, bf16[4,2000,128]{2,1,0:T(8,128)(2,1)}, bf16[4,2000,144]{1,2,0:T(8,128)(2,1)S(1)}, ...), condition=%wide.region_3.4_spmd, body=%wide.region_2.3_spmd.sunk | while | flops 1666138112 | bytes 26092116 | solution.py:67
  29.3 1.3 convert_bitcast_fusion.4
  30.9 0.7 fusion.100
  31.6 0.8 fusion.101
  32.4 0.8 fusion.102
  33.2 1.3 convert_bitcast_fusion.4
  34.9 0.7 fusion.100
  35.6 0.8 fusion.101
  36.4 0.8 fusion.102
  37.2 1.3 convert_bitcast_fusion.4
  38.8 0.7 fusion.100
  39.6 0.8 fusion.101
  40.4 0.9 fusion.102
  41.2 1.3 convert_bitcast_fusion.4
  42.8 0.7 fusion.100
  43.6 0.8 fusion.101
  44.3 0.8 fusion.102
  45.2 8.4 %convolution_convert_fusion = bf16[8,2000,128]{2,0,1:T(8,128)(2,1)S(1)} fusion(bf16[4,2000,128]{2,1,0:T(8,128)(2,1)} %get-tuple-element.135, s32[4]{0:T(128)S(1)} %multiply_add_fusion), kind=kOutput, calls=%fused_computation.41 | convolution fusion | flops 18432032 | bytes 6144016 | tf_op jit(solution)/shard_map/kj,jtx->ktx/dot_general | solution.py:85
  53.6 5.0 %copy.60 = bf16[4,2,2000,128]{3,1,2,0:T(2,128)(2,1)} copy(bf16[4,2,2000,128]{3,1,0,2:T(2,128)(2,1)S(1)} %bitcast.168) | data formatting | bytes 8192000 | tf_op jit(solution)/shard_map/reshape | solution.py:91
  58.6 5.1 %all-to-all-start.1 = ((bf16[4,2,2000,128]{3,1,2,0:T(2,128)(2,1)}), bf16[4,2,2000,128]{3,1,2,0:T(2,128)(2,1)}, u32[]{:S(2)}, u32[]{:S(2)}) async-start(bf16[4,2,2000,128]{3,1,2,0:T(2,128)(2,1)} %copy.60), calls=%async_computation.1 | async-start | bytes 8192000 | tf_op jit(solution)/shard_map/all_to_all | solution.py:96
  63.8 1.3 fusion.52
  65.5 0.5 broadcast.158
  66.0 0.6 reduce.3
  66.7 81.2 %all-to-all-done.1 = bf16[4,2,2000,128]{3,1,2,0:T(2,128)(2,1)} async-done(((bf16[4,2,2000,128]{3,1,2,0:T(2,128)(2,1)}), bf16[4,2,2000,128]{3,1,2,0:T(2,128)(2,1)}, u32[]{:S(2)}, u32[]{:S(2)}) %all-to-all-start.1) | async-done | bytes 4096032 | tf_op jit(solution)/shard_map/all_to_all | solution.py:96
  147.9 6.1 %copy.61 = bf16[4,2,2000,128]{3,1,0,2:T(2,128)(2,1)S(1)} copy(bf16[4,2,2000,128]{3,1,2,0:T(2,128)(2,1)} %all-to-all-done.1) | data formatting | bytes 8192000 | tf_op jit(solution)/shard_map/all_to_all | solution.py:96
  154.0 1.2 convolution_convert_fusion.1
  155.2 3.1 %fusion.72 = (bf16[4,2000,8]{2,0,1:T(4,128)(2,1)}, bf16[4,2000,8]{2,0,1:T(4,128)(2,1)}) fusion(bf16[4,2000,128]{2,0,1:T(4,128)(2,1)S(1)} %convolution_convert_fusion.1), kind=kLoop, calls=%fused_computation.87 | loop fusion | bytes 512000 | tf_op jit(solution)/shard_map/slice | solution.py:15
  158.3 2.8 %copy.62 = bf16[4,2000,8]{1,2,0:T(8,128)(2,1)S(1)} copy(bf16[4,2000,8]{2,0,1:T(4,128)(2,1)} %get-tuple-element.189) | data formatting | bytes 256000 | tf_op jit(solution)/shard_map/slice | solution.py:15
  161.1 5.1 %collective-permute-start.2 = (bf16[4,2000,8]{1,2,0:T(8,128)(2,1)S(1)}, bf16[4,2000,8]{1,2,0:T(8,128)(2,1)S(1)}, u32[]{:S(2)}, u32[]{:S(2)}) collective-permute-start(bf16[4,2000,8]{1,2,0:T(8,128)(2,1)S(1)} %copy.62), channel_id=1, source_target_pairs={{0,1},{1,2},{2,3},{3,4},{4,5},{5,6},{6,7},{7,8},{8,9},{9,10},{10,1... | collective-permute-start | bytes 384008 | tf_op jit(solution)/shard_map/ppermute | solution.py:14
  166.2 2.8 %copy.63 = bf16[4,2000,8]{1,2,0:T(8,128)(2,1)S(1)} copy(bf16[4,2000,8]{2,0,1:T(4,128)(2,1)} %get-tuple-element.190) | data formatting | bytes 256000 | tf_op jit(solution)/shard_map/slice | solution.py:17
  169.0 1.9 collective-permute-start.3
  171.3 2.4 %copy.64 = bf16[4,2000,8]{2,0,1:T(4,128)(2,1)} copy(bf16[4,2000,8]{1,2,0:T(8,128)(2,1)S(1)} %collective-permute-done.2) | data formatting | bytes 256000 | tf_op jit(solution)/shard_map/ppermute | solution.py:14
  173.8 9.7 %collective-permute-done.3 = bf16[4,2000,8]{1,2,0:T(8,128)(2,1)S(1)} collective-permute-done((bf16[4,2000,8]{1,2,0:T(8,128)(2,1)S(1)}, bf16[4,2000,8]{1,2,0:T(8,128)(2,1)S(1)}, u32[]{:S(2)}, u32[]{:S(2)}) %collective-permute-start.3) | collective-permute-done | bytes 128032 | tf_op jit(solution)/shard_map/ppermute | solution.py:17
  183.4 2.4 %copy.65 = bf16[4,2000,8]{2,0,1:T(4,128)(2,1)} copy(bf16[4,2000,8]{1,2,0:T(8,128)(2,1)S(1)} %collective-permute-done.3) | data formatting | bytes 256000 | tf_op jit(solution)/shard_map/ppermute | solution.py:17
  185.8 8.2 %pad_maximum_fusion = bf16[4,2000,144]{2,0,1:T(4,128)(2,1)} fusion(bf16[4,2000,8]{2,0,1:T(4,128)(2,1)} %copy.65, bf16[4,2000,128]{2,0,1:T(4,128)(2,1)S(1)} %convolution_convert_fusion.1, bf16[4,2000,8]{2,0,1:T(4,128)(2,1)} %copy.64), kind=kLoop, calls=%fused_computation.40 | loop fusion | flops 6912000 | bytes 4608000 | tf_op jit(solution)/shard_map/concatenate | solution.py:18
  194.1 5.7 %copy.66 = bf16[4,2000,144]{1,2,0:T(8,128)(2,1)S(1)} copy(bf16[4,2000,144]{2,0,1:T(4,128)(2,1)} %pad_maximum_fusion) | data formatting | bytes 4608000 | tf_op jit(solution)/shard_map/while | solution.py:110
  199.7 16.7 %while.25 = (s32[]{:T(128)}, f32[4,2000,128]{2,1,0:T(8,128)}, bf16[4,2000,144]{1,2,0:T(8,128)(2,1)S(1)}, bf16[8,144,128]{2,1,0:T(8,128)(2,1)S(1)}, bf16[8,256,128]{1,2,0:T(8,128)(2,1)S(1)}, /*index=5*/s32[]{:T(128)}, bf16[]{:T(256)}) while((s32[]{:T(128)}, f32[4,2000,128]{2,1,0:T(8,128)}, bf16[4,2000,144]{1,2,0:T(8,128)(2,1)S(1)}, ...), condition=%wide.region_5.6_spmd, body=%wide.region_4.5_spmd.sunk | while | flops 1665875968 | bytes 27640404 | solution.py:110
  199.8 1.3 convert_bitcast_fusion.5
  201.4 0.7 fusion.109
  202.1 0.8 fusion.110
  202.9 1.0 fusion.111
  203.9 1.3 convert_bitcast_fusion.5
  205.6 0.7 fusion.109
  206.3 0.8 fusion.110
  207.1 1.0 fusion.111
  208.1 1.3 convert_bitcast_fusion.5
  209.7 0.7 fusion.109
  210.5 0.8 fusion.110
  211.2 1.0 fusion.111
  212.3 1.3 convert_bitcast_fusion.5
  213.9 0.7 fusion.109
  214.6 0.8 fusion.110
  215.4 1.0 fusion.111
  216.4 0.7 copy-done.1
  (44 shorter events, 4.3 us)
Async XLA Ops:
  0.0 19.5 %copy-start = (bf16[8,64]{1,0:T(8,128)(2,1)S(1)}, bf16[8,64]{1,0:T(8,128)(2,1)}, u32[]{:S(2)}) copy-start(bf16[8,64]{1,0:T(8,128)(2,1)} %param.12) | copy-start | bytes 3076
  0.0 14.6 %copy-start.8 = (s32[4,1]{0,1:T(1,128)S(1)}, s32[4,1]{0,1:T(1,128)}, u32[]{:S(2)}) copy-start(s32[4,1]{0,1:T(1,128)} %param.15) | copy-start | bytes 52
  0.0 21.2 %copy-start.5 = (bf16[8,16]{1,0:T(8,128)(2,1)S(1)}, bf16[8,16]{1,0:T(8,128)(2,1)}, u32[]{:S(2)}) copy-start(bf16[8,16]{1,0:T(8,128)(2,1)} %param.11) | copy-start | bytes 772
  3.0 18.2 %copy-start.2 = (bf16[4,2000,128]{1,2,0:T(8,128)(2,1)}, bf16[4,2000,128]{1,2,0:T(8,128)(2,1)S(1)}, u32[]{:S(2)}) copy-start(bf16[4,2000,128]{1,2,0:T(8,128)(2,1)S(1)} %copy.54) | copy-start | bytes 6144004
  3.8 17.8 %collective-permute-start = (bf16[4,2000,8]{1,2,0:T(8,128)(2,1)}, bf16[4,2000,8]{1,2,0:T(8,128)(2,1)S(1)}, u32[]{:S(2)}, u32[]{:S(2)}) collective-permute-start(bf16[4,2000,8]{1,2,0:T(8,128)(2,1)} %get-tuple-element.187), channel_id=1, source_target_pairs={{0,1},{1,2},{2,3},{3,4},{4,5},{5,6},{6,7},{7,8},{8,9},{9,10},{10,1... | collective-permute-start | bytes 384008 | tf_op jit(solution)/shard_map/ppermute | solution.py:14
  12.7 14.7 %collective-permute-start.1 = (bf16[4,2000,8]{1,2,0:T(8,128)(2,1)}, bf16[4,2000,8]{1,2,0:T(8,128)(2,1)S(1)}, u32[]{:S(2)}, u32[]{:S(2)}) collective-permute-start(bf16[4,2000,8]{1,2,0:T(8,128)(2,1)} %get-tuple-element.188), channel_id=1, source_target_pairs={{1,0},{2,1},{3,2},{4,3},{5,4},{6,5},{7,6},{8,7},{9,8},{10,9},{11,1... | collective-permute-start | bytes 384008 | tf_op jit(solution)/shard_map/ppermute | solution.py:17
  15.6 43.0 %all-to-all-start = ((s32[4,1,2]{2,1,0:T(1,128)}), s32[4,1,2]{2,1,0:T(1,128)S(1)}, u32[]{:S(2)}, u32[]{:S(2)}) async-start(s32[4,1,2]{2,1,0:T(1,128)} %bitcast.28), calls=%async_computation | async-start | bytes 4096 | tf_op jit(solution)/shard_map/all_to_all | solution.py:97
  18.9 0.7 copy-start.3
  58.6 5.2 %copy-start.4 = (s32[256,128]{1,0:T(8,128)S(1)}, s32[256,128]{1,0:T(8,128)}, u32[]{:S(2)}) copy-start(s32[256,128]{1,0:T(8,128)} %copy-done.3) | copy-start | bytes 393220
  58.6 5.2 %copy-start.7 = (bf16[8,64]{1,0:T(8,128)(2,1)S(1)}, bf16[8,64]{1,0:T(8,128)(2,1)}, u32[]{:S(2)}) copy-start(bf16[8,64]{1,0:T(8,128)(2,1)} %param.14) | copy-start | bytes 3076
  58.6 89.3 %all-to-all-start.1 = ((bf16[4,2,2000,128]{3,1,2,0:T(2,128)(2,1)}), bf16[4,2,2000,128]{3,1,2,0:T(2,128)(2,1)}, u32[]{:S(2)}, u32[]{:S(2)}) async-start(bf16[4,2,2000,128]{3,1,2,0:T(2,128)(2,1)} %copy.60), calls=%async_computation.1 | async-start | bytes 8192000 | tf_op jit(solution)/shard_map/all_to_all | solution.py:96
  158.3 12.7 %copy-start.6 = (bf16[8,16]{1,0:T(8,128)(2,1)S(1)}, bf16[8,16]{1,0:T(8,128)(2,1)}, u32[]{:S(2)}) copy-start(bf16[8,16]{1,0:T(8,128)(2,1)} %param.13) | copy-start | bytes 772
  161.1 10.2 %collective-permute-start.2 = (bf16[4,2000,8]{1,2,0:T(8,128)(2,1)S(1)}, bf16[4,2000,8]{1,2,0:T(8,128)(2,1)S(1)}, u32[]{:S(2)}, u32[]{:S(2)}) collective-permute-start(bf16[4,2000,8]{1,2,0:T(8,128)(2,1)S(1)} %copy.62), channel_id=1, source_target_pairs={{0,1},{1,2},{2,3},{3,4},{4,5},{5,6},{6,7},{7,8},{8,9},{9,10},{10,1... | collective-permute-start | bytes 384008 | tf_op jit(solution)/shard_map/ppermute | solution.py:14
  169.0 14.4 %collective-permute-start.3 = (bf16[4,2000,8]{1,2,0:T(8,128)(2,1)S(1)}, bf16[4,2000,8]{1,2,0:T(8,128)(2,1)S(1)}, u32[]{:S(2)}, u32[]{:S(2)}) collective-permute-start(bf16[4,2000,8]{1,2,0:T(8,128)(2,1)S(1)} %copy.63), channel_id=1, source_target_pairs={{1,0},{2,1},{3,2},{4,3},{5,4},{6,5},{7,6},{8,7},{9,8},{10,9},{11,1... | collective-permute-start | bytes 384008 | tf_op jit(solution)/shard_map/ppermute | solution.py:17
  216.4 0.7 copy-start.1
where the time goes:
time: 218 us; the launch traced here: 217 us
  waiting for transfers between devices  96.8 us (44%)
  local copies, waits for them, and re-layouts  47.4 us (22%)
  matrix products  35.2 us (16%)
  starting transfers between devices  26.2 us (12%)
  other arithmetic  11 us (5%)
    all_to_all x1, waiting for transfers between devices, per_device(): lax.all_to_all(buffer, 'rcv', split_axis=0, concat_axis=0, tiled=True)  81.2 us
    ppermute x2, waiting for transfers between devices, padded_2(): lax.ppermute(lax.slice_in_dim(block, 0, width, axis=dim), axis, backward)  15.5 us
    ppermute x2, starting transfers between devices, padded_2(): lax.ppermute(lax.slice_in_dim(block, block.shape[dim] - width, None, axis...  14 us
    dot_general x8, matrix products, filter_block(): jnp.einsum('tu,fux->ftx', one_block, trace_mats, preferred_element_type=j...  10.3 us
    concatenate x2, other arithmetic, padded_2(): block = jnp.concatenate([low, block, high], axis=dim)  10.1 us
    dot_general x1, matrix products, per_device(): jnp.einsum('kj,jtx->ktx', pick_table.astype(jnp.bfloat16), first_pass, pr...  8.41 us
    slice x3, local copies, waits for them, and re-layouts, padded_2(): lax.slice_in_dim(block, block.shape[dim] - width, None, axis=dim)  6.7 us
    dot_general x8, matrix products, filter_block(): jnp.einsum('fwa,fiwx->iax', lower, pieces[:, 1:], preferred_element_type=...  6.17 us
  transfers between devices with their start and end apart: 6, of which 3 were waited for; matrix products, arithmetic and copies ran while one was open for 20% of the time, Pallas kernels for 0%

commit v1 on v0

v1 whole, which is shorter than its diff:
```python
import functools

import jax
import jax.numpy as jnp
from jax import lax
from jax.experimental import pallas as pl
from jax.experimental.pallas import tpu as pltpu
from jax.sharding import PartitionSpec as P

LANES = 128
EDGE = 8
SPAN = 256
REACH = 64
WIDE = SPAN - REACH


PARAMS = pltpu.CompilerParams(vmem_limit_bytes=16 * 2**20)


def chunk_bounds(samples):
    sizes = [384, 576, 576]
    bounds = [0]
    for size in sizes:
        if bounds[-1] + size + REACH <= samples:
            bounds.append(bounds[-1] + size)
    bounds.append(samples)
    return bounds


def segment_plan(rows):
    count = -(-rows // WIDE)
    width = min(WIDE, -(-rows // (16 * count)) * 16)
    return count, width


def weights_kernel(trace_ref, time_ref, _, mats_ref, times_ref):
    fans = trace_ref.shape[0]
    blocks = mats_ref.shape[0]
    for fan in range(fans):
        row = jnp.broadcast_to(trace_ref[fan : fan + 1, :], (LANES, SPAN))
        own = pltpu.roll(row, 0, 1, stride=1, stride_axis=0)[:, :LANES]
        left = pltpu.roll(row[:EDGE], SPAN - EDGE, 1, stride=1, stride_axis=0)[:, :LANES]
        right = pltpu.roll(row[:EDGE], LANES, 1, stride=1, stride_axis=0)[:, :LANES]
        pair, half = fan // 2, fan % 2
        cols = slice(half * LANES, (half + 1) * LANES)
        for block in range(blocks):
            before, after = EDGE * block, EDGE * (blocks - 1 - block)
            parts = []
            for piece in (left, right):
                if before:
                    parts.append(jnp.zeros((before, LANES), jnp.float32))
                parts.append(piece)
                if after:
                    parts.append(jnp.zeros((after, LANES), jnp.float32))
            parts.append(jnp.zeros((LANES - 2 * EDGE * blocks, LANES), jnp.float32))
            mats_ref[block, pair, :LANES, cols] = own.astype(jnp.bfloat16)
            mats_ref[block, pair, LANES:, cols] = jnp.concatenate(parts, axis=0).astype(
                jnp.bfloat16
            )
        taps = jnp.broadcast_to(time_ref[fan : fan + 1, :], (WIDE, SPAN))
        times_ref[:, fan * SPAN : (fan + 1) * SPAN] = pltpu.roll(
            taps, 0, 1, stride=1, stride_axis=0
        ).astype(jnp.bfloat16)


def weights(trace_taps, time_taps, after, blocks):
    fans, width = trace_taps.shape
    turned = jnp.pad(trace_taps[:, ::-1].astype(jnp.float32), ((0, 0), (0, SPAN - width)))
    turned = jnp.roll(turned, width // 2 - width + 1, axis=1)
    late = jnp.pad(time_taps.astype(jnp.float32), ((0, 0), (0, SPAN - time_taps.shape[1])))
    whole = pl.BlockSpec(memory_space=pltpu.VMEM)
    return pl.pallas_call(
        weights_kernel,
        in_specs=[whole, whole, pl.BlockSpec(memory_space=pl.ANY)],
        out_shape=(
            jax.ShapeDtypeStruct((blocks, fans // 2, 2 * LANES, 2 * LANES), jnp.bfloat16),
            jax.ShapeDtypeStruct((WIDE, fans * SPAN), jnp.bfloat16),
        ),
        cost_estimate=pl.CostEstimate(flops=1, bytes_accessed=1, transcendentals=0),
        compiler_params=PARAMS,
        name="weights",
    )(turned, late, after)


def edges_dot(tiles, out_ref):
    blocks = len(tiles)
    lane = lax.broadcasted_iota(jnp.int32, (LANES, LANES), 1)
    trace = lax.broadcasted_iota(jnp.int32, (LANES, LANES), 0)
    total = None
    for block, tile in enumerate(tiles):
        at = lane - EDGE * block
        last = (at >= 0) & (at < EDGE) & (trace == at + LANES - EDGE)
        at = at - EDGE * blocks
        first = (at >= 0) & (at < EDGE) & (trace == at)
        pick = jnp.where(last | first, 1.0, 0.0).astype(jnp.bfloat16)
        part = jnp.dot(tile, pick, preferred_element_type=jnp.float32)
        total = part if total is None else total + part
    out_ref[...] = total.astype(jnp.bfloat16)


def first_edges_kernel(x_ref, out_ref):
    edges_dot([x_ref[block] for block in range(x_ref.shape[0])], out_ref)


def first_edges(traces, start, stop):
    blocks = traces.shape[0]
    rows = stop - start
    return pl.pallas_call(
        first_edges_kernel,
        grid=(1,),
        in_specs=[
            pl.BlockSpec(
                (pl.Element(blocks), pl.Element(rows), pl.Element(LANES)),
                lambda i: (0, start, 0),
            )
        ],
        out_specs=pl.BlockSpec((rows, LANES), lambda i: (0, 0)),
        out_shape=jax.ShapeDtypeStruct((rows, LANES), jnp.bfloat16),
        cost_estimate=pl.CostEstimate(
            flops=1,
            bytes_accessed=1,
            transcendentals=0,
        ),
        compiler_params=PARAMS,
        name="first_edges",
    )(traces)


def second_edges_kernel(slot_ref, *refs):
    parts, (_, sorted_ref, out_ref, sem) = refs[:-4], refs[-4:]
    blocks, slot_cap = sorted_ref.shape[0], parts[0].shape[0]
    for block in range(blocks):
        slot = slot_ref[block]
        for offset, part in enumerate(parts):

            @pl.when(slot // slot_cap == offset)
            def _():
                pltpu.make_async_copy(
                    part.at[slot % slot_cap], sorted_ref.at[block], sem.at[block]
                ).start()

    for block in range(blocks):
        pltpu.make_async_copy(parts[0].at[0], sorted_ref.at[block], sem.at[block]).wait()
    edges_dot([sorted_ref[block] for block in range(blocks)], out_ref)


def second_edges(slots, arrived, after, blocks):
    rows = arrived[0].shape[1]
    return pl.pallas_call(
        second_edges_kernel,
        grid_spec=pltpu.PrefetchScalarGridSpec(
            num_scalar_prefetch=1,
            grid=(1,),
            in_specs=[pl.BlockSpec(memory_space=pl.ANY)] * (len(arrived) + 1),
            out_specs=[
                pl.BlockSpec((blocks, rows, LANES), lambda i, slot: (0, 0, 0)),
                pl.BlockSpec((rows, LANES), lambda i, slot: (0, 0)),
            ],
            scratch_shapes=[pltpu.SemaphoreType.DMA((blocks,))],
        ),
        out_shape=[
            jax.ShapeDtypeStruct((blocks, rows, LANES), jnp.bfloat16),
            jax.ShapeDtypeStruct((rows, LANES), jnp.bfloat16),
        ],
        cost_estimate=pl.CostEstimate(
            flops=1,
            bytes_accessed=1,
            transcendentals=0,
        ),
        compiler_params=PARAMS,
        name="second_edges",
    )(slots, *arrived, after)


def swap_edges(edges):
    count = lax.axis_size("shot")
    forward = [(i, i + 1) for i in range(count - 1)]
    backward = [(target, source) for source, target in forward]
    return lax.ppermute(edges, "shot", forward), lax.ppermute(edges, "shot", backward)


def merge_edges(low, high, blocks):
    lane = lax.broadcasted_iota(jnp.int32, low.shape, 1)
    return jnp.where(lane < EDGE * blocks, low, high)


def filter_window(window, fans_ref, mats_ref, times_ref, rows, give):
    pairs = mats_ref.shape[1]
    count, width = segment_plan(rows)

    def trace_step(pair, carry):
        for half in range(2):
            both = jnp.dot(
                window[half], mats_ref[half, pair], preferred_element_type=jnp.float32
            ).astype(jnp.bfloat16)
            cols = slice(half * LANES, (half + 1) * LANES)
            fans_ref[2 * pair, :, cols] = both[:, :LANES]
            fans_ref[2 * pair + 1, :, cols] = both[:, LANES:]
        return carry

    lax.fori_loop(0, pairs, trace_step, 0)

    def time_step(step, carry):
        start = pl.multiple_of(jnp.minimum(step * width, rows - width), 16)
        total = None
        for fan in range(2 * pairs):
            part = jnp.dot(
                times_ref[:width, fan * SPAN : (fan + 1) * SPAN],
                fans_ref[fan, pl.ds(start, SPAN), :],
                preferred_element_type=jnp.float32,
            )
            total = part if total is None else total + part
        give(start, total)
        return carry

    lax.fori_loop(0, count, time_step, 0)


def window_rows(rows):
    count, width = segment_plan(rows)
    return rows - width + SPAN


def pass_cost(rows, tall, blocks, fans, byte_count):
    return pl.CostEstimate(
        flops=1,
        bytes_accessed=1,
        transcendentals=0,
    )


def first_kernel(
    lead, key_ref, x_ref, low_ref, high_ref, mats_ref, times_ref, after_ref, *refs
):
    outs, (window, fans_ref, done, sem) = refs[:-4], refs[-4:]
    step = pl.program_id(0)
    held, tall, rows = x_ref.shape[1], window.shape[1], done.shape[1]
    blocks = done.shape[0]
    slot_cap = outs[0].shape[0]
    merged = merge_edges(low_ref[...], high_ref[...], blocks)
    for half in range(2):
        if lead:
            window[half, :lead, :] = jnp.zeros((lead, 2 * LANES), jnp.bfloat16)
        window[half, lead : lead + held, :LANES] = x_ref[half]
        window[half, lead : lead + held, LANES:] = merged
        if tall > lead + held:
            window[half, lead + held :, :] = jnp.zeros(
                (tall - lead - held, 2 * LANES), jnp.bfloat16
            )

    def give(start, values):
        values = values.astype(jnp.bfloat16)
        for half in range(2):
            done[2 * step + half, pl.ds(start, values.shape[0]), :] = values[
                :, half * LANES : (half + 1) * LANES
            ]

    filter_window(window, fans_ref, mats_ref, times_ref, rows, give)

    for half in range(2):
        block = 2 * step + half
        key = key_ref[block]
        for offset, out_ref in enumerate(outs):

            @pl.when(key // slot_cap == offset)
            def _():
                pltpu.make_async_copy(
                    done.at[block], out_ref.at[key % slot_cap], sem.at[block]
                ).start()

    @pl.when(step == pl.num_programs(0) - 1)
    def _():
        for block in range(blocks):
            pltpu.make_async_copy(done.at[block], outs[0].at[0], sem.at[block]).wait()


def first_pass(keys, owners, traces, edges, edges_at, mats, times, after, start, stop):
    blocks, samples, _ = traces.shape
    fans = 2 * mats.shape[1]
    rows = stop - start
    tall = window_rows(rows)
    begin, end = max(0, start - REACH // 2), min(samples, stop + REACH // 2)
    held = end - begin
    edge_spec = pl.BlockSpec(
        (pl.Element(held), pl.Element(LANES)), lambda i, key: (begin - edges_at, 0)
    )
    sent = jax.ShapeDtypeStruct((blocks // 2, rows, LANES), jnp.bfloat16)
    return pl.pallas_call(
        functools.partial(first_kernel, begin - (start - REACH // 2)),
        grid_spec=pltpu.PrefetchScalarGridSpec(
            num_scalar_prefetch=1,
            grid=(blocks // 2,),
            in_specs=[
                pl.BlockSpec(
                    (pl.Element(2), pl.Element(held), pl.Element(LANES)),
                    lambda i, key: (2 * i, begin, 0),
                ),
                edge_spec,
                edge_spec,
                pl.BlockSpec((2,) + mats.shape[1:], lambda i, key: (i, 0, 0, 0)),
                pl.BlockSpec(times.shape, lambda i, key: (0, 0)),
                pl.BlockSpec(memory_space=pl.ANY),
            ],
            out_specs=[pl.BlockSpec(memory_space=pl.ANY)] * owners,
            scratch_shapes=[
                pltpu.VMEM((2, tall, 2 * LANES), jnp.bfloat16),
                pltpu.VMEM((fans, tall, 2 * LANES), jnp.bfloat16),
                pltpu.VMEM((blocks, rows, LANES), jnp.bfloat16),
                pltpu.SemaphoreType.DMA((blocks,)),
            ],
        ),
        out_shape=[sent] * owners,
        cost_estimate=pass_cost(rows, tall, blocks, fans, 2 * blocks * rows * LANES * 2),
        compiler_params=PARAMS,
        name="first_pass",
    )(keys, traces, *edges, mats, times, after)


def second_kernel(blocks, at, has_past, has_out, *refs):
    refs = list(refs)
    take = lambda: refs.pop(0)
    past = [take() for _ in range(3)] if has_past else None
    now = [take() for _ in range(3)]
    mats_ref, times_ref, _ = take(), take(), take()
    if has_out:
        take()
    out_ref, token_ref, window, fans_ref, done, sem = refs
    token_ref[...] = jnp.zeros_like(token_ref)
    step = pl.program_id(0)
    tall, rows = window.shape[1], done.shape[1]
    lead = REACH if has_past else REACH // 2
    held = now[0].shape[1]
    if has_past:
        old = merge_edges(past[1][...], past[2][...], blocks)
    merged = merge_edges(now[1][...], now[2][...], blocks)
    for half in range(2):
        if has_past:
            window[half, :lead, :LANES] = past[0][half]
            window[half, :lead, LANES:] = old
        else:
            window[half, :lead, :] = jnp.zeros((lead, 2 * LANES), jnp.bfloat16)
        window[half, lead : lead + held, :LANES] = now[0][half]
        window[half, lead : lead + held, LANES:] = merged
        if tall > lead + held:
            window[half, lead + held :, :] = jnp.zeros(
                (tall - lead - held, 2 * LANES), jnp.bfloat16
            )

    def give(start, values):
        for half in range(2):
            done[2 * step + half, pl.ds(start, values.shape[0]), :] = values[
                :, half * LANES : (half + 1) * LANES
            ]

    filter_window(window, fans_ref, mats_ref, times_ref, rows, give)

    def copy(block):
        return pltpu.make_async_copy(
            done.at[block], out_ref.at[block, pl.ds(at, rows), :], sem.at[block]
        )

    for half in range(2):
        copy(2 * step + half).start()

    @pl.when(step == pl.num_programs(0) - 1)
    def _():
        for block in range(blocks):
            copy(block).wait()


def second_pass(blocks, samples, past, now, mats, times, after, out, at, rows):
    fans = 2 * mats.shape[1]
    tall = window_rows(rows)
    specs, operands = [], []
    for group, last in ((past, True), (now, False)):
        if group is None:
            continue
        arrived, low, high = group
        size = REACH if last else arrived.shape[1]
        tail = arrived.shape[1] // size - 1
        specs.append(
            pl.BlockSpec((2, size, LANES), functools.partial(lambda t, i: (i, t, 0), tail))
        )
        operands.append(arrived)
        for edge in (low, high):
            specs.append(pl.BlockSpec((size, LANES), functools.partial(lambda t, i: (t, 0), tail)))
            operands.append(edge)
    specs += [
        pl.BlockSpec((2,) + mats.shape[1:], lambda i: (i, 0, 0, 0)),
        pl.BlockSpec(times.shape, lambda i: (0, 0)),
        pl.BlockSpec(memory_space=pl.ANY),
    ]
    operands += [mats, times, after]
    aliases = {}
    if out is not None:
        specs.append(pl.BlockSpec(memory_space=pl.ANY))
        operands.append(out)
        aliases = {len(operands) - 1: 0}
    return pl.pallas_call(
        functools.partial(second_kernel, blocks, at, past is not None, out is not None),
        grid=(blocks // 2,),
        in_specs=specs,
        out_specs=[
            pl.BlockSpec(memory_space=pl.ANY),
            pl.BlockSpec((8, LANES), lambda i: (0, 0)),
        ],
        scratch_shapes=[
            pltpu.VMEM((2, tall, 2 * LANES), jnp.bfloat16),
            pltpu.VMEM((fans, tall, 2 * LANES), jnp.bfloat16),
            pltpu.VMEM((blocks, rows, LANES), jnp.float32),
            pltpu.SemaphoreType.DMA((blocks,)),
        ],
        out_shape=[
            jax.ShapeDtypeStruct((blocks, samples, LANES), jnp.float32),
            jax.ShapeDtypeStruct((8, LANES), jnp.float32),
        ],
        input_output_aliases=aliases,
        cost_estimate=pass_cost(rows, tall, blocks, fans, 3 * blocks * rows * LANES * 2),
        compiler_params=PARAMS,
        name="second_pass",
    )(*operands)


def per_device(
    traces, first_trace_taps, first_time_taps, second_trace_taps, second_time_taps, dest_row
):
    blocks, samples, _ = traces.shape
    owners = lax.axis_size("rcv")
    me = lax.axis_index("rcv")
    slot_cap = blocks // 2

    target = dest_row[:, 0]
    ids = jnp.arange(blocks, dtype=jnp.int32)

    def ranks(owner):
        return jnp.sum(
            (
                (ids[:, None] > ids[None, :]) & (owner[..., :, None] == owner[..., None, :])
            ).astype(jnp.int32),
            axis=-1,
        )

    def send(values, offset):
        pairs = [(i, (i + offset) % owners) for i in range(owners)]
        return lax.ppermute(values, "rcv", pairs) if offset else values

    owner = target // blocks
    keys = (owner - me + owners) % owners * slot_cap + ranks(owner)

    bounds = chunk_bounds(samples)
    count = len(bounds) - 1
    near = min(samples, bounds[1] + REACH // 2)
    far = bounds[1] - REACH // 2
    edges = swap_edges(first_edges(traces, 0, near))
    mats, times = weights(first_trace_taps, first_time_taps, traces, blocks)

    column = jnp.stack([send(target, offset) for offset in range(owners)])
    place = jnp.arange(owners, dtype=jnp.int32)[:, None] * slot_cap + ranks(column // blocks)
    mine = column[None] == (me * blocks + ids)[:, None, None]
    slots = jnp.sum(jnp.where(mine, place[None], 0), axis=(1, 2))

    def first(step, edges, edges_at, after):
        return first_pass(
            keys, owners, traces, edges, edges_at, mats, times, after,
            bounds[step], bounds[step + 1],
        )

    def exchange(sent, before):
        arrived = []
        for offset, part in enumerate(sent):
            if offset and before is not None:
                part, before[offset] = lax.optimization_barrier((part, before[offset]))
            arrived.append(send(part, offset))
        return arrived

    sent = [first(0, edges, 0, mats)]
    arrived = [exchange(sent[0], None)]
    edges = swap_edges(first_edges(traces, far, samples))
    second_mats, second_times = weights(
        second_trace_taps, second_time_taps, sent[0][0], blocks
    )
    if count > 1:
        sent.append(first(1, edges, far, sent[0][0]))

    out, past, token = None, None, None
    for step in range(count):
        if step + 1 < count:
            arrived.append(exchange(sent[step + 1], arrived[step]))
        after = token if step else sent[-1][0]
        gathered, rims = second_edges(slots, arrived[step], after, blocks)
        now = (gathered, *swap_edges(rims))
        if step + 2 < count:
            sent.append(first(step + 2, edges, far, rims))
        at = max(0, bounds[step] - REACH // 2)
        stop = bounds[step + 1] - REACH // 2 if step + 1 < count else samples
        out, token = second_pass(
            blocks, samples, past, now, second_mats, second_times, sent[-1][0], out, at, stop - at
        )
        past = now
    return out


def solution(mesh):
    in_specs = (P("rcv", None, "shot"), P(), P(), P(), P(), P("rcv", "shot"))
    out_specs = P("rcv", None, "shot")
    return jax.shard_map(
        per_device, mesh=mesh, in_specs=in_specs, out_specs=out_specs, check_vma=False
    )
```

time: 218 us -> 207 us (0.950)
  the two profiles are of different devices: /device:TPU:31 before, /device:TPU:192 now
where the time goes in v1:
time: 207 us; the launch traced here: 206 us
  waiting for transfers between devices  72.2 us (35%)
  starting transfers between devices  69.3 us (33%)
  Pallas kernels  57.8 us (28%)
  other arithmetic  3.77 us (2%)
    ppermute x6, waiting for transfers between devices, swap_edges(): lax.ppermute(edges, 'shot', forward)  50.5 us
    ppermute x6, starting transfers between devices, swap_edges(): lax.ppermute(edges, 'shot', backward)  34.2 us
    pallas_call x4, Pallas kernels, first_pass(): pl.pallas_call(functools.partial(first_kernel, begin - (start - REACH //...  24.9 us
    pallas_call x4, Pallas kernels, second_pass(): pl.pallas_call(functools.partial(second_kernel, blocks, at, past is not N...  23.3 us
    ppermute x15, starting transfers between devices, send(): return lax.ppermute(values, 'rcv', pairs) if offset else values  22.2 us
    ppermute x15, waiting for transfers between devices, send(): return lax.ppermute(values, 'rcv', pairs) if offset else values  20.2 us
    ppermute x6, starting transfers between devices, swap_edges(): lax.ppermute(edges, 'shot', forward)  13 us
    pallas_call x4, Pallas kernels, second_edges(): pl.pallas_call(second_edges_kernel, grid_spec=pltpu.PrefetchScalarGridSpe...  6.73 us
  transfers between devices with their start and end apart: 27, of which 8 were waited for; matrix products, arithmetic and copies ran while one was open for 2% of the time, Pallas kernels for 24%

profile of v1, /device:TPU:192, one launch (start us, length us, event | category | flops | bytes accessed | tf_op | source)
XLA Modules:
  0.0 205.6 jit_solution(1968219799397767347)
XLA Ops:
  0.0 1.6 copy-done
  1.6 0.9 first_edges.3
  2.5 6.5 %collective-permute-start.6 = (bf16[416,128]{1,0:T(8,128)(2,1)}, bf16[416,128]{1,0:T(8,128)(2,1)S(1)}, u32[]{:S(2)}, u32[]{:S(2)}) collective-permute-start(bf16[416,128]{1,0:T(8,128)(2,1)} %first_edges.3), channel_id=1, source_target_pairs={{1,0},{2,1},{3,2},{4,3},{5,4},{6,5},{7,6},{8,7},{9,8},{10,9},{11,1... | collective-permute-start | bytes 319496 | tf_op jit(solution)/shard_map/ppermute | solution.py:179
  9.0 1.9 collective-permute-start.5
  11.0 1.0 first_edges.2
  12.0 11.8 %collective-permute-start.4 = (bf16[1648,128]{1,0:T(8,128)(2,1)S(1)}, bf16[1648,128]{1,0:T(8,128)(2,1)S(1)}, u32[]{:S(2)}, u32[]{:S(2)}) collective-permute-start(bf16[1648,128]{1,0:T(8,128)(2,1)S(1)} %first_edges.2), channel_id=1, source_target_pairs={{1,0},{2,1},{3,2},{4,3},{5,4},{6,5},{7,6},{8,7},{9,8},{10,9},{11,1... | collective-permute-start | bytes 1265672 | tf_op jit(solution)/shard_map/ppermute | solution.py:179
  23.8 1.9 collective-permute-start.3
  25.7 0.2 collective-permute-start.2
  25.9 0.6 and_select_fusion.2
  26.5 0.5 fusion.5
  27.0 0.5 iota_multiply_fusion
  27.5 0.1 rev.6
  27.6 0.8 convert_reduce_fusion.1
  28.5 0.1 rev.7
  28.5 0.1 pad_slice_fusion.1
  28.6 0.1 pad_maximum_fusion.trace_ref
  28.7 0.5 weights.2
  29.2 4.3 %collective-permute-start.1 = (s32[4]{0:T(128)S(1)}, s32[4]{0:T(128)S(1)}, u32[]{:S(2)}, u32[]{:S(2)}) collective-permute-start(s32[4]{0:T(128)S(1)} %bitcast.11), channel_id=1, source_target_pairs={{0,128},{64,192},{128,0},{192,64},{1,129},{65,193},{129,1},{193,65... | collective-permute-start | bytes 56 | tf_op jit(solution)/shard_map/ppermute | solution.py:445
  33.5 0.0 collective-permute-done.5.low_ref
  33.5 5.2 %first_pass.4 = (bf16[2,384,128]{2,1,0:T(8,128)(2,1)S(1)}, bf16[2,384,128]{2,1,0:T(8,128)(2,1)S(1)}, bf16[2,384,128]{2,1,0:T(8,128)(2,1)S(1)}, bf16[2,384,128]{2,1,0:T(8,128)(2,1)S(1)}) custom-call(s32[4]{0:T(128)S(1)} %fusion.3.key_ref, bf16[4,2000,128]{2,1,0:T(8,128)(2,1)S(1)} %copy-done.1, bf16[416,128]{1,0:T(8,128)(2,1)S(1)} %collective-permute-done.5.low_ref, ...), custom_call_target="tpu_custom_call" | custom-call | flops 1 | bytes 1 | tf_op jit(solution)/shard_map/first_pass/pallas_call | solution.py:288
  38.7 1.6 collective-permute-start.7
  40.4 1.9 collective-permute-start.8
  42.3 2.5 %collective-permute-start.9 = (bf16[2,384,128]{2,1,0:T(8,128)(2,1)S(1)}, bf16[2,384,128]{2,1,0:T(8,128)(2,1)S(1)}, u32[]{:S(2)}, u32[]{:S(2)}) collective-permute-start(bf16[2,384,128]{2,1,0:T(8,128)(2,1)S(1)} %get-tuple-element.68), channel_id=1, source_target_pairs={{0,192},{64,0},{128,64},{192,128},{1,193},{65,1},{129,65},{193,129... | collective-permute-start | bytes 589832 | tf_op jit(solution)/shard_map/ppermute | solution.py:445
  44.8 0.6 pad_add_fusion
  45.5 0.2 convert_reduce_fusion
  45.7 5.7 %collective-permute-done.3.low_ref = bf16[1648,128]{1,0:T(8,128)(2,1)S(1)} collective-permute-done((bf16[1648,128]{1,0:T(8,128)(2,1)S(1)}, bf16[1648,128]{1,0:T(8,128)(2,1)S(1)}, u32[]{:S(2)}, u32[]{:S(2)}) %collective-permute-start.3) | collective-permute-done | bytes 421920 | tf_op jit(solution)/shard_map/ppermute | solution.py:179
  51.4 6.8 %first_pass.5 = (bf16[2,576,128]{2,1,0:T(8,128)(2,1)S(1)}, bf16[2,576,128]{2,1,0:T(8,128)(2,1)S(1)}, bf16[2,576,128]{2,1,0:T(8,128)(2,1)S(1)}, bf16[2,576,128]{2,1,0:T(8,128)(2,1)S(1)}) custom-call(s32[4]{0:T(128)S(1)} %fusion.3.key_ref, bf16[4,2000,128]{2,1,0:T(8,128)(2,1)S(1)} %copy-done.1, bf16[1648,128]{1,0:T(8,128)(2,1)S(1)} %collective-permute-done.3.low_ref, ...), custom_call_target="tpu_custom_call" | custom-call | flops 1 | bytes 1 | tf_op jit(solution)/shard_map/first_pass/pallas_call | solution.py:288
  58.2 0.0 copy-start.3
  58.2 4.2 %collective-permute-done.9.refs_3_ = bf16[2,384,128]{2,1,0:T(8,128)(2,1)S(1)} collective-permute-done((bf16[2,384,128]{2,1,0:T(8,128)(2,1)S(1)}, bf16[2,384,128]{2,1,0:T(8,128)(2,1)S(1)}, u32[]{:S(2)}, u32[]{:S(2)}) %collective-permute-start.9) | collective-permute-done | bytes 196640 | tf_op jit(solution)/shard_map/ppermute | solution.py:445
  62.4 2.5 %collective-permute-start.12 = (bf16[2,576,128]{2,1,0:T(8,128)(2,1)S(1)}, bf16[2,576,128]{2,1,0:T(8,128)(2,1)S(1)}, u32[]{:S(2)}, u32[]{:S(2)}) collective-permute-start(bf16[2,576,128]{2,1,0:T(8,128)(2,1)S(1)} %get-tuple-element.80), channel_id=1, source_target_pairs={{0,192},{64,0},{128,64},{192,128},{1,193},{65,1},{129,65},{193,129... | collective-permute-start | bytes 884744 | tf_op jit(solution)/shard_map/ppermute | solution.py:445
  64.9 1.5 collective-permute-start.10
  66.4 0.1 broadcast_add_fusion
  66.4 0.2 select_reduce_fusion.slot_ref
  66.7 1.5 second_edges.4
  68.1 6.8 %first_pass.6 = (bf16[2,576,128]{2,1,0:T(8,128)(2,1)S(1)}, bf16[2,576,128]{2,1,0:T(8,128)(2,1)S(1)}, bf16[2,576,128]{2,1,0:T(8,128)(2,1)S(1)}, bf16[2,576,128]{2,1,0:T(8,128)(2,1)S(1)}) custom-call(s32[4]{0:T(128)S(1)} %fusion.3.key_ref, bf16[4,2000,128]{2,1,0:T(8,128)(2,1)S(1)} %copy-done.1, bf16[1648,128]{1,0:T(8,128)(2,1)S(1)} %collective-permute-done.3.low_ref, ...), custom_call_target="tpu_custom_call" | custom-call | flops 1 | bytes 1 | tf_op jit(solution)/shard_map/first_pass/pallas_call | solution.py:288
  74.9 16.0 %collective-permute-done.10.refs_1_ = bf16[2,576,128]{2,1,0:T(8,128)(2,1)S(1)} collective-permute-done((bf16[2,576,128]{2,1,0:T(8,128)(2,1)S(1)}, bf16[2,576,128]{2,1,0:T(8,128)(2,1)S(1)}, u32[]{:S(2)}, u32[]{:S(2)}) %collective-permute-start.10) | collective-permute-done | bytes 294944 | tf_op jit(solution)/shard_map/ppermute | solution.py:445
  90.9 1.4 collective-permute-start.16
  92.3 2.0 collective-permute-start.15
  94.4 0.1 pad_slice_fusion
  94.4 10.1 %collective-permute-start.14 = (bf16[384,128]{1,0:T(8,128)(2,1)S(1)}, bf16[384,128]{1,0:T(8,128)(2,1)S(1)}, u32[]{:S(2)}, u32[]{:S(2)}) collective-permute-start(bf16[384,128]{1,0:T(8,128)(2,1)S(1)} %get-tuple-element.71.after_ref), channel_id=1, source_target_pairs={{1,0},{2,1},{3,2},{4,3},{5,4},{6,5},{7,6},{8,7},{9,8},{10,9},{11,1... | collective-permute-start | bytes 294920 | tf_op jit(solution)/shard_map/ppermute | solution.py:179
  104.6 1.9 collective-permute-start.13
  106.5 0.1 pad_maximum_fusion.1.trace_ref
  106.6 0.5 weights.3
  107.1 11.7 %collective-permute-done.13.refs_1_ = bf16[384,128]{1,0:T(8,128)(2,1)S(1)} collective-permute-done((bf16[384,128]{1,0:T(8,128)(2,1)S(1)}, bf16[384,128]{1,0:T(8,128)(2,1)S(1)}, u32[]{:S(2)}, u32[]{:S(2)}) %collective-permute-start.13) | collective-permute-done | bytes 98336 | tf_op jit(solution)/shard_map/ppermute | solution.py:179
  118.8 4.7 %second_pass.4 = (f32[4,2000,128]{2,1,0:T(8,128)}, f32[8,128]{1,0:T(8,128)S(1)}) custom-call(bf16[4,384,128]{2,1,0:T(8,128)(2,1)S(1)} %get-tuple-element.82.refs_0_, bf16[384,128]{1,0:T(8,128)(2,1)S(1)} %collective-permute-done.13.refs_1_, bf16[384,128]{1,0:T(8,128)(2,1)S(1)} %collective-permute-done.14.refs_2_, ...), custom_call_target="tpu_custom_call" | custom-call | flops 1 | bytes 1 | tf_op jit(solution)/shard_map/second_pass/pallas_call | solution.py:399
  123.5 1.8 second_edges.5
  125.3 1.9 collective-permute-start.19
  127.2 2.4 %collective-permute-start.18 = (bf16[576,128]{1,0:T(8,128)(2,1)S(1)}, bf16[576,128]{1,0:T(8,128)(2,1)S(1)}, u32[]{:S(2)}, u32[]{:S(2)}) collective-permute-start(bf16[576,128]{1,0:T(8,128)(2,1)S(1)} %get-tuple-element.86.after_ref), channel_id=1, source_target_pairs={{0,1},{1,2},{2,3},{3,4},{4,5},{5,6},{6,7},{7,8},{8,9},{9,10},{10,1... | collective-permute-start | bytes 442376 | tf_op jit(solution)/shard_map/ppermute | solution.py:179
  129.6 6.2 %first_pass.7 = (bf16[2,464,128]{2,1,0:T(8,128)(2,1)S(1)}, bf16[2,464,128]{2,1,0:T(8,128)(2,1)S(1)}, bf16[2,464,128]{2,1,0:T(8,128)(2,1)S(1)}, bf16[2,464,128]{2,1,0:T(8,128)(2,1)S(1)}) custom-call(s32[4]{0:T(128)S(1)} %fusion.3.key_ref, bf16[4,2000,128]{2,1,0:T(8,128)(2,1)S(1)} %copy-done.1, bf16[1648,128]{1,0:T(8,128)(2,1)S(1)} %collective-permute-done.3.low_ref, ...), custom_call_target="tpu_custom_call" | custom-call | flops 1 | bytes 1 | tf_op jit(solution)/shard_map/first_pass/pallas_call | solution.py:288
  135.8 0.9 collective-permute-start.24
  136.7 3.4 %collective-permute-start.23 = (bf16[2,464,128]{2,1,0:T(8,128)(2,1)S(1)}, bf16[2,464,128]{2,1,0:T(8,128)(2,1)S(1)}, u32[]{:S(2)}, u32[]{:S(2)}) collective-permute-start(bf16[2,464,128]{2,1,0:T(8,128)(2,1)S(1)} %get-tuple-element.103), channel_id=1, source_target_pairs={{0,128},{64,192},{128,0},{192,64},{1,129},{65,193},{129,1},{193,65... | collective-permute-start | bytes 712712 | tf_op jit(solution)/shard_map/ppermute | solution.py:445
  140.1 9.3 %collective-permute-done.18.refs_4_.refs_1_ = bf16[576,128]{1,0:T(8,128)(2,1)S(1)} collective-permute-done((bf16[576,128]{1,0:T(8,128)(2,1)S(1)}, bf16[576,128]{1,0:T(8,128)(2,1)S(1)}, u32[]{:S(2)}, u32[]{:S(2)}) %collective-permute-start.18) | collective-permute-done | bytes 147488 | tf_op jit(solution)/shard_map/ppermute | solution.py:179
  149.4 6.1 %second_pass.5 = (f32[4,2000,128]{2,1,0:T(8,128)}, f32[8,128]{1,0:T(8,128)S(1)}) custom-call(bf16[4,384,128]{2,1,0:T(8,128)(2,1)S(1)} %get-tuple-element.82.refs_0_, bf16[384,128]{1,0:T(8,128)(2,1)S(1)} %collective-permute-done.13.refs_1_, bf16[384,128]{1,0:T(8,128)(2,1)S(1)} %collective-permute-done.14.refs_2_, ...), custom_call_target="tpu_custom_call", output_to_operand_aliasing={{0}: (9, {})} | custom-call | flops 1 | bytes 1 | tf_op jit(solution)/shard_map/second_pass/pallas_call | solution.py:399
  155.5 1.8 second_edges.6
  157.3 1.9 collective-permute-start.21
  159.2 2.4 %collective-permute-start.20 = (bf16[576,128]{1,0:T(8,128)(2,1)S(1)}, bf16[576,128]{1,0:T(8,128)(2,1)S(1)}, u32[]{:S(2)}, u32[]{:S(2)}) collective-permute-start(bf16[576,128]{1,0:T(8,128)(2,1)S(1)} %get-tuple-element.101), channel_id=1, source_target_pairs={{0,1},{1,2},{2,3},{3,4},{4,5},{5,6},{6,7},{7,8},{8,9},{9,10},{10,1... | collective-permute-start | bytes 442376 | tf_op jit(solution)/shard_map/ppermute | solution.py:179
  161.6 1.4 collective-permute-done.21.refs_5_.refs_2_
  163.0 11.9 %collective-permute-done.20.refs_4_.refs_1_ = bf16[576,128]{1,0:T(8,128)(2,1)S(1)} collective-permute-done((bf16[576,128]{1,0:T(8,128)(2,1)S(1)}, bf16[576,128]{1,0:T(8,128)(2,1)S(1)}, u32[]{:S(2)}, u32[]{:S(2)}) %collective-permute-start.20) | collective-permute-done | bytes 147488 | tf_op jit(solution)/shard_map/ppermute | solution.py:179
  175.0 6.1 %second_pass.6 = (f32[4,2000,128]{2,1,0:T(8,128)}, f32[8,128]{1,0:T(8,128)S(1)}) custom-call(bf16[4,576,128]{2,1,0:T(8,128)(2,1)S(1)} %get-tuple-element.96.refs_3_.refs_0_, bf16[576,128]{1,0:T(8,128)(2,1)S(1)} %collective-permute-done.18.refs_4_.refs_1_, ...), custom_call_target="tpu_custom_call", output_to_operand_aliasing={{0}: (9, {})} | custom-call | flops 1 | bytes 1 | tf_op jit(solution)/shard_map/second_pass/pallas_call | solution.py:399
  181.1 1.7 second_edges.7
  182.8 1.9 collective-permute-start.26
  184.8 2.4 %collective-permute-start.25 = (bf16[464,128]{1,0:T(8,128)(2,1)S(1)}, bf16[464,128]{1,0:T(8,128)(2,1)S(1)}, u32[]{:S(2)}, u32[]{:S(2)}) collective-permute-start(bf16[464,128]{1,0:T(8,128)(2,1)S(1)} %get-tuple-element.108), channel_id=1, source_target_pairs={{0,1},{1,2},{2,3},{3,4},{4,5},{5,6},{6,7},{7,8},{8,9},{9,10},{10,1... | collective-permute-start | bytes 356360 | tf_op jit(solution)/shard_map/ppermute | solution.py:179
  187.2 11.9 %collective-permute-done.25.refs_4_ = bf16[464,128]{1,0:T(8,128)(2,1)S(1)} collective-permute-done((bf16[464,128]{1,0:T(8,128)(2,1)S(1)}, bf16[464,128]{1,0:T(8,128)(2,1)S(1)}, u32[]{:S(2)}, u32[]{:S(2)}) %collective-permute-start.25) | collective-permute-done | bytes 118816 | tf_op jit(solution)/shard_map/ppermute | solution.py:179
  199.0 6.4 %second_pass.7 = (f32[4,2000,128]{2,1,0:T(8,128)}, f32[8,128]{1,0:T(8,128)}) custom-call(bf16[4,576,128]{2,1,0:T(8,128)(2,1)S(1)} %get-tuple-element.100.refs_3_.refs_0_, bf16[576,128]{1,0:T(8,128)(2,1)S(1)} %collective-permute-done.20.refs_4_.refs_1_, bf16[576,128]{1,0:T(8,128)(2,1)S(1)} %collective-permute-done.21.refs_5_.refs_2_, ...), custom_call_target="tpu_custom_call", output_to_operand_aliasing={{0}: (9, {})} | custom-call | flops 1 | bytes 1 | tf_op jit(solution)/shard_map/second_pass/pallas_call | solution.py:399
  (45 shorter events, 0.1 us)
Async XLA Ops:
  0.0 1.6 copy-start
  1.6 24.1 %copy-start.6 = (s32[4,1]{0,1:T(1,128)S(1)}, s32[4,1]{0,1:T(1,128)}, u32[]{:S(2)}) copy-start(s32[4,1]{0,1:T(1,128)} %param.11) | copy-start | bytes 52
  1.6 25.9 %copy-start.4 = (bf16[8,16]{1,0:T(8,128)(2,1)S(1)}, bf16[8,16]{1,0:T(8,128)(2,1)}, u32[]{:S(2)}) copy-start(bf16[8,16]{1,0:T(8,128)(2,1)} %param.7) | copy-start | bytes 772
  1.6 26.9 %copy-start.5 = (bf16[8,16]{1,0:T(8,128)(2,1)S(1)}, bf16[8,16]{1,0:T(8,128)(2,1)}, u32[]{:S(2)}) copy-start(bf16[8,16]{1,0:T(8,128)(2,1)} %param.9) | copy-start | bytes 772
  1.6 27.0 %copy-start.2 = (bf16[8,64]{1,0:T(8,128)(2,1)S(1)}, bf16[8,64]{1,0:T(8,128)(2,1)}, u32[]{:S(2)}) copy-start(bf16[8,64]{1,0:T(8,128)(2,1)} %param.8) | copy-start | bytes 3076
  1.6 27.1 %copy-start.1 = (bf16[4,2000,128]{2,1,0:T(8,128)(2,1)S(1)}, bf16[4,2000,128]{2,1,0:T(8,128)(2,1)}, u32[]{:S(2)}) copy-start(bf16[4,2000,128]{2,1,0:T(8,128)(2,1)} %x_ref.11) | copy-start | bytes 6144004
  2.5 26.7 %collective-permute-start.6 = (bf16[416,128]{1,0:T(8,128)(2,1)}, bf16[416,128]{1,0:T(8,128)(2,1)S(1)}, u32[]{:S(2)}, u32[]{:S(2)}) collective-permute-start(bf16[416,128]{1,0:T(8,128)(2,1)} %first_edges.3), channel_id=1, source_target_pairs={{1,0},{2,1},{3,2},{4,3},{5,4},{6,5},{7,6},{8,7},{9,8},{10,9},{11,1... | collective-permute-start | bytes 319496 | tf_op jit(solution)/shard_map/ppermute | solution.py:179
  9.0 24.4 %collective-permute-start.5 = (bf16[416,128]{1,0:T(8,128)(2,1)}, bf16[416,128]{1,0:T(8,128)(2,1)S(1)}, u32[]{:S(2)}, u32[]{:S(2)}) collective-permute-start(bf16[416,128]{1,0:T(8,128)(2,1)} %first_edges.3), channel_id=1, source_target_pairs={{0,1},{1,2},{2,3},{3,4},{4,5},{5,6},{6,7},{7,8},{8,9},{9,10},{10,1... | collective-permute-start | bytes 319496 | tf_op jit(solution)/shard_map/ppermute | solution.py:179
  12.0 33.7 %collective-permute-start.4 = (bf16[1648,128]{1,0:T(8,128)(2,1)S(1)}, bf16[1648,128]{1,0:T(8,128)(2,1)S(1)}, u32[]{:S(2)}, u32[]{:S(2)}) collective-permute-start(bf16[1648,128]{1,0:T(8,128)(2,1)S(1)} %first_edges.2), channel_id=1, source_target_pairs={{1,0},{2,1},{3,2},{4,3},{5,4},{6,5},{7,6},{8,7},{9,8},{10,9},{11,1... | collective-permute-start | bytes 1265672 | tf_op jit(solution)/shard_map/ppermute | solution.py:179
  23.8 27.6 %collective-permute-start.3 = (bf16[1648,128]{1,0:T(8,128)(2,1)S(1)}, bf16[1648,128]{1,0:T(8,128)(2,1)S(1)}, u32[]{:S(2)}, u32[]{:S(2)}) collective-permute-start(bf16[1648,128]{1,0:T(8,128)(2,1)S(1)} %first_edges.2), channel_id=1, source_target_pairs={{0,1},{1,2},{2,3},{3,4},{4,5},{5,6},{6,7},{7,8},{8,9},{9,10},{10,1... | collective-permute-start | bytes 1265672 | tf_op jit(solution)/shard_map/ppermute | solution.py:179
  25.7 13.0 %collective-permute-start.2 = (s32[4]{0:T(128)S(1)}, s32[4]{0:T(128)}, u32[]{:S(2)}, u32[]{:S(2)}) collective-permute-start(s32[4]{0:T(128)S(1)} %bitcast.10), channel_id=1, source_target_pairs={{0,192},{64,0},{128,64},{192,128},{1,193},{65,1},{129,65},{193,129... | collective-permute-start | bytes 56 | tf_op jit(solution)/shard_map/ppermute | solution.py:445
  29.2 11.1 %collective-permute-start.1 = (s32[4]{0:T(128)S(1)}, s32[4]{0:T(128)S(1)}, u32[]{:S(2)}, u32[]{:S(2)}) collective-permute-start(s32[4]{0:T(128)S(1)} %bitcast.11), channel_id=1, source_target_pairs={{0,128},{64,192},{128,0},{192,64},{1,129},{65,193},{129,1},{193,65... | collective-permute-start | bytes 56 | tf_op jit(solution)/shard_map/ppermute | solution.py:445
  33.5 8.8 %collective-permute-start = (s32[4]{0:T(128)S(1)}, s32[4]{0:T(128)S(1)}, u32[]{:S(2)}, u32[]{:S(2)}) collective-permute-start(s32[4]{0:T(128)S(1)} %bitcast.12), channel_id=1, source_target_pairs={{0,64},{64,128},{128,192},{192,0},{1,65},{65,129},{129,193},{193,1... | collective-permute-start | bytes 56 | tf_op jit(solution)/shard_map/ppermute | solution.py:445
  38.7 27.6 %copy-start.7 = (s32[4]{0:T(128)S(1)}, s32[4]{0:T(128)}, u32[]{:S(2)}) copy-start(s32[4]{0:T(128)} %iota_multiply_fusion) | copy-start | bytes 52
  38.7 19.5 %collective-permute-start.7 = (bf16[2,384,128]{2,1,0:T(8,128)(2,1)S(1)}, bf16[2,384,128]{2,1,0:T(8,128)(2,1)S(1)}, u32[]{:S(2)}, u32[]{:S(2)}) collective-permute-start(bf16[2,384,128]{2,1,0:T(8,128)(2,1)S(1)} %get-tuple-element.62), channel_id=1, source_target_pairs={{0,64},{64,128},{128,192},{192,0},{1,65},{65,129},{129,193},{193,1... | collective-permute-start | bytes 589832 | tf_op jit(solution)/shard_map/ppermute | solution.py:445
  40.4 17.8 %collective-permute-start.8 = (bf16[2,384,128]{2,1,0:T(8,128)(2,1)S(1)}, bf16[2,384,128]{2,1,0:T(8,128)(2,1)S(1)}, u32[]{:S(2)}, u32[]{:S(2)}) collective-permute-start(bf16[2,384,128]{2,1,0:T(8,128)(2,1)S(1)} %get-tuple-element.65), channel_id=1, source_target_pairs={{0,128},{64,192},{128,0},{192,64},{1,129},{65,193},{129,1},{193,65... | collective-permute-start | bytes 589832 | tf_op jit(solution)/shard_map/ppermute | solution.py:445
  42.3 20.1 %collective-permute-start.9 = (bf16[2,384,128]{2,1,0:T(8,128)(2,1)S(1)}, bf16[2,384,128]{2,1,0:T(8,128)(2,1)S(1)}, u32[]{:S(2)}, u32[]{:S(2)}) collective-permute-start(bf16[2,384,128]{2,1,0:T(8,128)(2,1)S(1)} %get-tuple-element.68), channel_id=1, source_target_pairs={{0,192},{64,0},{128,64},{192,128},{1,193},{65,1},{129,65},{193,129... | collective-permute-start | bytes 589832 | tf_op jit(solution)/shard_map/ppermute | solution.py:445
  58.2 36.3 %copy-start.3 = (bf16[8,64]{1,0:T(8,128)(2,1)S(1)}, bf16[8,64]{1,0:T(8,128)(2,1)}, u32[]{:S(2)}) copy-start(bf16[8,64]{1,0:T(8,128)(2,1)} %param.10) | copy-start | bytes 3076
  62.4 28.5 %collective-permute-start.12 = (bf16[2,576,128]{2,1,0:T(8,128)(2,1)S(1)}, bf16[2,576,128]{2,1,0:T(8,128)(2,1)S(1)}, u32[]{:S(2)}, u32[]{:S(2)}) collective-permute-start(bf16[2,576,128]{2,1,0:T(8,128)(2,1)S(1)} %get-tuple-element.80), channel_id=1, source_target_pairs={{0,192},{64,0},{128,64},{192,128},{1,193},{65,1},{129,65},{193,129... | collective-permute-start | bytes 884744 | tf_op jit(solution)/shard_map/ppermute | solution.py:445
  64.9 26.0 %collective-permute-start.11 = (bf16[2,576,128]{2,1,0:T(8,128)(2,1)S(1)}, bf16[2,576,128]{2,1,0:T(8,128)(2,1)S(1)}, u32[]{:S(2)}, u32[]{:S(2)}) collective-permute-start(bf16[2,576,128]{2,1,0:T(8,128)(2,1)S(1)} %get-tuple-element.77), channel_id=1, source_target_pairs={{0,128},{64,192},{128,0},{192,64},{1,129},{65,193},{129,1},{193,65... | collective-permute-start | bytes 884744 | tf_op jit(solution)/shard_map/ppermute | solution.py:445
  64.9 26.0 %collective-permute-start.10 = (bf16[2,576,128]{2,1,0:T(8,128)(2,1)S(1)}, bf16[2,576,128]{2,1,0:T(8,128)(2,1)S(1)}, u32[]{:S(2)}, u32[]{:S(2)}) collective-permute-start(bf16[2,576,128]{2,1,0:T(8,128)(2,1)S(1)} %get-tuple-element.74), channel_id=1, source_target_pairs={{0,64},{64,128},{128,192},{192,0},{1,65},{65,129},{129,193},{193,1... | collective-permute-start | bytes 884744 | tf_op jit(solution)/shard_map/ppermute | solution.py:445
  90.9 44.9 %collective-permute-start.17 = (bf16[2,576,128]{2,1,0:T(8,128)(2,1)S(1)}, bf16[2,576,128]{2,1,0:T(8,128)(2,1)S(1)}, u32[]{:S(2)}, u32[]{:S(2)}) collective-permute-start(bf16[2,576,128]{2,1,0:T(8,128)(2,1)S(1)} %get-tuple-element.94), channel_id=1, source_target_pairs={{0,192},{64,0},{128,64},{192,128},{1,193},{65,1},{129,65},{193,129... | collective-permute-start | bytes 884744 | tf_op jit(solution)/shard_map/ppermute | solution.py:445
  90.9 44.9 %collective-permute-start.16 = (bf16[2,576,128]{2,1,0:T(8,128)(2,1)S(1)}, bf16[2,576,128]{2,1,0:T(8,128)(2,1)S(1)}, u32[]{:S(2)}, u32[]{:S(2)}) collective-permute-start(bf16[2,576,128]{2,1,0:T(8,128)(2,1)S(1)} %get-tuple-element.91), channel_id=1, source_target_pairs={{0,128},{64,192},{128,0},{192,64},{1,129},{65,193},{129,1},{193,65... | collective-permute-start | bytes 884744 | tf_op jit(solution)/shard_map/ppermute | solution.py:445
  92.3 43.5 %collective-permute-start.15 = (bf16[2,576,128]{2,1,0:T(8,128)(2,1)S(1)}, bf16[2,576,128]{2,1,0:T(8,128)(2,1)S(1)}, u32[]{:S(2)}, u32[]{:S(2)}) collective-permute-start(bf16[2,576,128]{2,1,0:T(8,128)(2,1)S(1)} %get-tuple-element.88), channel_id=1, source_target_pairs={{0,64},{64,128},{128,192},{192,0},{1,65},{65,129},{129,193},{193,1... | collective-permute-start | bytes 884744 | tf_op jit(solution)/shard_map/ppermute | solution.py:445
  94.4 12.6 %collective-permute-start.14 = (bf16[384,128]{1,0:T(8,128)(2,1)S(1)}, bf16[384,128]{1,0:T(8,128)(2,1)S(1)}, u32[]{:S(2)}, u32[]{:S(2)}) collective-permute-start(bf16[384,128]{1,0:T(8,128)(2,1)S(1)} %get-tuple-element.71.after_ref), channel_id=1, source_target_pairs={{1,0},{2,1},{3,2},{4,3},{5,4},{6,5},{7,6},{8,7},{9,8},{10,9},{11,1... | collective-permute-start | bytes 294920 | tf_op jit(solution)/shard_map/ppermute | solution.py:179
  104.6 14.2 %collective-permute-start.13 = (bf16[384,128]{1,0:T(8,128)(2,1)S(1)}, bf16[384,128]{1,0:T(8,128)(2,1)S(1)}, u32[]{:S(2)}, u32[]{:S(2)}) collective-permute-start(bf16[384,128]{1,0:T(8,128)(2,1)S(1)} %get-tuple-element.71.after_ref), channel_id=1, source_target_pairs={{0,1},{1,2},{2,3},{3,4},{4,5},{5,6},{6,7},{7,8},{8,9},{9,10},{10,1... | collective-permute-start | bytes 294920 | tf_op jit(solution)/shard_map/ppermute | solution.py:179
  125.3 14.8 %collective-permute-start.19 = (bf16[576,128]{1,0:T(8,128)(2,1)S(1)}, bf16[576,128]{1,0:T(8,128)(2,1)S(1)}, u32[]{:S(2)}, u32[]{:S(2)}) collective-permute-start(bf16[576,128]{1,0:T(8,128)(2,1)S(1)} %get-tuple-element.86.after_ref), channel_id=1, source_target_pairs={{1,0},{2,1},{3,2},{4,3},{5,4},{6,5},{7,6},{8,7},{9,8},{10,9},{11,1... | collective-permute-start | bytes 442376 | tf_op jit(solution)/shard_map/ppermute | solution.py:179
  127.2 22.2 %collective-permute-start.18 = (bf16[576,128]{1,0:T(8,128)(2,1)S(1)}, bf16[576,128]{1,0:T(8,128)(2,1)S(1)}, u32[]{:S(2)}, u32[]{:S(2)}) collective-permute-start(bf16[576,128]{1,0:T(8,128)(2,1)S(1)} %get-tuple-element.86.after_ref), channel_id=1, source_target_pairs={{0,1},{1,2},{2,3},{3,4},{4,5},{5,6},{6,7},{7,8},{8,9},{9,10},{10,1... | collective-permute-start | bytes 442376 | tf_op jit(solution)/shard_map/ppermute | solution.py:179
  135.8 45.2 %collective-permute-start.24 = (bf16[2,464,128]{2,1,0:T(8,128)(2,1)S(1)}, bf16[2,464,128]{2,1,0:T(8,128)(2,1)S(1)}, u32[]{:S(2)}, u32[]{:S(2)}) collective-permute-start(bf16[2,464,128]{2,1,0:T(8,128)(2,1)S(1)} %get-tuple-element.104), channel_id=1, source_target_pairs={{0,192},{64,0},{128,64},{192,128},{1,193},{65,1},{129,65},{193,129... | collective-permute-start | bytes 712712 | tf_op jit(solution)/shard_map/ppermute | solution.py:445
  136.7 44.4 %collective-permute-start.23 = (bf16[2,464,128]{2,1,0:T(8,128)(2,1)S(1)}, bf16[2,464,128]{2,1,0:T(8,128)(2,1)S(1)}, u32[]{:S(2)}, u32[]{:S(2)}) collective-permute-start(bf16[2,464,128]{2,1,0:T(8,128)(2,1)S(1)} %get-tuple-element.103), channel_id=1, source_target_pairs={{0,128},{64,192},{128,0},{192,64},{1,129},{65,193},{129,1},{193,65... | collective-permute-start | bytes 712712 | tf_op jit(solution)/shard_map/ppermute | solution.py:445
  140.1 41.0 %collective-permute-start.22 = (bf16[2,464,128]{2,1,0:T(8,128)(2,1)S(1)}, bf16[2,464,128]{2,1,0:T(8,128)(2,1)S(1)}, u32[]{:S(2)}, u32[]{:S(2)}) collective-permute-start(bf16[2,464,128]{2,1,0:T(8,128)(2,1)S(1)} %get-tuple-element.102), channel_id=1, source_target_pairs={{0,64},{64,128},{128,192},{192,0},{1,65},{65,129},{129,193},{193,1... | collective-permute-start | bytes 712712 | tf_op jit(solution)/shard_map/ppermute | solution.py:445
  157.3 5.7 %collective-permute-start.21 = (bf16[576,128]{1,0:T(8,128)(2,1)S(1)}, bf16[576,128]{1,0:T(8,128)(2,1)S(1)}, u32[]{:S(2)}, u32[]{:S(2)}) collective-permute-start(bf16[576,128]{1,0:T(8,128)(2,1)S(1)} %get-tuple-element.101), channel_id=1, source_target_pairs={{1,0},{2,1},{3,2},{4,3},{5,4},{6,5},{7,6},{8,7},{9,8},{10,9},{11,1... | collective-permute-start | bytes 442376 | tf_op jit(solution)/shard_map/ppermute | solution.py:179
  159.2 15.8 %collective-permute-start.20 = (bf16[576,128]{1,0:T(8,128)(2,1)S(1)}, bf16[576,128]{1,0:T(8,128)(2,1)S(1)}, u32[]{:S(2)}, u32[]{:S(2)}) collective-permute-start(bf16[576,128]{1,0:T(8,128)(2,1)S(1)} %get-tuple-element.101), channel_id=1, source_target_pairs={{0,1},{1,2},{2,3},{3,4},{4,5},{5,6},{6,7},{7,8},{8,9},{9,10},{10,1... | collective-permute-start | bytes 442376 | tf_op jit(solution)/shard_map/ppermute | solution.py:179
  182.8 4.3 %collective-permute-start.26 = (bf16[464,128]{1,0:T(8,128)(2,1)S(1)}, bf16[464,128]{1,0:T(8,128)(2,1)S(1)}, u32[]{:S(2)}, u32[]{:S(2)}) collective-permute-start(bf16[464,128]{1,0:T(8,128)(2,1)S(1)} %get-tuple-element.108), channel_id=1, source_target_pairs={{1,0},{2,1},{3,2},{4,3},{5,4},{6,5},{7,6},{8,7},{9,8},{10,9},{11,1... | collective-permute-start | bytes 356360 | tf_op jit(solution)/shard_map/ppermute | solution.py:179
  184.8 14.3 %collective-permute-start.25 = (bf16[464,128]{1,0:T(8,128)(2,1)S(1)}, bf16[464,128]{1,0:T(8,128)(2,1)S(1)}, u32[]{:S(2)}, u32[]{:S(2)}) collective-permute-start(bf16[464,128]{1,0:T(8,128)(2,1)S(1)} %get-tuple-element.108), channel_id=1, source_target_pairs={{0,1},{1,2},{2,3},{3,4},{4,5},{5,6},{6,7},{7,8},{8,9},{9,10},{10,1... | collective-permute-start | bytes 356360 | tf_op jit(solution)/shard_map/ppermute | solution.py:179

commit v2 on v0

v2 whole, which is shorter than its diff:
```python
import functools

import jax
import jax.numpy as jnp
from jax import lax
from jax.experimental import pallas as pl
from jax.experimental.pallas import tpu as pltpu
from jax.sharding import PartitionSpec as P

LANES = 128
EDGE = 8
SPAN = 256
REACH = 64
WIDE = SPAN - REACH
FOLD = 4
PARAMS = pltpu.CompilerParams(vmem_limit_bytes=16 * 2**20)
NO_COST = pl.CostEstimate(flops=1, bytes_accessed=1, transcendentals=0)
VMEM = pl.BlockSpec(memory_space=pltpu.VMEM)
SMEM = pl.BlockSpec(memory_space=pltpu.SMEM)
ANY = pl.BlockSpec(memory_space=pl.ANY)
HBM = pl.BlockSpec(memory_space=pltpu.HBM)
CHUNKS = (384, 576, 576)


def chunk_bounds(samples):
    bounds = [0]
    for size in CHUNKS:
        if bounds[-1] + size + REACH <= samples:
            bounds.append(bounds[-1] + size)
    bounds.append(samples)
    return bounds


def segment_plan(rows):
    count = -(-rows // WIDE)
    width = min(WIDE, -(-rows // (16 * count)) * 16)
    return count, width


def window_rows(rows):
    return rows - segment_plan(rows)[1] + SPAN


def folded_rows(rows):
    return -(-rows // (16 * FOLD)) * 16


def weights_kernel(even_ref, trace_ref, time_ref, *refs):
    mats_ref, times_ref = refs[-2:]
    fans = trace_ref.shape[0]
    blocks = mats_ref.shape[0]
    even = even_ref[0] == 1
    for fan in range(fans):
        row = jnp.broadcast_to(trace_ref[fan : fan + 1, :], (LANES, SPAN))
        own = pltpu.roll(row, 0, 1, stride=1, stride_axis=0)[:, :LANES]
        left = pltpu.roll(row[:EDGE], SPAN - EDGE, 1, stride=1, stride_axis=0)[:, :LANES]
        right = pltpu.roll(row[:EDGE], LANES, 1, stride=1, stride_axis=0)[:, :LANES]
        pieces = (jnp.where(even, right, left), jnp.where(even, left, right))
        pair, half = fan // 2, fan % 2
        cols = slice(half * LANES, (half + 1) * LANES)
        for block in range(blocks):
            before, after = EDGE * block, EDGE * (blocks - 1 - block)
            parts = []
            for piece in pieces:
                if before:
                    parts.append(jnp.zeros((before, LANES), jnp.float32))
                parts.append(piece)
                if after:
                    parts.append(jnp.zeros((after, LANES), jnp.float32))
            parts.append(jnp.zeros((LANES - 2 * EDGE * blocks, LANES), jnp.float32))
            mats_ref[block, pair, :LANES, cols] = own.astype(jnp.bfloat16)
            mats_ref[block, pair, LANES:, cols] = jnp.concatenate(parts, axis=0).astype(
                jnp.bfloat16
            )
        taps = jnp.broadcast_to(time_ref[fan : fan + 1, :], (WIDE, SPAN))
        times_ref[:, fan * SPAN : (fan + 1) * SPAN] = pltpu.roll(
            taps, 0, 1, stride=1, stride_axis=0
        ).astype(jnp.bfloat16)


def weights(even, trace_taps, time_taps, blocks, *after):
    fans, width = trace_taps.shape
    turned = jnp.pad(trace_taps[:, ::-1].astype(jnp.float32), ((0, 0), (0, SPAN - width)))
    turned = jnp.roll(turned, width // 2 - width + 1, axis=1)
    late = jnp.pad(time_taps.astype(jnp.float32), ((0, 0), (0, SPAN - time_taps.shape[1])))
    return pl.pallas_call(
        weights_kernel,
        in_specs=[SMEM, VMEM, VMEM] + [ANY] * len(after),
        out_specs=[VMEM, VMEM],
        out_shape=(
            jax.ShapeDtypeStruct((blocks, fans // 2, 2 * LANES, 2 * LANES), jnp.bfloat16),
            jax.ShapeDtypeStruct((WIDE, fans * SPAN), jnp.bfloat16),
        ),
        cost_estimate=NO_COST,
        compiler_params=PARAMS,
        name="weights",
    )(even, turned, late, *after)


def edge_picks(even, blocks):
    trace = lax.broadcasted_iota(jnp.int32, (2 * LANES, 2 * LANES), 0)
    lane = lax.broadcasted_iota(jnp.int32, (2 * LANES, 2 * LANES), 1)
    last = jnp.where(even, 1, 0)
    begin = jnp.where(lane < LANES, last, 1 - last) * (LANES - EDGE)
    lane = lane % LANES
    picks = []
    for pair in range(blocks // 2):
        at = lane - EDGE * (2 * pair + trace // LANES)
        pick = (at >= 0) & (at < EDGE) & (trace % LANES == at + begin)
        picks.append(jnp.where(pick, 1.0, 0.0).astype(jnp.bfloat16))
    return picks


def pick_part(picks, tiles_ref, start, stop):
    found = None
    for pair, pick in enumerate(picks):
        both = jnp.concatenate(
            [tiles_ref[2 * pair, start:stop, :], tiles_ref[2 * pair + 1, start:stop, :]], axis=1
        )
        one = jnp.dot(both, pick, preferred_element_type=jnp.float32)
        found = one if found is None else found + one
    return found


def pack_edges(picks, tiles_ref, packed_refs, ready):
    blocks, rows = tiles_ref.shape[:2]
    fold = folded_rows(rows)
    totals = [None, None]
    for part in range(FOLD):
        start, stop = part * fold, min(rows, (part + 1) * fold)
        ready(part)
        found = pick_part(picks, tiles_ref, start, stop)
        if stop - start < fold:
            found = jnp.concatenate(
                [found, jnp.zeros((fold - stop + start, 2 * LANES), jnp.float32)], axis=0
            )
        for way in range(2):
            piece = found[:, way * LANES : (way + 1) * LANES]
            if part:
                piece = pltpu.roll(piece, part * EDGE * blocks, 1)
            totals[way] = piece if totals[way] is None else totals[way] + piece
    for way in range(2):
        packed_refs[way][...] = totals[way].astype(jnp.bfloat16)


def unpack_edges(packed_refs, rows, blocks, start, stop, give):
    fold, width = packed_refs[0].shape[0], EDGE * blocks
    while start < stop:
        part = start // fold
        until = min(stop, (part + 1) * fold)
        pieces = []
        for way in range(2):
            piece = packed_refs[way][start - part * fold : until - part * fold, :]
            shift = (way - part) * width % LANES
            piece = piece.astype(jnp.float32)
            pieces.append(pltpu.roll(piece, shift, 1) if shift else piece)
        lane = lax.broadcasted_iota(jnp.int32, pieces[0].shape, 1)
        give(start, jnp.where(lane < width, pieces[0], pieces[1]).astype(jnp.bfloat16))
        start = until


def first_edges_kernel(even_ref, x_ref, out_a, out_b, picks_ref, held, sem):
    blocks, rows = held.shape[:2]
    fold = folded_rows(rows)

    def copy(part):
        span = pl.ds(part * fold, min(rows, (part + 1) * fold) - part * fold)
        return pltpu.make_async_copy(x_ref.at[:, span, :], held.at[:, span, :], sem.at[part])

    for part in range(FOLD):
        copy(part).start()
    picks = edge_picks(even_ref[0] == 1, blocks)
    for pair, pick in enumerate(picks):
        picks_ref[pair] = pick
    pack_edges(picks, held, (out_a, out_b), lambda part: copy(part).wait())


def first_edges(even, traces):
    blocks = traces.shape[0]
    packed = jax.ShapeDtypeStruct((folded_rows(traces.shape[1]), LANES), jnp.bfloat16)
    return pl.pallas_call(
        first_edges_kernel,
        in_specs=[SMEM, HBM],
        out_specs=[VMEM] * 4,
        out_shape=[
            packed,
            packed,
            jax.ShapeDtypeStruct((blocks // 2, 2 * LANES, 2 * LANES), jnp.bfloat16),
            jax.ShapeDtypeStruct(traces.shape, jnp.bfloat16),
        ],
        scratch_shapes=[pltpu.SemaphoreType.DMA((FOLD,))],
        cost_estimate=NO_COST,
        compiler_params=pltpu.CompilerParams(vmem_limit_bytes=50 * 2**20),
        name="first_edges",
    )(even, traces)


def second_edges_kernel(slot_ref, picks_ref, *refs):
    parts, (_, sorted_ref, out_a, out_b, sem) = refs[:-5], refs[-5:]
    blocks, slot_cap = sorted_ref.shape[0], parts[0].shape[0]
    for block in range(blocks):
        slot = slot_ref[block]
        for offset, part in enumerate(parts):

            @pl.when(slot // slot_cap == offset)
            def _():
                pltpu.make_async_copy(
                    part.at[slot % slot_cap], sorted_ref.at[block], sem.at[block]
                ).start()

    for block in range(blocks):
        pltpu.make_async_copy(parts[0].at[0], sorted_ref.at[block], sem.at[block]).wait()
    picks = [picks_ref[pair] for pair in range(blocks // 2)]
    pack_edges(picks, sorted_ref, (out_a, out_b), lambda part: None)


def second_edges(slots, picks, arrived, after, blocks):
    rows = arrived[0].shape[1]
    packed = jax.ShapeDtypeStruct((folded_rows(rows), LANES), jnp.bfloat16)
    return pl.pallas_call(
        second_edges_kernel,
        in_specs=[SMEM, VMEM] + [ANY] * (len(arrived) + 1),
        out_specs=[VMEM] * 3,
        scratch_shapes=[pltpu.SemaphoreType.DMA((blocks,))],
        out_shape=[jax.ShapeDtypeStruct((blocks, rows, LANES), jnp.bfloat16), packed, packed],
        cost_estimate=NO_COST,
        compiler_params=PARAMS,
        name="second_edges",
    )(slots, picks, *arrived, after)


def swap_edges(packed):
    count = lax.axis_size("shot")
    got = []
    for first, edges in enumerate(packed):
        pairs = []
        for low in range(first, count - 1, 2):
            pairs += [(low, low + 1), (low + 1, low)]
        got.append(lax.ppermute(edges, "shot", pairs))
    return got


def filter_window(pieces, merged, fans_ref, mats_ref, times_ref, rows, give):
    fan_pairs = mats_ref.shape[1]
    blocks = mats_ref.shape[0]
    tall = fans_ref.shape[1]
    count, width = segment_plan(rows)
    covered = 0
    for at, size, _ in list(pieces) + [(tall, 0, None)]:
        if at > covered:
            fans_ref[:, covered:at, :] = jnp.zeros(
                (fans_ref.shape[0], at - covered, fans_ref.shape[2]), jnp.bfloat16
            )
        covered = at + size
    def do_pair(pair, carry):
        for half in range(2):
            block = 2 * pair + half
            cols = slice(half * LANES, (half + 1) * LANES)
            for at, size, load in pieces:
                lhs = jnp.concatenate([load(block), merged[at : at + size, :]], axis=1)
                for fan_pair in range(fan_pairs):
                    both = jnp.dot(
                        lhs, mats_ref[block, fan_pair], preferred_element_type=jnp.float32
                    ).astype(jnp.bfloat16)
                    fans_ref[2 * fan_pair, at : at + size, cols] = both[:, :LANES]
                    fans_ref[2 * fan_pair + 1, at : at + size, cols] = both[:, LANES:]
        for step in range(count):
            start = min(step * width, rows - width)
            total = None
            for fan in range(2 * fan_pairs):
                part = jnp.dot(
                    times_ref[:width, fan * SPAN : (fan + 1) * SPAN],
                    fans_ref[fan, start : start + SPAN, :],
                    preferred_element_type=jnp.float32,
                )
                total = part if total is None else total + part
            give(pair, start, total)
        return carry

    lax.fori_loop(0, blocks // 2, do_pair, 0)


def first_kernel(start, stop, owners, key_ref, x_ref, edge_a, edge_b, mats_ref, times_ref, *refs):
    outs = refs[-4 - owners : -4]
    merged, fans_ref, done, sem = refs[-4:]
    blocks, rows = done.shape[:2]
    samples = x_ref.shape[1]
    slot_cap = outs[0].shape[0]
    window = start - REACH // 2
    begin, end = max(0, window), min(samples, stop + REACH // 2)

    def put(row, values):
        merged[row - window : row - window + values.shape[0], :] = values

    unpack_edges((edge_a, edge_b), samples, blocks, begin, end, put)

    def give(pair, at, values):
        values = values.astype(jnp.bfloat16)
        for half in range(2):
            done[2 * pair + half, at : at + values.shape[0], :] = values[
                :, half * LANES : (half + 1) * LANES
            ]
        if at + values.shape[0] == rows:
            for half in range(2):
                block = 2 * pair + half
                key = key_ref[block]
                for offset, out_ref in enumerate(outs):

                    @pl.when(key // slot_cap == offset)
                    def _():
                        pltpu.make_async_copy(
                            done.at[block], out_ref.at[key % slot_cap], sem.at[block]
                        ).start()

    pieces = [(begin - window, end - begin, lambda block: x_ref[block, begin:end, :])]
    filter_window(pieces, merged, fans_ref, mats_ref, times_ref, rows, give)
    for block in range(blocks):
        pltpu.make_async_copy(done.at[block], outs[0].at[0], sem.at[block]).wait()


def first_pass(keys, owners, traces, edges, mats, times, after, start, stop):
    blocks = traces.shape[0]
    fans = 2 * mats.shape[1]
    rows = stop - start
    tall = window_rows(rows)
    sent = jax.ShapeDtypeStruct((blocks // 2, rows, LANES), jnp.bfloat16)
    return pl.pallas_call(
        functools.partial(first_kernel, start, stop, owners),
        in_specs=[SMEM] + [VMEM] * 5 + [ANY] * len(after),
        out_specs=[ANY] * owners,
        scratch_shapes=[
            pltpu.VMEM((tall, LANES), jnp.bfloat16),
            pltpu.VMEM((fans, tall, 2 * LANES), jnp.bfloat16),
            pltpu.VMEM((blocks, rows, LANES), jnp.bfloat16),
            pltpu.SemaphoreType.DMA((blocks,)),
        ],
        out_shape=[sent] * owners,
        cost_estimate=NO_COST,
        compiler_params=PARAMS,
        name="first_pass",
    )(keys, traces, *edges, mats, times, *after)


def second_kernel(at, has_past, *refs):
    refs = list(refs)
    take = lambda: refs.pop(0)
    past = [take() for _ in range(3)] if has_past else None
    now = [take() for _ in range(3)]
    mats_ref, times_ref, _ = take(), take(), take()
    if has_past:
        take()
    out_ref, token_ref, merged, fans_ref, done, sem = refs
    token_ref[...] = jnp.zeros_like(token_ref)
    blocks, rows = done.shape[:2]
    lead = REACH if has_past else REACH // 2
    pieces = []

    def put(origin):
        def store(row, values):
            merged[row - origin : row - origin + values.shape[0], :] = values

        return store

    if has_past:
        held = past[0].shape[1]
        unpack_edges(past[1:], held, blocks, held - REACH, held, put(held - REACH))
        pieces.append((0, REACH, lambda block: past[0][block, held - REACH :, :]))
    size = now[0].shape[1]
    unpack_edges(now[1:], size, blocks, 0, size, put(-lead))
    pieces.append((lead, size, lambda block: now[0][block]))

    def copy(block):
        return pltpu.make_async_copy(
            done.at[block], out_ref.at[block, pl.ds(at, rows), :], sem.at[block]
        )

    def give(pair, start, values):
        for half in range(2):
            done[2 * pair + half, start : start + values.shape[0], :] = values[
                :, half * LANES : (half + 1) * LANES
            ]
        if start + values.shape[0] == rows:
            for half in range(2):
                copy(2 * pair + half).start()

    filter_window(pieces, merged, fans_ref, mats_ref, times_ref, rows, give)
    for block in range(blocks):
        copy(block).wait()


def second_pass(blocks, samples, past, now, mats, times, after, out, at, rows):
    fans = 2 * mats.shape[1]
    tall = window_rows(rows)
    operands = [*(past or ()), *now, mats, times, after]
    specs = [VMEM] * (len(operands) - 1) + [ANY]
    aliases = {}
    if out is not None:
        specs.append(ANY)
        operands.append(out)
        aliases = {len(operands) - 1: 0}
    return pl.pallas_call(
        functools.partial(second_kernel, at, past is not None),
        in_specs=specs,
        out_specs=[ANY, VMEM],
        scratch_shapes=[
            pltpu.VMEM((tall, LANES), jnp.bfloat16),
            pltpu.VMEM((fans, tall, 2 * LANES), jnp.bfloat16),
            pltpu.VMEM((blocks, rows, LANES), jnp.float32),
            pltpu.SemaphoreType.DMA((blocks,)),
        ],
        out_shape=[
            jax.ShapeDtypeStruct((blocks, samples, LANES), jnp.float32),
            jax.ShapeDtypeStruct((8, LANES), jnp.float32),
        ],
        input_output_aliases=aliases,
        cost_estimate=NO_COST,
        compiler_params=PARAMS,
        name="second_pass",
    )(*operands)


def per_device(
    traces, first_trace_taps, first_time_taps, second_trace_taps, second_time_taps, dest_row
):
    blocks, samples, _ = traces.shape
    owners = lax.axis_size("rcv")
    me = lax.axis_index("rcv")
    slot_cap = blocks // 2
    even = (1 - lax.axis_index("shot") % 2).astype(jnp.int32).reshape(1)

    target = dest_row[:, 0]
    ids = jnp.arange(blocks, dtype=jnp.int32)

    def ranks(owner):
        return jnp.sum(
            (
                (ids[:, None] > ids[None, :]) & (owner[..., :, None] == owner[..., None, :])
            ).astype(jnp.int32),
            axis=-1,
        )

    def send(values, offset):
        pairs = [(i, (i + offset) % owners) for i in range(owners)]
        return lax.ppermute(values, "rcv", pairs) if offset else values

    owner = target // blocks
    keys = (owner - me + owners) % owners * slot_cap + ranks(owner)

    bounds = chunk_bounds(samples)
    count = len(bounds) - 1
    *packed, picks, traces = first_edges(even, traces)
    edges = swap_edges(packed)
    late_target, _ = lax.optimization_barrier((target, packed[0]))
    column = jnp.stack([send(late_target, offset) for offset in range(owners)])
    place = jnp.arange(owners, dtype=jnp.int32)[:, None] * slot_cap + ranks(column // blocks)
    mine = column[None] == (me * blocks + ids)[:, None, None]
    slots = jnp.sum(jnp.where(mine, place[None], 0), axis=(1, 2))
    mats, times = weights(even, first_trace_taps, first_time_taps, blocks)

    def exchange(sent, before, token):
        arrived = []
        for offset, part in enumerate(sent):
            if offset and before is not None:
                part, before[offset] = lax.optimization_barrier((part, before[offset]))
            if offset and token is not None:
                part, _ = lax.optimization_barrier((part, token))
            arrived.append(send(part, offset))
        return arrived

    sent, after = [], [slots]
    for step in range(count):
        sent.append(
            first_pass(
                keys, owners, traces, edges, mats, times, after, bounds[step], bounds[step + 1]
            )
        )
        after = [sent[-1][0]]
    arrived = [exchange(sent[0], None, None)]

    mats, times = weights(even, second_trace_taps, second_time_taps, blocks, sent[0][0])
    out, past, token = None, None, None
    for step in range(count):
        if step + 1 < count:
            arrived.append(exchange(sent[step + 1], arrived[step], token))
        after = token if step else sent[min(2, count - 1)][0]
        gathered, *packed = second_edges(slots, picks, arrived[step], after, blocks)
        now = (gathered, *swap_edges(packed))
        at = max(0, bounds[step] - REACH // 2)
        stop = bounds[step + 1] - REACH // 2 if step + 1 < count else samples
        out, token = second_pass(
            blocks, samples, past, now, mats, times, sent[min(step + 3, count - 1)][0], out,
            at, stop - at,
        )
        past = now
    return out


def solution(mesh):
    in_specs = (P("rcv", None, "shot"), P(), P(), P(), P(), P("rcv", "shot"))
    out_specs = P("rcv", None, "shot")
    return jax.shard_map(
        per_device, mesh=mesh, in_specs=in_specs, out_specs=out_specs, check_vma=False
    )
```

time: 218 us -> 158 us (0.72)
  the two profiles are of different devices: /device:TPU:31 before, /device:TPU:192 now
where the time goes in v2:
time: 158 us; the launch traced here: 157 us
  starting transfers between devices  53.4 us (34%)
  Pallas kernels  47.2 us (30%)
  waiting for transfers between devices  43.2 us (27%)
  local copies, waits for them, and re-layouts  7.06 us (4%)
  other arithmetic  5.49 us (3%)
    ppermute x10, waiting for transfers between devices, swap_edges(): got.append(lax.ppermute(edges, 'shot', pairs))  37.6 us
    ppermute x15, starting transfers between devices, send(): return lax.ppermute(values, 'rcv', pairs) if offset else values  32.2 us
    ppermute x10, starting transfers between devices, swap_edges(): got.append(lax.ppermute(edges, 'shot', pairs))  21.2 us
    pallas_call x4, Pallas kernels, first_pass(): pl.pallas_call(functools.partial(first_kernel, start, stop, owners), in_s...  17.9 us
    pallas_call x4, Pallas kernels, second_pass(): pl.pallas_call(functools.partial(second_kernel, at, past is not None), in...  17.1 us
    pallas_call x4, Pallas kernels, second_edges(): pl.pallas_call(second_edges_kernel, in_specs=[SMEM, VMEM] + [ANY] * (len(...  7.63 us
    unnamed x16, local copies, waits for them, and re-layouts  6.06 us
    ppermute x15, waiting for transfers between devices, send(): return lax.ppermute(values, 'rcv', pairs) if offset else values  5.58 us
  transfers between devices with their start and end apart: 25, of which 7 were waited for; matrix products, arithmetic and copies ran while one was open for 4% of the time, Pallas kernels for 21%

profile of v2, /device:TPU:192, one launch (start us, length us, event | category | flops | bytes accessed | tf_op | source)
XLA Modules:
  0.0 156.9 jit_solution(17254645325863456946)
XLA Ops:
  0.0 3.6 %first_edges.1 = (bf16[512,128]{1,0:T(8,128)(2,1)S(1)}, bf16[512,128]{1,0:T(8,128)(2,1)}, bf16[2,256,256]{2,1,0:T(8,128)(2,1)S(1)}, bf16[4,2000,128]{2,1,0:T(8,128)(2,1)S(1)}) custom-call(s32[1]{0:T(128)} %bitcast.1.even_ref, bf16[4,2000,128]{2,1,0:T(8,128)(2,1)} %x_ref.1), custom_call_target="tpu_custom_call" | custom-call | flops 1 | bytes 1 | tf_op jit(solution)/shard_map/first_edges/pallas_call | solution.py:181
  3.6 1.3 copy-done
  4.9 1.0 collective-permute-start.2
  5.9 2.4 %collective-permute-start.1 = (s32[4]{0:T(128)}, s32[4]{0:T(128)}, u32[]{:S(2)}, u32[]{:S(2)}) collective-permute-start(s32[4]{0:T(128)} %bitcast.12), channel_id=1, source_target_pairs={{0,128},{64,192},{128,0},{192,64},{1,129},{65,193},{129,1},{193,65... | collective-permute-start | bytes 56 | tf_op jit(solution)/shard_map/ppermute | solution.py:444
  8.3 0.1 collective-permute-start
  8.4 8.0 %collective-permute-start.4 = (bf16[512,128]{1,0:T(8,128)(2,1)}, bf16[512,128]{1,0:T(8,128)(2,1)S(1)}, u32[]{:S(2)}, u32[]{:S(2)}) collective-permute-start(bf16[512,128]{1,0:T(8,128)(2,1)} %get-tuple-element.77), channel_id=1, source_target_pairs={{1,2},{2,1},{3,4},{4,3},{5,6},{6,5},{7,8},{8,7},{9,10},{10,9},{11,... | collective-permute-start | bytes 393224 | tf_op jit(solution)/shard_map/ppermute | solution.py:239
  16.4 0.7 and_select_fusion.2
  17.1 0.7 fusion.5
  17.7 0.6 iota_compare_fusion
  18.3 0.8 rev.6
  19.1 0.2 convert_reduce_fusion.1
  19.3 0.7 fusion.3.key_ref
  19.9 0.1 pad_slice_fusion.1
  20.0 0.7 pad_convert_fusion.1.time_ref
  20.7 0.1 pad_maximum_fusion.trace_ref
  20.8 0.5 weights.2
  21.3 0.7 pad_add_fusion
  22.0 0.9 convert_reduce_fusion
  22.9 0.1 broadcast_add_fusion
  22.9 0.2 select_reduce_fusion.refs_0_.slot_ref
  23.2 1.2 collective-permute-done.4.edge_b
  24.4 1.6 %copy-done.1 = bf16[4,2000,128]{2,1,0:T(8,128)(2,1)S(1)} copy-done((bf16[4,2000,128]{2,1,0:T(8,128)(2,1)S(1)}, bf16[4,2000,128]{2,1,0:T(8,128)(2,1)}, u32[]{:S(2)}) %copy-start.1) | copy-done | bytes 2048024
  26.0 3.7 %first_pass.4 = (bf16[2,384,128]{2,1,0:T(8,128)(2,1)S(1)}, bf16[2,384,128]{2,1,0:T(8,128)(2,1)}, bf16[2,384,128]{2,1,0:T(8,128)(2,1)}, bf16[2,384,128]{2,1,0:T(8,128)(2,1)}) custom-call(s32[4]{0:T(128)S(1)} %fusion.3.key_ref, bf16[4,2000,128]{2,1,0:T(8,128)(2,1)S(1)} %copy-done.1, bf16[512,128]{1,0:T(8,128)(2,1)S(1)} %collective-permute-done.3.edge_a, ...), custom_call_target="tpu_custom_call" | custom-call | flops 1 | bytes 1 | tf_op jit(solution)/shard_map/first_pass/pallas_call | solution.py:327
  29.7 0.7 copy-done.4
  30.4 0.6 collective-permute-start.5
  31.0 2.8 %collective-permute-start.7 = (bf16[2,384,128]{2,1,0:T(8,128)(2,1)}, bf16[2,384,128]{2,1,0:T(8,128)(2,1)}, u32[]{:S(2)}, u32[]{:S(2)}) collective-permute-start(bf16[2,384,128]{2,1,0:T(8,128)(2,1)} %get-tuple-element.91), channel_id=1, source_target_pairs={{0,128},{64,192},{128,0},{192,64},{1,129},{65,193},{129,1},{193,65... | collective-permute-start | bytes 589832 | tf_op jit(solution)/shard_map/ppermute | solution.py:444
  33.8 0.1 rev.7
  33.9 1.6 %copy-done.2 = bf16[4,2000,128]{2,1,0:T(8,128)(2,1)S(1)} copy-done((bf16[4,2000,128]{2,1,0:T(8,128)(2,1)S(1)}, bf16[4,2000,128]{2,1,0:T(8,128)(2,1)}, u32[]{:S(2)}) %copy-start.2) | copy-done | bytes 2048024
  35.5 0.9 copy-done.5
  36.4 4.9 %first_pass.5 = (bf16[2,576,128]{2,1,0:T(8,128)(2,1)S(1)}, bf16[2,576,128]{2,1,0:T(8,128)(2,1)S(1)}, bf16[2,576,128]{2,1,0:T(8,128)(2,1)S(1)}, bf16[2,576,128]{2,1,0:T(8,128)(2,1)S(1)}) custom-call(s32[4]{0:T(128)S(1)} %fusion.3.key_ref, bf16[4,2000,128]{2,1,0:T(8,128)(2,1)S(1)} %copy-done.2, bf16[512,128]{1,0:T(8,128)(2,1)S(1)} %collective-permute-done.3.edge_a, ...), custom_call_target="tpu_custom_call" | custom-call | flops 1 | bytes 1 | tf_op jit(solution)/shard_map/first_pass/pallas_call | solution.py:327
  41.3 4.3 %collective-permute-done.5.refs_1_ = bf16[2,384,128]{2,1,0:T(8,128)(2,1)} collective-permute-done((bf16[2,384,128]{2,1,0:T(8,128)(2,1)}, bf16[2,384,128]{2,1,0:T(8,128)(2,1)}, u32[]{:S(2)}, u32[]{:S(2)}) %collective-permute-start.5) | collective-permute-done | bytes 196640 | tf_op jit(solution)/shard_map/ppermute | solution.py:444
  45.6 6.4 %collective-permute-start.14 = (bf16[2,576,128]{2,1,0:T(8,128)(2,1)S(1)}, bf16[2,576,128]{2,1,0:T(8,128)(2,1)S(1)}, u32[]{:S(2)}, u32[]{:S(2)}) collective-permute-start(bf16[2,576,128]{2,1,0:T(8,128)(2,1)S(1)} %get-tuple-element.113), channel_id=1, source_target_pairs={{0,192},{64,0},{128,64},{192,128},{1,193},{65,1},{129,65},{193,129... | collective-permute-start | bytes 884744 | tf_op jit(solution)/shard_map/ppermute | solution.py:444
  52.0 4.3 %collective-permute-start.12 = (bf16[2,576,128]{2,1,0:T(8,128)(2,1)S(1)}, bf16[2,576,128]{2,1,0:T(8,128)(2,1)S(1)}, u32[]{:S(2)}, u32[]{:S(2)}) collective-permute-start(bf16[2,576,128]{2,1,0:T(8,128)(2,1)S(1)} %get-tuple-element.107), channel_id=1, source_target_pairs={{0,128},{64,192},{128,0},{192,64},{1,129},{65,193},{129,1},{193,65... | collective-permute-start | bytes 884744 | tf_op jit(solution)/shard_map/ppermute | solution.py:444
  56.4 4.9 %first_pass.6 = (bf16[2,576,128]{2,1,0:T(8,128)(2,1)S(1)}, bf16[2,576,128]{2,1,0:T(8,128)(2,1)S(1)}, bf16[2,576,128]{2,1,0:T(8,128)(2,1)S(1)}, bf16[2,576,128]{2,1,0:T(8,128)(2,1)S(1)}) custom-call(s32[4]{0:T(128)S(1)} %fusion.3.key_ref, bf16[4,2000,128]{2,1,0:T(8,128)(2,1)S(1)} %copy-done.2, bf16[512,128]{1,0:T(8,128)(2,1)S(1)} %collective-permute-done.3.edge_a, ...), custom_call_target="tpu_custom_call" | custom-call | flops 1 | bytes 1 | tf_op jit(solution)/shard_map/first_pass/pallas_call | solution.py:327
  61.3 2.1 %second_edges.4 = (bf16[4,384,128]{2,1,0:T(8,128)(2,1)S(1)}, bf16[96,128]{1,0:T(8,128)(2,1)S(1)}, bf16[96,128]{1,0:T(8,128)(2,1)S(1)}) custom-call(s32[4]{0:T(128)S(1)} %select_reduce_fusion.refs_0_.slot_ref, bf16[2,256,256]{2,1,0:T(8,128)(2,1)S(1)} %get-tuple-element.75.picks_ref, bf16[2,384,128]{2,1,0:T(8,128)(2,1)S(1)} %copy-done.5, ...), custom_call_target="tpu_custom_call" | custom-call | flops 1 | bytes 1 | tf_op jit(solution)/shard_map/second_edges/pallas_call | solution.py:220
  63.4 0.1 collective-permute-start.9
  63.5 3.3 %collective-permute-start.10 = (bf16[96,128]{1,0:T(8,128)(2,1)S(1)}, bf16[96,128]{1,0:T(8,128)(2,1)S(1)}, u32[]{:S(2)}, u32[]{:S(2)}) collective-permute-start(bf16[96,128]{1,0:T(8,128)(2,1)S(1)} %get-tuple-element.98), channel_id=1, source_target_pairs={{1,2},{2,1},{3,4},{4,3},{5,6},{6,5},{7,8},{8,7},{9,10},{10,9},{11,... | collective-permute-start | bytes 73736 | tf_op jit(solution)/shard_map/ppermute | solution.py:239
  66.9 0.1 pad_maximum_fusion.1.trace_ref
  66.9 0.5 weights.3
  67.4 4.4 %first_pass.7 = (bf16[2,464,128]{2,1,0:T(8,128)(2,1)S(1)}, bf16[2,464,128]{2,1,0:T(8,128)(2,1)S(1)}, bf16[2,464,128]{2,1,0:T(8,128)(2,1)S(1)}, bf16[2,464,128]{2,1,0:T(8,128)(2,1)S(1)}) custom-call(s32[4]{0:T(128)S(1)} %fusion.3.key_ref, bf16[4,2000,128]{2,1,0:T(8,128)(2,1)S(1)} %copy-done.3, bf16[512,128]{1,0:T(8,128)(2,1)S(1)} %collective-permute-done.3.edge_a, ...), custom_call_target="tpu_custom_call" | custom-call | flops 1 | bytes 1 | tf_op jit(solution)/shard_map/first_pass/pallas_call | solution.py:327
  71.8 5.2 %collective-permute-done.10.refs_2_ = bf16[96,128]{1,0:T(8,128)(2,1)S(1)} collective-permute-done((bf16[96,128]{1,0:T(8,128)(2,1)S(1)}, bf16[96,128]{1,0:T(8,128)(2,1)S(1)}, u32[]{:S(2)}, u32[]{:S(2)}) %collective-permute-start.10) | collective-permute-done | bytes 24608 | tf_op jit(solution)/shard_map/ppermute | solution.py:239
  77.1 2.9 %second_pass.4 = (f32[4,2000,128]{2,1,0:T(8,128)}, f32[8,128]{1,0:T(8,128)S(1)}) custom-call(bf16[4,384,128]{2,1,0:T(8,128)(2,1)S(1)} %get-tuple-element.96.refs_0_, bf16[96,128]{1,0:T(8,128)(2,1)S(1)} %collective-permute-done.9.refs_1_, bf16[96,128]{1,0:T(8,128)(2,1)S(1)} %collective-permute-done.10.refs_2_, ...), custom_call_target="tpu_custom_call" | custom-call | flops 1 | bytes 1 | tf_op jit(solution)/shard_map/second_pass/pallas_call | solution.py:401
  80.0 1.3 collective-permute-start.11
  81.3 2.0 %collective-permute-start.13 = (bf16[2,576,128]{2,1,0:T(8,128)(2,1)S(1)}, bf16[2,576,128]{2,1,0:T(8,128)(2,1)S(1)}, u32[]{:S(2)}, u32[]{:S(2)}) collective-permute-start(bf16[2,576,128]{2,1,0:T(8,128)(2,1)S(1)} %get-tuple-element.109), channel_id=1, source_target_pairs={{0,128},{64,192},{128,0},{192,64},{1,129},{65,193},{129,1},{193,65... | collective-permute-start | bytes 884744 | tf_op jit(solution)/shard_map/ppermute | solution.py:444
  83.3 0.1 collective-permute-start.15
  83.4 1.9 %second_edges.5 = (bf16[4,576,128]{2,1,0:T(8,128)(2,1)S(1)}, bf16[144,128]{1,0:T(8,128)(2,1)S(1)}, bf16[144,128]{1,0:T(8,128)(2,1)S(1)}) custom-call(s32[4]{0:T(128)S(1)} %select_reduce_fusion.refs_0_.slot_ref, bf16[2,256,256]{2,1,0:T(8,128)(2,1)S(1)} %get-tuple-element.75.picks_ref, bf16[2,576,128]{2,1,0:T(8,128)(2,1)S(1)} %get-tuple-element.81.refs_0_, ...), custom_call_target="tpu_custom_call" | custom-call | flops 1 | bytes 1 | tf_op jit(solution)/shard_map/second_edges/pallas_call | solution.py:220
  85.3 0.1 collective-permute-start.16
  85.4 4.6 %collective-permute-start.17 = (bf16[144,128]{1,0:T(8,128)(2,1)S(1)}, bf16[144,128]{1,0:T(8,128)(2,1)S(1)}, u32[]{:S(2)}, u32[]{:S(2)}) collective-permute-start(bf16[144,128]{1,0:T(8,128)(2,1)S(1)} %get-tuple-element.122), channel_id=1, source_target_pairs={{1,2},{2,1},{3,4},{4,3},{5,6},{6,5},{7,8},{8,7},{9,10},{10,9},{11,... | collective-permute-start | bytes 110600 | tf_op jit(solution)/shard_map/ppermute | solution.py:239
  90.1 9.3 %collective-permute-done.17.refs_5_.refs_2_ = bf16[144,128]{1,0:T(8,128)(2,1)S(1)} collective-permute-done((bf16[144,128]{1,0:T(8,128)(2,1)S(1)}, bf16[144,128]{1,0:T(8,128)(2,1)S(1)}, u32[]{:S(2)}, u32[]{:S(2)}) %collective-permute-start.17) | collective-permute-done | bytes 36896 | tf_op jit(solution)/shard_map/ppermute | solution.py:239
  99.3 4.6 %second_pass.5 = (f32[4,2000,128]{2,1,0:T(8,128)}, f32[8,128]{1,0:T(8,128)S(1)}) custom-call(bf16[4,384,128]{2,1,0:T(8,128)(2,1)S(1)} %get-tuple-element.96.refs_0_, bf16[96,128]{1,0:T(8,128)(2,1)S(1)} %collective-permute-done.9.refs_1_, bf16[96,128]{1,0:T(8,128)(2,1)S(1)} %collective-permute-done.10.refs_2_, ...), custom_call_target="tpu_custom_call", output_to_operand_aliasing={{0}: (9, {})} | custom-call | flops 1 | bytes 1 | tf_op jit(solution)/shard_map/second_pass/pallas_call | solution.py:401
  104.0 1.6 %collective-permute-start.20 = (bf16[2,464,128]{2,1,0:T(8,128)(2,1)S(1)}, bf16[2,464,128]{2,1,0:T(8,128)(2,1)S(1)}, u32[]{:S(2)}, u32[]{:S(2)}) collective-permute-start(bf16[2,464,128]{2,1,0:T(8,128)(2,1)S(1)} %get-tuple-element.129), channel_id=1, source_target_pairs={{0,64},{64,128},{128,192},{192,0},{1,65},{65,129},{129,193},{193,1... | collective-permute-start | bytes 712712 | tf_op jit(solution)/shard_map/ppermute | solution.py:444
  105.6 1.2 collective-permute-start.21
  106.8 1.3 collective-permute-done.15.refs_3_
  108.1 8.4 %collective-permute-start.22 = (bf16[2,464,128]{2,1,0:T(8,128)(2,1)S(1)}, bf16[2,464,128]{2,1,0:T(8,128)(2,1)S(1)}, u32[]{:S(2)}, u32[]{:S(2)}) collective-permute-start(bf16[2,464,128]{2,1,0:T(8,128)(2,1)S(1)} %get-tuple-element.133), channel_id=1, source_target_pairs={{0,192},{64,0},{128,64},{192,128},{1,193},{65,1},{129,65},{193,129... | collective-permute-start | bytes 712712 | tf_op jit(solution)/shard_map/ppermute | solution.py:444
  116.5 1.9 %second_edges.6 = (bf16[4,576,128]{2,1,0:T(8,128)(2,1)S(1)}, bf16[144,128]{1,0:T(8,128)(2,1)S(1)}, bf16[144,128]{1,0:T(8,128)(2,1)S(1)}) custom-call(s32[4]{0:T(128)S(1)} %select_reduce_fusion.refs_0_.slot_ref, bf16[2,256,256]{2,1,0:T(8,128)(2,1)S(1)} %get-tuple-element.75.picks_ref, bf16[2,576,128]{2,1,0:T(8,128)(2,1)S(1)} %get-tuple-element.82.refs_0_.refs_4_, ...), custom_call_target="tpu_custom_call" | custom-call | flops 1 | bytes 1 | tf_op jit(solution)/shard_map/second_edges/pallas_call | solution.py:220
  118.4 0.1 collective-permute-start.18
  118.5 1.9 %collective-permute-start.19 = (bf16[144,128]{1,0:T(8,128)(2,1)S(1)}, bf16[144,128]{1,0:T(8,128)(2,1)S(1)}, u32[]{:S(2)}, u32[]{:S(2)}) collective-permute-start(bf16[144,128]{1,0:T(8,128)(2,1)S(1)} %get-tuple-element.127), channel_id=1, source_target_pairs={{1,2},{2,1},{3,4},{4,3},{5,6},{6,5},{7,8},{8,7},{9,10},{10,9},{11,... | collective-permute-start | bytes 110600 | tf_op jit(solution)/shard_map/ppermute | solution.py:239
  120.4 11.5 %collective-permute-done.19.refs_5_.refs_2_ = bf16[144,128]{1,0:T(8,128)(2,1)S(1)} collective-permute-done((bf16[144,128]{1,0:T(8,128)(2,1)S(1)}, bf16[144,128]{1,0:T(8,128)(2,1)S(1)}, u32[]{:S(2)}, u32[]{:S(2)}) %collective-permute-start.19) | collective-permute-done | bytes 36896 | tf_op jit(solution)/shard_map/ppermute | solution.py:239
  131.9 4.6 %second_pass.6 = (f32[4,2000,128]{2,1,0:T(8,128)}, f32[8,128]{1,0:T(8,128)S(1)}) custom-call(bf16[4,576,128]{2,1,0:T(8,128)(2,1)S(1)} %get-tuple-element.120.refs_3_.refs_0_, bf16[144,128]{1,0:T(8,128)(2,1)S(1)} %collective-permute-done.16.refs_4_.refs_1_, ...), custom_call_target="tpu_custom_call", output_to_operand_aliasing={{0}: (9, {})} | custom-call | flops 1 | bytes 1 | tf_op jit(solution)/shard_map/second_pass/pallas_call | solution.py:401
  136.6 1.7 %second_edges.7 = (bf16[4,464,128]{2,1,0:T(8,128)(2,1)S(1)}, bf16[128,128]{1,0:T(8,128)(2,1)S(1)}, bf16[128,128]{1,0:T(8,128)(2,1)S(1)}) custom-call(s32[4]{0:T(128)S(1)} %select_reduce_fusion.refs_0_.slot_ref, bf16[2,256,256]{2,1,0:T(8,128)(2,1)S(1)} %get-tuple-element.75.picks_ref, bf16[2,464,128]{2,1,0:T(8,128)(2,1)S(1)} %get-tuple-element.101.refs_5_.refs_8_.refs_0_, ...), custom_call_target="tpu_custom_call" | custom-call | flops 1 | bytes 1 | tf_op jit(solution)/shard_map/second_edges/pallas_call | solution.py:220
  138.3 0.1 collective-permute-start.23
  138.4 2.9 %collective-permute-start.24 = (bf16[128,128]{1,0:T(8,128)(2,1)S(1)}, bf16[128,128]{1,0:T(8,128)(2,1)S(1)}, u32[]{:S(2)}, u32[]{:S(2)}) collective-permute-start(bf16[128,128]{1,0:T(8,128)(2,1)S(1)} %get-tuple-element.138), channel_id=1, source_target_pairs={{1,2},{2,1},{3,4},{4,3},{5,6},{6,5},{7,8},{8,7},{9,10},{10,9},{11,... | collective-permute-start | bytes 98312 | tf_op jit(solution)/shard_map/ppermute | solution.py:239
  141.3 10.4 %collective-permute-done.24.refs_5_ = bf16[128,128]{1,0:T(8,128)(2,1)S(1)} collective-permute-done((bf16[128,128]{1,0:T(8,128)(2,1)S(1)}, bf16[128,128]{1,0:T(8,128)(2,1)S(1)}, u32[]{:S(2)}, u32[]{:S(2)}) %collective-permute-start.24) | collective-permute-done | bytes 32800 | tf_op jit(solution)/shard_map/ppermute | solution.py:239
  151.7 4.9 %second_pass.7 = (f32[4,2000,128]{2,1,0:T(8,128)}, f32[8,128]{1,0:T(8,128)}) custom-call(bf16[4,576,128]{2,1,0:T(8,128)(2,1)S(1)} %get-tuple-element.125.refs_3_.refs_0_, bf16[144,128]{1,0:T(8,128)(2,1)S(1)} %collective-permute-done.18.refs_4_.refs_1_, bf16[144,128]{1,0:T(8,128)(2,1)S(1)} %collective-permute-done.19.refs_5_.refs_2_, ...), custom_call_target="tpu_custom_call", output_to_operand_aliasing={{0}: (9, {})} | custom-call | flops 1 | bytes 1 | tf_op jit(solution)/shard_map/second_pass/pallas_call | solution.py:401
  (40 shorter events, 0.2 us)
Async XLA Ops:
  0.0 33.8 %copy-start.7 = (bf16[8,16]{1,0:T(8,128)(2,1)S(1)}, bf16[8,16]{1,0:T(8,128)(2,1)}, u32[]{:S(2)}) copy-start(bf16[8,16]{1,0:T(8,128)(2,1)} %param.9) | copy-start | bytes 772
  3.6 1.3 copy-start
  4.9 16.4 %collective-permute-start.2 = (s32[4]{0:T(128)}, s32[4]{0:T(128)S(1)}, u32[]{:S(2)}, u32[]{:S(2)}) collective-permute-start(s32[4]{0:T(128)} %bitcast.11), channel_id=1, source_target_pairs={{0,192},{64,0},{128,64},{192,128},{1,193},{65,1},{129,65},{193,129... | collective-permute-start | bytes 56 | tf_op jit(solution)/shard_map/ppermute | solution.py:444
  5.9 15.4 %collective-permute-start.1 = (s32[4]{0:T(128)}, s32[4]{0:T(128)}, u32[]{:S(2)}, u32[]{:S(2)}) collective-permute-start(s32[4]{0:T(128)} %bitcast.12), channel_id=1, source_target_pairs={{0,128},{64,192},{128,0},{192,64},{1,129},{65,193},{129,1},{193,65... | collective-permute-start | bytes 56 | tf_op jit(solution)/shard_map/ppermute | solution.py:444
  8.3 13.0 %collective-permute-start = (s32[4]{0:T(128)}, s32[4]{0:T(128)}, u32[]{:S(2)}, u32[]{:S(2)}) collective-permute-start(s32[4]{0:T(128)} %bitcast.13), channel_id=1, source_target_pairs={{0,64},{64,128},{128,192},{192,0},{1,65},{65,129},{129,193},{193,1... | collective-permute-start | bytes 56 | tf_op jit(solution)/shard_map/ppermute | solution.py:444
  8.4 16.0 %collective-permute-start.3 = (bf16[512,128]{1,0:T(8,128)(2,1)S(1)}, bf16[512,128]{1,0:T(8,128)(2,1)S(1)}, u32[]{:S(2)}, u32[]{:S(2)}) collective-permute-start(bf16[512,128]{1,0:T(8,128)(2,1)S(1)} %get-tuple-element.73), channel_id=1, source_target_pairs={{0,1},{1,0},{2,3},{3,2},{4,5},{5,4},{6,7},{7,6},{8,9},{9,8},{10,11... | collective-permute-start | bytes 393224 | tf_op jit(solution)/shard_map/ppermute | solution.py:239
  8.4 16.0 %collective-permute-start.4 = (bf16[512,128]{1,0:T(8,128)(2,1)}, bf16[512,128]{1,0:T(8,128)(2,1)S(1)}, u32[]{:S(2)}, u32[]{:S(2)}) collective-permute-start(bf16[512,128]{1,0:T(8,128)(2,1)} %get-tuple-element.77), channel_id=1, source_target_pairs={{1,2},{2,1},{3,4},{4,3},{5,6},{6,5},{7,8},{8,7},{9,10},{10,9},{11,... | collective-permute-start | bytes 393224 | tf_op jit(solution)/shard_map/ppermute | solution.py:239
  24.4 1.6 %copy-start.1 = (bf16[4,2000,128]{2,1,0:T(8,128)(2,1)S(1)}, bf16[4,2000,128]{2,1,0:T(8,128)(2,1)}, u32[]{:S(2)}) copy-start(bf16[4,2000,128]{2,1,0:T(8,128)(2,1)} %copy-done) | copy-start | bytes 6144004
  26.0 30.4 %copy-start.6 = (bf16[8,64]{1,0:T(8,128)(2,1)S(1)}, bf16[8,64]{1,0:T(8,128)(2,1)}, u32[]{:S(2)}) copy-start(bf16[8,64]{1,0:T(8,128)(2,1)} %param.10) | copy-start | bytes 3076
  29.7 0.7 copy-start.4
  30.4 15.2 %collective-permute-start.5 = (bf16[2,384,128]{2,1,0:T(8,128)(2,1)}, bf16[2,384,128]{2,1,0:T(8,128)(2,1)}, u32[]{:S(2)}, u32[]{:S(2)}) collective-permute-start(bf16[2,384,128]{2,1,0:T(8,128)(2,1)} %get-tuple-element.86), channel_id=1, source_target_pairs={{0,64},{64,128},{128,192},{192,0},{1,65},{65,129},{129,193},{193,1... | collective-permute-start | bytes 589832 | tf_op jit(solution)/shard_map/ppermute | solution.py:444
  31.0 14.6 %collective-permute-start.7 = (bf16[2,384,128]{2,1,0:T(8,128)(2,1)}, bf16[2,384,128]{2,1,0:T(8,128)(2,1)}, u32[]{:S(2)}, u32[]{:S(2)}) collective-permute-start(bf16[2,384,128]{2,1,0:T(8,128)(2,1)} %get-tuple-element.91), channel_id=1, source_target_pairs={{0,128},{64,192},{128,0},{192,64},{1,129},{65,193},{129,1},{193,65... | collective-permute-start | bytes 589832 | tf_op jit(solution)/shard_map/ppermute | solution.py:444
  33.8 11.8 %collective-permute-start.8 = (bf16[2,384,128]{2,1,0:T(8,128)(2,1)}, bf16[2,384,128]{2,1,0:T(8,128)(2,1)}, u32[]{:S(2)}, u32[]{:S(2)}) collective-permute-start(bf16[2,384,128]{2,1,0:T(8,128)(2,1)} %get-tuple-element.94), channel_id=1, source_target_pairs={{0,192},{64,0},{128,64},{192,128},{1,193},{65,1},{129,65},{193,129... | collective-permute-start | bytes 589832 | tf_op jit(solution)/shard_map/ppermute | solution.py:444
  33.9 1.6 %copy-start.2 = (bf16[4,2000,128]{2,1,0:T(8,128)(2,1)S(1)}, bf16[4,2000,128]{2,1,0:T(8,128)(2,1)}, u32[]{:S(2)}) copy-start(bf16[4,2000,128]{2,1,0:T(8,128)(2,1)} %copy-done) | copy-start | bytes 6144004
  35.4 0.9 copy-start.5
  41.3 26.2 %copy-start.3 = (bf16[4,2000,128]{2,1,0:T(8,128)(2,1)S(1)}, bf16[4,2000,128]{2,1,0:T(8,128)(2,1)}, u32[]{:S(2)}) copy-start(bf16[4,2000,128]{2,1,0:T(8,128)(2,1)} %copy-done) | copy-start | bytes 6144004
  45.6 37.7 %collective-permute-start.14 = (bf16[2,576,128]{2,1,0:T(8,128)(2,1)S(1)}, bf16[2,576,128]{2,1,0:T(8,128)(2,1)S(1)}, u32[]{:S(2)}, u32[]{:S(2)}) collective-permute-start(bf16[2,576,128]{2,1,0:T(8,128)(2,1)S(1)} %get-tuple-element.113), channel_id=1, source_target_pairs={{0,192},{64,0},{128,64},{192,128},{1,193},{65,1},{129,65},{193,129... | collective-permute-start | bytes 884744 | tf_op jit(solution)/shard_map/ppermute | solution.py:444
  52.0 29.3 %collective-permute-start.12 = (bf16[2,576,128]{2,1,0:T(8,128)(2,1)S(1)}, bf16[2,576,128]{2,1,0:T(8,128)(2,1)S(1)}, u32[]{:S(2)}, u32[]{:S(2)}) collective-permute-start(bf16[2,576,128]{2,1,0:T(8,128)(2,1)S(1)} %get-tuple-element.107), channel_id=1, source_target_pairs={{0,128},{64,192},{128,0},{192,64},{1,129},{65,193},{129,1},{193,65... | collective-permute-start | bytes 884744 | tf_op jit(solution)/shard_map/ppermute | solution.py:444
  56.3 23.7 %collective-permute-start.6 = (bf16[2,576,128]{2,1,0:T(8,128)(2,1)S(1)}, bf16[2,576,128]{2,1,0:T(8,128)(2,1)S(1)}, u32[]{:S(2)}, u32[]{:S(2)}) collective-permute-start(bf16[2,576,128]{2,1,0:T(8,128)(2,1)S(1)} %get-tuple-element.87), channel_id=1, source_target_pairs={{0,64},{64,128},{128,192},{192,0},{1,65},{65,129},{129,193},{193,1... | collective-permute-start | bytes 884744 | tf_op jit(solution)/shard_map/ppermute | solution.py:444
  63.4 8.4 %collective-permute-start.9 = (bf16[96,128]{1,0:T(8,128)(2,1)S(1)}, bf16[96,128]{1,0:T(8,128)(2,1)S(1)}, u32[]{:S(2)}, u32[]{:S(2)}) collective-permute-start(bf16[96,128]{1,0:T(8,128)(2,1)S(1)} %get-tuple-element.97), channel_id=1, source_target_pairs={{0,1},{1,0},{2,3},{3,2},{4,5},{5,4},{6,7},{7,6},{8,9},{9,8},{10,11... | collective-permute-start | bytes 73736 | tf_op jit(solution)/shard_map/ppermute | solution.py:239
  63.5 13.5 %collective-permute-start.10 = (bf16[96,128]{1,0:T(8,128)(2,1)S(1)}, bf16[96,128]{1,0:T(8,128)(2,1)S(1)}, u32[]{:S(2)}, u32[]{:S(2)}) collective-permute-start(bf16[96,128]{1,0:T(8,128)(2,1)S(1)} %get-tuple-element.98), channel_id=1, source_target_pairs={{1,2},{2,1},{3,4},{4,3},{5,6},{6,5},{7,8},{8,7},{9,10},{10,9},{11,... | collective-permute-start | bytes 73736 | tf_op jit(solution)/shard_map/ppermute | solution.py:239
  80.0 24.0 %collective-permute-start.11 = (bf16[2,576,128]{2,1,0:T(8,128)(2,1)S(1)}, bf16[2,576,128]{2,1,0:T(8,128)(2,1)S(1)}, u32[]{:S(2)}, u32[]{:S(2)}) collective-permute-start(bf16[2,576,128]{2,1,0:T(8,128)(2,1)S(1)} %get-tuple-element.103), channel_id=1, source_target_pairs={{0,64},{64,128},{128,192},{192,0},{1,65},{65,129},{129,193},{193,1... | collective-permute-start | bytes 884744 | tf_op jit(solution)/shard_map/ppermute | solution.py:444
  81.3 24.3 %collective-permute-start.13 = (bf16[2,576,128]{2,1,0:T(8,128)(2,1)S(1)}, bf16[2,576,128]{2,1,0:T(8,128)(2,1)S(1)}, u32[]{:S(2)}, u32[]{:S(2)}) collective-permute-start(bf16[2,576,128]{2,1,0:T(8,128)(2,1)S(1)} %get-tuple-element.109), channel_id=1, source_target_pairs={{0,128},{64,192},{128,0},{192,64},{1,129},{65,193},{129,1},{193,65... | collective-permute-start | bytes 884744 | tf_op jit(solution)/shard_map/ppermute | solution.py:444
  83.3 24.8 %collective-permute-start.15 = (bf16[2,576,128]{2,1,0:T(8,128)(2,1)S(1)}, bf16[2,576,128]{2,1,0:T(8,128)(2,1)S(1)}, u32[]{:S(2)}, u32[]{:S(2)}) collective-permute-start(bf16[2,576,128]{2,1,0:T(8,128)(2,1)S(1)} %get-tuple-element.115), channel_id=1, source_target_pairs={{0,192},{64,0},{128,64},{192,128},{1,193},{65,1},{129,65},{193,129... | collective-permute-start | bytes 884744 | tf_op jit(solution)/shard_map/ppermute | solution.py:444
  85.3 4.7 %collective-permute-start.16 = (bf16[144,128]{1,0:T(8,128)(2,1)S(1)}, bf16[144,128]{1,0:T(8,128)(2,1)S(1)}, u32[]{:S(2)}, u32[]{:S(2)}) collective-permute-start(bf16[144,128]{1,0:T(8,128)(2,1)S(1)} %get-tuple-element.121), channel_id=1, source_target_pairs={{0,1},{1,0},{2,3},{3,2},{4,5},{5,4},{6,7},{7,6},{8,9},{9,8},{10,11... | collective-permute-start | bytes 110600 | tf_op jit(solution)/shard_map/ppermute | solution.py:239
  85.4 13.9 %collective-permute-start.17 = (bf16[144,128]{1,0:T(8,128)(2,1)S(1)}, bf16[144,128]{1,0:T(8,128)(2,1)S(1)}, u32[]{:S(2)}, u32[]{:S(2)}) collective-permute-start(bf16[144,128]{1,0:T(8,128)(2,1)S(1)} %get-tuple-element.122), channel_id=1, source_target_pairs={{1,2},{2,1},{3,4},{4,3},{5,6},{6,5},{7,8},{8,7},{9,10},{10,9},{11,... | collective-permute-start | bytes 110600 | tf_op jit(solution)/shard_map/ppermute | solution.py:239
  104.0 32.6 %collective-permute-start.20 = (bf16[2,464,128]{2,1,0:T(8,128)(2,1)S(1)}, bf16[2,464,128]{2,1,0:T(8,128)(2,1)S(1)}, u32[]{:S(2)}, u32[]{:S(2)}) collective-permute-start(bf16[2,464,128]{2,1,0:T(8,128)(2,1)S(1)} %get-tuple-element.129), channel_id=1, source_target_pairs={{0,64},{64,128},{128,192},{192,0},{1,65},{65,129},{129,193},{193,1... | collective-permute-start | bytes 712712 | tf_op jit(solution)/shard_map/ppermute | solution.py:444
  105.6 31.0 %collective-permute-start.21 = (bf16[2,464,128]{2,1,0:T(8,128)(2,1)S(1)}, bf16[2,464,128]{2,1,0:T(8,128)(2,1)S(1)}, u32[]{:S(2)}, u32[]{:S(2)}) collective-permute-start(bf16[2,464,128]{2,1,0:T(8,128)(2,1)S(1)} %get-tuple-element.131), channel_id=1, source_target_pairs={{0,128},{64,192},{128,0},{192,64},{1,129},{65,193},{129,1},{193,65... | collective-permute-start | bytes 712712 | tf_op jit(solution)/shard_map/ppermute | solution.py:444
  108.1 28.5 %collective-permute-start.22 = (bf16[2,464,128]{2,1,0:T(8,128)(2,1)S(1)}, bf16[2,464,128]{2,1,0:T(8,128)(2,1)S(1)}, u32[]{:S(2)}, u32[]{:S(2)}) collective-permute-start(bf16[2,464,128]{2,1,0:T(8,128)(2,1)S(1)} %get-tuple-element.133), channel_id=1, source_target_pairs={{0,192},{64,0},{128,64},{192,128},{1,193},{65,1},{129,65},{193,129... | collective-permute-start | bytes 712712 | tf_op jit(solution)/shard_map/ppermute | solution.py:444
  118.4 2.0 %collective-permute-start.18 = (bf16[144,128]{1,0:T(8,128)(2,1)S(1)}, bf16[144,128]{1,0:T(8,128)(2,1)S(1)}, u32[]{:S(2)}, u32[]{:S(2)}) collective-permute-start(bf16[144,128]{1,0:T(8,128)(2,1)S(1)} %get-tuple-element.126), channel_id=1, source_target_pairs={{0,1},{1,0},{2,3},{3,2},{4,5},{5,4},{6,7},{7,6},{8,9},{9,8},{10,11... | collective-permute-start | bytes 110600 | tf_op jit(solution)/shard_map/ppermute | solution.py:239
  118.5 13.4 %collective-permute-start.19 = (bf16[144,128]{1,0:T(8,128)(2,1)S(1)}, bf16[144,128]{1,0:T(8,128)(2,1)S(1)}, u32[]{:S(2)}, u32[]{:S(2)}) collective-permute-start(bf16[144,128]{1,0:T(8,128)(2,1)S(1)} %get-tuple-element.127), channel_id=1, source_target_pairs={{1,2},{2,1},{3,4},{4,3},{5,6},{6,5},{7,8},{8,7},{9,10},{10,9},{11,... | collective-permute-start | bytes 110600 | tf_op jit(solution)/shard_map/ppermute | solution.py:239
  138.3 3.0 %collective-permute-start.23 = (bf16[128,128]{1,0:T(8,128)(2,1)S(1)}, bf16[128,128]{1,0:T(8,128)(2,1)S(1)}, u32[]{:S(2)}, u32[]{:S(2)}) collective-permute-start(bf16[128,128]{1,0:T(8,128)(2,1)S(1)} %get-tuple-element.137), channel_id=1, source_target_pairs={{0,1},{1,0},{2,3},{3,2},{4,5},{5,4},{6,7},{7,6},{8,9},{9,8},{10,11... | collective-permute-start | bytes 98312 | tf_op jit(solution)/shard_map/ppermute | solution.py:239
  138.4 13.4 %collective-permute-start.24 = (bf16[128,128]{1,0:T(8,128)(2,1)S(1)}, bf16[128,128]{1,0:T(8,128)(2,1)S(1)}, u32[]{:S(2)}, u32[]{:S(2)}) collective-permute-start(bf16[128,128]{1,0:T(8,128)(2,1)S(1)} %get-tuple-element.138), channel_id=1, source_target_pairs={{1,2},{2,1},{3,4},{4,3},{5,6},{6,5},{7,8},{8,7},{9,10},{10,9},{11,... | collective-permute-start | bytes 98312 | tf_op jit(solution)/shard_map/ppermute | solution.py:239

commit v3 on v2

--- a/solution.py
+++ b/solution.py
@@ -45,13 +45,21 @@
     return -(-rows // (16 * FOLD)) * 16
 
 
-def weights_kernel(even_ref, trace_ref, time_ref, *refs):
-    mats_ref, times_ref = refs[-2:]
+def place_taps(taps_ref, origin, step):
+    width = taps_ref.shape[1]
+    tap = lax.broadcasted_iota(jnp.int32, (width, SPAN), 0)
+    at = lax.broadcasted_iota(jnp.int32, (width, SPAN), 1)
+    spread = jnp.where(at == (origin + step * tap + SPAN) % SPAN, 1.0, 0.0).astype(jnp.bfloat16)
+    return jnp.dot(taps_ref[...], spread, preferred_element_type=jnp.float32)
+
+
+def fill_weights(even, trace_ref, time_ref, mats_ref, times_ref):
     fans = trace_ref.shape[0]
     blocks = mats_ref.shape[0]
-    even = even_ref[0] == 1
+    trace_rows = place_taps(trace_ref, trace_ref.shape[1] // 2, -1)
+    time_rows = place_taps(time_ref, 0, 1)
     for fan in range(fans):
-        row = jnp.broadcast_to(trace_ref[fan : fan + 1, :], (LANES, SPAN))
+        row = jnp.broadcast_to(trace_rows[fan : fan + 1, :], (LANES, SPAN))
         own = pltpu.roll(row, 0, 1, stride=1, stride_axis=0)[:, :LANES]
         left = pltpu.roll(row[:EDGE], SPAN - EDGE, 1, stride=1, stride_axis=0)[:, :LANES]
         right = pltpu.roll(row[:EDGE], LANES, 1, stride=1, stride_axis=0)[:, :LANES]
@@ -72,29 +80,78 @@
             mats_ref[block, pair, LANES:, cols] = jnp.concatenate(parts, axis=0).astype(
                 jnp.bfloat16
             )
-        taps = jnp.broadcast_to(time_ref[fan : fan + 1, :], (WIDE, SPAN))
+        taps = jnp.broadcast_to(time_rows[fan : fan + 1, :], (WIDE, SPAN))
         times_ref[:, fan * SPAN : (fan + 1) * SPAN] = pltpu.roll(
             taps, 0, 1, stride=1, stride_axis=0
         ).astype(jnp.bfloat16)
 
 
-def weights(even, trace_taps, time_taps, blocks, *after):
-    fans, width = trace_taps.shape
-    turned = jnp.pad(trace_taps[:, ::-1].astype(jnp.float32), ((0, 0), (0, SPAN - width)))
-    turned = jnp.roll(turned, width // 2 - width + 1, axis=1)
-    late = jnp.pad(time_taps.astype(jnp.float32), ((0, 0), (0, SPAN - time_taps.shape[1])))
+def weights_kernel(even_ref, trace_ref, time_ref, mats_ref, times_ref):
+    fill_weights(even_ref[0] == 1, trace_ref, time_ref, mats_ref, times_ref)
+
+
+def ranks(targets, blocks):
+    owners = [lax.div(target, blocks) for target in targets]
+    order = []
+    for block, owner in enumerate(owners):
+        rank = jnp.int32(0)
+        for other in owners[:block]:
+            rank = rank + jnp.where(other == owner, 1, 0)
+        order.append(rank)
+    return owners, order
+
+
+def late_kernel(even_ref, me_ref, trace_ref, time_ref, *refs):
+    mats_ref, times_ref, slots_ref = refs[-3:]
+    columns = refs[:-4]
+    blocks, count, me = mats_ref.shape[0], len(columns), me_ref[0]
+    fill_weights(even_ref[0] == 1, trace_ref, time_ref, mats_ref, times_ref)
+    slot_cap = blocks // 2
+    near, far = [jnp.int32(0)] * blocks, [jnp.int32(0)] * blocks
+    for offset, column in enumerate(columns):
+        targets = [column[block] for block in range(blocks)]
+        order = ranks(targets, blocks)[1]
+        source = lax.rem(me - offset + count, count)
+        for target, rank in zip(targets, order):
+            for block in range(blocks):
+                found = target == me * blocks + block
+                near[block] = jnp.where(found, offset * slot_cap + rank, near[block])
+                far[block] = jnp.where(found, source * slot_cap + rank, far[block])
+    for block in range(blocks):
+        slots_ref[block] = near[block]
+        slots_ref[blocks + block] = far[block]
+
+
+def weight_shapes(blocks, fans):
+    return [
+        jax.ShapeDtypeStruct((blocks, fans // 2, 2 * LANES, 2 * LANES), jnp.bfloat16),
+        jax.ShapeDtypeStruct((WIDE, fans * SPAN), jnp.bfloat16),
+    ]
+
+
+def weights(even, trace_taps, time_taps, blocks):
     return pl.pallas_call(
         weights_kernel,
-        in_specs=[SMEM, VMEM, VMEM] + [ANY] * len(after),
+        in_specs=[SMEM, VMEM, VMEM],
         out_specs=[VMEM, VMEM],
-        out_shape=(
-            jax.ShapeDtypeStruct((blocks, fans // 2, 2 * LANES, 2 * LANES), jnp.bfloat16),
-            jax.ShapeDtypeStruct((WIDE, fans * SPAN), jnp.bfloat16),
-        ),
+        out_shape=weight_shapes(blocks, trace_taps.shape[0]),
         cost_estimate=NO_COST,
         compiler_params=PARAMS,
         name="weights",
-    )(even, turned, late, *after)
+    )(even, trace_taps, time_taps)
+
+
+def late_weights(even, me, trace_taps, time_taps, columns, after, blocks):
+    return pl.pallas_call(
+        late_kernel,
+        in_specs=[SMEM, SMEM, VMEM, VMEM] + [SMEM] * len(columns) + [ANY],
+        out_specs=[VMEM, VMEM, SMEM],
+        out_shape=weight_shapes(blocks, trace_taps.shape[0])
+        + [jax.ShapeDtypeStruct((2 * blocks,), jnp.int32)],
+        cost_estimate=NO_COST,
+        compiler_params=PARAMS,
+        name="late_weights",
+    )(even, me, trace_taps, time_taps, *columns, after)
 
 
 def edge_picks(even, blocks):
@@ -122,13 +179,12 @@
     return found
 
 
-def pack_edges(picks, tiles_ref, packed_refs, ready):
+def pack_edges(picks, tiles_ref, packed_refs):
     blocks, rows = tiles_ref.shape[:2]
     fold = folded_rows(rows)
     totals = [None, None]
     for part in range(FOLD):
         start, stop = part * fold, min(rows, (part + 1) * fold)
-        ready(part)
         found = pick_part(picks, tiles_ref, start, stop)
         if stop - start < fold:
             found = jnp.concatenate(
@@ -159,20 +215,12 @@
         start = until
 
 
-def first_edges_kernel(even_ref, x_ref, out_a, out_b, picks_ref, held, sem):
-    blocks, rows = held.shape[:2]
-    fold = folded_rows(rows)
-
-    def copy(part):
-        span = pl.ds(part * fold, min(rows, (part + 1) * fold) - part * fold)
-        return pltpu.make_async_copy(x_ref.at[:, span, :], held.at[:, span, :], sem.at[part])
-
-    for part in range(FOLD):
-        copy(part).start()
+def first_edges_kernel(even_ref, x_ref, out_a, out_b, picks_ref):
+    blocks = x_ref.shape[0]
     picks = edge_picks(even_ref[0] == 1, blocks)
     for pair, pick in enumerate(picks):
         picks_ref[pair] = pick
-    pack_edges(picks, held, (out_a, out_b), lambda part: copy(part).wait())
+    pack_edges(picks, x_ref, (out_a, out_b))
 
 
 def first_edges(even, traces):
@@ -180,26 +228,24 @@
     packed = jax.ShapeDtypeStruct((folded_rows(traces.shape[1]), LANES), jnp.bfloat16)
     return pl.pallas_call(
         first_edges_kernel,
-        in_specs=[SMEM, HBM],
-        out_specs=[VMEM] * 4,
+        in_specs=[SMEM, VMEM],
+        out_specs=[VMEM] * 3,
         out_shape=[
             packed,
             packed,
             jax.ShapeDtypeStruct((blocks // 2, 2 * LANES, 2 * LANES), jnp.bfloat16),
-            jax.ShapeDtypeStruct(traces.shape, jnp.bfloat16),
         ],
-        scratch_shapes=[pltpu.SemaphoreType.DMA((FOLD,))],
         cost_estimate=NO_COST,
-        compiler_params=pltpu.CompilerParams(vmem_limit_bytes=50 * 2**20),
+        compiler_params=PARAMS,
         name="first_edges",
     )(even, traces)
 
 
-def second_edges_kernel(slot_ref, picks_ref, *refs):
+def second_edges_kernel(base, slot_ref, picks_ref, *refs):
     parts, (_, sorted_ref, out_a, out_b, sem) = refs[:-5], refs[-5:]
     blocks, slot_cap = sorted_ref.shape[0], parts[0].shape[0]
     for block in range(blocks):
-        slot = slot_ref[block]
+        slot = slot_ref[base + block]
         for offset, part in enumerate(parts):
 
             @pl.when(slot // slot_cap == offset)
@@ -211,14 +257,14 @@
     for block in range(blocks):
         pltpu.make_async_copy(parts[0].at[0], sorted_ref.at[block], sem.at[block]).wait()
     picks = [picks_ref[pair] for pair in range(blocks // 2)]
-    pack_edges(picks, sorted_ref, (out_a, out_b), lambda part: None)
+    pack_edges(picks, sorted_ref, (out_a, out_b))
 
 
 def second_edges(slots, picks, arrived, after, blocks):
     rows = arrived[0].shape[1]
     packed = jax.ShapeDtypeStruct((folded_rows(rows), LANES), jnp.bfloat16)
     return pl.pallas_call(
-        second_edges_kernel,
+        functools.partial(second_edges_kernel, blocks if len(arrived) == 1 else 0),
         in_specs=[SMEM, VMEM] + [ANY] * (len(arrived) + 1),
         out_specs=[VMEM] * 3,
         scratch_shapes=[pltpu.SemaphoreType.DMA((blocks,))],
@@ -240,7 +286,7 @@
     return got
 
 
-def filter_window(pieces, merged, fans_ref, mats_ref, times_ref, rows, give):
+def filter_window(pieces, merged, fans_ref, mats_ref, times_ref, rows, give, finish):
     fan_pairs = mats_ref.shape[1]
     blocks = mats_ref.shape[0]
     tall = fans_ref.shape[1]
@@ -275,19 +321,26 @@
                 )
                 total = part if total is None else total + part
             give(pair, start, total)
+        finish(pair)
         return carry
 
     lax.fori_loop(0, blocks // 2, do_pair, 0)
 
 
-def first_kernel(start, stop, owners, key_ref, x_ref, edge_a, edge_b, mats_ref, times_ref, *refs):
-    outs = refs[-4 - owners : -4]
-    merged, fans_ref, done, sem = refs[-4:]
+def first_kernel(
+    start, sizes, samples, owners, me_ref, target_ref, x_ref, edge_a, edge_b, mats_ref, times_ref,
+    *refs
+):
+    outs, (merged, fans_ref, done, sem) = list(refs[-4 - sum(n for _, n in sizes) : -4]), refs[-4:]
     blocks, rows = done.shape[:2]
-    samples = x_ref.shape[1]
-    slot_cap = outs[0].shape[0]
     window = start - REACH // 2
-    begin, end = max(0, window), min(samples, stop + REACH // 2)
+    begin, end = max(0, window), min(samples, start + rows + REACH // 2)
+    targets, order = ranks([target_ref[block] for block in range(blocks)], blocks)
+    groups, at = [], 0
+    for size, number in sizes:
+        groups.append((at, size, outs[:number]))
+        outs = outs[number:]
+        at += size
 
     def put(row, values):
         merged[row - window : row - window + values.shape[0], :] = values
@@ -300,45 +353,72 @@
             done[2 * pair + half, at : at + values.shape[0], :] = values[
                 :, half * LANES : (half + 1) * LANES
             ]
-        if at + values.shape[0] == rows:
-            for half in range(2):
-                block = 2 * pair + half
-                key = key_ref[block]
-                for offset, out_ref in enumerate(outs):
-
-                    @pl.when(key // slot_cap == offset)
+
+    def pick(values, pair, half):
+        value = values[half]
+        for other in range(1, blocks // 2):
+            value = jnp.where(pair == other, values[2 * other + half], value)
+        return value
+
+    def finish(pair):
+        for half in range(2):
+            block = 2 * pair + half
+            owner, rank = pick(targets, pair, half), pick(order, pair, half)
+            away = lax.rem(owner - me_ref[0] + owners, owners)
+            for group, (at, size, arrays) in enumerate(groups):
+                part = done.at[block, pl.ds(at, size), :]
+                if len(arrays) == 1:
+                    slot = owner * (blocks // 2) + rank
+                    pltpu.make_async_copy(part, arrays[0].at[slot], sem.at[group, block]).start()
+                    continue
+                for offset, out_ref in enumerate(arrays):
+
+                    @pl.when(away == offset)
                     def _():
                         pltpu.make_async_copy(
-                            done.at[block], out_ref.at[key % slot_cap], sem.at[block]
+                            part, out_ref.at[rank], sem.at[group, block]
                         ).start()
 
-    pieces = [(begin - window, end - begin, lambda block: x_ref[block, begin:end, :])]
-    filter_window(pieces, merged, fans_ref, mats_ref, times_ref, rows, give)
-    for block in range(blocks):
-        pltpu.make_async_copy(done.at[block], outs[0].at[0], sem.at[block]).wait()
-
-
-def first_pass(keys, owners, traces, edges, mats, times, after, start, stop):
+    pieces = [
+        (begin - window, end - begin, lambda block: x_ref[block, begin:end, :])
+    ]
+    filter_window(pieces, merged, fans_ref, mats_ref, times_ref, rows, give, finish)
+    for group, (at, size, arrays) in enumerate(groups):
+        for block in range(blocks):
+            pltpu.make_async_copy(
+                done.at[block, pl.ds(at, size), :], arrays[0].at[0], sem.at[group, block]
+            ).wait()
+
+
+def first_pass(me, target, owners, traces, samples, edges, mats, times, after, start, sizes):
     blocks = traces.shape[0]
     fans = 2 * mats.shape[1]
-    rows = stop - start
+    rows = sum(size for size, _ in sizes)
     tall = window_rows(rows)
-    sent = jax.ShapeDtypeStruct((blocks // 2, rows, LANES), jnp.bfloat16)
-    return pl.pallas_call(
-        functools.partial(first_kernel, start, stop, owners),
-        in_specs=[SMEM] + [VMEM] * 5 + [ANY] * len(after),
-        out_specs=[ANY] * owners,
+    shapes = []
+    for size, number in sizes:
+        slots = owners * (blocks // 2) // number
+        shapes += [jax.ShapeDtypeStruct((slots, size, LANES), jnp.bfloat16)] * number
+    flat = pl.pallas_call(
+        functools.partial(first_kernel, start, sizes, samples, owners),
+        in_specs=[SMEM, SMEM] + [VMEM] * 5 + [ANY] * len(after),
+        out_specs=[ANY] * len(shapes),
         scratch_shapes=[
             pltpu.VMEM((tall, LANES), jnp.bfloat16),
             pltpu.VMEM((fans, tall, 2 * LANES), jnp.bfloat16),
             pltpu.VMEM((blocks, rows, LANES), jnp.bfloat16),
-            pltpu.SemaphoreType.DMA((blocks,)),
+            pltpu.SemaphoreType.DMA((len(sizes), blocks)),
         ],
-        out_shape=[sent] * owners,
+        out_shape=shapes,
         cost_estimate=NO_COST,
         compiler_params=PARAMS,
         name="first_pass",
-    )(keys, traces, *edges, mats, times, *after)
+    )(me, target, traces, *edges, mats, times, *after)
+    chunks = []
+    for _, number in sizes:
+        chunks.append(flat[:number])
+        flat = flat[number:]
+    return chunks
 
 
 def second_kernel(at, has_past, *refs):
@@ -379,11 +459,12 @@
             done[2 * pair + half, start : start + values.shape[0], :] = values[
                 :, half * LANES : (half + 1) * LANES
             ]
-        if start + values.shape[0] == rows:
-            for half in range(2):
-                copy(2 * pair + half).start()
-
-    filter_window(pieces, merged, fans_ref, mats_ref, times_ref, rows, give)
+
+    def finish(pair):
+        for half in range(2):
+            copy(2 * pair + half).start()
+
+    filter_window(pieces, merged, fans_ref, mats_ref, times_ref, rows, give, finish)
     for block in range(blocks):
         copy(block).wait()
 
@@ -424,74 +505,77 @@
 ):
     blocks, samples, _ = traces.shape
     owners = lax.axis_size("rcv")
-    me = lax.axis_index("rcv")
-    slot_cap = blocks // 2
+    me = lax.axis_index("rcv").astype(jnp.int32).reshape(1)
     even = (1 - lax.axis_index("shot") % 2).astype(jnp.int32).reshape(1)
-
-    target = dest_row[:, 0]
-    ids = jnp.arange(blocks, dtype=jnp.int32)
-
-    def ranks(owner):
-        return jnp.sum(
-            (
-                (ids[:, None] > ids[None, :]) & (owner[..., :, None] == owner[..., None, :])
-            ).astype(jnp.int32),
-            axis=-1,
-        )
+    target = dest_row.reshape(blocks)
 
     def send(values, offset):
         pairs = [(i, (i + offset) % owners) for i in range(owners)]
         return lax.ppermute(values, "rcv", pairs) if offset else values
 
-    owner = target // blocks
-    keys = (owner - me + owners) % owners * slot_cap + ranks(owner)
-
     bounds = chunk_bounds(samples)
     count = len(bounds) - 1
-    *packed, picks, traces = first_edges(even, traces)
+    sizes = [
+        (bounds[step + 1] - bounds[step], owners) for step in range(count)
+    ]
+    *packed, picks = first_edges(even, traces)
     edges = swap_edges(packed)
-    late_target, _ = lax.optimization_barrier((target, packed[0]))
-    column = jnp.stack([send(late_target, offset) for offset in range(owners)])
-    place = jnp.arange(owners, dtype=jnp.int32)[:, None] * slot_cap + ranks(column // blocks)
-    mine = column[None] == (me * blocks + ids)[:, None, None]
-    slots = jnp.sum(jnp.where(mine, place[None], 0), axis=(1, 2))
     mats, times = weights(even, first_trace_taps, first_time_taps, blocks)
 
-    def exchange(sent, before, token):
+    def first(after, start, sizes):
+        return first_pass(
+            me, target, owners, traces, samples, edges, mats, times, after, start, sizes
+        )
+
+    def exchange(sent, before, *after):
+        if len(sent) == 1:
+            part = sent[0]
+            if before is not None:
+                part, before[0], *_ = lax.optimization_barrier((part, before[0], *after))
+            return [lax.all_to_all(part, "rcv", split_axis=0, concat_axis=0, tiled=True)]
         arrived = []
         for offset, part in enumerate(sent):
             if offset and before is not None:
-                part, before[offset] = lax.optimization_barrier((part, before[offset]))
-            if offset and token is not None:
-                part, _ = lax.optimization_barrier((part, token))
+                part, before[offset], *_ = lax.optimization_barrier(
+                    (part, before[offset], *after)
+                )
             arrived.append(send(part, offset))
         return arrived
 
-    sent, after = [], [slots]
-    for step in range(count):
-        sent.append(
-            first_pass(
-                keys, owners, traces, edges, mats, times, after, bounds[step], bounds[step + 1]
-            )
+    sent = first([], 0, sizes[:1])
+    late_target, _ = lax.optimization_barrier((target, sent[0][0]))
+    columns = [send(late_target, offset) for offset in range(owners)]
+    arrived = [exchange(sent[0], None)]
+    if count > 1:
+        sent += first(columns[1:], bounds[1], sizes[1:])
+    mats, times, slots = late_weights(
+        even, me, second_trace_taps, second_time_taps, columns, sent[-1][0], blocks
+    )
+
+    out, past, now, token, rims = None, None, None, None, None
+
+    def second(step, after):
+        at = max(0, bounds[step] - REACH // 2)
+        stop = bounds[step + 1] - REACH // 2 if step + 1 < count else samples
+        return second_pass(
+            blocks, samples, past, now, mats, times, after, out, at, stop - at
         )
-        after = [sent[-1][0]]
-    arrived = [exchange(sent[0], None, None)]
-
-    mats, times = weights(even, second_trace_taps, second_time_taps, blocks, sent[0][0])
-    out, past, token = None, None, None
+
     for step in range(count):
         if step + 1 < count:
-            arrived.append(exchange(sent[step + 1], arrived[step], token))
-        after = token if step else sent[min(2, count - 1)][0]
-        gathered, *packed = second_edges(slots, picks, arrived[step], after, blocks)
-        now = (gathered, *swap_edges(packed))
-        at = max(0, bounds[step] - REACH // 2)
-        stop = bounds[step + 1] - REACH // 2 if step + 1 < count else samples
-        out, token = second_pass(
-            blocks, samples, past, now, mats, times, sent[min(step + 3, count - 1)][0], out,
-            at, stop - at,
+            ahead = [*now[1:]] if now else []
+            ahead += [token] if token is not None else []
+            arrived.append(exchange(sent[step + 1], arrived[step], *ahead))
+        gathered, *packed = second_edges(
+            slots, picks, arrived[step], times if token is None else token, blocks
         )
-        past = now
+        rims = packed[0]
+        coming = (gathered, *swap_edges(packed))
+        if step:
+            out, token = second(step - 1, rims)
+            past = now
+        now = coming
+    out, token = second(count - 1, slots)
     return out
 
 

time: 158 us -> 145 us (0.918)
  waiting for transfers between devices: 43.2 us -> 33.9 us
  starting transfers between devices: 53.4 us -> 60.2 us
  other arithmetic: 5.49 us -> 0 us
  Pallas kernels: 47.2 us -> 43.1 us
  local copies, waits for them, and re-layouts: 7.06 us -> 5.17 us
    ppermute x10, starting transfers between devices: 21.2 us -> 42.3 us  [swap_edges(): got.append(lax.ppermute(edges, 'shot', pairs))]
    ppermute x15, starting transfers between devices: 32.2 us -> 18 us  [send(): return lax.ppermute(values, 'rcv', pairs) if offset else values]
    ppermute x10, waiting for transfers between devices: 37.6 us -> 25.2 us  [swap_edges(): got.append(lax.ppermute(edges, 'shot', pairs))]
    pallas_call x11 -> x9, Pallas kernels: 30.1 us -> 25.4 us  [the longest x2 14.2 us: first_pass(): pl.pallas_call(functools.partial(first_kernel, start, sizes, samples, own...]
    ppermute x15, waiting for transfers between devices: 5.58 us -> 8.64 us  [send(): return lax.ppermute(values, 'rcv', pairs) if offset else values]
  transfers between devices with their start and end apart: 25 -> 25, of which waited for: 7 -> 8; matrix products, arithmetic and copies ran while one was open for 4% -> 0% of each run, Pallas kernels for 21% -> 23%
where the time goes in v3:
time: 145 us; the launch traced here: 143 us
  starting transfers between devices  60.2 us (42%)
  Pallas kernels  43.1 us (30%)
  waiting for transfers between devices  33.9 us (23%)
  local copies, waits for them, and re-layouts  5.17 us (4%)
    ppermute x10, starting transfers between devices, swap_edges(): got.append(lax.ppermute(edges, 'shot', pairs))  42.3 us
    ppermute x10, waiting for transfers between devices, swap_edges(): got.append(lax.ppermute(edges, 'shot', pairs))  25.2 us
    ppermute x15, starting transfers between devices, send(): return lax.ppermute(values, 'rcv', pairs) if offset else values  18 us
    pallas_call x4, Pallas kernels, second_pass(): pl.pallas_call(functools.partial(second_kernel, at, past is not None), in...  17.7 us
    pallas_call x2, Pallas kernels, first_pass(): pl.pallas_call(functools.partial(first_kernel, start, sizes, samples, own...  14.2 us
    ppermute x15, waiting for transfers between devices, send(): return lax.ppermute(values, 'rcv', pairs) if offset else values  8.64 us
    pallas_call x4, Pallas kernels, second_edges(): pl.pallas_call(functools.partial(second_edges_kernel, blocks if len(arriv...  7.13 us
    unnamed x16, local copies, waits for them, and re-layouts  5.17 us
  transfers between devices with their start and end apart: 25, of which 8 were waited for; matrix products, arithmetic and copies ran while one was open for 0% of the time, Pallas kernels for 23%

profile of v3, /device:TPU:192, one launch (start us, length us, event | category | flops | bytes accessed | tf_op | source)
XLA Modules:
  0.0 142.8 jit_solution(14537565536685558162)
XLA Ops:
  0.0 1.6 %copy-done = bf16[4,2000,128]{2,1,0:T(8,128)(2,1)S(1)} copy-done((bf16[4,2000,128]{2,1,0:T(8,128)(2,1)S(1)}, bf16[4,2000,128]{2,1,0:T(8,128)(2,1)}, u32[]{:S(2)}) %copy-start) | copy-done | bytes 2048024
  1.6 1.6 %first_edges.1 = (bf16[512,128]{1,0:T(8,128)(2,1)}, bf16[512,128]{1,0:T(8,128)(2,1)S(1)}, bf16[2,256,256]{2,1,0:T(8,128)(2,1)S(1)}) custom-call(s32[1]{0:T(128)} %bitcast.even_ref, bf16[4,2000,128]{2,1,0:T(8,128)(2,1)S(1)} %copy-done), custom_call_target="tpu_custom_call" | custom-call | flops 1 | bytes 1 | tf_op jit(solution)/shard_map/first_edges/pallas_call | solution.py:229
  3.2 0.0 collective-permute-start
  3.2 7.2 %collective-permute-start.1 = (bf16[512,128]{1,0:T(8,128)(2,1)S(1)}, bf16[512,128]{1,0:T(8,128)(2,1)S(1)}, u32[]{:S(2)}, u32[]{:S(2)}) collective-permute-start(bf16[512,128]{1,0:T(8,128)(2,1)S(1)} %get-tuple-element.67), channel_id=1, source_target_pairs={{1,2},{2,1},{3,4},{4,3},{5,6},{6,5},{7,8},{8,7},{9,10},{10,9},{11,... | collective-permute-start | bytes 393224 | tf_op jit(solution)/shard_map/ppermute | solution.py:285
  10.4 0.0 copy-start.6
  10.4 0.7 copy-done.6
  11.1 0.7 copy-done.7
  11.8 0.6 weights.1
  12.4 0.0 collective-permute-done.edge_a
  12.4 6.6 %collective-permute-done.1.edge_b = bf16[512,128]{1,0:T(8,128)(2,1)S(1)} collective-permute-done((bf16[512,128]{1,0:T(8,128)(2,1)S(1)}, bf16[512,128]{1,0:T(8,128)(2,1)S(1)}, u32[]{:S(2)}, u32[]{:S(2)}) %collective-permute-start.1) | collective-permute-done | bytes 131104 | tf_op jit(solution)/shard_map/ppermute | solution.py:285
  19.0 1.6 %copy-done.1 = bf16[4,2000,128]{2,1,0:T(8,128)(2,1)S(1)} copy-done((bf16[4,2000,128]{2,1,0:T(8,128)(2,1)S(1)}, bf16[4,2000,128]{2,1,0:T(8,128)(2,1)}, u32[]{:S(2)}) %copy-start.1) | copy-done | bytes 2048024
  20.6 0.7 copy-done.2
  21.3 3.4 %first_pass.2 = (bf16[2,384,128]{2,1,0:T(8,128)(2,1)S(1)}, bf16[2,384,128]{2,1,0:T(8,128)(2,1)S(1)}, bf16[2,384,128]{2,1,0:T(8,128)(2,1)S(1)}, bf16[2,384,128]{2,1,0:T(8,128)(2,1)S(1)}) custom-call(s32[1]{0:T(128)} %bitcast.1.me_ref, s32[4]{0:T(128)S(1)} %bitcast.3, bf16[4,2000,128]{2,1,0:T(8,128)(2,1)S(1)} %copy-done.1, ...), custom_call_target="tpu_custom_call" | custom-call | flops 1 | bytes 1 | tf_op jit(solution)/shard_map/first_pass/pallas_call | solution.py:402
  24.7 1.1 collective-permute-start.8
  25.8 1.1 collective-permute-start.7
  26.9 0.5 collective-permute-start.5
  27.4 1.5 %collective-permute-start.4 = (s32[4]{0:T(128)S(1)}, s32[4]{0:T(128)S(1)}, u32[]{:S(2)}, u32[]{:S(2)}) collective-permute-start(s32[4]{0:T(128)S(1)} %bitcast.4), channel_id=1, source_target_pairs={{0,192},{64,0},{128,64},{192,128},{1,193},{65,1},{129,65},{193,129... | collective-permute-start | bytes 56 | tf_op jit(solution)/shard_map/ppermute | solution.py:514
  28.9 3.6 %collective-permute-start.3 = (s32[4]{0:T(128)S(1)}, s32[4]{0:T(128)S(1)}, u32[]{:S(2)}, u32[]{:S(2)}) collective-permute-start(s32[4]{0:T(128)S(1)} %bitcast.5), channel_id=1, source_target_pairs={{0,128},{64,192},{128,0},{192,64},{1,129},{65,193},{129,1},{193,65... | collective-permute-start | bytes 56 | tf_op jit(solution)/shard_map/ppermute | solution.py:514
  32.5 2.8 %collective-permute-done.4.refs_2_.refs_3_ = s32[4]{0:T(128)S(1)} collective-permute-done((s32[4]{0:T(128)S(1)}, s32[4]{0:T(128)S(1)}, u32[]{:S(2)}, u32[]{:S(2)}) %collective-permute-start.4) | collective-permute-done | bytes 48 | tf_op jit(solution)/shard_map/ppermute | solution.py:514
  35.3 0.9 collective-permute-start.2
  36.2 0.0 collective-permute-done.3.refs_1_.refs_2_
  36.2 3.1 %collective-permute-done.2.refs_0_.refs_1_ = s32[4]{0:T(128)S(1)} collective-permute-done((s32[4]{0:T(128)S(1)}, s32[4]{0:T(128)S(1)}, u32[]{:S(2)}, u32[]{:S(2)}) %collective-permute-start.2) | collective-permute-done | bytes 48 | tf_op jit(solution)/shard_map/ppermute | solution.py:514
  39.3 10.8 %first_pass.3 = (bf16[2,576,128]{2,1,0:T(8,128)(2,1)S(1)}, bf16[2,576,128]{2,1,0:T(8,128)(2,1)S(1)}, bf16[2,576,128]{2,1,0:T(8,128)(2,1)S(1)}, bf16[2,576,128]{2...) custom-call(s32[1]{0:T(128)} %bitcast.1.me_ref, ...), custom_call_target="tpu_custom_call" | custom-call | flops 1 | bytes 1 | tf_op jit(solution)/shard_map/first_pass/pallas_call | solution.py:402
  50.1 0.0 collective-permute-done.8.refs_3_
  50.1 2.1 %collective-permute-start.13 = (bf16[2,576,128]{2,1,0:T(8,128)(2,1)S(1)}, bf16[2,576,128]{2,1,0:T(8,128)(2,1)S(1)}, u32[]{:S(2)}, u32[]{:S(2)}) collective-permute-start(bf16[2,576,128]{2,1,0:T(8,128)(2,1)S(1)} %get-tuple-element.98), channel_id=1, source_target_pairs={{0,192},{64,0},{128,64},{192,128},{1,193},{65,1},{129,65},{193,129... | collective-permute-start | bytes 884744 | tf_op jit(solution)/shard_map/ppermute | solution.py:514
  52.2 0.0 collective-permute-done.7.refs_2_
  52.2 0.8 collective-permute-start.12
  53.0 0.0 collective-permute-done.5.refs_1_
  53.0 0.8 collective-permute-start.6
  53.7 1.8 %late_weights.1 = (bf16[4,4,256,256]{3,2,1,0:T(8,128)(2,1)S(1)}, bf16[192,2048]{1,0:T(8,128)(2,1)S(1)}, s32[8]{0:T(128)S(1)}) custom-call(s32[1]{0:T(128)} %bitcast.even_ref, s32[1]{0:T(128)} %bitcast.1.me_ref, bf16[8,16]{1,0:T(8,128)(2,1)S(1)} %copy-done.4, bf16[8,64]{1,0:T(8,128)(2,1)S(1)} %copy-done.5, s32[4]{0:T(128)S(1)} %bitcast.8, ...), custom_call_target="tpu_custom_call" | custom-call | flops 1 | bytes 1 | tf_op jit(solution)/shard_map/late_weights/pallas_call | solution.py:145
  55.6 1.6 %second_edges.4 = (bf16[4,384,128]{2,1,0:T(8,128)(2,1)S(1)}, bf16[96,128]{1,0:T(8,128)(2,1)S(1)}, bf16[96,128]{1,0:T(8,128)(2,1)S(1)}) custom-call(s32[8]{0:T(128)S(1)} %get-tuple-element.73.slot_ref.refs_8_, bf16[2,256,256]{2,1,0:T(8,128)(2,1)S(1)} %get-tuple-element.74.picks_ref, bf16[2,384,128]{2,1,0:T(8,128)(2,1)S(1)} %get-tuple-element.70.refs_0_, ...), custom_call_target="tpu_custom_call" | custom-call | flops 1 | bytes 1 | tf_op jit(solution)/shard_map/second_edges/pallas_call | solution.py:266
  57.2 0.1 collective-permute-start.9
  57.3 4.5 %collective-permute-start.10 = (bf16[96,128]{1,0:T(8,128)(2,1)S(1)}, bf16[96,128]{1,0:T(8,128)(2,1)S(1)}, u32[]{:S(2)}, u32[]{:S(2)}) collective-permute-start(bf16[96,128]{1,0:T(8,128)(2,1)S(1)} %get-tuple-element.90), channel_id=1, source_target_pairs={{1,2},{2,1},{3,4},{4,3},{5,6},{6,5},{7,8},{8,7},{9,10},{10,9},{11,... | collective-permute-start | bytes 73736 | tf_op jit(solution)/shard_map/ppermute | solution.py:285
  61.8 0.0 collective-permute-done.9.refs_1_
  61.8 13.4 %collective-permute-done.10.refs_2_ = bf16[96,128]{1,0:T(8,128)(2,1)S(1)} collective-permute-done((bf16[96,128]{1,0:T(8,128)(2,1)S(1)}, bf16[96,128]{1,0:T(8,128)(2,1)S(1)}, u32[]{:S(2)}, u32[]{:S(2)}) %collective-permute-start.10) | collective-permute-done | bytes 24608 | tf_op jit(solution)/shard_map/ppermute | solution.py:285
  75.2 0.0 collective-permute-done.13.refs_3_
  75.2 0.0 collective-permute-start.17
  75.2 0.0 collective-permute-done.12.refs_2_
  75.2 2.3 %collective-permute-start.16 = (bf16[2,576,128]{2,1,0:T(8,128)(2,1)S(1)}, bf16[2,576,128]{2,1,0:T(8,128)(2,1)S(1)}, u32[]{:S(2)}, u32[]{:S(2)}) collective-permute-start(bf16[2,576,128]{2,1,0:T(8,128)(2,1)S(1)} %get-tuple-element.107), channel_id=1, source_target_pairs={{0,128},{64,192},{128,0},{192,64},{1,129},{65,193},{129,1},{193,65... | collective-permute-start | bytes 884744 | tf_op jit(solution)/shard_map/ppermute | solution.py:514
  77.5 0.0 collective-permute-done.6.refs_1_
  77.5 1.0 collective-permute-start.11
  78.5 1.9 %second_edges.5 = (bf16[4,576,128]{2,1,0:T(8,128)(2,1)S(1)}, bf16[144,128]{1,0:T(8,128)(2,1)S(1)}, bf16[144,128]{1,0:T(8,128)(2,1)S(1)}) custom-call(s32[8]{0:T(128)S(1)} %get-tuple-element.73.slot_ref.refs_8_, bf16[2,256,256]{2,1,0:T(8,128)(2,1)S(1)} %get-tuple-element.74.picks_ref, bf16[2,576,128]{2,1,0:T(8,128)(2,1)S(1)} %get-tuple-element.92.refs_0_, ...), custom_call_target="tpu_custom_call" | custom-call | flops 1 | bytes 1 | tf_op jit(solution)/shard_map/second_edges/pallas_call | solution.py:266
  80.4 16.6 %collective-permute-start.15 = (bf16[144,128]{1,0:T(8,128)(2,1)S(1)}, bf16[144,128]{1,0:T(8,128)(2,1)S(1)}, u32[]{:S(2)}, u32[]{:S(2)}) collective-permute-start(bf16[144,128]{1,0:T(8,128)(2,1)S(1)} %get-tuple-element.101), channel_id=1, source_target_pairs={{1,2},{2,1},{3,4},{4,3},{5,6},{6,5},{7,8},{8,7},{9,10},{10,9},{11,... | collective-permute-start | bytes 110600 | tf_op jit(solution)/shard_map/ppermute | solution.py:285
  96.9 0.1 collective-permute-start.14
  97.0 2.9 %second_pass.4 = (f32[4,2000,128]{2,1,0:T(8,128)}, f32[8,128]{1,0:T(8,128)S(1)}) custom-call(bf16[4,384,128]{2,1,0:T(8,128)(2,1)S(1)} %get-tuple-element.102.refs_0_, bf16[96,128]{1,0:T(8,128)(2,1)S(1)} %collective-permute-done.9.refs_1_, bf16[96,128]{1,0:T(8,128)(2,1)S(1)} %collective-permute-done.10.refs_2_, ...), custom_call_target="tpu_custom_call" | custom-call | flops 1 | bytes 1 | tf_op jit(solution)/shard_map/second_pass/pallas_call | solution.py:482
  100.0 2.5 %collective-permute-done.15.refs_5_.refs_2_ = bf16[144,128]{1,0:T(8,128)(2,1)S(1)} collective-permute-done((bf16[144,128]{1,0:T(8,128)(2,1)S(1)}, bf16[144,128]{1,0:T(8,128)(2,1)S(1)}, u32[]{:S(2)}, u32[]{:S(2)}) %collective-permute-start.15) | collective-permute-done | bytes 36896 | tf_op jit(solution)/shard_map/ppermute | solution.py:285
  102.5 0.0 collective-permute-done.14.refs_4_.refs_1_
  102.5 0.0 collective-permute-done.16.refs_2_
  102.5 0.0 collective-permute-done.11.refs_1_
  102.5 0.1 collective-permute-start.20
  102.6 0.7 collective-permute-start.21
  103.3 1.5 %collective-permute-start.22 = (bf16[2,464,128]{2,1,0:T(8,128)(2,1)S(1)}, bf16[2,464,128]{2,1,0:T(8,128)(2,1)S(1)}, u32[]{:S(2)}, u32[]{:S(2)}) collective-permute-start(bf16[2,464,128]{2,1,0:T(8,128)(2,1)S(1)} %get-tuple-element.117), channel_id=1, source_target_pairs={{0,192},{64,0},{128,64},{192,128},{1,193},{65,1},{129,65},{193,129... | collective-permute-start | bytes 712712 | tf_op jit(solution)/shard_map/ppermute | solution.py:514
  104.8 1.9 %second_edges.6 = (bf16[4,576,128]{2,1,0:T(8,128)(2,1)S(1)}, bf16[144,128]{1,0:T(8,128)(2,1)S(1)}, bf16[144,128]{1,0:T(8,128)(2,1)S(1)}) custom-call(s32[8]{0:T(128)S(1)} %get-tuple-element.73.slot_ref.refs_8_, bf16[2,256,256]{2,1,0:T(8,128)(2,1)S(1)} %get-tuple-element.74.picks_ref, bf16[2,576,128]{2,1,0:T(8,128)(2,1)S(1)} %get-tuple-element.75.refs_0_, ...), custom_call_target="tpu_custom_call" | custom-call | flops 1 | bytes 1 | tf_op jit(solution)/shard_map/second_edges/pallas_call | solution.py:266
  106.7 8.4 %collective-permute-start.19 = (bf16[144,128]{1,0:T(8,128)(2,1)S(1)}, bf16[144,128]{1,0:T(8,128)(2,1)S(1)}, u32[]{:S(2)}, u32[]{:S(2)}) collective-permute-start(bf16[144,128]{1,0:T(8,128)(2,1)S(1)} %get-tuple-element.114), channel_id=1, source_target_pairs={{1,2},{2,1},{3,4},{4,3},{5,6},{6,5},{7,8},{8,7},{9,10},{10,9},{11,... | collective-permute-start | bytes 110600 | tf_op jit(solution)/shard_map/ppermute | solution.py:285
  115.2 0.1 collective-permute-start.18
  115.3 4.7 %second_pass.5 = (f32[4,2000,128]{2,1,0:T(8,128)}, f32[8,128]{1,0:T(8,128)S(1)}) custom-call(bf16[4,384,128]{2,1,0:T(8,128)(2,1)S(1)} %get-tuple-element.102.refs_0_, bf16[96,128]{1,0:T(8,128)(2,1)S(1)} %collective-permute-done.9.refs_1_, bf16[96,128]{1,0:T(8,128)(2,1)S(1)} %collective-permute-done.10.refs_2_, ...), custom_call_target="tpu_custom_call", output_to_operand_aliasing={{0}: (9, {})} | custom-call | flops 1 | bytes 1 | tf_op jit(solution)/shard_map/second_pass/pallas_call | solution.py:482
  119.9 1.5 %collective-permute-done.20.refs_1_ = bf16[2,464,128]{2,1,0:T(8,128)(2,1)S(1)} collective-permute-done((bf16[2,464,128]{2,1,0:T(8,128)(2,1)S(1)}, bf16[2,464,128]{2,1,0:T(8,128)(2,1)S(1)}, u32[]{:S(2)}, u32[]{:S(2)}) %collective-permute-start.20) | collective-permute-done | bytes 237600 | tf_op jit(solution)/shard_map/ppermute | solution.py:514
  121.5 1.2 collective-permute-done.22.refs_3_
  122.7 1.7 %second_edges.7 = (bf16[4,464,128]{2,1,0:T(8,128)(2,1)S(1)}, bf16[128,128]{1,0:T(8,128)(2,1)S(1)}, bf16[128,128]{1,0:T(8,128)(2,1)S(1)}) custom-call(s32[8]{0:T(128)S(1)} %get-tuple-element.73.slot_ref.refs_8_, bf16[2,256,256]{2,1,0:T(8,128)(2,1)S(1)} %get-tuple-element.74.picks_ref, bf16[2,464,128]{2,1,0:T(8,128)(2,1)S(1)} %get-tuple-element.72.refs_4_.refs_0_, ...), custom_call_target="tpu_custom_call" | custom-call | flops 1 | bytes 1 | tf_op jit(solution)/shard_map/second_edges/pallas_call | solution.py:266
  124.4 5.0 %collective-permute-start.24 = (bf16[128,128]{1,0:T(8,128)(2,1)S(1)}, bf16[128,128]{1,0:T(8,128)(2,1)S(1)}, u32[]{:S(2)}, u32[]{:S(2)}) collective-permute-start(bf16[128,128]{1,0:T(8,128)(2,1)S(1)} %get-tuple-element.123), channel_id=1, source_target_pairs={{1,2},{2,1},{3,4},{4,3},{5,6},{6,5},{7,8},{8,7},{9,10},{10,9},{11,... | collective-permute-start | bytes 98312 | tf_op jit(solution)/shard_map/ppermute | solution.py:285
  129.4 0.3 collective-permute-start.23
  129.8 5.2 %second_pass.6 = (f32[4,2000,128]{2,1,0:T(8,128)}, f32[8,128]{1,0:T(8,128)}) custom-call(bf16[4,576,128]{2,1,0:T(8,128)(2,1)S(1)} %get-tuple-element.118.refs_3_.refs_0_, bf16[144,128]{1,0:T(8,128)(2,1)S(1)} %collective-permute-done.14.refs_4_.refs_1_, bf16[144,128]{1,0:T(8,128)(2,1)S(1)} %collective-permute-done.15.refs_5_.refs_2_, ...), custom_call_target="tpu_custom_call", output_to_operand_aliasing={{0}: (9, {})} | custom-call | flops 1 | bytes 1 | tf_op jit(solution)/shard_map/second_pass/pallas_call | solution.py:482
  135.0 2.7 %collective-permute-done.24.refs_5_ = bf16[128,128]{1,0:T(8,128)(2,1)S(1)} collective-permute-done((bf16[128,128]{1,0:T(8,128)(2,1)S(1)}, bf16[128,128]{1,0:T(8,128)(2,1)S(1)}, u32[]{:S(2)}, u32[]{:S(2)}) %collective-permute-start.24) | collective-permute-done | bytes 32800 | tf_op jit(solution)/shard_map/ppermute | solution.py:285
  137.7 4.9 %second_pass.7 = (f32[4,2000,128]{2,1,0:T(8,128)}, f32[8,128]{1,0:T(8,128)}) custom-call(bf16[4,576,128]{2,1,0:T(8,128)(2,1)S(1)} %get-tuple-element.112.refs_3_.refs_0_, bf16[144,128]{1,0:T(8,128)(2,1)S(1)} %collective-permute-done.18.refs_4_.refs_1_, bf16[144,128]{1,0:T(8,128)(2,1)S(1)} %collective-permute-done.19.refs_5_.refs_2_, ...), custom_call_target="tpu_custom_call", output_to_operand_aliasing={{0}: (9, {})} | custom-call | flops 1 | bytes 1 | tf_op jit(solution)/shard_map/second_pass/pallas_call | solution.py:482
  (15 shorter events, 0.0 us)
Async XLA Ops:
  0.0 1.6 %copy-start = (bf16[4,2000,128]{2,1,0:T(8,128)(2,1)S(1)}, bf16[4,2000,128]{2,1,0:T(8,128)(2,1)}, u32[]{:S(2)}) copy-start(bf16[4,2000,128]{2,1,0:T(8,128)(2,1)} %x_ref.5) | copy-start | bytes 6144004
  3.2 9.2 %collective-permute-start = (bf16[512,128]{1,0:T(8,128)(2,1)}, bf16[512,128]{1,0:T(8,128)(2,1)S(1)}, u32[]{:S(2)}, u32[]{:S(2)}) collective-permute-start(bf16[512,128]{1,0:T(8,128)(2,1)} %get-tuple-element.66), channel_id=1, source_target_pairs={{0,1},{1,0},{2,3},{3,2},{4,5},{5,4},{6,7},{7,6},{8,9},{9,8},{10,11... | collective-permute-start | bytes 393224 | tf_op jit(solution)/shard_map/ppermute | solution.py:285
  3.2 15.8 %collective-permute-start.1 = (bf16[512,128]{1,0:T(8,128)(2,1)S(1)}, bf16[512,128]{1,0:T(8,128)(2,1)S(1)}, u32[]{:S(2)}, u32[]{:S(2)}) collective-permute-start(bf16[512,128]{1,0:T(8,128)(2,1)S(1)} %get-tuple-element.67), channel_id=1, source_target_pairs={{1,2},{2,1},{3,4},{4,3},{5,6},{6,5},{7,8},{8,7},{9,10},{10,9},{11,... | collective-permute-start | bytes 393224 | tf_op jit(solution)/shard_map/ppermute | solution.py:285
  10.4 0.7 copy-start.6
  11.1 0.7 copy-start.7
  19.0 1.6 %copy-start.1 = (bf16[4,2000,128]{2,1,0:T(8,128)(2,1)S(1)}, bf16[4,2000,128]{2,1,0:T(8,128)(2,1)}, u32[]{:S(2)}) copy-start(bf16[4,2000,128]{2,1,0:T(8,128)(2,1)} %x_ref.5) | copy-start | bytes 6144004
  20.6 0.7 copy-start.2
  21.2 32.5 %copy-start.3 = (s32[4,1]{0,1:T(1,128)S(1)}, s32[4,1]{0,1:T(1,128)}, u32[]{:S(2)}) copy-start(s32[4,1]{0,1:T(1,128)} %param.11) | copy-start | bytes 52
  21.3 32.5 %copy-start.4 = (bf16[8,16]{1,0:T(8,128)(2,1)S(1)}, bf16[8,16]{1,0:T(8,128)(2,1)}, u32[]{:S(2)}) copy-start(bf16[8,16]{1,0:T(8,128)(2,1)} %trace_ref.3) | copy-start | bytes 772
  21.3 32.5 %copy-start.5 = (bf16[8,64]{1,0:T(8,128)(2,1)S(1)}, bf16[8,64]{1,0:T(8,128)(2,1)}, u32[]{:S(2)}) copy-start(bf16[8,64]{1,0:T(8,128)(2,1)} %time_ref.3) | copy-start | bytes 3076
  24.7 25.3 %collective-permute-start.8 = (bf16[2,384,128]{2,1,0:T(8,128)(2,1)S(1)}, bf16[2,384,128]{2,1,0:T(8,128)(2,1)S(1)}, u32[]{:S(2)}, u32[]{:S(2)}) collective-permute-start(bf16[2,384,128]{2,1,0:T(8,128)(2,1)S(1)} %get-tuple-element.86), channel_id=1, source_target_pairs={{0,192},{64,0},{128,64},{192,128},{1,193},{65,1},{129,65},{193,129... | collective-permute-start | bytes 589832 | tf_op jit(solution)/shard_map/ppermute | solution.py:514
  25.8 26.4 %collective-permute-start.7 = (bf16[2,384,128]{2,1,0:T(8,128)(2,1)S(1)}, bf16[2,384,128]{2,1,0:T(8,128)(2,1)S(1)}, u32[]{:S(2)}, u32[]{:S(2)}) collective-permute-start(bf16[2,384,128]{2,1,0:T(8,128)(2,1)S(1)} %get-tuple-element.83), channel_id=1, source_target_pairs={{0,128},{64,192},{128,0},{192,64},{1,129},{65,193},{129,1},{193,65... | collective-permute-start | bytes 589832 | tf_op jit(solution)/shard_map/ppermute | solution.py:514
  26.9 26.1 %collective-permute-start.5 = (bf16[2,384,128]{2,1,0:T(8,128)(2,1)S(1)}, bf16[2,384,128]{2,1,0:T(8,128)(2,1)S(1)}, u32[]{:S(2)}, u32[]{:S(2)}) collective-permute-start(bf16[2,384,128]{2,1,0:T(8,128)(2,1)S(1)} %get-tuple-element.79), channel_id=1, source_target_pairs={{0,64},{64,128},{128,192},{192,0},{1,65},{65,129},{129,193},{193,1... | collective-permute-start | bytes 589832 | tf_op jit(solution)/shard_map/ppermute | solution.py:514
  27.4 8.0 %collective-permute-start.4 = (s32[4]{0:T(128)S(1)}, s32[4]{0:T(128)S(1)}, u32[]{:S(2)}, u32[]{:S(2)}) collective-permute-start(s32[4]{0:T(128)S(1)} %bitcast.4), channel_id=1, source_target_pairs={{0,192},{64,0},{128,64},{192,128},{1,193},{65,1},{129,65},{193,129... | collective-permute-start | bytes 56 | tf_op jit(solution)/shard_map/ppermute | solution.py:514
  28.9 7.3 %collective-permute-start.3 = (s32[4]{0:T(128)S(1)}, s32[4]{0:T(128)S(1)}, u32[]{:S(2)}, u32[]{:S(2)}) collective-permute-start(s32[4]{0:T(128)S(1)} %bitcast.5), channel_id=1, source_target_pairs={{0,128},{64,192},{128,0},{192,64},{1,129},{65,193},{129,1},{193,65... | collective-permute-start | bytes 56 | tf_op jit(solution)/shard_map/ppermute | solution.py:514
  35.3 3.9 %collective-permute-start.2 = (s32[4]{0:T(128)S(1)}, s32[4]{0:T(128)S(1)}, u32[]{:S(2)}, u32[]{:S(2)}) collective-permute-start(s32[4]{0:T(128)S(1)} %bitcast.6), channel_id=1, source_target_pairs={{0,64},{64,128},{128,192},{192,0},{1,65},{65,129},{129,193},{193,1... | collective-permute-start | bytes 56 | tf_op jit(solution)/shard_map/ppermute | solution.py:514
  50.1 25.1 %collective-permute-start.13 = (bf16[2,576,128]{2,1,0:T(8,128)(2,1)S(1)}, bf16[2,576,128]{2,1,0:T(8,128)(2,1)S(1)}, u32[]{:S(2)}, u32[]{:S(2)}) collective-permute-start(bf16[2,576,128]{2,1,0:T(8,128)(2,1)S(1)} %get-tuple-element.98), channel_id=1, source_target_pairs={{0,192},{64,0},{128,64},{192,128},{1,193},{65,1},{129,65},{193,129... | collective-permute-start | bytes 884744 | tf_op jit(solution)/shard_map/ppermute | solution.py:514
  52.2 23.0 %collective-permute-start.12 = (bf16[2,576,128]{2,1,0:T(8,128)(2,1)S(1)}, bf16[2,576,128]{2,1,0:T(8,128)(2,1)S(1)}, u32[]{:S(2)}, u32[]{:S(2)}) collective-permute-start(bf16[2,576,128]{2,1,0:T(8,128)(2,1)S(1)} %get-tuple-element.95), channel_id=1, source_target_pairs={{0,128},{64,192},{128,0},{192,64},{1,129},{65,193},{129,1},{193,65... | collective-permute-start | bytes 884744 | tf_op jit(solution)/shard_map/ppermute | solution.py:514
  53.0 24.5 %collective-permute-start.6 = (bf16[2,576,128]{2,1,0:T(8,128)(2,1)S(1)}, bf16[2,576,128]{2,1,0:T(8,128)(2,1)S(1)}, u32[]{:S(2)}, u32[]{:S(2)}) collective-permute-start(bf16[2,576,128]{2,1,0:T(8,128)(2,1)S(1)} %get-tuple-element.80), channel_id=1, source_target_pairs={{0,64},{64,128},{128,192},{192,0},{1,65},{65,129},{129,193},{193,1... | collective-permute-start | bytes 884744 | tf_op jit(solution)/shard_map/ppermute | solution.py:514
  57.2 4.6 %collective-permute-start.9 = (bf16[96,128]{1,0:T(8,128)(2,1)S(1)}, bf16[96,128]{1,0:T(8,128)(2,1)S(1)}, u32[]{:S(2)}, u32[]{:S(2)}) collective-permute-start(bf16[96,128]{1,0:T(8,128)(2,1)S(1)} %get-tuple-element.89), channel_id=1, source_target_pairs={{0,1},{1,0},{2,3},{3,2},{4,5},{5,4},{6,7},{7,6},{8,9},{9,8},{10,11... | collective-permute-start | bytes 73736 | tf_op jit(solution)/shard_map/ppermute | solution.py:285
  57.3 17.8 %collective-permute-start.10 = (bf16[96,128]{1,0:T(8,128)(2,1)S(1)}, bf16[96,128]{1,0:T(8,128)(2,1)S(1)}, u32[]{:S(2)}, u32[]{:S(2)}) collective-permute-start(bf16[96,128]{1,0:T(8,128)(2,1)S(1)} %get-tuple-element.90), channel_id=1, source_target_pairs={{1,2},{2,1},{3,4},{4,3},{5,6},{6,5},{7,8},{8,7},{9,10},{10,9},{11,... | collective-permute-start | bytes 73736 | tf_op jit(solution)/shard_map/ppermute | solution.py:285
  75.2 27.3 %collective-permute-start.17 = (bf16[2,576,128]{2,1,0:T(8,128)(2,1)S(1)}, bf16[2,576,128]{2,1,0:T(8,128)(2,1)S(1)}, u32[]{:S(2)}, u32[]{:S(2)}) collective-permute-start(bf16[2,576,128]{2,1,0:T(8,128)(2,1)S(1)} %get-tuple-element.110), channel_id=1, source_target_pairs={{0,192},{64,0},{128,64},{192,128},{1,193},{65,1},{129,65},{193,129... | collective-permute-start | bytes 884744 | tf_op jit(solution)/shard_map/ppermute | solution.py:514
  75.2 27.3 %collective-permute-start.16 = (bf16[2,576,128]{2,1,0:T(8,128)(2,1)S(1)}, bf16[2,576,128]{2,1,0:T(8,128)(2,1)S(1)}, u32[]{:S(2)}, u32[]{:S(2)}) collective-permute-start(bf16[2,576,128]{2,1,0:T(8,128)(2,1)S(1)} %get-tuple-element.107), channel_id=1, source_target_pairs={{0,128},{64,192},{128,0},{192,64},{1,129},{65,193},{129,1},{193,65... | collective-permute-start | bytes 884744 | tf_op jit(solution)/shard_map/ppermute | solution.py:514
  77.5 25.0 %collective-permute-start.11 = (bf16[2,576,128]{2,1,0:T(8,128)(2,1)S(1)}, bf16[2,576,128]{2,1,0:T(8,128)(2,1)S(1)}, u32[]{:S(2)}, u32[]{:S(2)}) collective-permute-start(bf16[2,576,128]{2,1,0:T(8,128)(2,1)S(1)} %get-tuple-element.91), channel_id=1, source_target_pairs={{0,64},{64,128},{128,192},{192,0},{1,65},{65,129},{129,193},{193,1... | collective-permute-start | bytes 884744 | tf_op jit(solution)/shard_map/ppermute | solution.py:514
  80.4 22.1 %collective-permute-start.15 = (bf16[144,128]{1,0:T(8,128)(2,1)S(1)}, bf16[144,128]{1,0:T(8,128)(2,1)S(1)}, u32[]{:S(2)}, u32[]{:S(2)}) collective-permute-start(bf16[144,128]{1,0:T(8,128)(2,1)S(1)} %get-tuple-element.101), channel_id=1, source_target_pairs={{1,2},{2,1},{3,4},{4,3},{5,6},{6,5},{7,8},{8,7},{9,10},{10,9},{11,... | collective-permute-start | bytes 110600 | tf_op jit(solution)/shard_map/ppermute | solution.py:285
  96.9 5.6 %collective-permute-start.14 = (bf16[144,128]{1,0:T(8,128)(2,1)S(1)}, bf16[144,128]{1,0:T(8,128)(2,1)S(1)}, u32[]{:S(2)}, u32[]{:S(2)}) collective-permute-start(bf16[144,128]{1,0:T(8,128)(2,1)S(1)} %get-tuple-element.100.refs_5_), channel_id=1, source_target_pairs={{0,1},{1,0},{2,3},{3,2},{4,5},{5,4},{6,7},{7,6},{8,9},{9,8},{10,11... | collective-permute-start | bytes 110600 | tf_op jit(solution)/shard_map/ppermute | solution.py:285
  102.5 18.9 %collective-permute-start.20 = (bf16[2,464,128]{2,1,0:T(8,128)(2,1)S(1)}, bf16[2,464,128]{2,1,0:T(8,128)(2,1)S(1)}, u32[]{:S(2)}, u32[]{:S(2)}) collective-permute-start(bf16[2,464,128]{2,1,0:T(8,128)(2,1)S(1)} %get-tuple-element.115), channel_id=1, source_target_pairs={{0,64},{64,128},{128,192},{192,0},{1,65},{65,129},{129,193},{193,1... | collective-permute-start | bytes 712712 | tf_op jit(solution)/shard_map/ppermute | solution.py:514
  102.6 18.9 %collective-permute-start.21 = (bf16[2,464,128]{2,1,0:T(8,128)(2,1)S(1)}, bf16[2,464,128]{2,1,0:T(8,128)(2,1)S(1)}, u32[]{:S(2)}, u32[]{:S(2)}) collective-permute-start(bf16[2,464,128]{2,1,0:T(8,128)(2,1)S(1)} %get-tuple-element.116), channel_id=1, source_target_pairs={{0,128},{64,192},{128,0},{192,64},{1,129},{65,193},{129,1},{193,65... | collective-permute-start | bytes 712712 | tf_op jit(solution)/shard_map/ppermute | solution.py:514
  103.3 19.3 %collective-permute-start.22 = (bf16[2,464,128]{2,1,0:T(8,128)(2,1)S(1)}, bf16[2,464,128]{2,1,0:T(8,128)(2,1)S(1)}, u32[]{:S(2)}, u32[]{:S(2)}) collective-permute-start(bf16[2,464,128]{2,1,0:T(8,128)(2,1)S(1)} %get-tuple-element.117), channel_id=1, source_target_pairs={{0,192},{64,0},{128,64},{192,128},{1,193},{65,1},{129,65},{193,129... | collective-permute-start | bytes 712712 | tf_op jit(solution)/shard_map/ppermute | solution.py:514
  106.7 23.0 %collective-permute-start.19 = (bf16[144,128]{1,0:T(8,128)(2,1)S(1)}, bf16[144,128]{1,0:T(8,128)(2,1)S(1)}, u32[]{:S(2)}, u32[]{:S(2)}) collective-permute-start(bf16[144,128]{1,0:T(8,128)(2,1)S(1)} %get-tuple-element.114), channel_id=1, source_target_pairs={{1,2},{2,1},{3,4},{4,3},{5,6},{6,5},{7,8},{8,7},{9,10},{10,9},{11,... | collective-permute-start | bytes 110600 | tf_op jit(solution)/shard_map/ppermute | solution.py:285
  115.2 14.6 %collective-permute-start.18 = (bf16[144,128]{1,0:T(8,128)(2,1)S(1)}, bf16[144,128]{1,0:T(8,128)(2,1)S(1)}, u32[]{:S(2)}, u32[]{:S(2)}) collective-permute-start(bf16[144,128]{1,0:T(8,128)(2,1)S(1)} %get-tuple-element.113.refs_8_), channel_id=1, source_target_pairs={{0,1},{1,0},{2,3},{3,2},{4,5},{5,4},{6,7},{7,6},{8,9},{9,8},{10,11... | collective-permute-start | bytes 110600 | tf_op jit(solution)/shard_map/ppermute | solution.py:285
  124.4 13.4 %collective-permute-start.24 = (bf16[128,128]{1,0:T(8,128)(2,1)S(1)}, bf16[128,128]{1,0:T(8,128)(2,1)S(1)}, u32[]{:S(2)}, u32[]{:S(2)}) collective-permute-start(bf16[128,128]{1,0:T(8,128)(2,1)S(1)} %get-tuple-element.123), channel_id=1, source_target_pairs={{1,2},{2,1},{3,4},{4,3},{5,6},{6,5},{7,8},{8,7},{9,10},{10,9},{11,... | collective-permute-start | bytes 98312 | tf_op jit(solution)/shard_map/ppermute | solution.py:285
  129.4 8.3 %collective-permute-start.23 = (bf16[128,128]{1,0:T(8,128)(2,1)S(1)}, bf16[128,128]{1,0:T(8,128)(2,1)S(1)}, u32[]{:S(2)}, u32[]{:S(2)}) collective-permute-start(bf16[128,128]{1,0:T(8,128)(2,1)S(1)} %get-tuple-element.122.refs_8_), channel_id=1, source_target_pairs={{0,1},{1,0},{2,3},{3,2},{4,5},{5,4},{6,7},{7,6},{8,9},{9,8},{10,11... | collective-permute-start | bytes 98312 | tf_op jit(solution)/shard_map/ppermute | solution.py:285

commit v4 on v3

--- a/solution.py
+++ b/solution.py
@@ -20,6 +20,7 @@
 ANY = pl.BlockSpec(memory_space=pl.ANY)
 HBM = pl.BlockSpec(memory_space=pltpu.HBM)
 CHUNKS = (384, 576, 576)
+NOTE = 16
 
 
 def chunk_bounds(samples):
@@ -86,7 +87,7 @@
         ).astype(jnp.bfloat16)
 
 
-def weights_kernel(even_ref, trace_ref, time_ref, mats_ref, times_ref):
+def weights_kernel(even_ref, trace_ref, time_ref, _, mats_ref, times_ref):
     fill_weights(even_ref[0] == 1, trace_ref, time_ref, mats_ref, times_ref)
 
 
@@ -101,25 +102,38 @@
     return owners, order
 
 
-def late_kernel(even_ref, me_ref, trace_ref, time_ref, *refs):
-    mats_ref, times_ref, slots_ref = refs[-3:]
-    columns = refs[:-4]
-    blocks, count, me = mats_ref.shape[0], len(columns), me_ref[0]
+def late_kernel(even_ref, me_ref, target_ref, trace_ref, time_ref, *refs):
+    parts, (_, mats_ref, times_ref, slots_ref, notes, sem) = refs[:-6], refs[-6:]
+    blocks, me = mats_ref.shape[0], me_ref[0]
+    slot_cap, held = parts[0].shape[0], parts[0].shape[1]
+
+    def fetch(offset):
+        return pltpu.make_async_copy(
+            parts[offset].at[0, pl.ds(held - NOTE, NOTE), :], notes.at[offset], sem.at[offset]
+        )
+
+    for offset in range(1, len(parts)):
+        fetch(offset).start()
     fill_weights(even_ref[0] == 1, trace_ref, time_ref, mats_ref, times_ref)
-    slot_cap = blocks // 2
-    near, far = [jnp.int32(0)] * blocks, [jnp.int32(0)] * blocks
-    for offset, column in enumerate(columns):
-        targets = [column[block] for block in range(blocks)]
-        order = ranks(targets, blocks)[1]
-        source = lax.rem(me - offset + count, count)
-        for target, rank in zip(targets, order):
+    slots = [jnp.int32(0)] * blocks
+    lane = lax.broadcasted_iota(jnp.int32, (1, LANES), 1)
+    for offset in range(len(parts)):
+        if offset:
+            fetch(offset).wait()
+            note = notes[offset].astype(jnp.float32)[:1]
+            targets = [
+                jnp.sum(jnp.where(lane == block, note, 0.0)).astype(jnp.int32)
+                for block in range(blocks)
+            ]
+        else:
+            targets = [target_ref[block] for block in range(blocks)]
+        for target, rank in zip(targets, ranks(targets, blocks)[1]):
             for block in range(blocks):
-                found = target == me * blocks + block
-                near[block] = jnp.where(found, offset * slot_cap + rank, near[block])
-                far[block] = jnp.where(found, source * slot_cap + rank, far[block])
+                slots[block] = jnp.where(
+                    target == me * blocks + block, offset * slot_cap + rank, slots[block]
+                )
     for block in range(blocks):
-        slots_ref[block] = near[block]
-        slots_ref[blocks + block] = far[block]
+        slots_ref[block] = slots[block]
 
 
 def weight_shapes(blocks, fans):
@@ -129,29 +143,34 @@
     ]
 
 
-def weights(even, trace_taps, time_taps, blocks):
+def weights(even, trace_taps, time_taps, after, blocks):
     return pl.pallas_call(
         weights_kernel,
-        in_specs=[SMEM, VMEM, VMEM],
+        in_specs=[SMEM, VMEM, VMEM, ANY],
         out_specs=[VMEM, VMEM],
         out_shape=weight_shapes(blocks, trace_taps.shape[0]),
         cost_estimate=NO_COST,
         compiler_params=PARAMS,
         name="weights",
-    )(even, trace_taps, time_taps)
-
-
-def late_weights(even, me, trace_taps, time_taps, columns, after, blocks):
+    )(even, trace_taps, time_taps, after)
+
+
+def late_weights(even, me, target, trace_taps, time_taps, arrived, after):
+    blocks = target.shape[0]
     return pl.pallas_call(
         late_kernel,
-        in_specs=[SMEM, SMEM, VMEM, VMEM] + [SMEM] * len(columns) + [ANY],
+        in_specs=[SMEM, SMEM, SMEM, VMEM, VMEM] + [ANY] * (len(arrived) + 1),
         out_specs=[VMEM, VMEM, SMEM],
         out_shape=weight_shapes(blocks, trace_taps.shape[0])
-        + [jax.ShapeDtypeStruct((2 * blocks,), jnp.int32)],
+        + [jax.ShapeDtypeStruct((blocks,), jnp.int32)],
+        scratch_shapes=[
+            pltpu.VMEM((len(arrived), NOTE, LANES), jnp.bfloat16),
+            pltpu.SemaphoreType.DMA((len(arrived),)),
+        ],
         cost_estimate=NO_COST,
         compiler_params=PARAMS,
         name="late_weights",
-    )(even, me, trace_taps, time_taps, *columns, after)
+    )(even, me, target, trace_taps, time_taps, *arrived, after)
 
 
 def edge_picks(even, blocks):
@@ -241,30 +260,32 @@
     )(even, traces)
 
 
-def second_edges_kernel(base, slot_ref, picks_ref, *refs):
+def second_edges_kernel(slot_ref, picks_ref, *refs):
     parts, (_, sorted_ref, out_a, out_b, sem) = refs[:-5], refs[-5:]
-    blocks, slot_cap = sorted_ref.shape[0], parts[0].shape[0]
+    blocks, rows = sorted_ref.shape[:2]
+    slot_cap = parts[0].shape[0]
     for block in range(blocks):
-        slot = slot_ref[base + block]
+        slot = slot_ref[block]
         for offset, part in enumerate(parts):
 
             @pl.when(slot // slot_cap == offset)
             def _():
                 pltpu.make_async_copy(
-                    part.at[slot % slot_cap], sorted_ref.at[block], sem.at[block]
+                    part.at[slot % slot_cap, pl.ds(0, rows), :], sorted_ref.at[block], sem.at[block]
                 ).start()
 
     for block in range(blocks):
-        pltpu.make_async_copy(parts[0].at[0], sorted_ref.at[block], sem.at[block]).wait()
+        pltpu.make_async_copy(
+            parts[0].at[0, pl.ds(0, rows), :], sorted_ref.at[block], sem.at[block]
+        ).wait()
     picks = [picks_ref[pair] for pair in range(blocks // 2)]
     pack_edges(picks, sorted_ref, (out_a, out_b))
 
 
-def second_edges(slots, picks, arrived, after, blocks):
-    rows = arrived[0].shape[1]
+def second_edges(slots, picks, arrived, rows, after, blocks):
     packed = jax.ShapeDtypeStruct((folded_rows(rows), LANES), jnp.bfloat16)
     return pl.pallas_call(
-        functools.partial(second_edges_kernel, blocks if len(arrived) == 1 else 0),
+        second_edges_kernel,
         in_specs=[SMEM, VMEM] + [ANY] * (len(arrived) + 1),
         out_specs=[VMEM] * 3,
         scratch_shapes=[pltpu.SemaphoreType.DMA((blocks,))],
@@ -328,19 +349,34 @@
 
 
 def first_kernel(
-    start, sizes, samples, owners, me_ref, target_ref, x_ref, edge_a, edge_b, mats_ref, times_ref,
+    start, sizes, noted, owners, me_ref, target_ref, x_ref, edge_a, edge_b, mats_ref, times_ref,
     *refs
 ):
-    outs, (merged, fans_ref, done, sem) = list(refs[-4 - sum(n for _, n in sizes) : -4]), refs[-4:]
+    outs = refs[-6 - owners * len(sizes) : -6]
+    merged, fans_ref, done, note, sem, note_sem = refs[-6:]
     blocks, rows = done.shape[:2]
+    samples = x_ref.shape[1]
     window = start - REACH // 2
     begin, end = max(0, window), min(samples, start + rows + REACH // 2)
-    targets, order = ranks([target_ref[block] for block in range(blocks)], blocks)
+    homes, order = ranks([target_ref[block] for block in range(blocks)], blocks)
     groups, at = [], 0
-    for size, number in sizes:
-        groups.append((at, size, outs[:number]))
-        outs = outs[number:]
+    for group, size in enumerate(sizes):
+        groups.append((at, size, outs[group * owners : (group + 1) * owners]))
         at += size
+
+    def tell(offset):
+        return pltpu.make_async_copy(
+            note, groups[0][2][offset].at[0, pl.ds(sizes[0], NOTE), :], note_sem.at[offset]
+        )
+
+    if noted:
+        lane = lax.broadcasted_iota(jnp.int32, note.shape, 1)
+        row = jnp.zeros(note.shape, jnp.int32)
+        for block in range(blocks):
+            row = jnp.where(lane == block, target_ref[block], row)
+        note[...] = row.astype(jnp.float32).astype(jnp.bfloat16)
+        for offset in range(owners):
+            tell(offset).start()
 
     def put(row, values):
         merged[row - window : row - window + values.shape[0], :] = values
@@ -363,62 +399,59 @@
     def finish(pair):
         for half in range(2):
             block = 2 * pair + half
-            owner, rank = pick(targets, pair, half), pick(order, pair, half)
+            owner, rank = pick(homes, pair, half), pick(order, pair, half)
             away = lax.rem(owner - me_ref[0] + owners, owners)
             for group, (at, size, arrays) in enumerate(groups):
                 part = done.at[block, pl.ds(at, size), :]
-                if len(arrays) == 1:
-                    slot = owner * (blocks // 2) + rank
-                    pltpu.make_async_copy(part, arrays[0].at[slot], sem.at[group, block]).start()
-                    continue
                 for offset, out_ref in enumerate(arrays):
 
                     @pl.when(away == offset)
                     def _():
                         pltpu.make_async_copy(
-                            part, out_ref.at[rank], sem.at[group, block]
+                            part, out_ref.at[rank, pl.ds(0, size), :], sem.at[group, block]
                         ).start()
 
-    pieces = [
-        (begin - window, end - begin, lambda block: x_ref[block, begin:end, :])
-    ]
+    pieces = [(begin - window, end - begin, lambda block: x_ref[block, begin:end, :])]
     filter_window(pieces, merged, fans_ref, mats_ref, times_ref, rows, give, finish)
     for group, (at, size, arrays) in enumerate(groups):
         for block in range(blocks):
             pltpu.make_async_copy(
-                done.at[block, pl.ds(at, size), :], arrays[0].at[0], sem.at[group, block]
+                done.at[block, pl.ds(at, size), :],
+                arrays[0].at[0, pl.ds(0, size), :],
+                sem.at[group, block],
             ).wait()
-
-
-def first_pass(me, target, owners, traces, samples, edges, mats, times, after, start, sizes):
+    if noted:
+        for offset in range(owners):
+            tell(offset).wait()
+
+
+def first_pass(me, target, owners, traces, edges, mats, times, after, start, sizes, noted):
     blocks = traces.shape[0]
     fans = 2 * mats.shape[1]
-    rows = sum(size for size, _ in sizes)
+    rows = sum(sizes)
     tall = window_rows(rows)
     shapes = []
-    for size, number in sizes:
-        slots = owners * (blocks // 2) // number
-        shapes += [jax.ShapeDtypeStruct((slots, size, LANES), jnp.bfloat16)] * number
+    for group, size in enumerate(sizes):
+        size += NOTE if noted and not group else 0
+        shapes += [jax.ShapeDtypeStruct((blocks // 2, size, LANES), jnp.bfloat16)] * owners
     flat = pl.pallas_call(
-        functools.partial(first_kernel, start, sizes, samples, owners),
+        functools.partial(first_kernel, start, sizes, noted, owners),
         in_specs=[SMEM, SMEM] + [VMEM] * 5 + [ANY] * len(after),
         out_specs=[ANY] * len(shapes),
         scratch_shapes=[
             pltpu.VMEM((tall, LANES), jnp.bfloat16),
             pltpu.VMEM((fans, tall, 2 * LANES), jnp.bfloat16),
             pltpu.VMEM((blocks, rows, LANES), jnp.bfloat16),
+            pltpu.VMEM((NOTE, LANES), jnp.bfloat16),
             pltpu.SemaphoreType.DMA((len(sizes), blocks)),
+            pltpu.SemaphoreType.DMA((owners,)),
         ],
         out_shape=shapes,
         cost_estimate=NO_COST,
         compiler_params=PARAMS,
         name="first_pass",
     )(me, target, traces, *edges, mats, times, *after)
-    chunks = []
-    for _, number in sizes:
-        chunks.append(flat[:number])
-        flat = flat[number:]
-    return chunks
+    return [flat[group * owners : (group + 1) * owners] for group in range(len(sizes))]
 
 
 def second_kernel(at, has_past, *refs):
@@ -515,24 +548,17 @@
 
     bounds = chunk_bounds(samples)
     count = len(bounds) - 1
-    sizes = [
-        (bounds[step + 1] - bounds[step], owners) for step in range(count)
-    ]
+    sizes = [bounds[step + 1] - bounds[step] for step in range(count)]
     *packed, picks = first_edges(even, traces)
     edges = swap_edges(packed)
-    mats, times = weights(even, first_trace_taps, first_time_taps, blocks)
-
-    def first(after, start, sizes):
+    mats, times = weights(even, first_trace_taps, first_time_taps, traces, blocks)
+
+    def first(after, start, sizes, noted):
         return first_pass(
-            me, target, owners, traces, samples, edges, mats, times, after, start, sizes
+            me, target, owners, traces, edges, mats, times, after, start, sizes, noted
         )
 
     def exchange(sent, before, *after):
-        if len(sent) == 1:
-            part = sent[0]
-            if before is not None:
-                part, before[0], *_ = lax.optimization_barrier((part, before[0], *after))
-            return [lax.all_to_all(part, "rcv", split_axis=0, concat_axis=0, tiled=True)]
         arrived = []
         for offset, part in enumerate(sent):
             if offset and before is not None:
@@ -542,14 +568,12 @@
             arrived.append(send(part, offset))
         return arrived
 
-    sent = first([], 0, sizes[:1])
-    late_target, _ = lax.optimization_barrier((target, sent[0][0]))
-    columns = [send(late_target, offset) for offset in range(owners)]
+    sent = first([], 0, sizes[:1], True)
     arrived = [exchange(sent[0], None)]
     if count > 1:
-        sent += first(columns[1:], bounds[1], sizes[1:])
-    mats, times, slots = late_weights(
-        even, me, second_trace_taps, second_time_taps, columns, sent[-1][0], blocks
+        sent += first([sent[0][0]], bounds[1], sizes[1:], False)
+    second_mats, second_times, slots = late_weights(
+        even, me, target, second_trace_taps, second_time_taps, arrived[0], sent[-1][0]
     )
 
     out, past, now, token, rims = None, None, None, None, None
@@ -558,7 +582,7 @@
         at = max(0, bounds[step] - REACH // 2)
         stop = bounds[step + 1] - REACH // 2 if step + 1 < count else samples
         return second_pass(
-            blocks, samples, past, now, mats, times, after, out, at, stop - at
+            blocks, samples, past, now, second_mats, second_times, after, out, at, stop - at
         )
 
     for step in range(count):
@@ -567,7 +591,7 @@
             ahead += [token] if token is not None else []
             arrived.append(exchange(sent[step + 1], arrived[step], *ahead))
         gathered, *packed = second_edges(
-            slots, picks, arrived[step], times if token is None else token, blocks
+            slots, picks, arrived[step], sizes[step], slots if token is None else token, blocks
         )
         rims = packed[0]
         coming = (gathered, *swap_edges(packed))

time: 145 us -> 135 us (0.931)
  starting transfers between devices: 60.2 us -> 49.6 us
    ppermute x10, starting transfers between devices: 42.3 us -> 32.1 us  [swap_edges(): got.append(lax.ppermute(edges, 'shot', pairs))]
    ppermute x10, waiting for transfers between devices: 25.2 us -> 20.2 us  [swap_edges(): got.append(lax.ppermute(edges, 'shot', pairs))]
    ppermute x15 -> x12, waiting for transfers between devices: 8.64 us -> 12.9 us  [send(): return lax.ppermute(values, 'rcv', pairs) if offset else values]
    unnamed x16 -> x18, local copies, waits for them, and re-layouts: 5.17 us -> 5.87 us
    ppermute x15 -> x12, starting transfers between devices: 18 us -> 17.4 us  [send(): return lax.ppermute(values, 'rcv', pairs) if offset else values]
  transfers between devices with their start and end apart: 25 -> 22, of which waited for: 8 -> 9; matrix products, arithmetic and copies ran while one was open for 0% -> 0% of each run, Pallas kernels for 23% -> 25%
where the time goes in v4:
time: 135 us; the launch traced here: 133 us
  starting transfers between devices  49.6 us (37%)
  Pallas kernels  43.6 us (32%)
  waiting for transfers between devices  33.1 us (25%)
  local copies, waits for them, and re-layouts  5.87 us (4%)
    ppermute x10, starting transfers between devices, swap_edges(): got.append(lax.ppermute(edges, 'shot', pairs))  32.1 us
    ppermute x10, waiting for transfers between devices, swap_edges(): got.append(lax.ppermute(edges, 'shot', pairs))  20.2 us
    pallas_call x4, Pallas kernels, second_pass(): pl.pallas_call(functools.partial(second_kernel, at, past is not None), in...  17.7 us
    ppermute x12, starting transfers between devices, send(): return lax.ppermute(values, 'rcv', pairs) if offset else values  17.4 us
    pallas_call x2, Pallas kernels, first_pass(): pl.pallas_call(functools.partial(first_kernel, start, sizes, noted, owner...  14.3 us
    ppermute x12, waiting for transfers between devices, send(): return lax.ppermute(values, 'rcv', pairs) if offset else values  12.9 us
    pallas_call x4, Pallas kernels, second_edges(): pl.pallas_call(second_edges_kernel, in_specs=[SMEM, VMEM] + [ANY] * (len(...  7.13 us
    unnamed x18, local copies, waits for them, and re-layouts  5.87 us
  transfers between devices with their start and end apart: 22, of which 9 were waited for; matrix products, arithmetic and copies ran while one was open for 0% of the time, Pallas kernels for 25%

profile of v4, /device:TPU:192, one launch (start us, length us, event | category | flops | bytes accessed | tf_op | source)
XLA Modules:
  0.0 132.5 jit_solution(6444530239655081885)
XLA Ops:
  0.0 1.6 %copy-done = bf16[4,2000,128]{2,1,0:T(8,128)(2,1)S(1)} copy-done((bf16[4,2000,128]{2,1,0:T(8,128)(2,1)S(1)}, bf16[4,2000,128]{2,1,0:T(8,128)(2,1)}, u32[]{:S(2)}) %copy-start) | copy-done | bytes 2048024
  1.6 1.6 %first_edges.1 = (bf16[512,128]{1,0:T(8,128)(2,1)}, bf16[512,128]{1,0:T(8,128)(2,1)S(1)}, bf16[2,256,256]{2,1,0:T(8,128)(2,1)S(1)}) custom-call(s32[1]{0:T(128)} %bitcast.even_ref, bf16[4,2000,128]{2,1,0:T(8,128)(2,1)S(1)} %copy-done), custom_call_target="tpu_custom_call" | custom-call | flops 1 | bytes 1 | tf_op jit(solution)/shard_map/first_edges/pallas_call | solution.py:248
  3.2 0.0 collective-permute-start
  3.2 7.2 %collective-permute-start.1 = (bf16[512,128]{1,0:T(8,128)(2,1)S(1)}, bf16[512,128]{1,0:T(8,128)(2,1)S(1)}, u32[]{:S(2)}, u32[]{:S(2)}) collective-permute-start(bf16[512,128]{1,0:T(8,128)(2,1)S(1)} %get-tuple-element.66), channel_id=1, source_target_pairs={{1,2},{2,1},{3,4},{4,3},{5,6},{6,5},{7,8},{8,7},{9,10},{10,9},{11,... | collective-permute-start | bytes 393224 | tf_op jit(solution)/shard_map/ppermute | solution.py:306
  10.4 0.0 copy-start.5
  10.4 0.7 copy-done.5
  11.1 0.7 copy-done.6
  11.8 0.6 weights.1
  12.4 0.0 copy-start.2
  12.4 1.3 copy-done.2
  13.7 0.0 collective-permute-done.edge_a
  13.7 5.3 %collective-permute-done.1.edge_b = bf16[512,128]{1,0:T(8,128)(2,1)S(1)} collective-permute-done((bf16[512,128]{1,0:T(8,128)(2,1)S(1)}, bf16[512,128]{1,0:T(8,128)(2,1)S(1)}, u32[]{:S(2)}, u32[]{:S(2)}) %collective-permute-start.1) | collective-permute-done | bytes 131104 | tf_op jit(solution)/shard_map/ppermute | solution.py:306
  19.0 1.6 %copy-done.3 = bf16[4,4,256,256]{3,2,1,0:T(8,128)(2,1)S(1)} copy-done((bf16[4,4,256,256]{3,2,1,0:T(8,128)(2,1)S(1)}, bf16[4,4,256,256]{3,2,1,0:T(8,128)(2,1)}, u32[]{:S(2)}) %copy-start.3) | copy-done | bytes 2097176
  20.6 3.5 %first_pass.2 = (bf16[2,400,128]{2,1,0:T(8,128)(2,1)S(1)}, bf16[2,400,128]{2,1,0:T(8,128)(2,1)S(1)}, bf16[2,400,128]{2,1,0:T(8,128)(2,1)S(1)}, bf16[2,400,128]{2,1,0:T(8,128)(2,1)S(1)}) custom-call(s32[1]{0:T(128)} %bitcast.1.me_ref, s32[4]{0:T(128)S(1)} %bitcast.3, bf16[4,2000,128]{2,1,0:T(8,128)(2,1)S(1)} %copy-done.1, ...), custom_call_target="tpu_custom_call" | custom-call | flops 1 | bytes 1 | tf_op jit(solution)/shard_map/first_pass/pallas_call | solution.py:437
  24.2 1.1 collective-permute-start.4
  25.2 1.1 collective-permute-start.3
  26.3 0.5 collective-permute-start.2
  26.8 10.8 %first_pass.3 = (bf16[2,576,128]{2,1,0:T(8,128)(2,1)S(1)}, bf16[2,576,128]{2,1,0:T(8,128)(2,1)S(1)}, bf16[2,576,128]{2,1,0:T(8,128)(2,1)S(1)}, bf16[2,576,128]{2...) custom-call(s32[1]{0:T(128)} %bitcast.1.me_ref, ...), custom_call_target="tpu_custom_call" | custom-call | flops 1 | bytes 1 | tf_op jit(solution)/shard_map/first_pass/pallas_call | solution.py:437
  37.6 0.0 collective-permute-done.4.refs_3_
  37.6 1.6 %collective-permute-start.10 = (bf16[2,576,128]{2,1,0:T(8,128)(2,1)S(1)}, bf16[2,576,128]{2,1,0:T(8,128)(2,1)S(1)}, u32[]{:S(2)}, u32[]{:S(2)}) collective-permute-start(bf16[2,576,128]{2,1,0:T(8,128)(2,1)S(1)} %get-tuple-element.95), channel_id=1, source_target_pairs={{0,192},{64,0},{128,64},{192,128},{1,193},{65,1},{129,65},{193,129... | collective-permute-start | bytes 884744 | tf_op jit(solution)/shard_map/ppermute | solution.py:547
  39.2 0.0 collective-permute-done.3.refs_2_
  39.2 5.5 %collective-permute-start.9 = (bf16[2,576,128]{2,1,0:T(8,128)(2,1)S(1)}, bf16[2,576,128]{2,1,0:T(8,128)(2,1)S(1)}, u32[]{:S(2)}, u32[]{:S(2)}) collective-permute-start(bf16[2,576,128]{2,1,0:T(8,128)(2,1)S(1)} %get-tuple-element.92), channel_id=1, source_target_pairs={{0,128},{64,192},{128,0},{192,64},{1,129},{65,193},{129,1},{193,65... | collective-permute-start | bytes 884744 | tf_op jit(solution)/shard_map/ppermute | solution.py:547
  44.7 8.4 %collective-permute-done.2.refs_1_ = bf16[2,400,128]{2,1,0:T(8,128)(2,1)S(1)} collective-permute-done((bf16[2,400,128]{2,1,0:T(8,128)(2,1)S(1)}, bf16[2,400,128]{2,1,0:T(8,128)(2,1)S(1)}, u32[]{:S(2)}, u32[]{:S(2)}) %collective-permute-start.2) | collective-permute-done | bytes 204832 | tf_op jit(solution)/shard_map/ppermute | solution.py:547
  53.1 0.0 collective-permute-start.5
  53.1 2.2 %late_weights.1 = (bf16[4,4,256,256]{3,2,1,0:T(8,128)(2,1)S(1)}, bf16[192,2048]{1,0:T(8,128)(2,1)S(1)}, s32[4]{0:T(128)S(1)}) custom-call(s32[1]{0:T(128)} %bitcast.even_ref, s32[1]{0:T(128)} %bitcast.1.me_ref, s32[4]{0:T(128)S(1)} %bitcast.5, bf16[8,16]{1,0:T(8,128)(2,1)S(1)} %copy-done.7, bf16[8,64]{1,0:T(8,128)(2,1)S(1)} %copy-done.8, ...), custom_call_target="tpu_custom_call" | custom-call | flops 1 | bytes 1 | tf_op jit(solution)/shard_map/late_weights/pallas_call | solution.py:160
  55.3 1.6 %second_edges.4 = (bf16[4,384,128]{2,1,0:T(8,128)(2,1)S(1)}, bf16[96,128]{1,0:T(8,128)(2,1)S(1)}, bf16[96,128]{1,0:T(8,128)(2,1)S(1)}) custom-call(s32[4]{0:T(128)S(1)} %get-tuple-element.74.slot_ref.refs_4_.refs_8_, bf16[2,256,256]{2,1,0:T(8,128)(2,1)S(1)} %get-tuple-element.75.picks_ref, bf16[2,400,128]{2,1,0:T(8,128)(2,1)S(1)} %get-tuple-element.69.refs_0_, ...), custom_call_target="tpu_custom_call" | custom-call | flops 1 | bytes 1 | tf_op jit(solution)/shard_map/second_edges/pallas_call | solution.py:287
  56.9 0.3 collective-permute-start.6
  57.2 5.9 %collective-permute-start.7 = (bf16[96,128]{1,0:T(8,128)(2,1)S(1)}, bf16[96,128]{1,0:T(8,128)(2,1)S(1)}, u32[]{:S(2)}, u32[]{:S(2)}) collective-permute-start(bf16[96,128]{1,0:T(8,128)(2,1)S(1)} %get-tuple-element.87), channel_id=1, source_target_pairs={{1,2},{2,1},{3,4},{4,3},{5,6},{6,5},{7,8},{8,7},{9,10},{10,9},{11,... | collective-permute-start | bytes 73736 | tf_op jit(solution)/shard_map/ppermute | solution.py:306
  63.1 0.0 collective-permute-done.6.refs_1_
  63.1 9.6 %collective-permute-done.7.refs_2_ = bf16[96,128]{1,0:T(8,128)(2,1)S(1)} collective-permute-done((bf16[96,128]{1,0:T(8,128)(2,1)S(1)}, bf16[96,128]{1,0:T(8,128)(2,1)S(1)}, u32[]{:S(2)}, u32[]{:S(2)}) %collective-permute-start.7) | collective-permute-done | bytes 24608 | tf_op jit(solution)/shard_map/ppermute | solution.py:306
  72.8 0.0 collective-permute-done.10.refs_3_
  72.8 0.1 collective-permute-start.14
  72.9 0.0 collective-permute-done.9.refs_2_
  72.9 0.0 collective-permute-start.13
  72.9 0.0 collective-permute-done.5.refs_1_
  72.9 2.0 %collective-permute-start.8 = (bf16[2,576,128]{2,1,0:T(8,128)(2,1)S(1)}, bf16[2,576,128]{2,1,0:T(8,128)(2,1)S(1)}, u32[]{:S(2)}, u32[]{:S(2)}) collective-permute-start(bf16[2,576,128]{2,1,0:T(8,128)(2,1)S(1)} %get-tuple-element.88), channel_id=1, source_target_pairs={{0,64},{64,128},{128,192},{192,0},{1,65},{65,129},{129,193},{193,1... | collective-permute-start | bytes 884744 | tf_op jit(solution)/shard_map/ppermute | solution.py:547
  74.9 1.9 %second_edges.5 = (bf16[4,576,128]{2,1,0:T(8,128)(2,1)S(1)}, bf16[144,128]{1,0:T(8,128)(2,1)S(1)}, bf16[144,128]{1,0:T(8,128)(2,1)S(1)}) custom-call(s32[4]{0:T(128)S(1)} %get-tuple-element.74.slot_ref.refs_4_.refs_8_, bf16[2,256,256]{2,1,0:T(8,128)(2,1)S(1)} %get-tuple-element.75.picks_ref, bf16[2,576,128]{2,1,0:T(8,128)(2,1)S(1)} %get-tuple-element.89.refs_0_, ...), custom_call_target="tpu_custom_call" | custom-call | flops 1 | bytes 1 | tf_op jit(solution)/shard_map/second_edges/pallas_call | solution.py:287
  76.8 6.6 %collective-permute-start.12 = (bf16[144,128]{1,0:T(8,128)(2,1)S(1)}, bf16[144,128]{1,0:T(8,128)(2,1)S(1)}, u32[]{:S(2)}, u32[]{:S(2)}) collective-permute-start(bf16[144,128]{1,0:T(8,128)(2,1)S(1)} %get-tuple-element.98), channel_id=1, source_target_pairs={{1,2},{2,1},{3,4},{4,3},{5,6},{6,5},{7,8},{8,7},{9,10},{10,9},{11,... | collective-permute-start | bytes 110600 | tf_op jit(solution)/shard_map/ppermute | solution.py:306
  83.3 0.1 collective-permute-start.11
  83.4 2.9 %second_pass.4 = (f32[4,2000,128]{2,1,0:T(8,128)}, f32[8,128]{1,0:T(8,128)S(1)}) custom-call(bf16[4,384,128]{2,1,0:T(8,128)(2,1)S(1)} %get-tuple-element.99.refs_0_, bf16[96,128]{1,0:T(8,128)(2,1)S(1)} %collective-permute-done.6.refs_1_, bf16[96,128]{1,0:T(8,128)(2,1)S(1)} %collective-permute-done.7.refs_2_, ...), custom_call_target="tpu_custom_call" | custom-call | flops 1 | bytes 1 | tf_op jit(solution)/shard_map/second_pass/pallas_call | solution.py:515
  86.4 4.2 %collective-permute-done.12.refs_5_.refs_2_ = bf16[144,128]{1,0:T(8,128)(2,1)S(1)} collective-permute-done((bf16[144,128]{1,0:T(8,128)(2,1)S(1)}, bf16[144,128]{1,0:T(8,128)(2,1)S(1)}, u32[]{:S(2)}, u32[]{:S(2)}) %collective-permute-start.12) | collective-permute-done | bytes 36896 | tf_op jit(solution)/shard_map/ppermute | solution.py:306
  90.6 0.0 collective-permute-done.11.refs_4_.refs_1_
  90.6 0.0 collective-permute-done.14.refs_3_
  90.6 0.1 collective-permute-done.13.refs_2_
  90.7 0.7 collective-permute-done.8.refs_1_
  91.4 1.4 %collective-permute-start.17 = (bf16[2,464,128]{2,1,0:T(8,128)(2,1)S(1)}, bf16[2,464,128]{2,1,0:T(8,128)(2,1)S(1)}, u32[]{:S(2)}, u32[]{:S(2)}) collective-permute-start(bf16[2,464,128]{2,1,0:T(8,128)(2,1)S(1)} %get-tuple-element.113), channel_id=1, source_target_pairs={{0,64},{64,128},{128,192},{192,0},{1,65},{65,129},{129,193},{193,1... | collective-permute-start | bytes 712712 | tf_op jit(solution)/shard_map/ppermute | solution.py:547
  92.8 1.3 collective-permute-start.18
  94.1 2.9 %collective-permute-start.19 = (bf16[2,464,128]{2,1,0:T(8,128)(2,1)S(1)}, bf16[2,464,128]{2,1,0:T(8,128)(2,1)S(1)}, u32[]{:S(2)}, u32[]{:S(2)}) collective-permute-start(bf16[2,464,128]{2,1,0:T(8,128)(2,1)S(1)} %get-tuple-element.115), channel_id=1, source_target_pairs={{0,192},{64,0},{128,64},{192,128},{1,193},{65,1},{129,65},{193,129... | collective-permute-start | bytes 712712 | tf_op jit(solution)/shard_map/ppermute | solution.py:547
  97.0 1.9 %second_edges.6 = (bf16[4,576,128]{2,1,0:T(8,128)(2,1)S(1)}, bf16[144,128]{1,0:T(8,128)(2,1)S(1)}, bf16[144,128]{1,0:T(8,128)(2,1)S(1)}) custom-call(s32[4]{0:T(128)S(1)} %get-tuple-element.74.slot_ref.refs_4_.refs_8_, bf16[2,256,256]{2,1,0:T(8,128)(2,1)S(1)} %get-tuple-element.75.picks_ref, bf16[2,576,128]{2,1,0:T(8,128)(2,1)S(1)} %get-tuple-element.76.refs_0_, ...), custom_call_target="tpu_custom_call" | custom-call | flops 1 | bytes 1 | tf_op jit(solution)/shard_map/second_edges/pallas_call | solution.py:287
  98.9 5.0 %collective-permute-start.16 = (bf16[144,128]{1,0:T(8,128)(2,1)S(1)}, bf16[144,128]{1,0:T(8,128)(2,1)S(1)}, u32[]{:S(2)}, u32[]{:S(2)}) collective-permute-start(bf16[144,128]{1,0:T(8,128)(2,1)S(1)} %get-tuple-element.112), channel_id=1, source_target_pairs={{1,2},{2,1},{3,4},{4,3},{5,6},{6,5},{7,8},{8,7},{9,10},{10,9},{11,... | collective-permute-start | bytes 110600 | tf_op jit(solution)/shard_map/ppermute | solution.py:306
  103.9 0.1 collective-permute-start.15
  104.0 4.6 %second_pass.5 = (f32[4,2000,128]{2,1,0:T(8,128)}, f32[8,128]{1,0:T(8,128)S(1)}) custom-call(bf16[4,384,128]{2,1,0:T(8,128)(2,1)S(1)} %get-tuple-element.99.refs_0_, bf16[96,128]{1,0:T(8,128)(2,1)S(1)} %collective-permute-done.6.refs_1_, bf16[96,128]{1,0:T(8,128)(2,1)S(1)} %collective-permute-done.7.refs_2_, ...), custom_call_target="tpu_custom_call", output_to_operand_aliasing={{0}: (9, {})} | custom-call | flops 1 | bytes 1 | tf_op jit(solution)/shard_map/second_pass/pallas_call | solution.py:515
  108.6 1.7 %collective-permute-done.17.refs_1_ = bf16[2,464,128]{2,1,0:T(8,128)(2,1)S(1)} collective-permute-done((bf16[2,464,128]{2,1,0:T(8,128)(2,1)S(1)}, bf16[2,464,128]{2,1,0:T(8,128)(2,1)S(1)}, u32[]{:S(2)}, u32[]{:S(2)}) %collective-permute-start.17) | collective-permute-done | bytes 237600 | tf_op jit(solution)/shard_map/ppermute | solution.py:547
  110.3 0.0 collective-permute-done.18.refs_2_
  110.3 2.0 %collective-permute-done.19.refs_3_ = bf16[2,464,128]{2,1,0:T(8,128)(2,1)S(1)} collective-permute-done((bf16[2,464,128]{2,1,0:T(8,128)(2,1)S(1)}, bf16[2,464,128]{2,1,0:T(8,128)(2,1)S(1)}, u32[]{:S(2)}, u32[]{:S(2)}) %collective-permute-start.19) | collective-permute-done | bytes 237600 | tf_op jit(solution)/shard_map/ppermute | solution.py:547
  112.4 1.7 %second_edges.7 = (bf16[4,464,128]{2,1,0:T(8,128)(2,1)S(1)}, bf16[128,128]{1,0:T(8,128)(2,1)S(1)}, bf16[128,128]{1,0:T(8,128)(2,1)S(1)}) custom-call(s32[4]{0:T(128)S(1)} %get-tuple-element.74.slot_ref.refs_4_.refs_8_, bf16[2,256,256]{2,1,0:T(8,128)(2,1)S(1)} %get-tuple-element.75.picks_ref, bf16[2,464,128]{2,1,0:T(8,128)(2,1)S(1)} %get-tuple-element.73.refs_4_.refs_0_, ...), custom_call_target="tpu_custom_call" | custom-call | flops 1 | bytes 1 | tf_op jit(solution)/shard_map/second_edges/pallas_call | solution.py:287
  114.1 6.7 %collective-permute-start.21 = (bf16[128,128]{1,0:T(8,128)(2,1)S(1)}, bf16[128,128]{1,0:T(8,128)(2,1)S(1)}, u32[]{:S(2)}, u32[]{:S(2)}) collective-permute-start(bf16[128,128]{1,0:T(8,128)(2,1)S(1)} %get-tuple-element.121), channel_id=1, source_target_pairs={{1,2},{2,1},{3,4},{4,3},{5,6},{6,5},{7,8},{8,7},{9,10},{10,9},{11,... | collective-permute-start | bytes 98312 | tf_op jit(solution)/shard_map/ppermute | solution.py:306
  120.8 0.3 collective-permute-start.20
  121.1 0.0 collective-permute-done.16.refs_5_.refs_2_
  121.1 0.0 collective-permute-done.15.refs_4_.refs_1_
  121.1 5.2 %second_pass.6 = (f32[4,2000,128]{2,1,0:T(8,128)}, f32[8,128]{1,0:T(8,128)}) custom-call(bf16[4,576,128]{2,1,0:T(8,128)(2,1)S(1)} %get-tuple-element.116.refs_3_.refs_0_, bf16[144,128]{1,0:T(8,128)(2,1)S(1)} %collective-permute-done.11.refs_4_.refs_1_, bf16[144,128]{1,0:T(8,128)(2,1)S(1)} %collective-permute-done.12.refs_5_.refs_2_, ...), custom_call_target="tpu_custom_call", output_to_operand_aliasing={{0}: (9, {})} | custom-call | flops 1 | bytes 1 | tf_op jit(solution)/shard_map/second_pass/pallas_call | solution.py:515
  126.4 1.1 collective-permute-done.21.refs_5_
  127.4 0.0 collective-permute-done.20.refs_4_
  127.4 4.9 %second_pass.7 = (f32[4,2000,128]{2,1,0:T(8,128)}, f32[8,128]{1,0:T(8,128)}) custom-call(bf16[4,576,128]{2,1,0:T(8,128)(2,1)S(1)} %get-tuple-element.110.refs_3_.refs_0_, bf16[144,128]{1,0:T(8,128)(2,1)S(1)} %collective-permute-done.15.refs_4_.refs_1_, bf16[144,128]{1,0:T(8,128)(2,1)S(1)} %collective-permute-done.16.refs_5_.refs_2_, ...), custom_call_target="tpu_custom_call", output_to_operand_aliasing={{0}: (9, {})} | custom-call | flops 1 | bytes 1 | tf_op jit(solution)/shard_map/second_pass/pallas_call | solution.py:515
  (11 shorter events, 0.0 us)
Async XLA Ops:
  0.0 19.0 %copy-start.4 = (s32[4,1]{0,1:T(1,128)S(1)}, s32[4,1]{0,1:T(1,128)}, u32[]{:S(2)}) copy-start(s32[4,1]{0,1:T(1,128)} %param.11) | copy-start | bytes 52
  0.0 1.6 %copy-start = (bf16[4,2000,128]{2,1,0:T(8,128)(2,1)S(1)}, bf16[4,2000,128]{2,1,0:T(8,128)(2,1)}, u32[]{:S(2)}) copy-start(bf16[4,2000,128]{2,1,0:T(8,128)(2,1)} %x_ref.5) | copy-start | bytes 6144004
  1.6 17.4 %copy-start.1 = (bf16[4,2000,128]{2,1,0:T(8,128)(2,1)S(1)}, bf16[4,2000,128]{2,1,0:T(8,128)(2,1)}, u32[]{:S(2)}) copy-start(bf16[4,2000,128]{2,1,0:T(8,128)(2,1)} %x_ref.5) | copy-start | bytes 6144004
  3.2 10.5 %collective-permute-start = (bf16[512,128]{1,0:T(8,128)(2,1)}, bf16[512,128]{1,0:T(8,128)(2,1)S(1)}, u32[]{:S(2)}, u32[]{:S(2)}) collective-permute-start(bf16[512,128]{1,0:T(8,128)(2,1)} %get-tuple-element.65), channel_id=1, source_target_pairs={{0,1},{1,0},{2,3},{3,2},{4,5},{5,4},{6,7},{7,6},{8,9},{9,8},{10,11... | collective-permute-start | bytes 393224 | tf_op jit(solution)/shard_map/ppermute | solution.py:306
  3.2 15.8 %collective-permute-start.1 = (bf16[512,128]{1,0:T(8,128)(2,1)S(1)}, bf16[512,128]{1,0:T(8,128)(2,1)S(1)}, u32[]{:S(2)}, u32[]{:S(2)}) collective-permute-start(bf16[512,128]{1,0:T(8,128)(2,1)S(1)} %get-tuple-element.66), channel_id=1, source_target_pairs={{1,2},{2,1},{3,4},{4,3},{5,6},{6,5},{7,8},{8,7},{9,10},{10,9},{11,... | collective-permute-start | bytes 393224 | tf_op jit(solution)/shard_map/ppermute | solution.py:306
  10.4 0.7 copy-start.5
  11.1 0.7 copy-start.6
  12.4 1.3 copy-start.2
  19.0 1.6 %copy-start.3 = (bf16[4,4,256,256]{3,2,1,0:T(8,128)(2,1)S(1)}, bf16[4,4,256,256]{3,2,1,0:T(8,128)(2,1)}, u32[]{:S(2)}) copy-start(bf16[4,4,256,256]{3,2,1,0:T(8,128)(2,1)} %copy-done.2) | copy-start | bytes 6291460
  20.6 32.4 %copy-start.7 = (bf16[8,16]{1,0:T(8,128)(2,1)S(1)}, bf16[8,16]{1,0:T(8,128)(2,1)}, u32[]{:S(2)}) copy-start(bf16[8,16]{1,0:T(8,128)(2,1)} %trace_ref.3) | copy-start | bytes 772
  20.6 32.4 %copy-start.8 = (bf16[8,64]{1,0:T(8,128)(2,1)S(1)}, bf16[8,64]{1,0:T(8,128)(2,1)}, u32[]{:S(2)}) copy-start(bf16[8,64]{1,0:T(8,128)(2,1)} %time_ref.3) | copy-start | bytes 3076
  24.2 13.5 %collective-permute-start.4 = (bf16[2,400,128]{2,1,0:T(8,128)(2,1)S(1)}, bf16[2,400,128]{2,1,0:T(8,128)(2,1)S(1)}, u32[]{:S(2)}, u32[]{:S(2)}) collective-permute-start(bf16[2,400,128]{2,1,0:T(8,128)(2,1)S(1)} %get-tuple-element.72), channel_id=1, source_target_pairs={{0,192},{64,0},{128,64},{192,128},{1,193},{65,1},{129,65},{193,129... | collective-permute-start | bytes 614408 | tf_op jit(solution)/shard_map/ppermute | solution.py:547
  25.2 14.0 %collective-permute-start.3 = (bf16[2,400,128]{2,1,0:T(8,128)(2,1)S(1)}, bf16[2,400,128]{2,1,0:T(8,128)(2,1)S(1)}, u32[]{:S(2)}, u32[]{:S(2)}) collective-permute-start(bf16[2,400,128]{2,1,0:T(8,128)(2,1)S(1)} %get-tuple-element.71), channel_id=1, source_target_pairs={{0,128},{64,192},{128,0},{192,64},{1,129},{65,193},{129,1},{193,65... | collective-permute-start | bytes 614408 | tf_op jit(solution)/shard_map/ppermute | solution.py:547
  26.3 26.7 %collective-permute-start.2 = (bf16[2,400,128]{2,1,0:T(8,128)(2,1)S(1)}, bf16[2,400,128]{2,1,0:T(8,128)(2,1)S(1)}, u32[]{:S(2)}, u32[]{:S(2)}) collective-permute-start(bf16[2,400,128]{2,1,0:T(8,128)(2,1)S(1)} %get-tuple-element.70), channel_id=1, source_target_pairs={{0,64},{64,128},{128,192},{192,0},{1,65},{65,129},{129,193},{193,1... | collective-permute-start | bytes 614408 | tf_op jit(solution)/shard_map/ppermute | solution.py:547
  37.6 35.1 %collective-permute-start.10 = (bf16[2,576,128]{2,1,0:T(8,128)(2,1)S(1)}, bf16[2,576,128]{2,1,0:T(8,128)(2,1)S(1)}, u32[]{:S(2)}, u32[]{:S(2)}) collective-permute-start(bf16[2,576,128]{2,1,0:T(8,128)(2,1)S(1)} %get-tuple-element.95), channel_id=1, source_target_pairs={{0,192},{64,0},{128,64},{192,128},{1,193},{65,1},{129,65},{193,129... | collective-permute-start | bytes 884744 | tf_op jit(solution)/shard_map/ppermute | solution.py:547
  39.2 33.6 %collective-permute-start.9 = (bf16[2,576,128]{2,1,0:T(8,128)(2,1)S(1)}, bf16[2,576,128]{2,1,0:T(8,128)(2,1)S(1)}, u32[]{:S(2)}, u32[]{:S(2)}) collective-permute-start(bf16[2,576,128]{2,1,0:T(8,128)(2,1)S(1)} %get-tuple-element.92), channel_id=1, source_target_pairs={{0,128},{64,192},{128,0},{192,64},{1,129},{65,193},{129,1},{193,65... | collective-permute-start | bytes 884744 | tf_op jit(solution)/shard_map/ppermute | solution.py:547
  53.1 19.8 %collective-permute-start.5 = (bf16[2,576,128]{2,1,0:T(8,128)(2,1)S(1)}, bf16[2,576,128]{2,1,0:T(8,128)(2,1)S(1)}, u32[]{:S(2)}, u32[]{:S(2)}) collective-permute-start(bf16[2,576,128]{2,1,0:T(8,128)(2,1)S(1)} %get-tuple-element.80), channel_id=1, source_target_pairs={{0,64},{64,128},{128,192},{192,0},{1,65},{65,129},{129,193},{193,1... | collective-permute-start | bytes 884744 | tf_op jit(solution)/shard_map/ppermute | solution.py:547
  56.9 6.2 %collective-permute-start.6 = (bf16[96,128]{1,0:T(8,128)(2,1)S(1)}, bf16[96,128]{1,0:T(8,128)(2,1)S(1)}, u32[]{:S(2)}, u32[]{:S(2)}) collective-permute-start(bf16[96,128]{1,0:T(8,128)(2,1)S(1)} %get-tuple-element.86), channel_id=1, source_target_pairs={{0,1},{1,0},{2,3},{3,2},{4,5},{5,4},{6,7},{7,6},{8,9},{9,8},{10,11... | collective-permute-start | bytes 73736 | tf_op jit(solution)/shard_map/ppermute | solution.py:306
  57.2 15.5 %collective-permute-start.7 = (bf16[96,128]{1,0:T(8,128)(2,1)S(1)}, bf16[96,128]{1,0:T(8,128)(2,1)S(1)}, u32[]{:S(2)}, u32[]{:S(2)}) collective-permute-start(bf16[96,128]{1,0:T(8,128)(2,1)S(1)} %get-tuple-element.87), channel_id=1, source_target_pairs={{1,2},{2,1},{3,4},{4,3},{5,6},{6,5},{7,8},{8,7},{9,10},{10,9},{11,... | collective-permute-start | bytes 73736 | tf_op jit(solution)/shard_map/ppermute | solution.py:306
  72.8 17.8 %collective-permute-start.14 = (bf16[2,576,128]{2,1,0:T(8,128)(2,1)S(1)}, bf16[2,576,128]{2,1,0:T(8,128)(2,1)S(1)}, u32[]{:S(2)}, u32[]{:S(2)}) collective-permute-start(bf16[2,576,128]{2,1,0:T(8,128)(2,1)S(1)} %get-tuple-element.108), channel_id=1, source_target_pairs={{0,192},{64,0},{128,64},{192,128},{1,193},{65,1},{129,65},{193,129... | collective-permute-start | bytes 884744 | tf_op jit(solution)/shard_map/ppermute | solution.py:547
  72.9 17.8 %collective-permute-start.13 = (bf16[2,576,128]{2,1,0:T(8,128)(2,1)S(1)}, bf16[2,576,128]{2,1,0:T(8,128)(2,1)S(1)}, u32[]{:S(2)}, u32[]{:S(2)}) collective-permute-start(bf16[2,576,128]{2,1,0:T(8,128)(2,1)S(1)} %get-tuple-element.105), channel_id=1, source_target_pairs={{0,128},{64,192},{128,0},{192,64},{1,129},{65,193},{129,1},{193,65... | collective-permute-start | bytes 884744 | tf_op jit(solution)/shard_map/ppermute | solution.py:547
  72.9 18.5 %collective-permute-start.8 = (bf16[2,576,128]{2,1,0:T(8,128)(2,1)S(1)}, bf16[2,576,128]{2,1,0:T(8,128)(2,1)S(1)}, u32[]{:S(2)}, u32[]{:S(2)}) collective-permute-start(bf16[2,576,128]{2,1,0:T(8,128)(2,1)S(1)} %get-tuple-element.88), channel_id=1, source_target_pairs={{0,64},{64,128},{128,192},{192,0},{1,65},{65,129},{129,193},{193,1... | collective-permute-start | bytes 884744 | tf_op jit(solution)/shard_map/ppermute | solution.py:547
  76.8 13.8 %collective-permute-start.12 = (bf16[144,128]{1,0:T(8,128)(2,1)S(1)}, bf16[144,128]{1,0:T(8,128)(2,1)S(1)}, u32[]{:S(2)}, u32[]{:S(2)}) collective-permute-start(bf16[144,128]{1,0:T(8,128)(2,1)S(1)} %get-tuple-element.98), channel_id=1, source_target_pairs={{1,2},{2,1},{3,4},{4,3},{5,6},{6,5},{7,8},{8,7},{9,10},{10,9},{11,... | collective-permute-start | bytes 110600 | tf_op jit(solution)/shard_map/ppermute | solution.py:306
  83.3 7.2 %collective-permute-start.11 = (bf16[144,128]{1,0:T(8,128)(2,1)S(1)}, bf16[144,128]{1,0:T(8,128)(2,1)S(1)}, u32[]{:S(2)}, u32[]{:S(2)}) collective-permute-start(bf16[144,128]{1,0:T(8,128)(2,1)S(1)} %get-tuple-element.97.refs_5_), channel_id=1, source_target_pairs={{0,1},{1,0},{2,3},{3,2},{4,5},{5,4},{6,7},{7,6},{8,9},{9,8},{10,11... | collective-permute-start | bytes 110600 | tf_op jit(solution)/shard_map/ppermute | solution.py:306
  91.4 18.9 %collective-permute-start.17 = (bf16[2,464,128]{2,1,0:T(8,128)(2,1)S(1)}, bf16[2,464,128]{2,1,0:T(8,128)(2,1)S(1)}, u32[]{:S(2)}, u32[]{:S(2)}) collective-permute-start(bf16[2,464,128]{2,1,0:T(8,128)(2,1)S(1)} %get-tuple-element.113), channel_id=1, source_target_pairs={{0,64},{64,128},{128,192},{192,0},{1,65},{65,129},{129,193},{193,1... | collective-permute-start | bytes 712712 | tf_op jit(solution)/shard_map/ppermute | solution.py:547
  92.8 17.5 %collective-permute-start.18 = (bf16[2,464,128]{2,1,0:T(8,128)(2,1)S(1)}, bf16[2,464,128]{2,1,0:T(8,128)(2,1)S(1)}, u32[]{:S(2)}, u32[]{:S(2)}) collective-permute-start(bf16[2,464,128]{2,1,0:T(8,128)(2,1)S(1)} %get-tuple-element.114), channel_id=1, source_target_pairs={{0,128},{64,192},{128,0},{192,64},{1,129},{65,193},{129,1},{193,65... | collective-permute-start | bytes 712712 | tf_op jit(solution)/shard_map/ppermute | solution.py:547
  94.1 18.3 %collective-permute-start.19 = (bf16[2,464,128]{2,1,0:T(8,128)(2,1)S(1)}, bf16[2,464,128]{2,1,0:T(8,128)(2,1)S(1)}, u32[]{:S(2)}, u32[]{:S(2)}) collective-permute-start(bf16[2,464,128]{2,1,0:T(8,128)(2,1)S(1)} %get-tuple-element.115), channel_id=1, source_target_pairs={{0,192},{64,0},{128,64},{192,128},{1,193},{65,1},{129,65},{193,129... | collective-permute-start | bytes 712712 | tf_op jit(solution)/shard_map/ppermute | solution.py:547
  98.9 22.2 %collective-permute-start.16 = (bf16[144,128]{1,0:T(8,128)(2,1)S(1)}, bf16[144,128]{1,0:T(8,128)(2,1)S(1)}, u32[]{:S(2)}, u32[]{:S(2)}) collective-permute-start(bf16[144,128]{1,0:T(8,128)(2,1)S(1)} %get-tuple-element.112), channel_id=1, source_target_pairs={{1,2},{2,1},{3,4},{4,3},{5,6},{6,5},{7,8},{8,7},{9,10},{10,9},{11,... | collective-permute-start | bytes 110600 | tf_op jit(solution)/shard_map/ppermute | solution.py:306
  103.9 17.2 %collective-permute-start.15 = (bf16[144,128]{1,0:T(8,128)(2,1)S(1)}, bf16[144,128]{1,0:T(8,128)(2,1)S(1)}, u32[]{:S(2)}, u32[]{:S(2)}) collective-permute-start(bf16[144,128]{1,0:T(8,128)(2,1)S(1)} %get-tuple-element.111.refs_8_), channel_id=1, source_target_pairs={{0,1},{1,0},{2,3},{3,2},{4,5},{5,4},{6,7},{7,6},{8,9},{9,8},{10,11... | collective-permute-start | bytes 110600 | tf_op jit(solution)/shard_map/ppermute | solution.py:306
  114.1 13.4 %collective-permute-start.21 = (bf16[128,128]{1,0:T(8,128)(2,1)S(1)}, bf16[128,128]{1,0:T(8,128)(2,1)S(1)}, u32[]{:S(2)}, u32[]{:S(2)}) collective-permute-start(bf16[128,128]{1,0:T(8,128)(2,1)S(1)} %get-tuple-element.121), channel_id=1, source_target_pairs={{1,2},{2,1},{3,4},{4,3},{5,6},{6,5},{7,8},{8,7},{9,10},{10,9},{11,... | collective-permute-start | bytes 98312 | tf_op jit(solution)/shard_map/ppermute | solution.py:306
  120.8 6.7 %collective-permute-start.20 = (bf16[128,128]{1,0:T(8,128)(2,1)S(1)}, bf16[128,128]{1,0:T(8,128)(2,1)S(1)}, u32[]{:S(2)}, u32[]{:S(2)}) collective-permute-start(bf16[128,128]{1,0:T(8,128)(2,1)S(1)} %get-tuple-element.120.refs_8_), channel_id=1, source_target_pairs={{0,1},{1,0},{2,3},{3,2},{4,5},{5,4},{6,7},{7,6},{8,9},{9,8},{10,11... | collective-permute-start | bytes 98312 | tf_op jit(solution)/shard_map/ppermute | solution.py:306

commit v5 on v4

--- a/solution.py
+++ b/solution.py
@@ -20,6 +20,7 @@
 ANY = pl.BlockSpec(memory_space=pl.ANY)
 HBM = pl.BlockSpec(memory_space=pltpu.HBM)
 CHUNKS = (384, 576, 576)
+RIM_FOLD = 8
 NOTE = 16
 
 
@@ -44,6 +45,10 @@
 
 def folded_rows(rows):
     return -(-rows // (16 * FOLD)) * 16
+
+
+def rim_rows(rows):
+    return -(-rows // (16 * RIM_FOLD)) * 16
 
 
 def place_taps(taps_ref, origin, step):
@@ -215,11 +220,11 @@
                 piece = pltpu.roll(piece, part * EDGE * blocks, 1)
             totals[way] = piece if totals[way] is None else totals[way] + piece
     for way in range(2):
-        packed_refs[way][...] = totals[way].astype(jnp.bfloat16)
+        packed_refs[way][:fold, :] = totals[way].astype(jnp.bfloat16)
 
 
 def unpack_edges(packed_refs, rows, blocks, start, stop, give):
-    fold, width = packed_refs[0].shape[0], EDGE * blocks
+    fold, width = folded_rows(rows), EDGE * blocks
     while start < stop:
         part = start // fold
         until = min(stop, (part + 1) * fold)
@@ -260,40 +265,73 @@
     )(even, traces)
 
 
-def second_edges_kernel(slot_ref, picks_ref, *refs):
-    parts, (_, sorted_ref, out_a, out_b, sem) = refs[:-5], refs[-5:]
+def gather_rows(slot_ref, parts, held_ref, sem, start):
+    blocks, rows = held_ref.shape[:2]
+    slot_cap = parts[0].shape[0]
+
+    def begin():
+        for block in range(blocks):
+            slot = slot_ref[block]
+            for offset, part in enumerate(parts):
+
+                @pl.when(slot // slot_cap == offset)
+                def _():
+                    pltpu.make_async_copy(
+                        part.at[slot % slot_cap, pl.ds(start, rows), :],
+                        held_ref.at[block],
+                        sem.at[block],
+                    ).start()
+
+    def wait():
+        for block in range(blocks):
+            pltpu.make_async_copy(
+                parts[0].at[0, pl.ds(start, rows), :], held_ref.at[block], sem.at[block]
+            ).wait()
+
+    return begin, wait
+
+
+def second_edges_kernel(even_ref, slot_ref, picks_ref, *refs):
+    parts, (_, sorted_ref, out_a, out_b, rims_ref, sem, rim_sem) = refs[:-7], refs[-7:]
     blocks, rows = sorted_ref.shape[:2]
-    slot_cap = parts[0].shape[0]
-    for block in range(blocks):
-        slot = slot_ref[block]
-        for offset, part in enumerate(parts):
-
-            @pl.when(slot // slot_cap == offset)
-            def _():
-                pltpu.make_async_copy(
-                    part.at[slot % slot_cap, pl.ds(0, rows), :], sorted_ref.at[block], sem.at[block]
-                ).start()
-
-    for block in range(blocks):
-        pltpu.make_async_copy(
-            parts[0].at[0, pl.ds(0, rows), :], sorted_ref.at[block], sem.at[block]
-        ).wait()
+    begin, wait = gather_rows(slot_ref, parts, sorted_ref, sem, 0)
+    begin()
+    fold = folded_rows(rows)
+    rimmed = out_a.shape[0] > fold
+    if rimmed:
+        rim_begin, rim_wait = gather_rows(slot_ref, parts, rims_ref, rim_sem, rows)
+        rim_begin()
+    wait()
     picks = [picks_ref[pair] for pair in range(blocks // 2)]
     pack_edges(picks, sorted_ref, (out_a, out_b))
-
-
-def second_edges(slots, picks, arrived, rows, after, blocks):
-    packed = jax.ShapeDtypeStruct((folded_rows(rows), LANES), jnp.bfloat16)
+    if rimmed:
+        rim_wait()
+        size = rims_ref.shape[1]
+        even = even_ref[0] == 1
+        for block in range(blocks):
+            first = rims_ref[block].astype(jnp.float32)
+            last = pltpu.roll(first, LANES - EDGE, 1)
+            span = slice(fold + block * size, fold + (block + 1) * size)
+            out_a[span, :] = jnp.where(even, last, first).astype(jnp.bfloat16)
+            out_b[span, :] = jnp.where(even, first, last).astype(jnp.bfloat16)
+
+
+def second_edges(even, slots, picks, arrived, rows, rims, after, blocks):
+    packed = jax.ShapeDtypeStruct((folded_rows(rows) + blocks * rims, LANES), jnp.bfloat16)
     return pl.pallas_call(
         second_edges_kernel,
-        in_specs=[SMEM, VMEM] + [ANY] * (len(arrived) + 1),
+        in_specs=[SMEM, SMEM, VMEM] + [ANY] * (len(arrived) + 1),
         out_specs=[VMEM] * 3,
-        scratch_shapes=[pltpu.SemaphoreType.DMA((blocks,))],
+        scratch_shapes=[
+            pltpu.VMEM((blocks, rims or 16, LANES), jnp.bfloat16),
+            pltpu.SemaphoreType.DMA((blocks,)),
+            pltpu.SemaphoreType.DMA((blocks,)),
+        ],
         out_shape=[jax.ShapeDtypeStruct((blocks, rows, LANES), jnp.bfloat16), packed, packed],
         cost_estimate=NO_COST,
         compiler_params=PARAMS,
         name="second_edges",
-    )(slots, picks, *arrived, after)
+    )(even, slots, picks, *arrived, after)
 
 
 def swap_edges(packed):
@@ -352,8 +390,8 @@
     start, sizes, noted, owners, me_ref, target_ref, x_ref, edge_a, edge_b, mats_ref, times_ref,
     *refs
 ):
-    outs = refs[-6 - owners * len(sizes) : -6]
-    merged, fans_ref, done, note, sem, note_sem = refs[-6:]
+    outs = refs[-8 - owners * len(sizes) : -8]
+    merged, fans_ref, done, note, rims, sem, note_sem, rim_sem = refs[-8:]
     blocks, rows = done.shape[:2]
     samples = x_ref.shape[1]
     window = start - REACH // 2
@@ -396,9 +434,31 @@
             value = jnp.where(pair == other, values[2 * other + half], value)
         return value
 
+    def pack_rim(block):
+        at, size, _ = groups[-1]
+        trace = lax.broadcasted_iota(jnp.int32, (LANES, LANES), 0)
+        lane = lax.broadcasted_iota(jnp.int32, (LANES, LANES), 1)
+        wanted = jnp.where(lane < EDGE, lane, lane + LANES - 2 * EDGE)
+        chosen = jnp.where((lane < 2 * EDGE) & (trace == wanted), 1.0, 0.0).astype(jnp.bfloat16)
+        found = jnp.dot(done[block, at : at + size, :], chosen, preferred_element_type=jnp.float32)
+        fold, total = rims.shape[1], None
+        for part in range(-(-size // fold)):
+            piece = found[part * fold : (part + 1) * fold]
+            if piece.shape[0] < fold:
+                rest = jnp.zeros((fold - piece.shape[0], LANES), jnp.float32)
+                piece = jnp.concatenate([piece, rest], axis=0)
+            if part:
+                piece = pltpu.roll(piece, 2 * EDGE * part, 1)
+            total = piece if total is None else total + piece
+        rims[block] = total.astype(jnp.bfloat16)
+
+    rim_group = None if noted else len(groups) - 2
+
     def finish(pair):
         for half in range(2):
             block = 2 * pair + half
+            if not noted:
+                pack_rim(block)
             owner, rank = pick(homes, pair, half), pick(order, pair, half)
             away = lax.rem(owner - me_ref[0] + owners, owners)
             for group, (at, size, arrays) in enumerate(groups):
@@ -410,6 +470,12 @@
                         pltpu.make_async_copy(
                             part, out_ref.at[rank, pl.ds(0, size), :], sem.at[group, block]
                         ).start()
+                        if group == rim_group:
+                            pltpu.make_async_copy(
+                                rims.at[block],
+                                out_ref.at[rank, pl.ds(size, rims.shape[1]), :],
+                                rim_sem.at[block],
+                            ).start()
 
     pieces = [(begin - window, end - begin, lambda block: x_ref[block, begin:end, :])]
     filter_window(pieces, merged, fans_ref, mats_ref, times_ref, rows, give, finish)
@@ -423,6 +489,14 @@
     if noted:
         for offset in range(owners):
             tell(offset).wait()
+    else:
+        _, size, arrays = groups[rim_group]
+        for block in range(blocks):
+            pltpu.make_async_copy(
+                rims.at[block],
+                arrays[0].at[0, pl.ds(size, rims.shape[1]), :],
+                rim_sem.at[block],
+            ).wait()
 
 
 def first_pass(me, target, owners, traces, edges, mats, times, after, start, sizes, noted):
@@ -432,7 +506,7 @@
     tall = window_rows(rows)
     shapes = []
     for group, size in enumerate(sizes):
-        size += NOTE if noted and not group else 0
+        size += NOTE if noted else rim_rows(sizes[-1]) if group == len(sizes) - 2 else 0
         shapes += [jax.ShapeDtypeStruct((blocks // 2, size, LANES), jnp.bfloat16)] * owners
     flat = pl.pallas_call(
         functools.partial(first_kernel, start, sizes, noted, owners),
@@ -443,8 +517,10 @@
             pltpu.VMEM((fans, tall, 2 * LANES), jnp.bfloat16),
             pltpu.VMEM((blocks, rows, LANES), jnp.bfloat16),
             pltpu.VMEM((NOTE, LANES), jnp.bfloat16),
+            pltpu.VMEM((blocks, rim_rows(sizes[-1]), LANES), jnp.bfloat16),
             pltpu.SemaphoreType.DMA((len(sizes), blocks)),
             pltpu.SemaphoreType.DMA((owners,)),
+            pltpu.SemaphoreType.DMA((blocks,)),
         ],
         out_shape=shapes,
         cost_estimate=NO_COST,
@@ -533,6 +609,85 @@
     )(*operands)
 
 
+def last_kernel(
+    at, slot_ref, past_ref, edge_a, edge_b, mats_ref, times_ref, _, *refs
+):
+    parts, (out_ref, merged, fans_ref, held, done, in_sem, sem) = refs[:-7], refs[-7:]
+    blocks, rows = done.shape[:2]
+    before, size = past_ref.shape[1], held.shape[1]
+    begin, wait = gather_rows(slot_ref, parts, held, in_sem, 0)
+    begin()
+    origin = before - REACH
+
+    def put(row, values):
+        merged[row - origin : row - origin + values.shape[0], :] = values
+
+    unpack_edges((edge_a, edge_b), before, blocks, origin, before, put)
+    fold, base = rim_rows(size), folded_rows(before)
+    for part in range(-(-size // fold)):
+        count = min(fold, size - part * fold)
+        lane = lax.broadcasted_iota(jnp.int32, (count, LANES), 1)
+        total = jnp.zeros((count, LANES), jnp.float32)
+        for way, edge in enumerate((edge_a, edge_b)):
+            for block in range(blocks):
+                to = EDGE * (way * blocks + block)
+                top = base + block * fold
+                piece = edge[top : top + count, :].astype(jnp.float32)
+                shift = (to - 2 * EDGE * part) % LANES
+                piece = pltpu.roll(piece, shift, 1) if shift else piece
+                total = jnp.where((lane >= to) & (lane < to + EDGE), piece, total)
+        row = REACH + part * fold
+        merged[row : row + count, :] = total.astype(jnp.bfloat16)
+    wait()
+
+    def copy(block):
+        return pltpu.make_async_copy(
+            done.at[block], out_ref.at[block, pl.ds(at, rows), :], sem.at[block]
+        )
+
+    def give(pair, start, values):
+        for half in range(2):
+            done[2 * pair + half, start : start + values.shape[0], :] = values[
+                :, half * LANES : (half + 1) * LANES
+            ]
+
+    def finish(pair):
+        for half in range(2):
+            copy(2 * pair + half).start()
+
+    pieces = [
+        (0, REACH, lambda block: past_ref[block, origin:, :]),
+        (REACH, size, lambda block: held[block]),
+    ]
+    filter_window(pieces, merged, fans_ref, mats_ref, times_ref, rows, give, finish)
+    for block in range(blocks):
+        copy(block).wait()
+
+
+def last_pass(slots, past, parts, size, mats, times, out, at, rows):
+    blocks, samples, _ = out.shape
+    fans = 2 * mats.shape[1]
+    tall = window_rows(rows)
+    return pl.pallas_call(
+        functools.partial(last_kernel, at),
+        in_specs=[SMEM] + [VMEM] * 5 + [ANY] * (1 + len(parts)),
+        out_specs=ANY,
+        scratch_shapes=[
+            pltpu.VMEM((tall, LANES), jnp.bfloat16),
+            pltpu.VMEM((fans, tall, 2 * LANES), jnp.bfloat16),
+            pltpu.VMEM((blocks, size, LANES), jnp.bfloat16),
+            pltpu.VMEM((blocks, rows, LANES), jnp.float32),
+            pltpu.SemaphoreType.DMA((blocks,)),
+            pltpu.SemaphoreType.DMA((blocks,)),
+        ],
+        out_shape=jax.ShapeDtypeStruct(out.shape, jnp.float32),
+        input_output_aliases={6: 0},
+        cost_estimate=NO_COST,
+        compiler_params=PARAMS,
+        name="last_pass",
+    )(slots, *past, mats, times, out, *parts)
+
+
 def per_device(
     traces, first_trace_taps, first_time_taps, second_trace_taps, second_time_taps, dest_row
 ):
@@ -570,8 +725,7 @@
 
     sent = first([], 0, sizes[:1], True)
     arrived = [exchange(sent[0], None)]
-    if count > 1:
-        sent += first([sent[0][0]], bounds[1], sizes[1:], False)
+    sent += first([sent[0][0]], bounds[1], sizes[1:], False)
     second_mats, second_times, slots = late_weights(
         even, me, target, second_trace_taps, second_time_taps, arrived[0], sent[-1][0]
     )
@@ -585,13 +739,19 @@
             blocks, samples, past, now, second_mats, second_times, after, out, at, stop - at
         )
 
-    for step in range(count):
-        if step + 1 < count:
-            ahead = [*now[1:]] if now else []
-            ahead += [token] if token is not None else []
-            arrived.append(exchange(sent[step + 1], arrived[step], *ahead))
+    for step in range(count - 1):
+        ahead = [*now[1:]] if now else []
+        ahead += [token] if token is not None else []
+        arrived.append(exchange(sent[step + 1], arrived[step], *ahead))
         gathered, *packed = second_edges(
-            slots, picks, arrived[step], sizes[step], slots if token is None else token, blocks
+            even,
+            slots,
+            picks,
+            arrived[step],
+            sizes[step],
+            rim_rows(sizes[-1]) if step == count - 2 else 0,
+            slots if token is None else token,
+            blocks,
         )
         rims = packed[0]
         coming = (gathered, *swap_edges(packed))
@@ -599,8 +759,11 @@
             out, token = second(step - 1, rims)
             past = now
         now = coming
-    out, token = second(count - 1, slots)
-    return out
+    out, token = second(count - 2, slots)
+    at = bounds[count - 1] - REACH // 2
+    return last_pass(
+        slots, now, arrived[-1], sizes[-1], second_mats, second_times, out, at, samples - at
+    )
 
 
 def solution(mesh):

time: 135 us -> 129 us (0.956)
  waiting for transfers between devices: 33.1 us -> 28.4 us
  starting transfers between devices: 49.6 us -> 47.8 us
  Pallas kernels: 43.6 us -> 45.2 us
    ppermute x12, waiting for transfers between devices: 12.9 us -> 4.19 us  [send(): return lax.ppermute(values, 'rcv', pairs) if offset else values]
    pallas_call x4, Pallas kernels: 7.13 us -> 11.7 us  [the longest x1 5.84 us: last_pass(): pl.pallas_call(functools.partial(last_kernel, at), in_specs=[SMEM] + [VME...]
    pallas_call x4 -> x3, Pallas kernels: 17.7 us -> 13.3 us  [second_pass(): pl.pallas_call(functools.partial(second_kernel, at, past is not None), in...]
    ppermute x10 -> x8, waiting for transfers between devices: 20.2 us -> 24.2 us  [swap_edges(): got.append(lax.ppermute(edges, 'shot', pairs))]
    pallas_call x2, Pallas kernels: 14.3 us -> 15.8 us  [first_pass(): pl.pallas_call(functools.partial(first_kernel, start, sizes, noted, owner...]
    ppermute x10 -> x8, starting transfers between devices: 32.1 us -> 31.5 us  [swap_edges(): got.append(lax.ppermute(edges, 'shot', pairs))]
  transfers between devices with their start and end apart: 22 -> 20, of which waited for: 9 -> 5; matrix products, arithmetic and copies ran while one was open for 0% -> 0% of each run, Pallas kernels for 25% -> 27%
where the time goes in v5:
time: 129 us; the launch traced here: 128 us
  starting transfers between devices  47.8 us (37%)
  Pallas kernels  45.2 us (35%)
  waiting for transfers between devices  28.4 us (22%)
  local copies, waits for them, and re-layouts  5.87 us (5%)
    ppermute x8, starting transfers between devices, swap_edges(): got.append(lax.ppermute(edges, 'shot', pairs))  31.5 us
    ppermute x8, waiting for transfers between devices, swap_edges(): got.append(lax.ppermute(edges, 'shot', pairs))  24.2 us
    ppermute x12, starting transfers between devices, send(): return lax.ppermute(values, 'rcv', pairs) if offset else values  16.3 us
    pallas_call x2, Pallas kernels, first_pass(): pl.pallas_call(functools.partial(first_kernel, start, sizes, noted, owner...  15.8 us
    pallas_call x3, Pallas kernels, second_pass(): pl.pallas_call(functools.partial(second_kernel, at, past is not None), in...  13.3 us
    unnamed x18, local copies, waits for them, and re-layouts  5.87 us
    pallas_call x1, Pallas kernels, last_pass(): pl.pallas_call(functools.partial(last_kernel, at), in_specs=[SMEM] + [VME...  5.84 us
    pallas_call x3, Pallas kernels, second_edges(): pl.pallas_call(second_edges_kernel, in_specs=[SMEM, SMEM, VMEM] + [ANY] *...  5.82 us
  transfers between devices with their start and end apart: 20, of which 5 were waited for; matrix products, arithmetic and copies ran while one was open for 0% of the time, Pallas kernels for 27%

profile of v5, /device:TPU:192, one launch (start us, length us, event | category | flops | bytes accessed | tf_op | source)
XLA Modules:
  0.0 127.7 jit_solution(11646219029403852608)
XLA Ops:
  0.0 0.0 copy-start.4
  0.0 1.6 %copy-done = bf16[4,2000,128]{2,1,0:T(8,128)(2,1)S(1)} copy-done((bf16[4,2000,128]{2,1,0:T(8,128)(2,1)S(1)}, bf16[4,2000,128]{2,1,0:T(8,128)(2,1)}, u32[]{:S(2)}) %copy-start) | copy-done | bytes 2048024
  1.6 1.6 %first_edges.1 = (bf16[512,128]{1,0:T(8,128)(2,1)}, bf16[512,128]{1,0:T(8,128)(2,1)S(1)}, bf16[2,256,256]{2,1,0:T(8,128)(2,1)S(1)}) custom-call(s32[1]{0:T(128)} %bitcast.even_ref, bf16[4,2000,128]{2,1,0:T(8,128)(2,1)S(1)} %copy-done), custom_call_target="tpu_custom_call" | custom-call | flops 1 | bytes 1 | tf_op jit(solution)/shard_map/first_edges/pallas_call | solution.py:253
  3.2 0.0 collective-permute-start
  3.2 7.2 %collective-permute-start.1 = (bf16[512,128]{1,0:T(8,128)(2,1)S(1)}, bf16[512,128]{1,0:T(8,128)(2,1)S(1)}, u32[]{:S(2)}, u32[]{:S(2)}) collective-permute-start(bf16[512,128]{1,0:T(8,128)(2,1)S(1)} %get-tuple-element.61), channel_id=1, source_target_pairs={{1,2},{2,1},{3,4},{4,3},{5,6},{6,5},{7,8},{8,7},{9,10},{10,9},{11,... | collective-permute-start | bytes 393224 | tf_op jit(solution)/shard_map/ppermute | solution.py:344
  10.4 0.0 copy-start.5
  10.4 0.7 copy-done.5
  11.1 0.7 copy-done.6
  11.8 0.6 weights.1
  12.4 0.0 copy-start.2
  12.4 1.3 %copy-done.2 = bf16[4,4,256,256]{3,2,1,0:T(8,128)(2,1)} copy-done((bf16[4,4,256,256]{3,2,1,0:T(8,128)(2,1)}, bf16[4,4,256,256]{3,2,1,0:T(8,128)(2,1)S(1)}, u32[]{:S(2)}) %copy-start.2) | copy-done | bytes 2097176
  13.7 0.0 collective-permute-done.edge_a
  13.7 5.3 %collective-permute-done.1.edge_b = bf16[512,128]{1,0:T(8,128)(2,1)S(1)} collective-permute-done((bf16[512,128]{1,0:T(8,128)(2,1)S(1)}, bf16[512,128]{1,0:T(8,128)(2,1)S(1)}, u32[]{:S(2)}, u32[]{:S(2)}) %collective-permute-start.1) | collective-permute-done | bytes 131104 | tf_op jit(solution)/shard_map/ppermute | solution.py:344
  19.0 0.0 copy-done.4
  19.0 0.0 copy-done.1
  19.0 1.6 %copy-done.3 = bf16[4,4,256,256]{3,2,1,0:T(8,128)(2,1)S(1)} copy-done((bf16[4,4,256,256]{3,2,1,0:T(8,128)(2,1)S(1)}, bf16[4,4,256,256]{3,2,1,0:T(8,128)(2,1)}, u32[]{:S(2)}) %copy-start.3) | copy-done | bytes 2097176
  20.6 3.6 %first_pass.2 = (bf16[2,400,128]{2,1,0:T(8,128)(2,1)S(1)}, bf16[2,400,128]{2,1,0:T(8,128)(2,1)S(1)}, bf16[2,400,128]{2,1,0:T(8,128)(2,1)S(1)}, bf16[2,400,128]{2,1,0:T(8,128)(2,1)S(1)}) custom-call(s32[1]{0:T(128)} %bitcast.1.me_ref, s32[4]{0:T(128)S(1)} %bitcast.3, bf16[4,2000,128]{2,1,0:T(8,128)(2,1)S(1)} %copy-done.1, ...), custom_call_target="tpu_custom_call" | custom-call | flops 1 | bytes 1 | tf_op jit(solution)/shard_map/first_pass/pallas_call | solution.py:511
  24.2 1.1 collective-permute-start.4
  25.3 1.1 collective-permute-start.3
  26.3 0.5 collective-permute-start.2
  26.8 12.2 %first_pass.3 = (bf16[2,576,128]{2,1,0:T(8,128)(2,1)S(1)}, bf16[2,576,128]{2,1,0:T(8,128)(2,1)S(1)}, bf16[2,576,128]{2,1,0:T(8,128)(2,1)S(1)}, bf16[2,576,128]{2...) custom-call(s32[1]{0:T(128)} %bitcast.1.me_ref, ...), custom_call_target="tpu_custom_call" | custom-call | flops 1 | bytes 1 | tf_op jit(solution)/shard_map/first_pass/pallas_call | solution.py:511
  39.0 0.0 collective-permute-done.4.refs_3_
  39.1 1.6 %collective-permute-start.10 = (bf16[2,576,128]{2,1,0:T(8,128)(2,1)S(1)}, bf16[2,576,128]{2,1,0:T(8,128)(2,1)S(1)}, u32[]{:S(2)}, u32[]{:S(2)}) collective-permute-start(bf16[2,576,128]{2,1,0:T(8,128)(2,1)S(1)} %get-tuple-element.90), channel_id=1, source_target_pairs={{0,192},{64,0},{128,64},{192,128},{1,193},{65,1},{129,65},{193,129... | collective-permute-start | bytes 884744 | tf_op jit(solution)/shard_map/ppermute | solution.py:702
  40.7 0.0 collective-permute-done.3.refs_2_
  40.7 5.5 %collective-permute-start.9 = (bf16[2,576,128]{2,1,0:T(8,128)(2,1)S(1)}, bf16[2,576,128]{2,1,0:T(8,128)(2,1)S(1)}, u32[]{:S(2)}, u32[]{:S(2)}) collective-permute-start(bf16[2,576,128]{2,1,0:T(8,128)(2,1)S(1)} %get-tuple-element.87), channel_id=1, source_target_pairs={{0,128},{64,192},{128,0},{192,64},{1,129},{65,193},{129,1},{193,65... | collective-permute-start | bytes 884744 | tf_op jit(solution)/shard_map/ppermute | solution.py:702
  46.1 0.0 collective-permute-done.2.refs_1_
  46.2 0.0 collective-permute-start.5
  46.2 0.0 copy-done.7
  46.2 0.0 copy-done.8
  46.2 2.2 %late_weights.1 = (bf16[4,4,256,256]{3,2,1,0:T(8,128)(2,1)S(1)}, bf16[192,2048]{1,0:T(8,128)(2,1)S(1)}, s32[4]{0:T(128)S(1)}) custom-call(s32[1]{0:T(128)} %bitcast.even_ref, s32[1]{0:T(128)} %bitcast.1.me_ref, s32[4]{0:T(128)S(1)} %bitcast.5, bf16[8,16]{1,0:T(8,128)(2,1)S(1)} %copy-done.7, bf16[8,64]{1,0:T(8,128)(2,1)S(1)} %copy-done.8, ...), custom_call_target="tpu_custom_call" | custom-call | flops 1 | bytes 1 | tf_op jit(solution)/shard_map/late_weights/pallas_call | solution.py:165
  48.4 1.7 %second_edges.3 = (bf16[4,384,128]{2,1,0:T(8,128)(2,1)S(1)}, bf16[96,128]{1,0:T(8,128)(2,1)S(1)}, bf16[96,128]{1,0:T(8,128)(2,1)S(1)}) custom-call(s32[1]{0:T(128)} %bitcast.even_ref, s32[4]{0:T(128)S(1)} %get-tuple-element.69.slot_ref.refs_4_.refs_8_, bf16[2,256,256]{2,1,0:T(8,128)(2,1)S(1)} %get-tuple-element.70.picks_ref, ...), custom_call_target="tpu_custom_call" | custom-call | flops 1 | bytes 1 | tf_op jit(solution)/shard_map/second_edges/pallas_call | solution.py:321
  50.1 0.1 collective-permute-start.6
  50.2 5.9 %collective-permute-start.7 = (bf16[96,128]{1,0:T(8,128)(2,1)S(1)}, bf16[96,128]{1,0:T(8,128)(2,1)S(1)}, u32[]{:S(2)}, u32[]{:S(2)}) collective-permute-start(bf16[96,128]{1,0:T(8,128)(2,1)S(1)} %get-tuple-element.82), channel_id=1, source_target_pairs={{1,2},{2,1},{3,4},{4,3},{5,6},{6,5},{7,8},{8,7},{9,10},{10,9},{11,... | collective-permute-start | bytes 73736 | tf_op jit(solution)/shard_map/ppermute | solution.py:344
  56.1 0.0 collective-permute-done.6.refs_1_
  56.1 7.4 %collective-permute-done.7.refs_2_ = bf16[96,128]{1,0:T(8,128)(2,1)S(1)} collective-permute-done((bf16[96,128]{1,0:T(8,128)(2,1)S(1)}, bf16[96,128]{1,0:T(8,128)(2,1)S(1)}, u32[]{:S(2)}, u32[]{:S(2)}) %collective-permute-start.7) | collective-permute-done | bytes 24608 | tf_op jit(solution)/shard_map/ppermute | solution.py:344
  63.5 0.0 collective-permute-done.10.refs_3_
  63.5 4.5 %collective-permute-start.14 = (bf16[2,640,128]{2,1,0:T(8,128)(2,1)S(1)}, bf16[2,640,128]{2,1,0:T(8,128)(2,1)S(1)}, u32[]{:S(2)}, u32[]{:S(2)}) collective-permute-start(bf16[2,640,128]{2,1,0:T(8,128)(2,1)S(1)} %get-tuple-element.103), channel_id=1, source_target_pairs={{0,192},{64,0},{128,64},{192,128},{1,193},{65,1},{129,65},{193,129... | collective-permute-start | bytes 983048 | tf_op jit(solution)/shard_map/ppermute | solution.py:702
  68.0 0.0 collective-permute-done.9.refs_2_
  68.0 0.0 collective-permute-start.13
  68.0 4.2 %collective-permute-done.5.refs_1_ = bf16[2,576,128]{2,1,0:T(8,128)(2,1)S(1)} collective-permute-done((bf16[2,576,128]{2,1,0:T(8,128)(2,1)S(1)}, bf16[2,576,128]{2,1,0:T(8,128)(2,1)S(1)}, u32[]{:S(2)}, u32[]{:S(2)}) %collective-permute-start.5) | collective-permute-done | bytes 294944 | tf_op jit(solution)/shard_map/ppermute | solution.py:702
  72.1 0.0 collective-permute-start.8
  72.1 1.9 %second_edges.4 = (bf16[4,576,128]{2,1,0:T(8,128)(2,1)S(1)}, bf16[144,128]{1,0:T(8,128)(2,1)S(1)}, bf16[144,128]{1,0:T(8,128)(2,1)S(1)}) custom-call(s32[1]{0:T(128)} %bitcast.even_ref, s32[4]{0:T(128)S(1)} %get-tuple-element.69.slot_ref.refs_4_.refs_8_, bf16[2,256,256]{2,1,0:T(8,128)(2,1)S(1)} %get-tuple-element.70.picks_ref, ...), custom_call_target="tpu_custom_call" | custom-call | flops 1 | bytes 1 | tf_op jit(solution)/shard_map/second_edges/pallas_call | solution.py:321
  74.1 12.4 %collective-permute-start.12 = (bf16[144,128]{1,0:T(8,128)(2,1)S(1)}, bf16[144,128]{1,0:T(8,128)(2,1)S(1)}, u32[]{:S(2)}, u32[]{:S(2)}) collective-permute-start(bf16[144,128]{1,0:T(8,128)(2,1)S(1)} %get-tuple-element.93), channel_id=1, source_target_pairs={{1,2},{2,1},{3,4},{4,3},{5,6},{6,5},{7,8},{8,7},{9,10},{10,9},{11,... | collective-permute-start | bytes 110600 | tf_op jit(solution)/shard_map/ppermute | solution.py:344
  86.5 0.1 collective-permute-start.11
  86.6 2.9 %second_pass.3 = (f32[4,2000,128]{2,1,0:T(8,128)}, f32[8,128]{1,0:T(8,128)S(1)}) custom-call(bf16[4,384,128]{2,1,0:T(8,128)(2,1)S(1)} %get-tuple-element.94.refs_0_, bf16[96,128]{1,0:T(8,128)(2,1)S(1)} %collective-permute-done.6.refs_1_, bf16[96,128]{1,0:T(8,128)(2,1)S(1)} %collective-permute-done.7.refs_2_, ...), custom_call_target="tpu_custom_call" | custom-call | flops 1 | bytes 1 | tf_op jit(solution)/shard_map/second_pass/pallas_call | solution.py:591
  89.5 7.1 %collective-permute-done.12.refs_5_.refs_2_ = bf16[144,128]{1,0:T(8,128)(2,1)S(1)} collective-permute-done((bf16[144,128]{1,0:T(8,128)(2,1)S(1)}, bf16[144,128]{1,0:T(8,128)(2,1)S(1)}, u32[]{:S(2)}, u32[]{:S(2)}) %collective-permute-start.12) | collective-permute-done | bytes 36896 | tf_op jit(solution)/shard_map/ppermute | solution.py:344
  96.6 0.0 collective-permute-done.11.refs_4_.refs_1_
  96.7 0.0 collective-permute-done.14.refs_3_
  96.7 0.0 collective-permute-done.13.refs_2_
  96.7 0.0 collective-permute-done.8.refs_1_
  96.7 0.1 collective-permute-start.17
  96.8 0.1 collective-permute-start.18
  96.9 1.9 %collective-permute-start.19 = (bf16[2,464,128]{2,1,0:T(8,128)(2,1)S(1)}, bf16[2,464,128]{2,1,0:T(8,128)(2,1)S(1)}, u32[]{:S(2)}, u32[]{:S(2)}) collective-permute-start(bf16[2,464,128]{2,1,0:T(8,128)(2,1)S(1)} %get-tuple-element.114), channel_id=1, source_target_pairs={{0,192},{64,0},{128,64},{192,128},{1,193},{65,1},{129,65},{193,129... | collective-permute-start | bytes 712712 | tf_op jit(solution)/shard_map/ppermute | solution.py:702
  98.8 2.2 %second_edges.5 = (bf16[4,576,128]{2,1,0:T(8,128)(2,1)S(1)}, bf16[400,128]{1,0:T(8,128)(2,1)S(1)}, bf16[400,128]{1,0:T(8,128)(2,1)S(1)}) custom-call(s32[1]{0:T(128)} %bitcast.even_ref, s32[4]{0:T(128)S(1)} %get-tuple-element.69.slot_ref.refs_4_.refs_8_, bf16[2,256,256]{2,1,0:T(8,128)(2,1)S(1)} %get-tuple-element.70.picks_ref, ...), custom_call_target="tpu_custom_call" | custom-call | flops 1 | bytes 1 | tf_op jit(solution)/shard_map/second_edges/pallas_call | solution.py:321
  101.0 5.5 %collective-permute-start.16 = (bf16[400,128]{1,0:T(8,128)(2,1)S(1)}, bf16[400,128]{1,0:T(8,128)(2,1)S(1)}, u32[]{:S(2)}, u32[]{:S(2)}) collective-permute-start(bf16[400,128]{1,0:T(8,128)(2,1)S(1)} %get-tuple-element.107), channel_id=1, source_target_pairs={{1,2},{2,1},{3,4},{4,3},{5,6},{6,5},{7,8},{8,7},{9,10},{10,9},{11,... | collective-permute-start | bytes 307208 | tf_op jit(solution)/shard_map/ppermute | solution.py:344
  106.5 0.3 collective-permute-start.15
  106.8 5.2 %second_pass.4 = (f32[4,2000,128]{2,1,0:T(8,128)}, f32[8,128]{1,0:T(8,128)}) custom-call(bf16[4,384,128]{2,1,0:T(8,128)(2,1)S(1)} %get-tuple-element.94.refs_0_, bf16[96,128]{1,0:T(8,128)(2,1)S(1)} %collective-permute-done.6.refs_1_, bf16[96,128]{1,0:T(8,128)(2,1)S(1)} %collective-permute-done.7.refs_2_, ...), custom_call_target="tpu_custom_call", output_to_operand_aliasing={{0}: (9, {})} | custom-call | flops 1 | bytes 1 | tf_op jit(solution)/shard_map/second_pass/pallas_call | solution.py:591
  112.0 4.4 %collective-permute-done.16.refs_5_.edge_b = bf16[400,128]{1,0:T(8,128)(2,1)S(1)} collective-permute-done((bf16[400,128]{1,0:T(8,128)(2,1)S(1)}, bf16[400,128]{1,0:T(8,128)(2,1)S(1)}, u32[]{:S(2)}, u32[]{:S(2)}) %collective-permute-start.16) | collective-permute-done | bytes 102432 | tf_op jit(solution)/shard_map/ppermute | solution.py:344
  116.4 0.0 collective-permute-done.15.refs_4_.edge_a
  116.4 5.2 %second_pass.5 = (f32[4,2000,128]{2,1,0:T(8,128)}, f32[8,128]{1,0:T(8,128)}) custom-call(bf16[4,576,128]{2,1,0:T(8,128)(2,1)S(1)} %get-tuple-element.108.refs_3_.refs_0_, bf16[144,128]{1,0:T(8,128)(2,1)S(1)} %collective-permute-done.11.refs_4_.refs_1_, bf16[144,128]{1,0:T(8,128)(2,1)S(1)} %collective-permute-done.12.refs_5_.refs_2_, ...), custom_call_target="tpu_custom_call", output_to_operand_aliasing={{0}: (9, {})} | custom-call | flops 1 | bytes 1 | tf_op jit(solution)/shard_map/second_pass/pallas_call | solution.py:591
  121.6 0.0 collective-permute-done.17.refs_1_
  121.7 0.0 collective-permute-done.18.refs_2_
  121.7 0.0 collective-permute-done.19.refs_3_
  121.7 5.8 %last_pass.1 = f32[4,2000,128]{2,1,0:T(8,128)} custom-call(s32[4]{0:T(128)S(1)} %get-tuple-element.69.slot_ref.refs_4_.refs_8_, bf16[4,576,128]{2,1,0:T(8,128)(2,1)S(1)} %get-tuple-element.105.refs_3_.past_ref, bf16[400,128]{1,0:T(8,128)(2,1)S(1)} %collective-permute-done.15.refs_4_.edge_a, ...), custom_call_target="tpu_custom_call", output_to_operand_aliasing={{}: (6, {})} | custom-call | flops 1 | bytes 1 | tf_op jit(solution)/shard_map/last_pass/pallas_call | solution.py:671
  (6 shorter events, 0.0 us)
Async XLA Ops:
  0.0 19.0 %copy-start.4 = (s32[4,1]{0,1:T(1,128)S(1)}, s32[4,1]{0,1:T(1,128)}, u32[]{:S(2)}) copy-start(s32[4,1]{0,1:T(1,128)} %param.11) | copy-start | bytes 52
  0.0 1.6 %copy-start = (bf16[4,2000,128]{2,1,0:T(8,128)(2,1)S(1)}, bf16[4,2000,128]{2,1,0:T(8,128)(2,1)}, u32[]{:S(2)}) copy-start(bf16[4,2000,128]{2,1,0:T(8,128)(2,1)} %x_ref.5) | copy-start | bytes 6144004
  1.6 17.4 %copy-start.1 = (bf16[4,2000,128]{2,1,0:T(8,128)(2,1)S(1)}, bf16[4,2000,128]{2,1,0:T(8,128)(2,1)}, u32[]{:S(2)}) copy-start(bf16[4,2000,128]{2,1,0:T(8,128)(2,1)} %x_ref.5) | copy-start | bytes 6144004
  3.2 10.5 %collective-permute-start = (bf16[512,128]{1,0:T(8,128)(2,1)}, bf16[512,128]{1,0:T(8,128)(2,1)S(1)}, u32[]{:S(2)}, u32[]{:S(2)}) collective-permute-start(bf16[512,128]{1,0:T(8,128)(2,1)} %get-tuple-element.60), channel_id=1, source_target_pairs={{0,1},{1,0},{2,3},{3,2},{4,5},{5,4},{6,7},{7,6},{8,9},{9,8},{10,11... | collective-permute-start | bytes 393224 | tf_op jit(solution)/shard_map/ppermute | solution.py:344
  3.2 15.8 %collective-permute-start.1 = (bf16[512,128]{1,0:T(8,128)(2,1)S(1)}, bf16[512,128]{1,0:T(8,128)(2,1)S(1)}, u32[]{:S(2)}, u32[]{:S(2)}) collective-permute-start(bf16[512,128]{1,0:T(8,128)(2,1)S(1)} %get-tuple-element.61), channel_id=1, source_target_pairs={{1,2},{2,1},{3,4},{4,3},{5,6},{6,5},{7,8},{8,7},{9,10},{10,9},{11,... | collective-permute-start | bytes 393224 | tf_op jit(solution)/shard_map/ppermute | solution.py:344
  10.4 0.7 copy-start.5
  11.1 0.7 copy-start.6
  12.4 1.3 %copy-start.2 = (bf16[4,4,256,256]{3,2,1,0:T(8,128)(2,1)}, bf16[4,4,256,256]{3,2,1,0:T(8,128)(2,1)S(1)}, u32[]{:S(2)}) copy-start(bf16[4,4,256,256]{3,2,1,0:T(8,128)(2,1)S(1)} %get-tuple-element.62.mats_ref) | copy-start | bytes 6291460
  19.0 1.6 %copy-start.3 = (bf16[4,4,256,256]{3,2,1,0:T(8,128)(2,1)S(1)}, bf16[4,4,256,256]{3,2,1,0:T(8,128)(2,1)}, u32[]{:S(2)}) copy-start(bf16[4,4,256,256]{3,2,1,0:T(8,128)(2,1)} %copy-done.2) | copy-start | bytes 6291460
  20.6 25.5 %copy-start.7 = (bf16[8,16]{1,0:T(8,128)(2,1)S(1)}, bf16[8,16]{1,0:T(8,128)(2,1)}, u32[]{:S(2)}) copy-start(bf16[8,16]{1,0:T(8,128)(2,1)} %trace_ref.3) | copy-start | bytes 772
  20.6 25.5 %copy-start.8 = (bf16[8,64]{1,0:T(8,128)(2,1)S(1)}, bf16[8,64]{1,0:T(8,128)(2,1)}, u32[]{:S(2)}) copy-start(bf16[8,64]{1,0:T(8,128)(2,1)} %time_ref.3) | copy-start | bytes 3076
  24.2 14.9 %collective-permute-start.4 = (bf16[2,400,128]{2,1,0:T(8,128)(2,1)S(1)}, bf16[2,400,128]{2,1,0:T(8,128)(2,1)S(1)}, u32[]{:S(2)}, u32[]{:S(2)}) collective-permute-start(bf16[2,400,128]{2,1,0:T(8,128)(2,1)S(1)} %get-tuple-element.67), channel_id=1, source_target_pairs={{0,192},{64,0},{128,64},{192,128},{1,193},{65,1},{129,65},{193,129... | collective-permute-start | bytes 614408 | tf_op jit(solution)/shard_map/ppermute | solution.py:702
  25.3 15.4 %collective-permute-start.3 = (bf16[2,400,128]{2,1,0:T(8,128)(2,1)S(1)}, bf16[2,400,128]{2,1,0:T(8,128)(2,1)S(1)}, u32[]{:S(2)}, u32[]{:S(2)}) collective-permute-start(bf16[2,400,128]{2,1,0:T(8,128)(2,1)S(1)} %get-tuple-element.66), channel_id=1, source_target_pairs={{0,128},{64,192},{128,0},{192,64},{1,129},{65,193},{129,1},{193,65... | collective-permute-start | bytes 614408 | tf_op jit(solution)/shard_map/ppermute | solution.py:702
  26.3 19.8 %collective-permute-start.2 = (bf16[2,400,128]{2,1,0:T(8,128)(2,1)S(1)}, bf16[2,400,128]{2,1,0:T(8,128)(2,1)S(1)}, u32[]{:S(2)}, u32[]{:S(2)}) collective-permute-start(bf16[2,400,128]{2,1,0:T(8,128)(2,1)S(1)} %get-tuple-element.65), channel_id=1, source_target_pairs={{0,64},{64,128},{128,192},{192,0},{1,65},{65,129},{129,193},{193,1... | collective-permute-start | bytes 614408 | tf_op jit(solution)/shard_map/ppermute | solution.py:702
  39.1 24.4 %collective-permute-start.10 = (bf16[2,576,128]{2,1,0:T(8,128)(2,1)S(1)}, bf16[2,576,128]{2,1,0:T(8,128)(2,1)S(1)}, u32[]{:S(2)}, u32[]{:S(2)}) collective-permute-start(bf16[2,576,128]{2,1,0:T(8,128)(2,1)S(1)} %get-tuple-element.90), channel_id=1, source_target_pairs={{0,192},{64,0},{128,64},{192,128},{1,193},{65,1},{129,65},{193,129... | collective-permute-start | bytes 884744 | tf_op jit(solution)/shard_map/ppermute | solution.py:702
  40.7 27.3 %collective-permute-start.9 = (bf16[2,576,128]{2,1,0:T(8,128)(2,1)S(1)}, bf16[2,576,128]{2,1,0:T(8,128)(2,1)S(1)}, u32[]{:S(2)}, u32[]{:S(2)}) collective-permute-start(bf16[2,576,128]{2,1,0:T(8,128)(2,1)S(1)} %get-tuple-element.87), channel_id=1, source_target_pairs={{0,128},{64,192},{128,0},{192,64},{1,129},{65,193},{129,1},{193,65... | collective-permute-start | bytes 884744 | tf_op jit(solution)/shard_map/ppermute | solution.py:702
  46.2 26.0 %collective-permute-start.5 = (bf16[2,576,128]{2,1,0:T(8,128)(2,1)S(1)}, bf16[2,576,128]{2,1,0:T(8,128)(2,1)S(1)}, u32[]{:S(2)}, u32[]{:S(2)}) collective-permute-start(bf16[2,576,128]{2,1,0:T(8,128)(2,1)S(1)} %get-tuple-element.75), channel_id=1, source_target_pairs={{0,64},{64,128},{128,192},{192,0},{1,65},{65,129},{129,193},{193,1... | collective-permute-start | bytes 884744 | tf_op jit(solution)/shard_map/ppermute | solution.py:702
  50.1 6.0 %collective-permute-start.6 = (bf16[96,128]{1,0:T(8,128)(2,1)S(1)}, bf16[96,128]{1,0:T(8,128)(2,1)S(1)}, u32[]{:S(2)}, u32[]{:S(2)}) collective-permute-start(bf16[96,128]{1,0:T(8,128)(2,1)S(1)} %get-tuple-element.81), channel_id=1, source_target_pairs={{0,1},{1,0},{2,3},{3,2},{4,5},{5,4},{6,7},{7,6},{8,9},{9,8},{10,11... | collective-permute-start | bytes 73736 | tf_op jit(solution)/shard_map/ppermute | solution.py:344
  50.2 13.3 %collective-permute-start.7 = (bf16[96,128]{1,0:T(8,128)(2,1)S(1)}, bf16[96,128]{1,0:T(8,128)(2,1)S(1)}, u32[]{:S(2)}, u32[]{:S(2)}) collective-permute-start(bf16[96,128]{1,0:T(8,128)(2,1)S(1)} %get-tuple-element.82), channel_id=1, source_target_pairs={{1,2},{2,1},{3,4},{4,3},{5,6},{6,5},{7,8},{8,7},{9,10},{10,9},{11,... | collective-permute-start | bytes 73736 | tf_op jit(solution)/shard_map/ppermute | solution.py:344
  63.5 33.2 %collective-permute-start.14 = (bf16[2,640,128]{2,1,0:T(8,128)(2,1)S(1)}, bf16[2,640,128]{2,1,0:T(8,128)(2,1)S(1)}, u32[]{:S(2)}, u32[]{:S(2)}) collective-permute-start(bf16[2,640,128]{2,1,0:T(8,128)(2,1)S(1)} %get-tuple-element.103), channel_id=1, source_target_pairs={{0,192},{64,0},{128,64},{192,128},{1,193},{65,1},{129,65},{193,129... | collective-permute-start | bytes 983048 | tf_op jit(solution)/shard_map/ppermute | solution.py:702
  68.0 28.7 %collective-permute-start.13 = (bf16[2,640,128]{2,1,0:T(8,128)(2,1)S(1)}, bf16[2,640,128]{2,1,0:T(8,128)(2,1)S(1)}, u32[]{:S(2)}, u32[]{:S(2)}) collective-permute-start(bf16[2,640,128]{2,1,0:T(8,128)(2,1)S(1)} %get-tuple-element.100), channel_id=1, source_target_pairs={{0,128},{64,192},{128,0},{192,64},{1,129},{65,193},{129,1},{193,65... | collective-permute-start | bytes 983048 | tf_op jit(solution)/shard_map/ppermute | solution.py:702
  72.1 24.5 %collective-permute-start.8 = (bf16[2,640,128]{2,1,0:T(8,128)(2,1)S(1)}, bf16[2,640,128]{2,1,0:T(8,128)(2,1)S(1)}, u32[]{:S(2)}, u32[]{:S(2)}) collective-permute-start(bf16[2,640,128]{2,1,0:T(8,128)(2,1)S(1)} %get-tuple-element.83), channel_id=1, source_target_pairs={{0,64},{64,128},{128,192},{192,0},{1,65},{65,129},{129,193},{193,1... | collective-permute-start | bytes 983048 | tf_op jit(solution)/shard_map/ppermute | solution.py:702
  74.1 22.6 %collective-permute-start.12 = (bf16[144,128]{1,0:T(8,128)(2,1)S(1)}, bf16[144,128]{1,0:T(8,128)(2,1)S(1)}, u32[]{:S(2)}, u32[]{:S(2)}) collective-permute-start(bf16[144,128]{1,0:T(8,128)(2,1)S(1)} %get-tuple-element.93), channel_id=1, source_target_pairs={{1,2},{2,1},{3,4},{4,3},{5,6},{6,5},{7,8},{8,7},{9,10},{10,9},{11,... | collective-permute-start | bytes 110600 | tf_op jit(solution)/shard_map/ppermute | solution.py:344
  86.5 10.2 %collective-permute-start.11 = (bf16[144,128]{1,0:T(8,128)(2,1)S(1)}, bf16[144,128]{1,0:T(8,128)(2,1)S(1)}, u32[]{:S(2)}, u32[]{:S(2)}) collective-permute-start(bf16[144,128]{1,0:T(8,128)(2,1)S(1)} %get-tuple-element.92.refs_5_), channel_id=1, source_target_pairs={{0,1},{1,0},{2,3},{3,2},{4,5},{5,4},{6,7},{7,6},{8,9},{9,8},{10,11... | collective-permute-start | bytes 110600 | tf_op jit(solution)/shard_map/ppermute | solution.py:344
  96.7 25.0 %collective-permute-start.17 = (bf16[2,464,128]{2,1,0:T(8,128)(2,1)S(1)}, bf16[2,464,128]{2,1,0:T(8,128)(2,1)S(1)}, u32[]{:S(2)}, u32[]{:S(2)}) collective-permute-start(bf16[2,464,128]{2,1,0:T(8,128)(2,1)S(1)} %get-tuple-element.112), channel_id=1, source_target_pairs={{0,64},{64,128},{128,192},{192,0},{1,65},{65,129},{129,193},{193,1... | collective-permute-start | bytes 712712 | tf_op jit(solution)/shard_map/ppermute | solution.py:702
  96.8 24.9 %collective-permute-start.18 = (bf16[2,464,128]{2,1,0:T(8,128)(2,1)S(1)}, bf16[2,464,128]{2,1,0:T(8,128)(2,1)S(1)}, u32[]{:S(2)}, u32[]{:S(2)}) collective-permute-start(bf16[2,464,128]{2,1,0:T(8,128)(2,1)S(1)} %get-tuple-element.113), channel_id=1, source_target_pairs={{0,128},{64,192},{128,0},{192,64},{1,129},{65,193},{129,1},{193,65... | collective-permute-start | bytes 712712 | tf_op jit(solution)/shard_map/ppermute | solution.py:702
  96.9 24.8 %collective-permute-start.19 = (bf16[2,464,128]{2,1,0:T(8,128)(2,1)S(1)}, bf16[2,464,128]{2,1,0:T(8,128)(2,1)S(1)}, u32[]{:S(2)}, u32[]{:S(2)}) collective-permute-start(bf16[2,464,128]{2,1,0:T(8,128)(2,1)S(1)} %get-tuple-element.114), channel_id=1, source_target_pairs={{0,192},{64,0},{128,64},{192,128},{1,193},{65,1},{129,65},{193,129... | collective-permute-start | bytes 712712 | tf_op jit(solution)/shard_map/ppermute | solution.py:702
  101.0 15.4 %collective-permute-start.16 = (bf16[400,128]{1,0:T(8,128)(2,1)S(1)}, bf16[400,128]{1,0:T(8,128)(2,1)S(1)}, u32[]{:S(2)}, u32[]{:S(2)}) collective-permute-start(bf16[400,128]{1,0:T(8,128)(2,1)S(1)} %get-tuple-element.107), channel_id=1, source_target_pairs={{1,2},{2,1},{3,4},{4,3},{5,6},{6,5},{7,8},{8,7},{9,10},{10,9},{11,... | collective-permute-start | bytes 307208 | tf_op jit(solution)/shard_map/ppermute | solution.py:344
  106.5 9.9 %collective-permute-start.15 = (bf16[400,128]{1,0:T(8,128)(2,1)S(1)}, bf16[400,128]{1,0:T(8,128)(2,1)S(1)}, u32[]{:S(2)}, u32[]{:S(2)}) collective-permute-start(bf16[400,128]{1,0:T(8,128)(2,1)S(1)} %get-tuple-element.106.refs_8_), channel_id=1, source_target_pairs={{0,1},{1,0},{2,3},{3,2},{4,5},{5,4},{6,7},{7,6},{8,9},{9,8},{10,11... | collective-permute-start | bytes 307208 | tf_op jit(solution)/shard_map/ppermute | solution.py:344

commit v6 on v5

--- a/solution.py
+++ b/solution.py
@@ -19,7 +19,7 @@
 SMEM = pl.BlockSpec(memory_space=pltpu.SMEM)
 ANY = pl.BlockSpec(memory_space=pl.ANY)
 HBM = pl.BlockSpec(memory_space=pltpu.HBM)
-CHUNKS = (384, 576, 576)
+CHUNKS = (384, 576, 512)
 RIM_FOLD = 8
 NOTE = 16
 
@@ -59,9 +59,9 @@
     return jnp.dot(taps_ref[...], spread, preferred_element_type=jnp.float32)
 
 
-def fill_weights(even, trace_ref, time_ref, mats_ref, times_ref):
+def fill_weights(even, trace_ref, time_ref, own_ref, halo_ref, times_ref):
     fans = trace_ref.shape[0]
-    blocks = mats_ref.shape[0]
+    blocks = halo_ref.shape[0]
     trace_rows = place_taps(trace_ref, trace_ref.shape[1] // 2, -1)
     time_rows = place_taps(time_ref, 0, 1)
     for fan in range(fans):
@@ -72,6 +72,7 @@
         pieces = (jnp.where(even, right, left), jnp.where(even, left, right))
         pair, half = fan // 2, fan % 2
         cols = slice(half * LANES, (half + 1) * LANES)
+        own_ref[pair, :, cols] = own.astype(jnp.bfloat16)
         for block in range(blocks):
             before, after = EDGE * block, EDGE * (blocks - 1 - block)
             parts = []
@@ -82,18 +83,15 @@
                 if after:
                     parts.append(jnp.zeros((after, LANES), jnp.float32))
             parts.append(jnp.zeros((LANES - 2 * EDGE * blocks, LANES), jnp.float32))
-            mats_ref[block, pair, :LANES, cols] = own.astype(jnp.bfloat16)
-            mats_ref[block, pair, LANES:, cols] = jnp.concatenate(parts, axis=0).astype(
-                jnp.bfloat16
-            )
+            halo_ref[block, pair, :, cols] = jnp.concatenate(parts, axis=0).astype(jnp.bfloat16)
         taps = jnp.broadcast_to(time_rows[fan : fan + 1, :], (WIDE, SPAN))
         times_ref[:, fan * SPAN : (fan + 1) * SPAN] = pltpu.roll(
             taps, 0, 1, stride=1, stride_axis=0
         ).astype(jnp.bfloat16)
 
 
-def weights_kernel(even_ref, trace_ref, time_ref, _, mats_ref, times_ref):
-    fill_weights(even_ref[0] == 1, trace_ref, time_ref, mats_ref, times_ref)
+def weights_kernel(even_ref, trace_ref, time_ref, _, *refs):
+    fill_weights(even_ref[0] == 1, trace_ref, time_ref, *refs)
 
 
 def ranks(targets, blocks):
@@ -108,8 +106,8 @@
 
 
 def late_kernel(even_ref, me_ref, target_ref, trace_ref, time_ref, *refs):
-    parts, (_, mats_ref, times_ref, slots_ref, notes, sem) = refs[:-6], refs[-6:]
-    blocks, me = mats_ref.shape[0], me_ref[0]
+    parts, (_, own_ref, halo_ref, times_ref, slots_ref, notes, sem) = refs[:-7], refs[-7:]
+    blocks, me = halo_ref.shape[0], me_ref[0]
     slot_cap, held = parts[0].shape[0], parts[0].shape[1]
 
     def fetch(offset):
@@ -119,7 +117,7 @@
 
     for offset in range(1, len(parts)):
         fetch(offset).start()
-    fill_weights(even_ref[0] == 1, trace_ref, time_ref, mats_ref, times_ref)
+    fill_weights(even_ref[0] == 1, trace_ref, time_ref, own_ref, halo_ref, times_ref)
     slots = [jnp.int32(0)] * blocks
     lane = lax.broadcasted_iota(jnp.int32, (1, LANES), 1)
     for offset in range(len(parts)):
@@ -143,7 +141,8 @@
 
 def weight_shapes(blocks, fans):
     return [
-        jax.ShapeDtypeStruct((blocks, fans // 2, 2 * LANES, 2 * LANES), jnp.bfloat16),
+        jax.ShapeDtypeStruct((fans // 2, LANES, 2 * LANES), jnp.bfloat16),
+        jax.ShapeDtypeStruct((blocks, fans // 2, LANES, 2 * LANES), jnp.bfloat16),
         jax.ShapeDtypeStruct((WIDE, fans * SPAN), jnp.bfloat16),
     ]
 
@@ -152,7 +151,7 @@
     return pl.pallas_call(
         weights_kernel,
         in_specs=[SMEM, VMEM, VMEM, ANY],
-        out_specs=[VMEM, VMEM],
+        out_specs=[VMEM] * 3,
         out_shape=weight_shapes(blocks, trace_taps.shape[0]),
         cost_estimate=NO_COST,
         compiler_params=PARAMS,
@@ -165,7 +164,7 @@
     return pl.pallas_call(
         late_kernel,
         in_specs=[SMEM, SMEM, SMEM, VMEM, VMEM] + [ANY] * (len(arrived) + 1),
-        out_specs=[VMEM, VMEM, SMEM],
+        out_specs=[VMEM] * 3 + [SMEM],
         out_shape=weight_shapes(blocks, trace_taps.shape[0])
         + [jax.ShapeDtypeStruct((blocks,), jnp.int32)],
         scratch_shapes=[
@@ -345,9 +344,9 @@
     return got
 
 
-def filter_window(pieces, merged, fans_ref, mats_ref, times_ref, rows, give, finish):
-    fan_pairs = mats_ref.shape[1]
-    blocks = mats_ref.shape[0]
+def filter_window(pieces, merged, fans_ref, mats, times_ref, rows, give, finish):
+    own_ref, halo_ref = mats
+    blocks, fan_pairs = halo_ref.shape[:2]
     tall = fans_ref.shape[1]
     count, width = segment_plan(rows)
     covered = 0
@@ -364,9 +363,10 @@
             for at, size, load in pieces:
                 lhs = jnp.concatenate([load(block), merged[at : at + size, :]], axis=1)
                 for fan_pair in range(fan_pairs):
-                    both = jnp.dot(
-                        lhs, mats_ref[block, fan_pair], preferred_element_type=jnp.float32
-                    ).astype(jnp.bfloat16)
+                    rhs = jnp.concatenate([own_ref[fan_pair], halo_ref[block, fan_pair]], axis=0)
+                    both = jnp.dot(lhs, rhs, preferred_element_type=jnp.float32).astype(
+                        jnp.bfloat16
+                    )
                     fans_ref[2 * fan_pair, at : at + size, cols] = both[:, :LANES]
                     fans_ref[2 * fan_pair + 1, at : at + size, cols] = both[:, LANES:]
         for step in range(count):
@@ -387,8 +387,8 @@
 
 
 def first_kernel(
-    start, sizes, noted, owners, me_ref, target_ref, x_ref, edge_a, edge_b, mats_ref, times_ref,
-    *refs
+    start, sizes, noted, owners, me_ref, target_ref, x_ref, edge_a, edge_b, own_ref, halo_ref,
+    times_ref, *refs
 ):
     outs = refs[-8 - owners * len(sizes) : -8]
     merged, fans_ref, done, note, rims, sem, note_sem, rim_sem = refs[-8:]
@@ -478,7 +478,7 @@
                             ).start()
 
     pieces = [(begin - window, end - begin, lambda block: x_ref[block, begin:end, :])]
-    filter_window(pieces, merged, fans_ref, mats_ref, times_ref, rows, give, finish)
+    filter_window(pieces, merged, fans_ref, (own_ref, halo_ref), times_ref, rows, give, finish)
     for group, (at, size, arrays) in enumerate(groups):
         for block in range(blocks):
             pltpu.make_async_copy(
@@ -501,7 +501,7 @@
 
 def first_pass(me, target, owners, traces, edges, mats, times, after, start, sizes, noted):
     blocks = traces.shape[0]
-    fans = 2 * mats.shape[1]
+    fans = 2 * mats[1].shape[1]
     rows = sum(sizes)
     tall = window_rows(rows)
     shapes = []
@@ -510,7 +510,7 @@
         shapes += [jax.ShapeDtypeStruct((blocks // 2, size, LANES), jnp.bfloat16)] * owners
     flat = pl.pallas_call(
         functools.partial(first_kernel, start, sizes, noted, owners),
-        in_specs=[SMEM, SMEM] + [VMEM] * 5 + [ANY] * len(after),
+        in_specs=[SMEM, SMEM] + [VMEM] * 6 + [ANY] * len(after),
         out_specs=[ANY] * len(shapes),
         scratch_shapes=[
             pltpu.VMEM((tall, LANES), jnp.bfloat16),
@@ -526,7 +526,7 @@
         cost_estimate=NO_COST,
         compiler_params=PARAMS,
         name="first_pass",
-    )(me, target, traces, *edges, mats, times, *after)
+    )(me, target, traces, *edges, *mats, times, *after)
     return [flat[group * owners : (group + 1) * owners] for group in range(len(sizes))]
 
 
@@ -535,7 +535,7 @@
     take = lambda: refs.pop(0)
     past = [take() for _ in range(3)] if has_past else None
     now = [take() for _ in range(3)]
-    mats_ref, times_ref, _ = take(), take(), take()
+    own_ref, halo_ref, times_ref, _ = take(), take(), take(), take()
     if has_past:
         take()
     out_ref, token_ref, merged, fans_ref, done, sem = refs
@@ -573,15 +573,15 @@
         for half in range(2):
             copy(2 * pair + half).start()
 
-    filter_window(pieces, merged, fans_ref, mats_ref, times_ref, rows, give, finish)
+    filter_window(pieces, merged, fans_ref, (own_ref, halo_ref), times_ref, rows, give, finish)
     for block in range(blocks):
         copy(block).wait()
 
 
 def second_pass(blocks, samples, past, now, mats, times, after, out, at, rows):
-    fans = 2 * mats.shape[1]
+    fans = 2 * mats[1].shape[1]
     tall = window_rows(rows)
-    operands = [*(past or ()), *now, mats, times, after]
+    operands = [*(past or ()), *now, *mats, times, after]
     specs = [VMEM] * (len(operands) - 1) + [ANY]
     aliases = {}
     if out is not None:
@@ -610,7 +610,7 @@
 
 
 def last_kernel(
-    at, slot_ref, past_ref, edge_a, edge_b, mats_ref, times_ref, _, *refs
+    at, slot_ref, past_ref, edge_a, edge_b, own_ref, halo_ref, times_ref, _, *refs
 ):
     parts, (out_ref, merged, fans_ref, held, done, in_sem, sem) = refs[:-7], refs[-7:]
     blocks, rows = done.shape[:2]
@@ -659,18 +659,18 @@
         (0, REACH, lambda block: past_ref[block, origin:, :]),
         (REACH, size, lambda block: held[block]),
     ]
-    filter_window(pieces, merged, fans_ref, mats_ref, times_ref, rows, give, finish)
+    filter_window(pieces, merged, fans_ref, (own_ref, halo_ref), times_ref, rows, give, finish)
     for block in range(blocks):
         copy(block).wait()
 
 
 def last_pass(slots, past, parts, size, mats, times, out, at, rows):
     blocks, samples, _ = out.shape
-    fans = 2 * mats.shape[1]
+    fans = 2 * mats[1].shape[1]
     tall = window_rows(rows)
     return pl.pallas_call(
         functools.partial(last_kernel, at),
-        in_specs=[SMEM] + [VMEM] * 5 + [ANY] * (1 + len(parts)),
+        in_specs=[SMEM] + [VMEM] * 6 + [ANY] * (1 + len(parts)),
         out_specs=ANY,
         scratch_shapes=[
             pltpu.VMEM((tall, LANES), jnp.bfloat16),
@@ -681,11 +681,11 @@
             pltpu.SemaphoreType.DMA((blocks,)),
         ],
         out_shape=jax.ShapeDtypeStruct(out.shape, jnp.float32),
-        input_output_aliases={6: 0},
+        input_output_aliases={7: 0},
         cost_estimate=NO_COST,
         compiler_params=PARAMS,
         name="last_pass",
-    )(slots, *past, mats, times, out, *parts)
+    )(slots, *past, *mats, times, out, *parts)
 
 
 def per_device(
@@ -706,7 +706,7 @@
     sizes = [bounds[step + 1] - bounds[step] for step in range(count)]
     *packed, picks = first_edges(even, traces)
     edges = swap_edges(packed)
-    mats, times = weights(even, first_trace_taps, first_time_taps, traces, blocks)
+    *mats, times = weights(even, first_trace_taps, first_time_taps, traces, blocks)
 
     def first(after, start, sizes, noted):
         return first_pass(
@@ -726,7 +726,7 @@
     sent = first([], 0, sizes[:1], True)
     arrived = [exchange(sent[0], None)]
     sent += first([sent[0][0]], bounds[1], sizes[1:], False)
-    second_mats, second_times, slots = late_weights(
+    *second_mats, second_times, slots = late_weights(
         even, me, target, second_trace_taps, second_time_taps, arrived[0], sent[-1][0]
     )
 

time: 129 us -> 131 us (1.016)
  waiting for transfers between devices: 28.4 us -> 32.3 us
  starting transfers between devices: 47.8 us -> 45.2 us
    ppermute x8, waiting for transfers between devices: 24.2 us -> 27.8 us  [swap_edges(): got.append(lax.ppermute(edges, 'shot', pairs))]
    ppermute x8, starting transfers between devices: 31.5 us -> 29.6 us  [swap_edges(): got.append(lax.ppermute(edges, 'shot', pairs))]
    unnamed x18 -> x22, local copies, waits for them, and re-layouts: 5.87 us -> 6.62 us
  transfers between devices with their start and end apart: 20 -> 20, of which waited for: 5 -> 6; matrix products, arithmetic and copies ran while one was open for 0% -> 0% of each run, Pallas kernels for 27% -> 26%
where the time goes in v6:
time: 131 us
  Pallas kernels  46.2 us (35%)
  starting transfers between devices  45.2 us (35%)
  waiting for transfers between devices  32.3 us (25%)
  local copies, waits for them, and re-layouts  6.62 us (5%)
    ppermute x8, starting transfers between devices, swap_edges(): got.append(lax.ppermute(edges, 'shot', pairs))  29.6 us
    ppermute x8, waiting for transfers between devices, swap_edges(): got.append(lax.ppermute(edges, 'shot', pairs))  27.8 us
    pallas_call x2, Pallas kernels, first_pass(): pl.pallas_call(functools.partial(first_kernel, start, sizes, noted, owner...  16.6 us
    ppermute x12, starting transfers between devices, send(): return lax.ppermute(values, 'rcv', pairs) if offset else values  15.6 us
    pallas_call x3, Pallas kernels, second_pass(): pl.pallas_call(functools.partial(second_kernel, at, past is not None), in...  13.1 us
    unnamed x22, local copies, waits for them, and re-layouts  6.62 us
    pallas_call x1, Pallas kernels, last_pass(): pl.pallas_call(functools.partial(last_kernel, at), in_specs=[SMEM] + [VME...  6.23 us
    pallas_call x3, Pallas kernels, second_edges(): pl.pallas_call(second_edges_kernel, in_specs=[SMEM, SMEM, VMEM] + [ANY] *...  5.75 us
  transfers between devices with their start and end apart: 20, of which 6 were waited for; matrix products, arithmetic and copies ran while one was open for 0% of the time, Pallas kernels for 26%

profile of v6, /device:TPU:192, one launch (start us, length us, event | category | flops | bytes accessed | tf_op | source)
XLA Modules:
  0.0 130.8 jit_solution(3839905096222615865)
XLA Ops:
  0.0 1.6 %copy-done = bf16[4,2000,128]{2,1,0:T(8,128)(2,1)S(1)} copy-done((bf16[4,2000,128]{2,1,0:T(8,128)(2,1)S(1)}, bf16[4,2000,128]{2,1,0:T(8,128)(2,1)}, u32[]{:S(2)}) %copy-start) | copy-done | bytes 2048024
  1.6 1.7 %first_edges.1 = (bf16[512,128]{1,0:T(8,128)(2,1)}, bf16[512,128]{1,0:T(8,128)(2,1)}, bf16[2,256,256]{2,1,0:T(8,128)(2,1)S(1)}) custom-call(s32[1]{0:T(128)} %bitcast.even_ref, bf16[4,2000,128]{2,1,0:T(8,128)(2,1)S(1)} %copy-done), custom_call_target="tpu_custom_call" | custom-call | flops 1 | bytes 1 | tf_op jit(solution)/shard_map/first_edges/pallas_call | solution.py:252
  3.3 0.0 collective-permute-start
  3.3 7.2 %collective-permute-start.1 = (bf16[512,128]{1,0:T(8,128)(2,1)}, bf16[512,128]{1,0:T(8,128)(2,1)}, u32[]{:S(2)}, u32[]{:S(2)}) collective-permute-start(bf16[512,128]{1,0:T(8,128)(2,1)} %get-tuple-element.63), channel_id=1, source_target_pairs={{1,2},{2,1},{3,4},{4,3},{5,6},{6,5},{7,8},{8,7},{9,10},{10,9},{11,... | collective-permute-start | bytes 393224 | tf_op jit(solution)/shard_map/ppermute | solution.py:343
  10.5 0.0 copy-start.7
  10.5 0.7 copy-done.7
  11.2 0.7 copy-done.8
  11.9 0.6 weights.1
  12.5 0.0 copy-start.2
  12.5 0.9 copy-done.2
  13.3 0.7 copy-done.4
  14.1 0.0 collective-permute-done.edge_a
  14.1 5.4 %collective-permute-done.1.edge_b = bf16[512,128]{1,0:T(8,128)(2,1)} collective-permute-done((bf16[512,128]{1,0:T(8,128)(2,1)}, bf16[512,128]{1,0:T(8,128)(2,1)}, u32[]{:S(2)}, u32[]{:S(2)}) %collective-permute-start.1) | collective-permute-done | bytes 131104 | tf_op jit(solution)/shard_map/ppermute | solution.py:343
  19.4 0.0 copy-done.6
  19.4 0.0 copy-done.1
  19.4 1.1 copy-done.3
  20.6 0.9 copy-done.5
  21.5 4.0 %first_pass.2 = (bf16[2,400,128]{2,1,0:T(8,128)(2,1)S(1)}, bf16[2,400,128]{2,1,0:T(8,128)(2,1)S(1)}, bf16[2,400,128]{2,1,0:T(8,128)(2,1)S(1)}, bf16[2,400,128]{2,1,0:T(8,128)(2,1)S(1)}) custom-call(s32[1]{0:T(128)} %bitcast.1.me_ref, s32[4]{0:T(128)S(1)} %bitcast.3, bf16[4,2000,128]{2,1,0:T(8,128)(2,1)S(1)} %copy-done.1, ...), custom_call_target="tpu_custom_call" | custom-call | flops 1 | bytes 1 | tf_op jit(solution)/shard_map/first_pass/pallas_call | solution.py:511
  25.5 1.1 collective-permute-start.4
  26.6 1.1 collective-permute-start.3
  27.6 0.5 collective-permute-start.2
  28.1 12.7 %first_pass.3 = (bf16[2,576,128]{2,1,0:T(8,128)(2,1)S(1)}, bf16[2,576,128]{2,1,0:T(8,128)(2,1)S(1)}, bf16[2,576,128]{2,1,0:T(8,128)(2,1)S(1)}, bf16[2,576,128]{2...) custom-call(s32[1]{0:T(128)} %bitcast.1.me_ref, ...), custom_call_target="tpu_custom_call" | custom-call | flops 1 | bytes 1 | tf_op jit(solution)/shard_map/first_pass/pallas_call | solution.py:511
  40.8 0.0 collective-permute-done.4.refs_3_
  40.8 1.6 %collective-permute-start.10 = (bf16[2,576,128]{2,1,0:T(8,128)(2,1)S(1)}, bf16[2,576,128]{2,1,0:T(8,128)(2,1)S(1)}, u32[]{:S(2)}, u32[]{:S(2)}) collective-permute-start(bf16[2,576,128]{2,1,0:T(8,128)(2,1)S(1)} %get-tuple-element.93), channel_id=1, source_target_pairs={{0,192},{64,0},{128,64},{192,128},{1,193},{65,1},{129,65},{193,129... | collective-permute-start | bytes 884744 | tf_op jit(solution)/shard_map/ppermute | solution.py:702
  42.4 0.0 collective-permute-done.3.refs_2_
  42.4 3.7 %collective-permute-start.9 = (bf16[2,576,128]{2,1,0:T(8,128)(2,1)S(1)}, bf16[2,576,128]{2,1,0:T(8,128)(2,1)S(1)}, u32[]{:S(2)}, u32[]{:S(2)}) collective-permute-start(bf16[2,576,128]{2,1,0:T(8,128)(2,1)S(1)} %get-tuple-element.90), channel_id=1, source_target_pairs={{0,128},{64,192},{128,0},{192,64},{1,129},{65,193},{129,1},{193,65... | collective-permute-start | bytes 884744 | tf_op jit(solution)/shard_map/ppermute | solution.py:702
  46.1 0.1 collective-permute-done.2.refs_1_
  46.2 0.0 collective-permute-start.5
  46.2 0.0 copy-done.9
  46.2 2.2 %late_weights.1 = (bf16[4,128,256]{2,1,0:T(8,128)(2,1)S(1)}, bf16[4,4,128,256]{3,2,1,0:T(8,128)(2,1)S(1)}, bf16[192,2048]{1,0:T(8,128)(2,1)S(1)}, s32[4]{0:T(128)S(1)}) custom-call(s32[1]{0:T(128)} %bitcast.even_ref, s32[1]{0:T(128)} %bitcast.1.me_ref, s32[4]{0:T(128)S(1)} %bitcast.5, bf16[8,16]{1,0:T(8,128)(2,1)S(1)} %copy-done.9, ...), custom_call_target="tpu_custom_call" | custom-call | flops 1 | bytes 1 | tf_op jit(solution)/shard_map/late_weights/pallas_call | solution.py:164
  48.4 1.7 %second_edges.3 = (bf16[4,384,128]{2,1,0:T(8,128)(2,1)S(1)}, bf16[96,128]{1,0:T(8,128)(2,1)S(1)}, bf16[96,128]{1,0:T(8,128)(2,1)S(1)}) custom-call(s32[1]{0:T(128)} %bitcast.even_ref, s32[4]{0:T(128)S(1)} %get-tuple-element.72.slot_ref.refs_4_.refs_9_, bf16[2,256,256]{2,1,0:T(8,128)(2,1)S(1)} %get-tuple-element.73.picks_ref, ...), custom_call_target="tpu_custom_call" | custom-call | flops 1 | bytes 1 | tf_op jit(solution)/shard_map/second_edges/pallas_call | solution.py:320
  50.1 0.1 collective-permute-start.6
  50.2 5.9 %collective-permute-start.7 = (bf16[96,128]{1,0:T(8,128)(2,1)S(1)}, bf16[96,128]{1,0:T(8,128)(2,1)S(1)}, u32[]{:S(2)}, u32[]{:S(2)}) collective-permute-start(bf16[96,128]{1,0:T(8,128)(2,1)S(1)} %get-tuple-element.85), channel_id=1, source_target_pairs={{1,2},{2,1},{3,4},{4,3},{5,6},{6,5},{7,8},{8,7},{9,10},{10,9},{11,... | collective-permute-start | bytes 73736 | tf_op jit(solution)/shard_map/ppermute | solution.py:343
  56.1 0.0 collective-permute-done.6.refs_1_
  56.1 7.5 %collective-permute-done.7.refs_2_ = bf16[96,128]{1,0:T(8,128)(2,1)S(1)} collective-permute-done((bf16[96,128]{1,0:T(8,128)(2,1)S(1)}, bf16[96,128]{1,0:T(8,128)(2,1)S(1)}, u32[]{:S(2)}, u32[]{:S(2)}) %collective-permute-start.7) | collective-permute-done | bytes 24608 | tf_op jit(solution)/shard_map/ppermute | solution.py:343
  63.6 0.0 collective-permute-done.10.refs_3_
  63.6 5.6 %collective-permute-start.14 = (bf16[2,592,128]{2,1,0:T(8,128)(2,1)S(1)}, bf16[2,592,128]{2,1,0:T(8,128)(2,1)S(1)}, u32[]{:S(2)}, u32[]{:S(2)}) collective-permute-start(bf16[2,592,128]{2,1,0:T(8,128)(2,1)S(1)} %get-tuple-element.107), channel_id=1, source_target_pairs={{0,192},{64,0},{128,64},{192,128},{1,193},{65,1},{129,65},{193,129... | collective-permute-start | bytes 909320 | tf_op jit(solution)/shard_map/ppermute | solution.py:702
  69.3 0.0 collective-permute-done.9.refs_2_
  69.3 0.0 collective-permute-start.13
  69.3 4.4 %collective-permute-done.5.refs_1_ = bf16[2,576,128]{2,1,0:T(8,128)(2,1)S(1)} collective-permute-done((bf16[2,576,128]{2,1,0:T(8,128)(2,1)S(1)}, bf16[2,576,128]{2,1,0:T(8,128)(2,1)S(1)}, u32[]{:S(2)}, u32[]{:S(2)}) %collective-permute-start.5) | collective-permute-done | bytes 294944 | tf_op jit(solution)/shard_map/ppermute | solution.py:702
  73.7 0.0 collective-permute-start.8
  73.7 1.9 %second_edges.4 = (bf16[4,576,128]{2,1,0:T(8,128)(2,1)S(1)}, bf16[144,128]{1,0:T(8,128)(2,1)S(1)}, bf16[144,128]{1,0:T(8,128)(2,1)S(1)}) custom-call(s32[1]{0:T(128)} %bitcast.even_ref, s32[4]{0:T(128)S(1)} %get-tuple-element.72.slot_ref.refs_4_.refs_9_, bf16[2,256,256]{2,1,0:T(8,128)(2,1)S(1)} %get-tuple-element.73.picks_ref, ...), custom_call_target="tpu_custom_call" | custom-call | flops 1 | bytes 1 | tf_op jit(solution)/shard_map/second_edges/pallas_call | solution.py:320
  75.6 10.6 %collective-permute-start.12 = (bf16[144,128]{1,0:T(8,128)(2,1)S(1)}, bf16[144,128]{1,0:T(8,128)(2,1)S(1)}, u32[]{:S(2)}, u32[]{:S(2)}) collective-permute-start(bf16[144,128]{1,0:T(8,128)(2,1)S(1)} %get-tuple-element.96), channel_id=1, source_target_pairs={{1,2},{2,1},{3,4},{4,3},{5,6},{6,5},{7,8},{8,7},{9,10},{10,9},{11,... | collective-permute-start | bytes 110600 | tf_op jit(solution)/shard_map/ppermute | solution.py:343
  86.3 0.1 collective-permute-start.11
  86.4 2.9 %second_pass.3 = (f32[4,2000,128]{2,1,0:T(8,128)}, f32[8,128]{1,0:T(8,128)S(1)}) custom-call(bf16[4,384,128]{2,1,0:T(8,128)(2,1)S(1)} %get-tuple-element.97.refs_0_, bf16[96,128]{1,0:T(8,128)(2,1)S(1)} %collective-permute-done.6.refs_1_, bf16[96,128]{1,0:T(8,128)(2,1)S(1)} %collective-permute-done.7.refs_2_, ...), custom_call_target="tpu_custom_call" | custom-call | flops 1 | bytes 1 | tf_op jit(solution)/shard_map/second_pass/pallas_call | solution.py:591
  89.3 6.5 %collective-permute-done.12.refs_5_.refs_2_ = bf16[144,128]{1,0:T(8,128)(2,1)S(1)} collective-permute-done((bf16[144,128]{1,0:T(8,128)(2,1)S(1)}, bf16[144,128]{1,0:T(8,128)(2,1)S(1)}, u32[]{:S(2)}, u32[]{:S(2)}) %collective-permute-start.12) | collective-permute-done | bytes 36896 | tf_op jit(solution)/shard_map/ppermute | solution.py:343
  95.8 0.0 collective-permute-done.11.refs_4_.refs_1_
  95.8 0.0 collective-permute-done.14.refs_3_
  95.8 0.0 collective-permute-done.13.refs_2_
  95.8 0.0 collective-permute-done.8.refs_1_
  95.9 0.1 collective-permute-start.17
  95.9 0.1 collective-permute-start.18
  96.0 1.9 %collective-permute-start.19 = (bf16[2,528,128]{2,1,0:T(8,128)(2,1)S(1)}, bf16[2,528,128]{2,1,0:T(8,128)(2,1)S(1)}, u32[]{:S(2)}, u32[]{:S(2)}) collective-permute-start(bf16[2,528,128]{2,1,0:T(8,128)(2,1)S(1)} %get-tuple-element.118), channel_id=1, source_target_pairs={{0,192},{64,0},{128,64},{192,128},{1,193},{65,1},{129,65},{193,129... | collective-permute-start | bytes 811016 | tf_op jit(solution)/shard_map/ppermute | solution.py:702
  98.0 2.2 %second_edges.5 = (bf16[4,512,128]{2,1,0:T(8,128)(2,1)S(1)}, bf16[448,128]{1,0:T(8,128)(2,1)S(1)}, bf16[448,128]{1,0:T(8,128)(2,1)S(1)}) custom-call(s32[1]{0:T(128)} %bitcast.even_ref, s32[4]{0:T(128)S(1)} %get-tuple-element.72.slot_ref.refs_4_.refs_9_, bf16[2,256,256]{2,1,0:T(8,128)(2,1)S(1)} %get-tuple-element.73.picks_ref, ...), custom_call_target="tpu_custom_call" | custom-call | flops 1 | bytes 1 | tf_op jit(solution)/shard_map/second_edges/pallas_call | solution.py:320
  100.1 5.4 %collective-permute-start.16 = (bf16[448,128]{1,0:T(8,128)(2,1)S(1)}, bf16[448,128]{1,0:T(8,128)(2,1)S(1)}, u32[]{:S(2)}, u32[]{:S(2)}) collective-permute-start(bf16[448,128]{1,0:T(8,128)(2,1)S(1)} %get-tuple-element.111), channel_id=1, source_target_pairs={{1,2},{2,1},{3,4},{4,3},{5,6},{6,5},{7,8},{8,7},{9,10},{10,9},{11,... | collective-permute-start | bytes 344072 | tf_op jit(solution)/shard_map/ppermute | solution.py:343
  105.5 0.3 collective-permute-start.15
  105.8 5.2 %second_pass.4 = (f32[4,2000,128]{2,1,0:T(8,128)}, f32[8,128]{1,0:T(8,128)}) custom-call(bf16[4,384,128]{2,1,0:T(8,128)(2,1)S(1)} %get-tuple-element.97.refs_0_, bf16[96,128]{1,0:T(8,128)(2,1)S(1)} %collective-permute-done.6.refs_1_, bf16[96,128]{1,0:T(8,128)(2,1)S(1)} %collective-permute-done.7.refs_2_, ...), custom_call_target="tpu_custom_call", output_to_operand_aliasing={{0}: (10, {})} | custom-call | flops 1 | bytes 1 | tf_op jit(solution)/shard_map/second_pass/pallas_call | solution.py:591
  111.1 8.3 %collective-permute-done.16.refs_5_.edge_b = bf16[448,128]{1,0:T(8,128)(2,1)S(1)} collective-permute-done((bf16[448,128]{1,0:T(8,128)(2,1)S(1)}, bf16[448,128]{1,0:T(8,128)(2,1)S(1)}, u32[]{:S(2)}, u32[]{:S(2)}) %collective-permute-start.16) | collective-permute-done | bytes 114720 | tf_op jit(solution)/shard_map/ppermute | solution.py:343
  119.4 0.0 collective-permute-done.15.refs_4_.edge_a
  119.4 5.0 %second_pass.5 = (f32[4,2000,128]{2,1,0:T(8,128)}, f32[8,128]{1,0:T(8,128)}) custom-call(bf16[4,576,128]{2,1,0:T(8,128)(2,1)S(1)} %get-tuple-element.112.refs_3_.refs_0_, bf16[144,128]{1,0:T(8,128)(2,1)S(1)} %collective-permute-done.11.refs_4_.refs_1_, ...), custom_call_target="tpu_custom_call", output_to_operand_aliasing={{0}: (10, {})} | custom-call | flops 1 | bytes 1 | tf_op jit(solution)/shard_map/second_pass/pallas_call | solution.py:591
  124.4 0.0 collective-permute-done.17.refs_1_
  124.4 0.0 collective-permute-done.18.refs_2_
  124.4 0.0 collective-permute-done.19.refs_3_
  124.4 6.2 %last_pass.1 = f32[4,2000,128]{2,1,0:T(8,128)} custom-call(s32[4]{0:T(128)S(1)} %get-tuple-element.72.slot_ref.refs_4_.refs_9_, bf16[4,512,128]{2,1,0:T(8,128)(2,1)S(1)} %get-tuple-element.109.refs_3_.past_ref, bf16[448,128]{1,0:T(8,128)(2,1)S(1)} %collective-permute-done.15.refs_4_.edge_a, ...), custom_call_target="tpu_custom_call", output_to_operand_aliasing={{}: (7, {})} | custom-call | flops 1 | bytes 1 | tf_op jit(solution)/shard_map/last_pass/pallas_call | solution.py:671
  (10 shorter events, 0.0 us)
Async XLA Ops:
  0.0 19.4 %copy-start.6 = (s32[4,1]{0,1:T(1,128)S(1)}, s32[4,1]{0,1:T(1,128)}, u32[]{:S(2)}) copy-start(s32[4,1]{0,1:T(1,128)} %param.11) | copy-start | bytes 52
  0.0 1.6 %copy-start = (bf16[4,2000,128]{2,1,0:T(8,128)(2,1)S(1)}, bf16[4,2000,128]{2,1,0:T(8,128)(2,1)}, u32[]{:S(2)}) copy-start(bf16[4,2000,128]{2,1,0:T(8,128)(2,1)} %x_ref.5) | copy-start | bytes 6144004
  1.6 17.8 %copy-start.1 = (bf16[4,2000,128]{2,1,0:T(8,128)(2,1)S(1)}, bf16[4,2000,128]{2,1,0:T(8,128)(2,1)}, u32[]{:S(2)}) copy-start(bf16[4,2000,128]{2,1,0:T(8,128)(2,1)} %x_ref.5) | copy-start | bytes 6144004
  3.3 10.8 %collective-permute-start = (bf16[512,128]{1,0:T(8,128)(2,1)}, bf16[512,128]{1,0:T(8,128)(2,1)S(1)}, u32[]{:S(2)}, u32[]{:S(2)}) collective-permute-start(bf16[512,128]{1,0:T(8,128)(2,1)} %get-tuple-element.62), channel_id=1, source_target_pairs={{0,1},{1,0},{2,3},{3,2},{4,5},{5,4},{6,7},{7,6},{8,9},{9,8},{10,11... | collective-permute-start | bytes 393224 | tf_op jit(solution)/shard_map/ppermute | solution.py:343
  3.3 16.1 %collective-permute-start.1 = (bf16[512,128]{1,0:T(8,128)(2,1)}, bf16[512,128]{1,0:T(8,128)(2,1)}, u32[]{:S(2)}, u32[]{:S(2)}) collective-permute-start(bf16[512,128]{1,0:T(8,128)(2,1)} %get-tuple-element.63), channel_id=1, source_target_pairs={{1,2},{2,1},{3,4},{4,3},{5,6},{6,5},{7,8},{8,7},{9,10},{10,9},{11,... | collective-permute-start | bytes 393224 | tf_op jit(solution)/shard_map/ppermute | solution.py:343
  10.5 0.7 copy-start.7
  11.2 0.7 copy-start.8
  12.5 0.9 copy-start.2
  13.3 0.7 copy-start.4
  19.4 1.1 copy-start.3
  20.6 0.9 copy-start.5
  21.5 24.7 %copy-start.9 = (bf16[8,16]{1,0:T(8,128)(2,1)S(1)}, bf16[8,16]{1,0:T(8,128)(2,1)}, u32[]{:S(2)}) copy-start(bf16[8,16]{1,0:T(8,128)(2,1)} %trace_ref.3) | copy-start | bytes 772
  21.5 24.7 %copy-start.10 = (bf16[8,64]{1,0:T(8,128)(2,1)S(1)}, bf16[8,64]{1,0:T(8,128)(2,1)}, u32[]{:S(2)}) copy-start(bf16[8,64]{1,0:T(8,128)(2,1)} %time_ref.3) | copy-start | bytes 3076
  25.5 15.3 %collective-permute-start.4 = (bf16[2,400,128]{2,1,0:T(8,128)(2,1)S(1)}, bf16[2,400,128]{2,1,0:T(8,128)(2,1)S(1)}, u32[]{:S(2)}, u32[]{:S(2)}) collective-permute-start(bf16[2,400,128]{2,1,0:T(8,128)(2,1)S(1)} %get-tuple-element.70), channel_id=1, source_target_pairs={{0,192},{64,0},{128,64},{192,128},{1,193},{65,1},{129,65},{193,129... | collective-permute-start | bytes 614408 | tf_op jit(solution)/shard_map/ppermute | solution.py:702
  26.6 15.9 %collective-permute-start.3 = (bf16[2,400,128]{2,1,0:T(8,128)(2,1)S(1)}, bf16[2,400,128]{2,1,0:T(8,128)(2,1)S(1)}, u32[]{:S(2)}, u32[]{:S(2)}) collective-permute-start(bf16[2,400,128]{2,1,0:T(8,128)(2,1)S(1)} %get-tuple-element.69), channel_id=1, source_target_pairs={{0,128},{64,192},{128,0},{192,64},{1,129},{65,193},{129,1},{193,65... | collective-permute-start | bytes 614408 | tf_op jit(solution)/shard_map/ppermute | solution.py:702
  27.6 18.6 %collective-permute-start.2 = (bf16[2,400,128]{2,1,0:T(8,128)(2,1)S(1)}, bf16[2,400,128]{2,1,0:T(8,128)(2,1)S(1)}, u32[]{:S(2)}, u32[]{:S(2)}) collective-permute-start(bf16[2,400,128]{2,1,0:T(8,128)(2,1)S(1)} %get-tuple-element.68), channel_id=1, source_target_pairs={{0,64},{64,128},{128,192},{192,0},{1,65},{65,129},{129,193},{193,1... | collective-permute-start | bytes 614408 | tf_op jit(solution)/shard_map/ppermute | solution.py:702
  40.8 22.8 %collective-permute-start.10 = (bf16[2,576,128]{2,1,0:T(8,128)(2,1)S(1)}, bf16[2,576,128]{2,1,0:T(8,128)(2,1)S(1)}, u32[]{:S(2)}, u32[]{:S(2)}) collective-permute-start(bf16[2,576,128]{2,1,0:T(8,128)(2,1)S(1)} %get-tuple-element.93), channel_id=1, source_target_pairs={{0,192},{64,0},{128,64},{192,128},{1,193},{65,1},{129,65},{193,129... | collective-permute-start | bytes 884744 | tf_op jit(solution)/shard_map/ppermute | solution.py:702
  42.4 26.8 %collective-permute-start.9 = (bf16[2,576,128]{2,1,0:T(8,128)(2,1)S(1)}, bf16[2,576,128]{2,1,0:T(8,128)(2,1)S(1)}, u32[]{:S(2)}, u32[]{:S(2)}) collective-permute-start(bf16[2,576,128]{2,1,0:T(8,128)(2,1)S(1)} %get-tuple-element.90), channel_id=1, source_target_pairs={{0,128},{64,192},{128,0},{192,64},{1,129},{65,193},{129,1},{193,65... | collective-permute-start | bytes 884744 | tf_op jit(solution)/shard_map/ppermute | solution.py:702
  46.2 27.5 %collective-permute-start.5 = (bf16[2,576,128]{2,1,0:T(8,128)(2,1)S(1)}, bf16[2,576,128]{2,1,0:T(8,128)(2,1)S(1)}, u32[]{:S(2)}, u32[]{:S(2)}) collective-permute-start(bf16[2,576,128]{2,1,0:T(8,128)(2,1)S(1)} %get-tuple-element.78), channel_id=1, source_target_pairs={{0,64},{64,128},{128,192},{192,0},{1,65},{65,129},{129,193},{193,1... | collective-permute-start | bytes 884744 | tf_op jit(solution)/shard_map/ppermute | solution.py:702
  50.1 6.0 %collective-permute-start.6 = (bf16[96,128]{1,0:T(8,128)(2,1)S(1)}, bf16[96,128]{1,0:T(8,128)(2,1)S(1)}, u32[]{:S(2)}, u32[]{:S(2)}) collective-permute-start(bf16[96,128]{1,0:T(8,128)(2,1)S(1)} %get-tuple-element.84), channel_id=1, source_target_pairs={{0,1},{1,0},{2,3},{3,2},{4,5},{5,4},{6,7},{7,6},{8,9},{9,8},{10,11... | collective-permute-start | bytes 73736 | tf_op jit(solution)/shard_map/ppermute | solution.py:343
  50.2 13.4 %collective-permute-start.7 = (bf16[96,128]{1,0:T(8,128)(2,1)S(1)}, bf16[96,128]{1,0:T(8,128)(2,1)S(1)}, u32[]{:S(2)}, u32[]{:S(2)}) collective-permute-start(bf16[96,128]{1,0:T(8,128)(2,1)S(1)} %get-tuple-element.85), channel_id=1, source_target_pairs={{1,2},{2,1},{3,4},{4,3},{5,6},{6,5},{7,8},{8,7},{9,10},{10,9},{11,... | collective-permute-start | bytes 73736 | tf_op jit(solution)/shard_map/ppermute | solution.py:343
  63.6 32.2 %collective-permute-start.14 = (bf16[2,592,128]{2,1,0:T(8,128)(2,1)S(1)}, bf16[2,592,128]{2,1,0:T(8,128)(2,1)S(1)}, u32[]{:S(2)}, u32[]{:S(2)}) collective-permute-start(bf16[2,592,128]{2,1,0:T(8,128)(2,1)S(1)} %get-tuple-element.107), channel_id=1, source_target_pairs={{0,192},{64,0},{128,64},{192,128},{1,193},{65,1},{129,65},{193,129... | collective-permute-start | bytes 909320 | tf_op jit(solution)/shard_map/ppermute | solution.py:702
  69.3 26.6 %collective-permute-start.13 = (bf16[2,592,128]{2,1,0:T(8,128)(2,1)S(1)}, bf16[2,592,128]{2,1,0:T(8,128)(2,1)S(1)}, u32[]{:S(2)}, u32[]{:S(2)}) collective-permute-start(bf16[2,592,128]{2,1,0:T(8,128)(2,1)S(1)} %get-tuple-element.104), channel_id=1, source_target_pairs={{0,128},{64,192},{128,0},{192,64},{1,129},{65,193},{129,1},{193,65... | collective-permute-start | bytes 909320 | tf_op jit(solution)/shard_map/ppermute | solution.py:702
  73.7 22.2 %collective-permute-start.8 = (bf16[2,592,128]{2,1,0:T(8,128)(2,1)S(1)}, bf16[2,592,128]{2,1,0:T(8,128)(2,1)S(1)}, u32[]{:S(2)}, u32[]{:S(2)}) collective-permute-start(bf16[2,592,128]{2,1,0:T(8,128)(2,1)S(1)} %get-tuple-element.86), channel_id=1, source_target_pairs={{0,64},{64,128},{128,192},{192,0},{1,65},{65,129},{129,193},{193,1... | collective-permute-start | bytes 909320 | tf_op jit(solution)/shard_map/ppermute | solution.py:702
  75.6 20.2 %collective-permute-start.12 = (bf16[144,128]{1,0:T(8,128)(2,1)S(1)}, bf16[144,128]{1,0:T(8,128)(2,1)S(1)}, u32[]{:S(2)}, u32[]{:S(2)}) collective-permute-start(bf16[144,128]{1,0:T(8,128)(2,1)S(1)} %get-tuple-element.96), channel_id=1, source_target_pairs={{1,2},{2,1},{3,4},{4,3},{5,6},{6,5},{7,8},{8,7},{9,10},{10,9},{11,... | collective-permute-start | bytes 110600 | tf_op jit(solution)/shard_map/ppermute | solution.py:343
  86.3 9.6 %collective-permute-start.11 = (bf16[144,128]{1,0:T(8,128)(2,1)S(1)}, bf16[144,128]{1,0:T(8,128)(2,1)S(1)}, u32[]{:S(2)}, u32[]{:S(2)}) collective-permute-start(bf16[144,128]{1,0:T(8,128)(2,1)S(1)} %get-tuple-element.95.refs_6_), channel_id=1, source_target_pairs={{0,1},{1,0},{2,3},{3,2},{4,5},{5,4},{6,7},{7,6},{8,9},{9,8},{10,11... | collective-permute-start | bytes 110600 | tf_op jit(solution)/shard_map/ppermute | solution.py:343
  95.9 28.5 %collective-permute-start.17 = (bf16[2,528,128]{2,1,0:T(8,128)(2,1)S(1)}, bf16[2,528,128]{2,1,0:T(8,128)(2,1)S(1)}, u32[]{:S(2)}, u32[]{:S(2)}) collective-permute-start(bf16[2,528,128]{2,1,0:T(8,128)(2,1)S(1)} %get-tuple-element.116), channel_id=1, source_target_pairs={{0,64},{64,128},{128,192},{192,0},{1,65},{65,129},{129,193},{193,1... | collective-permute-start | bytes 811016 | tf_op jit(solution)/shard_map/ppermute | solution.py:702
  95.9 28.4 %collective-permute-start.18 = (bf16[2,528,128]{2,1,0:T(8,128)(2,1)S(1)}, bf16[2,528,128]{2,1,0:T(8,128)(2,1)S(1)}, u32[]{:S(2)}, u32[]{:S(2)}) collective-permute-start(bf16[2,528,128]{2,1,0:T(8,128)(2,1)S(1)} %get-tuple-element.117), channel_id=1, source_target_pairs={{0,128},{64,192},{128,0},{192,64},{1,129},{65,193},{129,1},{193,65... | collective-permute-start | bytes 811016 | tf_op jit(solution)/shard_map/ppermute | solution.py:702
  96.0 28.3 %collective-permute-start.19 = (bf16[2,528,128]{2,1,0:T(8,128)(2,1)S(1)}, bf16[2,528,128]{2,1,0:T(8,128)(2,1)S(1)}, u32[]{:S(2)}, u32[]{:S(2)}) collective-permute-start(bf16[2,528,128]{2,1,0:T(8,128)(2,1)S(1)} %get-tuple-element.118), channel_id=1, source_target_pairs={{0,192},{64,0},{128,64},{192,128},{1,193},{65,1},{129,65},{193,129... | collective-permute-start | bytes 811016 | tf_op jit(solution)/shard_map/ppermute | solution.py:702
  100.1 19.3 %collective-permute-start.16 = (bf16[448,128]{1,0:T(8,128)(2,1)S(1)}, bf16[448,128]{1,0:T(8,128)(2,1)S(1)}, u32[]{:S(2)}, u32[]{:S(2)}) collective-permute-start(bf16[448,128]{1,0:T(8,128)(2,1)S(1)} %get-tuple-element.111), channel_id=1, source_target_pairs={{1,2},{2,1},{3,4},{4,3},{5,6},{6,5},{7,8},{8,7},{9,10},{10,9},{11,... | collective-permute-start | bytes 344072 | tf_op jit(solution)/shard_map/ppermute | solution.py:343
  105.5 13.9 %collective-permute-start.15 = (bf16[448,128]{1,0:T(8,128)(2,1)S(1)}, bf16[448,128]{1,0:T(8,128)(2,1)S(1)}, u32[]{:S(2)}, u32[]{:S(2)}) collective-permute-start(bf16[448,128]{1,0:T(8,128)(2,1)S(1)} %get-tuple-element.110.refs_9_), channel_id=1, source_target_pairs={{0,1},{1,0},{2,3},{3,2},{4,5},{5,4},{6,7},{7,6},{8,9},{9,8},{10,11... | collective-permute-start | bytes 344072 | tf_op jit(solution)/shard_map/ppermute | solution.py:343

commit v7 on v5

--- a/solution.py
+++ b/solution.py
@@ -308,16 +308,19 @@
         rim_wait()
         size = rims_ref.shape[1]
         even = even_ref[0] == 1
-        for block in range(blocks):
-            first = rims_ref[block].astype(jnp.float32)
-            last = pltpu.roll(first, LANES - EDGE, 1)
-            span = slice(fold + block * size, fold + (block + 1) * size)
+        lane = lax.broadcasted_iota(jnp.int32, (size, LANES), 1)
+        low = lane % (2 * EDGE) < EDGE
+        for pair in range(blocks // 2):
+            one, two = (rims_ref[2 * pair + half].astype(jnp.float32) for half in range(2))
+            first = jnp.where(low, one, pltpu.roll(two, EDGE, 1))
+            last = jnp.where(low, pltpu.roll(one, LANES - EDGE, 1), two)
+            span = slice(fold + pair * size, fold + (pair + 1) * size)
             out_a[span, :] = jnp.where(even, last, first).astype(jnp.bfloat16)
             out_b[span, :] = jnp.where(even, first, last).astype(jnp.bfloat16)
 
 
 def second_edges(even, slots, picks, arrived, rows, rims, after, blocks):
-    packed = jax.ShapeDtypeStruct((folded_rows(rows) + blocks * rims, LANES), jnp.bfloat16)
+    packed = jax.ShapeDtypeStruct((folded_rows(rows) + blocks // 2 * rims, LANES), jnp.bfloat16)
     return pl.pallas_call(
         second_edges_kernel,
         in_specs=[SMEM, SMEM, VMEM] + [ANY] * (len(arrived) + 1),
@@ -631,9 +634,9 @@
         for way, edge in enumerate((edge_a, edge_b)):
             for block in range(blocks):
                 to = EDGE * (way * blocks + block)
-                top = base + block * fold
+                top = base + block // 2 * fold
                 piece = edge[top : top + count, :].astype(jnp.float32)
-                shift = (to - 2 * EDGE * part) % LANES
+                shift = (to - EDGE * (2 * part + block % 2)) % LANES
                 piece = pltpu.roll(piece, shift, 1) if shift else piece
                 total = jnp.where((lane >= to) & (lane < to + EDGE), piece, total)
         row = REACH + part * fold

time: 129 us -> 129 us (level)
  no operation moved by 1% of the time
where the time goes in v7:
time: 129 us; the launch traced here: 127 us
  starting transfers between devices  47.8 us (37%)
  Pallas kernels  45.1 us (35%)
  waiting for transfers between devices  28 us (22%)
  local copies, waits for them, and re-layouts  5.87 us (5%)
    ppermute x8, starting transfers between devices, swap_edges(): got.append(lax.ppermute(edges, 'shot', pairs))  31.5 us
    ppermute x8, waiting for transfers between devices, swap_edges(): got.append(lax.ppermute(edges, 'shot', pairs))  23.9 us
    ppermute x12, starting transfers between devices, send(): return lax.ppermute(values, 'rcv', pairs) if offset else values  16.3 us
    pallas_call x2, Pallas kernels, first_pass(): pl.pallas_call(functools.partial(first_kernel, start, sizes, noted, owner...  15.8 us
    pallas_call x3, Pallas kernels, second_pass(): pl.pallas_call(functools.partial(second_kernel, at, past is not None), in...  13.3 us
    unnamed x18, local copies, waits for them, and re-layouts  5.87 us
    pallas_call x3, Pallas kernels, second_edges(): pl.pallas_call(second_edges_kernel, in_specs=[SMEM, SMEM, VMEM] + [ANY] *...  5.83 us
    pallas_call x1, Pallas kernels, last_pass(): pl.pallas_call(functools.partial(last_kernel, at), in_specs=[SMEM] + [VME...  5.71 us
  transfers between devices with their start and end apart: 20, of which 5 were waited for; matrix products, arithmetic and copies ran while one was open for 0% of the time, Pallas kernels for 27%

profile of v7, /device:TPU:192, one launch (start us, length us, event | category | flops | bytes accessed | tf_op | source)
XLA Modules:
  0.0 127.2 jit_solution(16012590612717541581)
XLA Ops:
  0.0 0.0 copy-start.4
  0.0 1.6 %copy-done = bf16[4,2000,128]{2,1,0:T(8,128)(2,1)S(1)} copy-done((bf16[4,2000,128]{2,1,0:T(8,128)(2,1)S(1)}, bf16[4,2000,128]{2,1,0:T(8,128)(2,1)}, u32[]{:S(2)}) %copy-start) | copy-done | bytes 2048024
  1.6 1.6 %first_edges.1 = (bf16[512,128]{1,0:T(8,128)(2,1)}, bf16[512,128]{1,0:T(8,128)(2,1)S(1)}, bf16[2,256,256]{2,1,0:T(8,128)(2,1)S(1)}) custom-call(s32[1]{0:T(128)} %bitcast.even_ref, bf16[4,2000,128]{2,1,0:T(8,128)(2,1)S(1)} %copy-done), custom_call_target="tpu_custom_call" | custom-call | flops 1 | bytes 1 | tf_op jit(solution)/shard_map/first_edges/pallas_call | solution.py:253
  3.2 0.0 collective-permute-start
  3.2 7.2 %collective-permute-start.1 = (bf16[512,128]{1,0:T(8,128)(2,1)S(1)}, bf16[512,128]{1,0:T(8,128)(2,1)S(1)}, u32[]{:S(2)}, u32[]{:S(2)}) collective-permute-start(bf16[512,128]{1,0:T(8,128)(2,1)S(1)} %get-tuple-element.61), channel_id=1, source_target_pairs={{1,2},{2,1},{3,4},{4,3},{5,6},{6,5},{7,8},{8,7},{9,10},{10,9},{11,... | collective-permute-start | bytes 393224 | tf_op jit(solution)/shard_map/ppermute | solution.py:347
  10.4 0.0 copy-start.5
  10.4 0.7 copy-done.5
  11.1 0.7 copy-done.6
  11.8 0.6 weights.1
  12.4 0.0 copy-start.2
  12.4 1.3 %copy-done.2 = bf16[4,4,256,256]{3,2,1,0:T(8,128)(2,1)} copy-done((bf16[4,4,256,256]{3,2,1,0:T(8,128)(2,1)}, bf16[4,4,256,256]{3,2,1,0:T(8,128)(2,1)S(1)}, u32[]{:S(2)}) %copy-start.2) | copy-done | bytes 2097176
  13.7 0.0 collective-permute-done.edge_a
  13.7 5.3 %collective-permute-done.1.edge_b = bf16[512,128]{1,0:T(8,128)(2,1)S(1)} collective-permute-done((bf16[512,128]{1,0:T(8,128)(2,1)S(1)}, bf16[512,128]{1,0:T(8,128)(2,1)S(1)}, u32[]{:S(2)}, u32[]{:S(2)}) %collective-permute-start.1) | collective-permute-done | bytes 131104 | tf_op jit(solution)/shard_map/ppermute | solution.py:347
  19.0 0.0 copy-done.4
  19.0 0.0 copy-done.1
  19.0 1.6 %copy-done.3 = bf16[4,4,256,256]{3,2,1,0:T(8,128)(2,1)S(1)} copy-done((bf16[4,4,256,256]{3,2,1,0:T(8,128)(2,1)S(1)}, bf16[4,4,256,256]{3,2,1,0:T(8,128)(2,1)}, u32[]{:S(2)}) %copy-start.3) | copy-done | bytes 2097176
  20.6 3.6 %first_pass.2 = (bf16[2,400,128]{2,1,0:T(8,128)(2,1)S(1)}, bf16[2,400,128]{2,1,0:T(8,128)(2,1)S(1)}, bf16[2,400,128]{2,1,0:T(8,128)(2,1)S(1)}, bf16[2,400,128]{2,1,0:T(8,128)(2,1)S(1)}) custom-call(s32[1]{0:T(128)} %bitcast.1.me_ref, s32[4]{0:T(128)S(1)} %bitcast.3, bf16[4,2000,128]{2,1,0:T(8,128)(2,1)S(1)} %copy-done.1, ...), custom_call_target="tpu_custom_call" | custom-call | flops 1 | bytes 1 | tf_op jit(solution)/shard_map/first_pass/pallas_call | solution.py:514
  24.2 1.1 collective-permute-start.4
  25.3 1.1 collective-permute-start.3
  26.3 0.5 collective-permute-start.2
  26.8 12.2 %first_pass.3 = (bf16[2,576,128]{2,1,0:T(8,128)(2,1)S(1)}, bf16[2,576,128]{2,1,0:T(8,128)(2,1)S(1)}, bf16[2,576,128]{2,1,0:T(8,128)(2,1)S(1)}, bf16[2,576,128]{2...) custom-call(s32[1]{0:T(128)} %bitcast.1.me_ref, ...), custom_call_target="tpu_custom_call" | custom-call | flops 1 | bytes 1 | tf_op jit(solution)/shard_map/first_pass/pallas_call | solution.py:514
  39.0 0.0 collective-permute-done.4.refs_3_
  39.1 1.6 %collective-permute-start.10 = (bf16[2,576,128]{2,1,0:T(8,128)(2,1)S(1)}, bf16[2,576,128]{2,1,0:T(8,128)(2,1)S(1)}, u32[]{:S(2)}, u32[]{:S(2)}) collective-permute-start(bf16[2,576,128]{2,1,0:T(8,128)(2,1)S(1)} %get-tuple-element.90), channel_id=1, source_target_pairs={{0,192},{64,0},{128,64},{192,128},{1,193},{65,1},{129,65},{193,129... | collective-permute-start | bytes 884744 | tf_op jit(solution)/shard_map/ppermute | solution.py:705
  40.7 0.0 collective-permute-done.3.refs_2_
  40.7 5.5 %collective-permute-start.9 = (bf16[2,576,128]{2,1,0:T(8,128)(2,1)S(1)}, bf16[2,576,128]{2,1,0:T(8,128)(2,1)S(1)}, u32[]{:S(2)}, u32[]{:S(2)}) collective-permute-start(bf16[2,576,128]{2,1,0:T(8,128)(2,1)S(1)} %get-tuple-element.87), channel_id=1, source_target_pairs={{0,128},{64,192},{128,0},{192,64},{1,129},{65,193},{129,1},{193,65... | collective-permute-start | bytes 884744 | tf_op jit(solution)/shard_map/ppermute | solution.py:705
  46.2 0.0 collective-permute-done.2.refs_1_
  46.2 0.0 collective-permute-start.5
  46.2 0.0 copy-done.7
  46.2 0.0 copy-done.8
  46.2 2.2 %late_weights.1 = (bf16[4,4,256,256]{3,2,1,0:T(8,128)(2,1)S(1)}, bf16[192,2048]{1,0:T(8,128)(2,1)S(1)}, s32[4]{0:T(128)S(1)}) custom-call(s32[1]{0:T(128)} %bitcast.even_ref, s32[1]{0:T(128)} %bitcast.1.me_ref, s32[4]{0:T(128)S(1)} %bitcast.5, bf16[8,16]{1,0:T(8,128)(2,1)S(1)} %copy-done.7, bf16[8,64]{1,0:T(8,128)(2,1)S(1)} %copy-done.8, ...), custom_call_target="tpu_custom_call" | custom-call | flops 1 | bytes 1 | tf_op jit(solution)/shard_map/late_weights/pallas_call | solution.py:165
  48.5 1.7 %second_edges.3 = (bf16[4,384,128]{2,1,0:T(8,128)(2,1)S(1)}, bf16[96,128]{1,0:T(8,128)(2,1)S(1)}, bf16[96,128]{1,0:T(8,128)(2,1)S(1)}) custom-call(s32[1]{0:T(128)} %bitcast.even_ref, s32[4]{0:T(128)S(1)} %get-tuple-element.69.slot_ref.refs_4_.refs_8_, bf16[2,256,256]{2,1,0:T(8,128)(2,1)S(1)} %get-tuple-element.70.picks_ref, ...), custom_call_target="tpu_custom_call" | custom-call | flops 1 | bytes 1 | tf_op jit(solution)/shard_map/second_edges/pallas_call | solution.py:324
  50.1 0.1 collective-permute-start.6
  50.2 5.9 %collective-permute-start.7 = (bf16[96,128]{1,0:T(8,128)(2,1)S(1)}, bf16[96,128]{1,0:T(8,128)(2,1)S(1)}, u32[]{:S(2)}, u32[]{:S(2)}) collective-permute-start(bf16[96,128]{1,0:T(8,128)(2,1)S(1)} %get-tuple-element.82), channel_id=1, source_target_pairs={{1,2},{2,1},{3,4},{4,3},{5,6},{6,5},{7,8},{8,7},{9,10},{10,9},{11,... | collective-permute-start | bytes 73736 | tf_op jit(solution)/shard_map/ppermute | solution.py:347
  56.1 0.0 collective-permute-done.6.refs_1_
  56.1 7.4 %collective-permute-done.7.refs_2_ = bf16[96,128]{1,0:T(8,128)(2,1)S(1)} collective-permute-done((bf16[96,128]{1,0:T(8,128)(2,1)S(1)}, bf16[96,128]{1,0:T(8,128)(2,1)S(1)}, u32[]{:S(2)}, u32[]{:S(2)}) %collective-permute-start.7) | collective-permute-done | bytes 24608 | tf_op jit(solution)/shard_map/ppermute | solution.py:347
  63.5 0.0 collective-permute-done.10.refs_3_
  63.5 4.4 %collective-permute-start.14 = (bf16[2,640,128]{2,1,0:T(8,128)(2,1)S(1)}, bf16[2,640,128]{2,1,0:T(8,128)(2,1)S(1)}, u32[]{:S(2)}, u32[]{:S(2)}) collective-permute-start(bf16[2,640,128]{2,1,0:T(8,128)(2,1)S(1)} %get-tuple-element.103), channel_id=1, source_target_pairs={{0,192},{64,0},{128,64},{192,128},{1,193},{65,1},{129,65},{193,129... | collective-permute-start | bytes 983048 | tf_op jit(solution)/shard_map/ppermute | solution.py:705
  68.0 0.0 collective-permute-done.9.refs_2_
  68.0 0.0 collective-permute-start.13
  68.0 4.1 %collective-permute-done.5.refs_1_ = bf16[2,576,128]{2,1,0:T(8,128)(2,1)S(1)} collective-permute-done((bf16[2,576,128]{2,1,0:T(8,128)(2,1)S(1)}, bf16[2,576,128]{2,1,0:T(8,128)(2,1)S(1)}, u32[]{:S(2)}, u32[]{:S(2)}) %collective-permute-start.5) | collective-permute-done | bytes 294944 | tf_op jit(solution)/shard_map/ppermute | solution.py:705
  72.1 0.0 collective-permute-start.8
  72.1 1.9 %second_edges.4 = (bf16[4,576,128]{2,1,0:T(8,128)(2,1)S(1)}, bf16[144,128]{1,0:T(8,128)(2,1)S(1)}, bf16[144,128]{1,0:T(8,128)(2,1)S(1)}) custom-call(s32[1]{0:T(128)} %bitcast.even_ref, s32[4]{0:T(128)S(1)} %get-tuple-element.69.slot_ref.refs_4_.refs_8_, bf16[2,256,256]{2,1,0:T(8,128)(2,1)S(1)} %get-tuple-element.70.picks_ref, ...), custom_call_target="tpu_custom_call" | custom-call | flops 1 | bytes 1 | tf_op jit(solution)/shard_map/second_edges/pallas_call | solution.py:324
  74.0 12.4 %collective-permute-start.12 = (bf16[144,128]{1,0:T(8,128)(2,1)S(1)}, bf16[144,128]{1,0:T(8,128)(2,1)S(1)}, u32[]{:S(2)}, u32[]{:S(2)}) collective-permute-start(bf16[144,128]{1,0:T(8,128)(2,1)S(1)} %get-tuple-element.93), channel_id=1, source_target_pairs={{1,2},{2,1},{3,4},{4,3},{5,6},{6,5},{7,8},{8,7},{9,10},{10,9},{11,... | collective-permute-start | bytes 110600 | tf_op jit(solution)/shard_map/ppermute | solution.py:347
  86.5 0.1 collective-permute-start.11
  86.6 2.9 %second_pass.3 = (f32[4,2000,128]{2,1,0:T(8,128)}, f32[8,128]{1,0:T(8,128)S(1)}) custom-call(bf16[4,384,128]{2,1,0:T(8,128)(2,1)S(1)} %get-tuple-element.94.refs_0_, bf16[96,128]{1,0:T(8,128)(2,1)S(1)} %collective-permute-done.6.refs_1_, bf16[96,128]{1,0:T(8,128)(2,1)S(1)} %collective-permute-done.7.refs_2_, ...), custom_call_target="tpu_custom_call" | custom-call | flops 1 | bytes 1 | tf_op jit(solution)/shard_map/second_pass/pallas_call | solution.py:594
  89.5 7.1 %collective-permute-done.12.refs_5_.refs_2_ = bf16[144,128]{1,0:T(8,128)(2,1)S(1)} collective-permute-done((bf16[144,128]{1,0:T(8,128)(2,1)S(1)}, bf16[144,128]{1,0:T(8,128)(2,1)S(1)}, u32[]{:S(2)}, u32[]{:S(2)}) %collective-permute-start.12) | collective-permute-done | bytes 36896 | tf_op jit(solution)/shard_map/ppermute | solution.py:347
  96.7 0.0 collective-permute-done.11.refs_4_.refs_1_
  96.7 0.0 collective-permute-done.14.refs_3_
  96.7 0.0 collective-permute-done.13.refs_2_
  96.7 0.0 collective-permute-done.8.refs_1_
  96.7 0.1 collective-permute-start.17
  96.8 0.1 collective-permute-start.18
  96.9 1.9 %collective-permute-start.19 = (bf16[2,464,128]{2,1,0:T(8,128)(2,1)S(1)}, bf16[2,464,128]{2,1,0:T(8,128)(2,1)S(1)}, u32[]{:S(2)}, u32[]{:S(2)}) collective-permute-start(bf16[2,464,128]{2,1,0:T(8,128)(2,1)S(1)} %get-tuple-element.114), channel_id=1, source_target_pairs={{0,192},{64,0},{128,64},{192,128},{1,193},{65,1},{129,65},{193,129... | collective-permute-start | bytes 712712 | tf_op jit(solution)/shard_map/ppermute | solution.py:705
  98.8 2.2 %second_edges.5 = (bf16[4,576,128]{2,1,0:T(8,128)(2,1)S(1)}, bf16[272,128]{1,0:T(8,128)(2,1)S(1)}, bf16[272,128]{1,0:T(8,128)(2,1)S(1)}) custom-call(s32[1]{0:T(128)} %bitcast.even_ref, s32[4]{0:T(128)S(1)} %get-tuple-element.69.slot_ref.refs_4_.refs_8_, bf16[2,256,256]{2,1,0:T(8,128)(2,1)S(1)} %get-tuple-element.70.picks_ref, ...), custom_call_target="tpu_custom_call" | custom-call | flops 1 | bytes 1 | tf_op jit(solution)/shard_map/second_edges/pallas_call | solution.py:324
  101.0 5.5 %collective-permute-start.16 = (bf16[272,128]{1,0:T(8,128)(2,1)S(1)}, bf16[272,128]{1,0:T(8,128)(2,1)S(1)}, u32[]{:S(2)}, u32[]{:S(2)}) collective-permute-start(bf16[272,128]{1,0:T(8,128)(2,1)S(1)} %get-tuple-element.107), channel_id=1, source_target_pairs={{1,2},{2,1},{3,4},{4,3},{5,6},{6,5},{7,8},{8,7},{9,10},{10,9},{11,... | collective-permute-start | bytes 208904 | tf_op jit(solution)/shard_map/ppermute | solution.py:347
  106.5 0.3 collective-permute-start.15
  106.8 5.2 %second_pass.4 = (f32[4,2000,128]{2,1,0:T(8,128)}, f32[8,128]{1,0:T(8,128)}) custom-call(bf16[4,384,128]{2,1,0:T(8,128)(2,1)S(1)} %get-tuple-element.94.refs_0_, bf16[96,128]{1,0:T(8,128)(2,1)S(1)} %collective-permute-done.6.refs_1_, bf16[96,128]{1,0:T(8,128)(2,1)S(1)} %collective-permute-done.7.refs_2_, ...), custom_call_target="tpu_custom_call", output_to_operand_aliasing={{0}: (9, {})} | custom-call | flops 1 | bytes 1 | tf_op jit(solution)/shard_map/second_pass/pallas_call | solution.py:594
  112.0 4.0 %collective-permute-done.16.refs_5_.edge_b = bf16[272,128]{1,0:T(8,128)(2,1)S(1)} collective-permute-done((bf16[272,128]{1,0:T(8,128)(2,1)S(1)}, bf16[272,128]{1,0:T(8,128)(2,1)S(1)}, u32[]{:S(2)}, u32[]{:S(2)}) %collective-permute-start.16) | collective-permute-done | bytes 69664 | tf_op jit(solution)/shard_map/ppermute | solution.py:347
  116.1 0.0 collective-permute-done.15.refs_4_.edge_a
  116.1 5.2 %second_pass.5 = (f32[4,2000,128]{2,1,0:T(8,128)}, f32[8,128]{1,0:T(8,128)}) custom-call(bf16[4,576,128]{2,1,0:T(8,128)(2,1)S(1)} %get-tuple-element.108.refs_3_.refs_0_, bf16[144,128]{1,0:T(8,128)(2,1)S(1)} %collective-permute-done.11.refs_4_.refs_1_, bf16[144,128]{1,0:T(8,128)(2,1)S(1)} %collective-permute-done.12.refs_5_.refs_2_, ...), custom_call_target="tpu_custom_call", output_to_operand_aliasing={{0}: (9, {})} | custom-call | flops 1 | bytes 1 | tf_op jit(solution)/shard_map/second_pass/pallas_call | solution.py:594
  121.3 0.0 collective-permute-done.17.refs_1_
  121.3 0.0 collective-permute-done.18.refs_2_
  121.3 0.0 collective-permute-done.19.refs_3_
  121.3 5.7 %last_pass.1 = f32[4,2000,128]{2,1,0:T(8,128)} custom-call(s32[4]{0:T(128)S(1)} %get-tuple-element.69.slot_ref.refs_4_.refs_8_, bf16[4,576,128]{2,1,0:T(8,128)(2,1)S(1)} %get-tuple-element.105.refs_3_.past_ref, bf16[272,128]{1,0:T(8,128)(2,1)S(1)} %collective-permute-done.15.refs_4_.edge_a, ...), custom_call_target="tpu_custom_call", output_to_operand_aliasing={{}: (6, {})} | custom-call | flops 1 | bytes 1 | tf_op jit(solution)/shard_map/last_pass/pallas_call | solution.py:674
  (6 shorter events, 0.0 us)
Async XLA Ops:
  0.0 19.0 %copy-start.4 = (s32[4,1]{0,1:T(1,128)S(1)}, s32[4,1]{0,1:T(1,128)}, u32[]{:S(2)}) copy-start(s32[4,1]{0,1:T(1,128)} %param.11) | copy-start | bytes 52
  0.0 1.6 %copy-start = (bf16[4,2000,128]{2,1,0:T(8,128)(2,1)S(1)}, bf16[4,2000,128]{2,1,0:T(8,128)(2,1)}, u32[]{:S(2)}) copy-start(bf16[4,2000,128]{2,1,0:T(8,128)(2,1)} %x_ref.5) | copy-start | bytes 6144004
  1.6 17.4 %copy-start.1 = (bf16[4,2000,128]{2,1,0:T(8,128)(2,1)S(1)}, bf16[4,2000,128]{2,1,0:T(8,128)(2,1)}, u32[]{:S(2)}) copy-start(bf16[4,2000,128]{2,1,0:T(8,128)(2,1)} %x_ref.5) | copy-start | bytes 6144004
  3.2 10.5 %collective-permute-start = (bf16[512,128]{1,0:T(8,128)(2,1)}, bf16[512,128]{1,0:T(8,128)(2,1)S(1)}, u32[]{:S(2)}, u32[]{:S(2)}) collective-permute-start(bf16[512,128]{1,0:T(8,128)(2,1)} %get-tuple-element.60), channel_id=1, source_target_pairs={{0,1},{1,0},{2,3},{3,2},{4,5},{5,4},{6,7},{7,6},{8,9},{9,8},{10,11... | collective-permute-start | bytes 393224 | tf_op jit(solution)/shard_map/ppermute | solution.py:347
  3.2 15.8 %collective-permute-start.1 = (bf16[512,128]{1,0:T(8,128)(2,1)S(1)}, bf16[512,128]{1,0:T(8,128)(2,1)S(1)}, u32[]{:S(2)}, u32[]{:S(2)}) collective-permute-start(bf16[512,128]{1,0:T(8,128)(2,1)S(1)} %get-tuple-element.61), channel_id=1, source_target_pairs={{1,2},{2,1},{3,4},{4,3},{5,6},{6,5},{7,8},{8,7},{9,10},{10,9},{11,... | collective-permute-start | bytes 393224 | tf_op jit(solution)/shard_map/ppermute | solution.py:347
  10.4 0.7 copy-start.5
  11.1 0.7 copy-start.6
  12.4 1.3 %copy-start.2 = (bf16[4,4,256,256]{3,2,1,0:T(8,128)(2,1)}, bf16[4,4,256,256]{3,2,1,0:T(8,128)(2,1)S(1)}, u32[]{:S(2)}) copy-start(bf16[4,4,256,256]{3,2,1,0:T(8,128)(2,1)S(1)} %get-tuple-element.62.mats_ref) | copy-start | bytes 6291460
  19.0 1.6 %copy-start.3 = (bf16[4,4,256,256]{3,2,1,0:T(8,128)(2,1)S(1)}, bf16[4,4,256,256]{3,2,1,0:T(8,128)(2,1)}, u32[]{:S(2)}) copy-start(bf16[4,4,256,256]{3,2,1,0:T(8,128)(2,1)} %copy-done.2) | copy-start | bytes 6291460
  20.6 25.6 %copy-start.7 = (bf16[8,16]{1,0:T(8,128)(2,1)S(1)}, bf16[8,16]{1,0:T(8,128)(2,1)}, u32[]{:S(2)}) copy-start(bf16[8,16]{1,0:T(8,128)(2,1)} %trace_ref.3) | copy-start | bytes 772
  20.6 25.6 %copy-start.8 = (bf16[8,64]{1,0:T(8,128)(2,1)S(1)}, bf16[8,64]{1,0:T(8,128)(2,1)}, u32[]{:S(2)}) copy-start(bf16[8,64]{1,0:T(8,128)(2,1)} %time_ref.3) | copy-start | bytes 3076
  24.2 14.9 %collective-permute-start.4 = (bf16[2,400,128]{2,1,0:T(8,128)(2,1)S(1)}, bf16[2,400,128]{2,1,0:T(8,128)(2,1)S(1)}, u32[]{:S(2)}, u32[]{:S(2)}) collective-permute-start(bf16[2,400,128]{2,1,0:T(8,128)(2,1)S(1)} %get-tuple-element.67), channel_id=1, source_target_pairs={{0,192},{64,0},{128,64},{192,128},{1,193},{65,1},{129,65},{193,129... | collective-permute-start | bytes 614408 | tf_op jit(solution)/shard_map/ppermute | solution.py:705
  25.3 15.4 %collective-permute-start.3 = (bf16[2,400,128]{2,1,0:T(8,128)(2,1)S(1)}, bf16[2,400,128]{2,1,0:T(8,128)(2,1)S(1)}, u32[]{:S(2)}, u32[]{:S(2)}) collective-permute-start(bf16[2,400,128]{2,1,0:T(8,128)(2,1)S(1)} %get-tuple-element.66), channel_id=1, source_target_pairs={{0,128},{64,192},{128,0},{192,64},{1,129},{65,193},{129,1},{193,65... | collective-permute-start | bytes 614408 | tf_op jit(solution)/shard_map/ppermute | solution.py:705
  26.3 19.8 %collective-permute-start.2 = (bf16[2,400,128]{2,1,0:T(8,128)(2,1)S(1)}, bf16[2,400,128]{2,1,0:T(8,128)(2,1)S(1)}, u32[]{:S(2)}, u32[]{:S(2)}) collective-permute-start(bf16[2,400,128]{2,1,0:T(8,128)(2,1)S(1)} %get-tuple-element.65), channel_id=1, source_target_pairs={{0,64},{64,128},{128,192},{192,0},{1,65},{65,129},{129,193},{193,1... | collective-permute-start | bytes 614408 | tf_op jit(solution)/shard_map/ppermute | solution.py:705
  39.1 24.5 %collective-permute-start.10 = (bf16[2,576,128]{2,1,0:T(8,128)(2,1)S(1)}, bf16[2,576,128]{2,1,0:T(8,128)(2,1)S(1)}, u32[]{:S(2)}, u32[]{:S(2)}) collective-permute-start(bf16[2,576,128]{2,1,0:T(8,128)(2,1)S(1)} %get-tuple-element.90), channel_id=1, source_target_pairs={{0,192},{64,0},{128,64},{192,128},{1,193},{65,1},{129,65},{193,129... | collective-permute-start | bytes 884744 | tf_op jit(solution)/shard_map/ppermute | solution.py:705
  40.7 27.3 %collective-permute-start.9 = (bf16[2,576,128]{2,1,0:T(8,128)(2,1)S(1)}, bf16[2,576,128]{2,1,0:T(8,128)(2,1)S(1)}, u32[]{:S(2)}, u32[]{:S(2)}) collective-permute-start(bf16[2,576,128]{2,1,0:T(8,128)(2,1)S(1)} %get-tuple-element.87), channel_id=1, source_target_pairs={{0,128},{64,192},{128,0},{192,64},{1,129},{65,193},{129,1},{193,65... | collective-permute-start | bytes 884744 | tf_op jit(solution)/shard_map/ppermute | solution.py:705
  46.2 25.9 %collective-permute-start.5 = (bf16[2,576,128]{2,1,0:T(8,128)(2,1)S(1)}, bf16[2,576,128]{2,1,0:T(8,128)(2,1)S(1)}, u32[]{:S(2)}, u32[]{:S(2)}) collective-permute-start(bf16[2,576,128]{2,1,0:T(8,128)(2,1)S(1)} %get-tuple-element.75), channel_id=1, source_target_pairs={{0,64},{64,128},{128,192},{192,0},{1,65},{65,129},{129,193},{193,1... | collective-permute-start | bytes 884744 | tf_op jit(solution)/shard_map/ppermute | solution.py:705
  50.1 6.0 %collective-permute-start.6 = (bf16[96,128]{1,0:T(8,128)(2,1)S(1)}, bf16[96,128]{1,0:T(8,128)(2,1)S(1)}, u32[]{:S(2)}, u32[]{:S(2)}) collective-permute-start(bf16[96,128]{1,0:T(8,128)(2,1)S(1)} %get-tuple-element.81), channel_id=1, source_target_pairs={{0,1},{1,0},{2,3},{3,2},{4,5},{5,4},{6,7},{7,6},{8,9},{9,8},{10,11... | collective-permute-start | bytes 73736 | tf_op jit(solution)/shard_map/ppermute | solution.py:347
  50.2 13.3 %collective-permute-start.7 = (bf16[96,128]{1,0:T(8,128)(2,1)S(1)}, bf16[96,128]{1,0:T(8,128)(2,1)S(1)}, u32[]{:S(2)}, u32[]{:S(2)}) collective-permute-start(bf16[96,128]{1,0:T(8,128)(2,1)S(1)} %get-tuple-element.82), channel_id=1, source_target_pairs={{1,2},{2,1},{3,4},{4,3},{5,6},{6,5},{7,8},{8,7},{9,10},{10,9},{11,... | collective-permute-start | bytes 73736 | tf_op jit(solution)/shard_map/ppermute | solution.py:347
  63.5 33.1 %collective-permute-start.14 = (bf16[2,640,128]{2,1,0:T(8,128)(2,1)S(1)}, bf16[2,640,128]{2,1,0:T(8,128)(2,1)S(1)}, u32[]{:S(2)}, u32[]{:S(2)}) collective-permute-start(bf16[2,640,128]{2,1,0:T(8,128)(2,1)S(1)} %get-tuple-element.103), channel_id=1, source_target_pairs={{0,192},{64,0},{128,64},{192,128},{1,193},{65,1},{129,65},{193,129... | collective-permute-start | bytes 983048 | tf_op jit(solution)/shard_map/ppermute | solution.py:705
  68.0 28.7 %collective-permute-start.13 = (bf16[2,640,128]{2,1,0:T(8,128)(2,1)S(1)}, bf16[2,640,128]{2,1,0:T(8,128)(2,1)S(1)}, u32[]{:S(2)}, u32[]{:S(2)}) collective-permute-start(bf16[2,640,128]{2,1,0:T(8,128)(2,1)S(1)} %get-tuple-element.100), channel_id=1, source_target_pairs={{0,128},{64,192},{128,0},{192,64},{1,129},{65,193},{129,1},{193,65... | collective-permute-start | bytes 983048 | tf_op jit(solution)/shard_map/ppermute | solution.py:705
  72.1 24.6 %collective-permute-start.8 = (bf16[2,640,128]{2,1,0:T(8,128)(2,1)S(1)}, bf16[2,640,128]{2,1,0:T(8,128)(2,1)S(1)}, u32[]{:S(2)}, u32[]{:S(2)}) collective-permute-start(bf16[2,640,128]{2,1,0:T(8,128)(2,1)S(1)} %get-tuple-element.83), channel_id=1, source_target_pairs={{0,64},{64,128},{128,192},{192,0},{1,65},{65,129},{129,193},{193,1... | collective-permute-start | bytes 983048 | tf_op jit(solution)/shard_map/ppermute | solution.py:705
  74.0 22.6 %collective-permute-start.12 = (bf16[144,128]{1,0:T(8,128)(2,1)S(1)}, bf16[144,128]{1,0:T(8,128)(2,1)S(1)}, u32[]{:S(2)}, u32[]{:S(2)}) collective-permute-start(bf16[144,128]{1,0:T(8,128)(2,1)S(1)} %get-tuple-element.93), channel_id=1, source_target_pairs={{1,2},{2,1},{3,4},{4,3},{5,6},{6,5},{7,8},{8,7},{9,10},{10,9},{11,... | collective-permute-start | bytes 110600 | tf_op jit(solution)/shard_map/ppermute | solution.py:347
  86.5 10.2 %collective-permute-start.11 = (bf16[144,128]{1,0:T(8,128)(2,1)S(1)}, bf16[144,128]{1,0:T(8,128)(2,1)S(1)}, u32[]{:S(2)}, u32[]{:S(2)}) collective-permute-start(bf16[144,128]{1,0:T(8,128)(2,1)S(1)} %get-tuple-element.92.refs_5_), channel_id=1, source_target_pairs={{0,1},{1,0},{2,3},{3,2},{4,5},{5,4},{6,7},{7,6},{8,9},{9,8},{10,11... | collective-permute-start | bytes 110600 | tf_op jit(solution)/shard_map/ppermute | solution.py:347
  96.7 24.6 %collective-permute-start.17 = (bf16[2,464,128]{2,1,0:T(8,128)(2,1)S(1)}, bf16[2,464,128]{2,1,0:T(8,128)(2,1)S(1)}, u32[]{:S(2)}, u32[]{:S(2)}) collective-permute-start(bf16[2,464,128]{2,1,0:T(8,128)(2,1)S(1)} %get-tuple-element.112), channel_id=1, source_target_pairs={{0,64},{64,128},{128,192},{192,0},{1,65},{65,129},{129,193},{193,1... | collective-permute-start | bytes 712712 | tf_op jit(solution)/shard_map/ppermute | solution.py:705
  96.8 24.5 %collective-permute-start.18 = (bf16[2,464,128]{2,1,0:T(8,128)(2,1)S(1)}, bf16[2,464,128]{2,1,0:T(8,128)(2,1)S(1)}, u32[]{:S(2)}, u32[]{:S(2)}) collective-permute-start(bf16[2,464,128]{2,1,0:T(8,128)(2,1)S(1)} %get-tuple-element.113), channel_id=1, source_target_pairs={{0,128},{64,192},{128,0},{192,64},{1,129},{65,193},{129,1},{193,65... | collective-permute-start | bytes 712712 | tf_op jit(solution)/shard_map/ppermute | solution.py:705
  96.9 24.5 %collective-permute-start.19 = (bf16[2,464,128]{2,1,0:T(8,128)(2,1)S(1)}, bf16[2,464,128]{2,1,0:T(8,128)(2,1)S(1)}, u32[]{:S(2)}, u32[]{:S(2)}) collective-permute-start(bf16[2,464,128]{2,1,0:T(8,128)(2,1)S(1)} %get-tuple-element.114), channel_id=1, source_target_pairs={{0,192},{64,0},{128,64},{192,128},{1,193},{65,1},{129,65},{193,129... | collective-permute-start | bytes 712712 | tf_op jit(solution)/shard_map/ppermute | solution.py:705
  101.0 15.0 %collective-permute-start.16 = (bf16[272,128]{1,0:T(8,128)(2,1)S(1)}, bf16[272,128]{1,0:T(8,128)(2,1)S(1)}, u32[]{:S(2)}, u32[]{:S(2)}) collective-permute-start(bf16[272,128]{1,0:T(8,128)(2,1)S(1)} %get-tuple-element.107), channel_id=1, source_target_pairs={{1,2},{2,1},{3,4},{4,3},{5,6},{6,5},{7,8},{8,7},{9,10},{10,9},{11,... | collective-permute-start | bytes 208904 | tf_op jit(solution)/shard_map/ppermute | solution.py:347
  106.5 9.6 %collective-permute-start.15 = (bf16[272,128]{1,0:T(8,128)(2,1)S(1)}, bf16[272,128]{1,0:T(8,128)(2,1)S(1)}, u32[]{:S(2)}, u32[]{:S(2)}) collective-permute-start(bf16[272,128]{1,0:T(8,128)(2,1)S(1)} %get-tuple-element.106.refs_8_), channel_id=1, source_target_pairs={{0,1},{1,0},{2,3},{3,2},{4,5},{5,4},{6,7},{7,6},{8,9},{9,8},{10,11... | collective-permute-start | bytes 208904 | tf_op jit(solution)/shard_map/ppermute | solution.py:347

commit v8 on v7

--- a/solution.py
+++ b/solution.py
@@ -746,6 +746,10 @@
         ahead = [*now[1:]] if now else []
         ahead += [token] if token is not None else []
         arrived.append(exchange(sent[step + 1], arrived[step], *ahead))
+        early = 0 < step == count - 2
+        if early:
+            out, token = second(step - 1, slots)
+            past = now
         gathered, *packed = second_edges(
             even,
             slots,
@@ -758,7 +762,7 @@
         )
         rims = packed[0]
         coming = (gathered, *swap_edges(packed))
-        if step:
+        if step and not early:
             out, token = second(step - 1, rims)
             past = now
         now = coming

time: 129 us -> 133 us (1.031)
  waiting for transfers between devices: 28 us -> 33.8 us
  starting transfers between devices: 47.8 us -> 46 us
    ppermute x8, starting transfers between devices: 31.5 us -> 27.3 us  [swap_edges(): got.append(lax.ppermute(edges, 'shot', pairs))]
    ppermute x8, waiting for transfers between devices: 23.9 us -> 27.4 us  [swap_edges(): got.append(lax.ppermute(edges, 'shot', pairs))]
    ppermute x12, starting transfers between devices: 16.3 us -> 18.8 us  [send(): return lax.ppermute(values, 'rcv', pairs) if offset else values]
    ppermute x12, waiting for transfers between devices: 4.16 us -> 6.35 us  [send(): return lax.ppermute(values, 'rcv', pairs) if offset else values]
  transfers between devices with their start and end apart: 20 -> 20, of which waited for: 5 -> 7; matrix products, arithmetic and copies ran while one was open for 0% -> 0% of each run, Pallas kernels for 27% -> 26%
where the time goes in v8:
time: 133 us; the launch traced here: 131 us
  starting transfers between devices  46 us (35%)
  Pallas kernels  45.1 us (34%)
  waiting for transfers between devices  33.8 us (25%)
  local copies, waits for them, and re-layouts  5.87 us (4%)
    ppermute x8, waiting for transfers between devices, swap_edges(): got.append(lax.ppermute(edges, 'shot', pairs))  27.4 us
    ppermute x8, starting transfers between devices, swap_edges(): got.append(lax.ppermute(edges, 'shot', pairs))  27.3 us
    ppermute x12, starting transfers between devices, send(): return lax.ppermute(values, 'rcv', pairs) if offset else values  18.8 us
    pallas_call x2, Pallas kernels, first_pass(): pl.pallas_call(functools.partial(first_kernel, start, sizes, noted, owner...  15.8 us
    pallas_call x3, Pallas kernels, second_pass(): pl.pallas_call(functools.partial(second_kernel, at, past is not None), in...  13.3 us
    ppermute x12, waiting for transfers between devices, send(): return lax.ppermute(values, 'rcv', pairs) if offset else values  6.35 us
    unnamed x18, local copies, waits for them, and re-layouts  5.87 us
    pallas_call x3, Pallas kernels, second_edges(): pl.pallas_call(second_edges_kernel, in_specs=[SMEM, SMEM, VMEM] + [ANY] *...  5.83 us
  transfers between devices with their start and end apart: 20, of which 7 were waited for; matrix products, arithmetic and copies ran while one was open for 0% of the time, Pallas kernels for 26%

profile of v8, /device:TPU:192, one launch (start us, length us, event | category | flops | bytes accessed | tf_op | source)
XLA Modules:
  0.0 131.2 jit_solution(8942549055529888300)
XLA Ops:
  0.0 0.0 copy-start.4
  0.0 1.6 %copy-done = bf16[4,2000,128]{2,1,0:T(8,128)(2,1)S(1)} copy-done((bf16[4,2000,128]{2,1,0:T(8,128)(2,1)S(1)}, bf16[4,2000,128]{2,1,0:T(8,128)(2,1)}, u32[]{:S(2)}) %copy-start) | copy-done | bytes 2048024
  1.6 1.6 %first_edges.1 = (bf16[512,128]{1,0:T(8,128)(2,1)}, bf16[512,128]{1,0:T(8,128)(2,1)S(1)}, bf16[2,256,256]{2,1,0:T(8,128)(2,1)S(1)}) custom-call(s32[1]{0:T(128)} %bitcast.even_ref, bf16[4,2000,128]{2,1,0:T(8,128)(2,1)S(1)} %copy-done), custom_call_target="tpu_custom_call" | custom-call | flops 1 | bytes 1 | tf_op jit(solution)/shard_map/first_edges/pallas_call | solution.py:253
  3.2 0.0 collective-permute-start
  3.2 7.2 %collective-permute-start.1 = (bf16[512,128]{1,0:T(8,128)(2,1)S(1)}, bf16[512,128]{1,0:T(8,128)(2,1)S(1)}, u32[]{:S(2)}, u32[]{:S(2)}) collective-permute-start(bf16[512,128]{1,0:T(8,128)(2,1)S(1)} %get-tuple-element.62), channel_id=1, source_target_pairs={{1,2},{2,1},{3,4},{4,3},{5,6},{6,5},{7,8},{8,7},{9,10},{10,9},{11,... | collective-permute-start | bytes 393224 | tf_op jit(solution)/shard_map/ppermute | solution.py:347
  10.4 0.0 copy-start.5
  10.4 0.7 copy-done.5
  11.1 0.7 copy-done.6
  11.8 0.6 weights.1
  12.4 0.0 copy-start.2
  12.4 1.3 copy-done.2
  13.7 0.0 collective-permute-done.edge_a
  13.7 5.3 %collective-permute-done.1.edge_b = bf16[512,128]{1,0:T(8,128)(2,1)S(1)} collective-permute-done((bf16[512,128]{1,0:T(8,128)(2,1)S(1)}, bf16[512,128]{1,0:T(8,128)(2,1)S(1)}, u32[]{:S(2)}, u32[]{:S(2)}) %collective-permute-start.1) | collective-permute-done | bytes 131104 | tf_op jit(solution)/shard_map/ppermute | solution.py:347
  19.0 0.0 copy-done.4
  19.0 0.0 copy-done.1
  19.0 1.6 %copy-done.3 = bf16[4,4,256,256]{3,2,1,0:T(8,128)(2,1)S(1)} copy-done((bf16[4,4,256,256]{3,2,1,0:T(8,128)(2,1)S(1)}, bf16[4,4,256,256]{3,2,1,0:T(8,128)(2,1)}, u32[]{:S(2)}) %copy-start.3) | copy-done | bytes 2097176
  20.6 3.6 %first_pass.2 = (bf16[2,400,128]{2,1,0:T(8,128)(2,1)S(1)}, bf16[2,400,128]{2,1,0:T(8,128)(2,1)S(1)}, bf16[2,400,128]{2,1,0:T(8,128)(2,1)S(1)}, bf16[2,400,128]{2,1,0:T(8,128)(2,1)S(1)}) custom-call(s32[1]{0:T(128)} %bitcast.1.me_ref, s32[4]{0:T(128)S(1)} %bitcast.3, bf16[4,2000,128]{2,1,0:T(8,128)(2,1)S(1)} %copy-done.1, ...), custom_call_target="tpu_custom_call" | custom-call | flops 1 | bytes 1 | tf_op jit(solution)/shard_map/first_pass/pallas_call | solution.py:514
  24.2 0.1 collective-permute-start.2
  24.3 2.5 %collective-permute-start.3 = (bf16[2,400,128]{2,1,0:T(8,128)(2,1)S(1)}, bf16[2,400,128]{2,1,0:T(8,128)(2,1)S(1)}, u32[]{:S(2)}, u32[]{:S(2)}) collective-permute-start(bf16[2,400,128]{2,1,0:T(8,128)(2,1)S(1)} %get-tuple-element.67), channel_id=1, source_target_pairs={{0,128},{64,192},{128,0},{192,64},{1,129},{65,193},{129,1},{193,65... | collective-permute-start | bytes 614408 | tf_op jit(solution)/shard_map/ppermute | solution.py:705
  26.7 0.6 collective-permute-start.4
  27.3 12.2 %first_pass.3 = (bf16[2,576,128]{2,1,0:T(8,128)(2,1)S(1)}, bf16[2,576,128]{2,1,0:T(8,128)(2,1)S(1)}, bf16[2,576,128]{2,1,0:T(8,128)(2,1)S(1)}, bf16[2,576,128]{2...) custom-call(s32[1]{0:T(128)} %bitcast.1.me_ref, ...), custom_call_target="tpu_custom_call" | custom-call | flops 1 | bytes 1 | tf_op jit(solution)/shard_map/first_pass/pallas_call | solution.py:514
  39.5 0.0 collective-permute-done.2.refs_1_
  39.6 1.5 %collective-permute-start.5 = (bf16[2,576,128]{2,1,0:T(8,128)(2,1)S(1)}, bf16[2,576,128]{2,1,0:T(8,128)(2,1)S(1)}, u32[]{:S(2)}, u32[]{:S(2)}) collective-permute-start(bf16[2,576,128]{2,1,0:T(8,128)(2,1)S(1)} %get-tuple-element.76), channel_id=1, source_target_pairs={{0,64},{64,128},{128,192},{192,0},{1,65},{65,129},{129,193},{193,1... | collective-permute-start | bytes 884744 | tf_op jit(solution)/shard_map/ppermute | solution.py:705
  41.1 0.0 collective-permute-done.3.refs_2_
  41.1 1.5 %collective-permute-start.9 = (bf16[2,576,128]{2,1,0:T(8,128)(2,1)S(1)}, bf16[2,576,128]{2,1,0:T(8,128)(2,1)S(1)}, u32[]{:S(2)}, u32[]{:S(2)}) collective-permute-start(bf16[2,576,128]{2,1,0:T(8,128)(2,1)S(1)} %get-tuple-element.88), channel_id=1, source_target_pairs={{0,128},{64,192},{128,0},{192,64},{1,129},{65,193},{129,1},{193,65... | collective-permute-start | bytes 884744 | tf_op jit(solution)/shard_map/ppermute | solution.py:705
  42.5 1.3 %collective-permute-done.4.refs_3_ = bf16[2,400,128]{2,1,0:T(8,128)(2,1)S(1)} collective-permute-done((bf16[2,400,128]{2,1,0:T(8,128)(2,1)S(1)}, bf16[2,400,128]{2,1,0:T(8,128)(2,1)S(1)}, u32[]{:S(2)}, u32[]{:S(2)}) %collective-permute-start.4) | collective-permute-done | bytes 204832 | tf_op jit(solution)/shard_map/ppermute | solution.py:705
  43.8 3.4 %collective-permute-start.10 = (bf16[2,576,128]{2,1,0:T(8,128)(2,1)S(1)}, bf16[2,576,128]{2,1,0:T(8,128)(2,1)S(1)}, u32[]{:S(2)}, u32[]{:S(2)}) collective-permute-start(bf16[2,576,128]{2,1,0:T(8,128)(2,1)S(1)} %get-tuple-element.91), channel_id=1, source_target_pairs={{0,192},{64,0},{128,64},{192,128},{1,193},{65,1},{129,65},{193,129... | collective-permute-start | bytes 884744 | tf_op jit(solution)/shard_map/ppermute | solution.py:705
  47.2 0.0 copy-done.7
  47.2 0.0 copy-done.8
  47.2 2.2 %late_weights.1 = (bf16[4,4,256,256]{3,2,1,0:T(8,128)(2,1)S(1)}, bf16[192,2048]{1,0:T(8,128)(2,1)S(1)}, s32[4]{0:T(128)S(1)}) custom-call(s32[1]{0:T(128)} %bitcast.even_ref, s32[1]{0:T(128)} %bitcast.1.me_ref, s32[4]{0:T(128)S(1)} %bitcast.5, bf16[8,16]{1,0:T(8,128)(2,1)S(1)} %copy-done.7, bf16[8,64]{1,0:T(8,128)(2,1)S(1)} %copy-done.8, ...), custom_call_target="tpu_custom_call" | custom-call | flops 1 | bytes 1 | tf_op jit(solution)/shard_map/late_weights/pallas_call | solution.py:165
  49.5 1.7 %second_edges.3 = (bf16[4,384,128]{2,1,0:T(8,128)(2,1)S(1)}, bf16[96,128]{1,0:T(8,128)(2,1)S(1)}, bf16[96,128]{1,0:T(8,128)(2,1)S(1)}) custom-call(s32[1]{0:T(128)} %bitcast.even_ref, s32[4]{0:T(128)S(1)} %get-tuple-element.70.slot_ref.refs_4_.refs_8_, bf16[2,256,256]{2,1,0:T(8,128)(2,1)S(1)} %get-tuple-element.71.picks_ref, ...), custom_call_target="tpu_custom_call" | custom-call | flops 1 | bytes 1 | tf_op jit(solution)/shard_map/second_edges/pallas_call | solution.py:324
  51.1 0.1 collective-permute-start.6
  51.2 2.9 %collective-permute-start.7 = (bf16[96,128]{1,0:T(8,128)(2,1)S(1)}, bf16[96,128]{1,0:T(8,128)(2,1)S(1)}, u32[]{:S(2)}, u32[]{:S(2)}) collective-permute-start(bf16[96,128]{1,0:T(8,128)(2,1)S(1)} %get-tuple-element.83), channel_id=1, source_target_pairs={{1,2},{2,1},{3,4},{4,3},{5,6},{6,5},{7,8},{8,7},{9,10},{10,9},{11,... | collective-permute-start | bytes 73736 | tf_op jit(solution)/shard_map/ppermute | solution.py:347
  54.1 0.0 collective-permute-done.6.refs_1_
  54.2 12.4 %collective-permute-done.7.refs_2_ = bf16[96,128]{1,0:T(8,128)(2,1)S(1)} collective-permute-done((bf16[96,128]{1,0:T(8,128)(2,1)S(1)}, bf16[96,128]{1,0:T(8,128)(2,1)S(1)}, u32[]{:S(2)}, u32[]{:S(2)}) %collective-permute-start.7) | collective-permute-done | bytes 24608 | tf_op jit(solution)/shard_map/ppermute | solution.py:347
  66.5 0.0 collective-permute-done.5.refs_1_
  66.6 0.0 collective-permute-start.8
  66.6 0.0 collective-permute-done.9.refs_2_
  66.6 0.1 collective-permute-start.13
  66.7 3.4 %collective-permute-done.10.refs_3_ = bf16[2,576,128]{2,1,0:T(8,128)(2,1)S(1)} collective-permute-done((bf16[2,576,128]{2,1,0:T(8,128)(2,1)S(1)}, bf16[2,576,128]{2,1,0:T(8,128)(2,1)S(1)}, u32[]{:S(2)}, u32[]{:S(2)}) %collective-permute-start.10) | collective-permute-done | bytes 294944 | tf_op jit(solution)/shard_map/ppermute | solution.py:705
  70.1 3.0 %collective-permute-start.14 = (bf16[2,640,128]{2,1,0:T(8,128)(2,1)S(1)}, bf16[2,640,128]{2,1,0:T(8,128)(2,1)S(1)}, u32[]{:S(2)}, u32[]{:S(2)}) collective-permute-start(bf16[2,640,128]{2,1,0:T(8,128)(2,1)S(1)} %get-tuple-element.104), channel_id=1, source_target_pairs={{0,192},{64,0},{128,64},{192,128},{1,193},{65,1},{129,65},{193,129... | collective-permute-start | bytes 983048 | tf_op jit(solution)/shard_map/ppermute | solution.py:705
  73.1 1.9 %second_edges.4 = (bf16[4,576,128]{2,1,0:T(8,128)(2,1)S(1)}, bf16[144,128]{1,0:T(8,128)(2,1)S(1)}, bf16[144,128]{1,0:T(8,128)(2,1)S(1)}) custom-call(s32[1]{0:T(128)} %bitcast.even_ref, s32[4]{0:T(128)S(1)} %get-tuple-element.70.slot_ref.refs_4_.refs_8_, bf16[2,256,256]{2,1,0:T(8,128)(2,1)S(1)} %get-tuple-element.71.picks_ref, ...), custom_call_target="tpu_custom_call" | custom-call | flops 1 | bytes 1 | tf_op jit(solution)/shard_map/second_edges/pallas_call | solution.py:324
  75.0 0.1 collective-permute-start.11
  75.1 10.8 %collective-permute-start.12 = (bf16[144,128]{1,0:T(8,128)(2,1)S(1)}, bf16[144,128]{1,0:T(8,128)(2,1)S(1)}, u32[]{:S(2)}, u32[]{:S(2)}) collective-permute-start(bf16[144,128]{1,0:T(8,128)(2,1)S(1)} %get-tuple-element.94), channel_id=1, source_target_pairs={{1,2},{2,1},{3,4},{4,3},{5,6},{6,5},{7,8},{8,7},{9,10},{10,9},{11,... | collective-permute-start | bytes 110600 | tf_op jit(solution)/shard_map/ppermute | solution.py:347
  85.9 3.5 %second_pass.3 = (f32[4,2000,128]{2,1,0:T(8,128)}, f32[8,128]{1,0:T(8,128)}) custom-call(bf16[4,384,128]{2,1,0:T(8,128)(2,1)S(1)} %get-tuple-element.95.refs_0_, bf16[96,128]{1,0:T(8,128)(2,1)S(1)} %collective-permute-done.6.refs_1_, bf16[96,128]{1,0:T(8,128)(2,1)S(1)} %collective-permute-done.7.refs_2_, ...), custom_call_target="tpu_custom_call" | custom-call | flops 1 | bytes 1 | tf_op jit(solution)/shard_map/second_pass/pallas_call | solution.py:594
  89.4 0.0 collective-permute-done.11.refs_4_.refs_1_
  89.4 0.8 collective-permute-done.12.refs_5_.refs_2_
  90.2 0.0 collective-permute-done.8.refs_1_
  90.2 0.0 collective-permute-done.13.refs_2_
  90.2 1.6 %collective-permute-done.14.refs_3_ = bf16[2,640,128]{2,1,0:T(8,128)(2,1)S(1)} collective-permute-done((bf16[2,640,128]{2,1,0:T(8,128)(2,1)S(1)}, bf16[2,640,128]{2,1,0:T(8,128)(2,1)S(1)}, u32[]{:S(2)}, u32[]{:S(2)}) %collective-permute-start.14) | collective-permute-done | bytes 327712 | tf_op jit(solution)/shard_map/ppermute | solution.py:705
  91.8 0.5 collective-permute-start.17
  92.3 5.8 %collective-permute-start.18 = (bf16[2,464,128]{2,1,0:T(8,128)(2,1)S(1)}, bf16[2,464,128]{2,1,0:T(8,128)(2,1)S(1)}, u32[]{:S(2)}, u32[]{:S(2)}) collective-permute-start(bf16[2,464,128]{2,1,0:T(8,128)(2,1)S(1)} %get-tuple-element.115), channel_id=1, source_target_pairs={{0,128},{64,192},{128,0},{192,64},{1,129},{65,193},{129,1},{193,65... | collective-permute-start | bytes 712712 | tf_op jit(solution)/shard_map/ppermute | solution.py:705
  98.0 0.0 collective-permute-start.19
  98.0 4.6 %second_pass.4 = (f32[4,2000,128]{2,1,0:T(8,128)}, f32[8,128]{1,0:T(8,128)S(1)}) custom-call(bf16[4,384,128]{2,1,0:T(8,128)(2,1)S(1)} %get-tuple-element.95.refs_0_, bf16[96,128]{1,0:T(8,128)(2,1)S(1)} %collective-permute-done.6.refs_1_, bf16[96,128]{1,0:T(8,128)(2,1)S(1)} %collective-permute-done.7.refs_2_, ...), custom_call_target="tpu_custom_call", output_to_operand_aliasing={{0}: (9, {})} | custom-call | flops 1 | bytes 1 | tf_op jit(solution)/shard_map/second_pass/pallas_call | solution.py:594
  102.7 2.2 %second_edges.5 = (bf16[4,576,128]{2,1,0:T(8,128)(2,1)S(1)}, bf16[272,128]{1,0:T(8,128)(2,1)S(1)}, bf16[272,128]{1,0:T(8,128)(2,1)S(1)}) custom-call(s32[1]{0:T(128)} %bitcast.even_ref, s32[4]{0:T(128)S(1)} %get-tuple-element.70.slot_ref.refs_4_.refs_8_, bf16[2,256,256]{2,1,0:T(8,128)(2,1)S(1)} %get-tuple-element.71.picks_ref, ...), custom_call_target="tpu_custom_call" | custom-call | flops 1 | bytes 1 | tf_op jit(solution)/shard_map/second_edges/pallas_call | solution.py:324
  104.9 0.1 collective-permute-start.15
  105.0 6.1 %collective-permute-start.16 = (bf16[272,128]{1,0:T(8,128)(2,1)S(1)}, bf16[272,128]{1,0:T(8,128)(2,1)S(1)}, u32[]{:S(2)}, u32[]{:S(2)}) collective-permute-start(bf16[272,128]{1,0:T(8,128)(2,1)S(1)} %get-tuple-element.111), channel_id=1, source_target_pairs={{1,2},{2,1},{3,4},{4,3},{5,6},{6,5},{7,8},{8,7},{9,10},{10,9},{11,... | collective-permute-start | bytes 208904 | tf_op jit(solution)/shard_map/ppermute | solution.py:347
  111.1 0.0 collective-permute-done.15.refs_4_.edge_a
  111.1 8.9 %collective-permute-done.16.refs_5_.edge_b = bf16[272,128]{1,0:T(8,128)(2,1)S(1)} collective-permute-done((bf16[272,128]{1,0:T(8,128)(2,1)S(1)}, bf16[272,128]{1,0:T(8,128)(2,1)S(1)}, u32[]{:S(2)}, u32[]{:S(2)}) %collective-permute-start.16) | collective-permute-done | bytes 69664 | tf_op jit(solution)/shard_map/ppermute | solution.py:347
  120.0 5.2 %second_pass.5 = (f32[4,2000,128]{2,1,0:T(8,128)}, f32[8,128]{1,0:T(8,128)}) custom-call(bf16[4,576,128]{2,1,0:T(8,128)(2,1)S(1)} %get-tuple-element.106.refs_3_.refs_0_, bf16[144,128]{1,0:T(8,128)(2,1)S(1)} %collective-permute-done.11.refs_4_.refs_1_, bf16[144,128]{1,0:T(8,128)(2,1)S(1)} %collective-permute-done.12.refs_5_.refs_2_, ...), custom_call_target="tpu_custom_call", output_to_operand_aliasing={{0}: (9, {})} | custom-call | flops 1 | bytes 1 | tf_op jit(solution)/shard_map/second_pass/pallas_call | solution.py:594
  125.2 0.0 collective-permute-done.17.refs_1_
  125.2 0.0 collective-permute-done.18.refs_2_
  125.3 0.0 collective-permute-done.19.refs_3_
  125.3 5.7 %last_pass.1 = f32[4,2000,128]{2,1,0:T(8,128)} custom-call(s32[4]{0:T(128)S(1)} %get-tuple-element.70.slot_ref.refs_4_.refs_8_, bf16[4,576,128]{2,1,0:T(8,128)(2,1)S(1)} %get-tuple-element.109.refs_3_.past_ref, bf16[272,128]{1,0:T(8,128)(2,1)S(1)} %collective-permute-done.15.refs_4_.edge_a, ...), custom_call_target="tpu_custom_call", output_to_operand_aliasing={{}: (6, {})} | custom-call | flops 1 | bytes 1 | tf_op jit(solution)/shard_map/last_pass/pallas_call | solution.py:674
  (6 shorter events, 0.0 us)
Async XLA Ops:
  0.0 19.0 %copy-start.4 = (s32[4,1]{0,1:T(1,128)S(1)}, s32[4,1]{0,1:T(1,128)}, u32[]{:S(2)}) copy-start(s32[4,1]{0,1:T(1,128)} %param.11) | copy-start | bytes 52
  0.0 1.6 %copy-start = (bf16[4,2000,128]{2,1,0:T(8,128)(2,1)S(1)}, bf16[4,2000,128]{2,1,0:T(8,128)(2,1)}, u32[]{:S(2)}) copy-start(bf16[4,2000,128]{2,1,0:T(8,128)(2,1)} %x_ref.5) | copy-start | bytes 6144004
  1.6 17.4 %copy-start.1 = (bf16[4,2000,128]{2,1,0:T(8,128)(2,1)S(1)}, bf16[4,2000,128]{2,1,0:T(8,128)(2,1)}, u32[]{:S(2)}) copy-start(bf16[4,2000,128]{2,1,0:T(8,128)(2,1)} %x_ref.5) | copy-start | bytes 6144004
  3.2 10.5 %collective-permute-start = (bf16[512,128]{1,0:T(8,128)(2,1)}, bf16[512,128]{1,0:T(8,128)(2,1)S(1)}, u32[]{:S(2)}, u32[]{:S(2)}) collective-permute-start(bf16[512,128]{1,0:T(8,128)(2,1)} %get-tuple-element.61), channel_id=1, source_target_pairs={{0,1},{1,0},{2,3},{3,2},{4,5},{5,4},{6,7},{7,6},{8,9},{9,8},{10,11... | collective-permute-start | bytes 393224 | tf_op jit(solution)/shard_map/ppermute | solution.py:347
  3.2 15.8 %collective-permute-start.1 = (bf16[512,128]{1,0:T(8,128)(2,1)S(1)}, bf16[512,128]{1,0:T(8,128)(2,1)S(1)}, u32[]{:S(2)}, u32[]{:S(2)}) collective-permute-start(bf16[512,128]{1,0:T(8,128)(2,1)S(1)} %get-tuple-element.62), channel_id=1, source_target_pairs={{1,2},{2,1},{3,4},{4,3},{5,6},{6,5},{7,8},{8,7},{9,10},{10,9},{11,... | collective-permute-start | bytes 393224 | tf_op jit(solution)/shard_map/ppermute | solution.py:347
  10.4 0.7 copy-start.5
  11.1 0.7 copy-start.6
  12.4 1.3 %copy-start.2 = (bf16[4,4,256,256]{3,2,1,0:T(8,128)(2,1)}, bf16[4,4,256,256]{3,2,1,0:T(8,128)(2,1)S(1)}, u32[]{:S(2)}) copy-start(bf16[4,4,256,256]{3,2,1,0:T(8,128)(2,1)S(1)} %get-tuple-element.63.mats_ref) | copy-start | bytes 6291460
  19.0 1.6 %copy-start.3 = (bf16[4,4,256,256]{3,2,1,0:T(8,128)(2,1)S(1)}, bf16[4,4,256,256]{3,2,1,0:T(8,128)(2,1)}, u32[]{:S(2)}) copy-start(bf16[4,4,256,256]{3,2,1,0:T(8,128)(2,1)} %copy-done.2) | copy-start | bytes 6291460
  20.6 26.6 %copy-start.7 = (bf16[8,16]{1,0:T(8,128)(2,1)S(1)}, bf16[8,16]{1,0:T(8,128)(2,1)}, u32[]{:S(2)}) copy-start(bf16[8,16]{1,0:T(8,128)(2,1)} %trace_ref.3) | copy-start | bytes 772
  20.6 26.6 %copy-start.8 = (bf16[8,64]{1,0:T(8,128)(2,1)S(1)}, bf16[8,64]{1,0:T(8,128)(2,1)}, u32[]{:S(2)}) copy-start(bf16[8,64]{1,0:T(8,128)(2,1)} %time_ref.3) | copy-start | bytes 3076
  24.2 15.4 %collective-permute-start.2 = (bf16[2,400,128]{2,1,0:T(8,128)(2,1)S(1)}, bf16[2,400,128]{2,1,0:T(8,128)(2,1)S(1)}, u32[]{:S(2)}, u32[]{:S(2)}) collective-permute-start(bf16[2,400,128]{2,1,0:T(8,128)(2,1)S(1)} %get-tuple-element.66), channel_id=1, source_target_pairs={{0,64},{64,128},{128,192},{192,0},{1,65},{65,129},{129,193},{193,1... | collective-permute-start | bytes 614408 | tf_op jit(solution)/shard_map/ppermute | solution.py:705
  24.3 16.8 %collective-permute-start.3 = (bf16[2,400,128]{2,1,0:T(8,128)(2,1)S(1)}, bf16[2,400,128]{2,1,0:T(8,128)(2,1)S(1)}, u32[]{:S(2)}, u32[]{:S(2)}) collective-permute-start(bf16[2,400,128]{2,1,0:T(8,128)(2,1)S(1)} %get-tuple-element.67), channel_id=1, source_target_pairs={{0,128},{64,192},{128,0},{192,64},{1,129},{65,193},{129,1},{193,65... | collective-permute-start | bytes 614408 | tf_op jit(solution)/shard_map/ppermute | solution.py:705
  26.7 17.1 %collective-permute-start.4 = (bf16[2,400,128]{2,1,0:T(8,128)(2,1)S(1)}, bf16[2,400,128]{2,1,0:T(8,128)(2,1)S(1)}, u32[]{:S(2)}, u32[]{:S(2)}) collective-permute-start(bf16[2,400,128]{2,1,0:T(8,128)(2,1)S(1)} %get-tuple-element.68), channel_id=1, source_target_pairs={{0,192},{64,0},{128,64},{192,128},{1,193},{65,1},{129,65},{193,129... | collective-permute-start | bytes 614408 | tf_op jit(solution)/shard_map/ppermute | solution.py:705
  39.6 27.0 %collective-permute-start.5 = (bf16[2,576,128]{2,1,0:T(8,128)(2,1)S(1)}, bf16[2,576,128]{2,1,0:T(8,128)(2,1)S(1)}, u32[]{:S(2)}, u32[]{:S(2)}) collective-permute-start(bf16[2,576,128]{2,1,0:T(8,128)(2,1)S(1)} %get-tuple-element.76), channel_id=1, source_target_pairs={{0,64},{64,128},{128,192},{192,0},{1,65},{65,129},{129,193},{193,1... | collective-permute-start | bytes 884744 | tf_op jit(solution)/shard_map/ppermute | solution.py:705
  41.1 25.5 %collective-permute-start.9 = (bf16[2,576,128]{2,1,0:T(8,128)(2,1)S(1)}, bf16[2,576,128]{2,1,0:T(8,128)(2,1)S(1)}, u32[]{:S(2)}, u32[]{:S(2)}) collective-permute-start(bf16[2,576,128]{2,1,0:T(8,128)(2,1)S(1)} %get-tuple-element.88), channel_id=1, source_target_pairs={{0,128},{64,192},{128,0},{192,64},{1,129},{65,193},{129,1},{193,65... | collective-permute-start | bytes 884744 | tf_op jit(solution)/shard_map/ppermute | solution.py:705
  43.8 26.3 %collective-permute-start.10 = (bf16[2,576,128]{2,1,0:T(8,128)(2,1)S(1)}, bf16[2,576,128]{2,1,0:T(8,128)(2,1)S(1)}, u32[]{:S(2)}, u32[]{:S(2)}) collective-permute-start(bf16[2,576,128]{2,1,0:T(8,128)(2,1)S(1)} %get-tuple-element.91), channel_id=1, source_target_pairs={{0,192},{64,0},{128,64},{192,128},{1,193},{65,1},{129,65},{193,129... | collective-permute-start | bytes 884744 | tf_op jit(solution)/shard_map/ppermute | solution.py:705
  51.1 3.0 %collective-permute-start.6 = (bf16[96,128]{1,0:T(8,128)(2,1)S(1)}, bf16[96,128]{1,0:T(8,128)(2,1)S(1)}, u32[]{:S(2)}, u32[]{:S(2)}) collective-permute-start(bf16[96,128]{1,0:T(8,128)(2,1)S(1)} %get-tuple-element.82), channel_id=1, source_target_pairs={{0,1},{1,0},{2,3},{3,2},{4,5},{5,4},{6,7},{7,6},{8,9},{9,8},{10,11... | collective-permute-start | bytes 73736 | tf_op jit(solution)/shard_map/ppermute | solution.py:347
  51.2 15.3 %collective-permute-start.7 = (bf16[96,128]{1,0:T(8,128)(2,1)S(1)}, bf16[96,128]{1,0:T(8,128)(2,1)S(1)}, u32[]{:S(2)}, u32[]{:S(2)}) collective-permute-start(bf16[96,128]{1,0:T(8,128)(2,1)S(1)} %get-tuple-element.83), channel_id=1, source_target_pairs={{1,2},{2,1},{3,4},{4,3},{5,6},{6,5},{7,8},{8,7},{9,10},{10,9},{11,... | collective-permute-start | bytes 73736 | tf_op jit(solution)/shard_map/ppermute | solution.py:347
  66.6 23.7 %collective-permute-start.8 = (bf16[2,640,128]{2,1,0:T(8,128)(2,1)S(1)}, bf16[2,640,128]{2,1,0:T(8,128)(2,1)S(1)}, u32[]{:S(2)}, u32[]{:S(2)}) collective-permute-start(bf16[2,640,128]{2,1,0:T(8,128)(2,1)S(1)} %get-tuple-element.84), channel_id=1, source_target_pairs={{0,64},{64,128},{128,192},{192,0},{1,65},{65,129},{129,193},{193,1... | collective-permute-start | bytes 983048 | tf_op jit(solution)/shard_map/ppermute | solution.py:705
  66.6 23.7 %collective-permute-start.13 = (bf16[2,640,128]{2,1,0:T(8,128)(2,1)S(1)}, bf16[2,640,128]{2,1,0:T(8,128)(2,1)S(1)}, u32[]{:S(2)}, u32[]{:S(2)}) collective-permute-start(bf16[2,640,128]{2,1,0:T(8,128)(2,1)S(1)} %get-tuple-element.101), channel_id=1, source_target_pairs={{0,128},{64,192},{128,0},{192,64},{1,129},{65,193},{129,1},{193,65... | collective-permute-start | bytes 983048 | tf_op jit(solution)/shard_map/ppermute | solution.py:705
  70.1 21.7 %collective-permute-start.14 = (bf16[2,640,128]{2,1,0:T(8,128)(2,1)S(1)}, bf16[2,640,128]{2,1,0:T(8,128)(2,1)S(1)}, u32[]{:S(2)}, u32[]{:S(2)}) collective-permute-start(bf16[2,640,128]{2,1,0:T(8,128)(2,1)S(1)} %get-tuple-element.104), channel_id=1, source_target_pairs={{0,192},{64,0},{128,64},{192,128},{1,193},{65,1},{129,65},{193,129... | collective-permute-start | bytes 983048 | tf_op jit(solution)/shard_map/ppermute | solution.py:705
  75.0 14.4 %collective-permute-start.11 = (bf16[144,128]{1,0:T(8,128)(2,1)S(1)}, bf16[144,128]{1,0:T(8,128)(2,1)S(1)}, u32[]{:S(2)}, u32[]{:S(2)}) collective-permute-start(bf16[144,128]{1,0:T(8,128)(2,1)S(1)} %get-tuple-element.93.refs_5_), channel_id=1, source_target_pairs={{0,1},{1,0},{2,3},{3,2},{4,5},{5,4},{6,7},{7,6},{8,9},{9,8},{10,11... | collective-permute-start | bytes 110600 | tf_op jit(solution)/shard_map/ppermute | solution.py:347
  75.1 15.1 %collective-permute-start.12 = (bf16[144,128]{1,0:T(8,128)(2,1)S(1)}, bf16[144,128]{1,0:T(8,128)(2,1)S(1)}, u32[]{:S(2)}, u32[]{:S(2)}) collective-permute-start(bf16[144,128]{1,0:T(8,128)(2,1)S(1)} %get-tuple-element.94), channel_id=1, source_target_pairs={{1,2},{2,1},{3,4},{4,3},{5,6},{6,5},{7,8},{8,7},{9,10},{10,9},{11,... | collective-permute-start | bytes 110600 | tf_op jit(solution)/shard_map/ppermute | solution.py:347
  91.8 33.4 %collective-permute-start.17 = (bf16[2,464,128]{2,1,0:T(8,128)(2,1)S(1)}, bf16[2,464,128]{2,1,0:T(8,128)(2,1)S(1)}, u32[]{:S(2)}, u32[]{:S(2)}) collective-permute-start(bf16[2,464,128]{2,1,0:T(8,128)(2,1)S(1)} %get-tuple-element.114), channel_id=1, source_target_pairs={{0,64},{64,128},{128,192},{192,0},{1,65},{65,129},{129,193},{193,1... | collective-permute-start | bytes 712712 | tf_op jit(solution)/shard_map/ppermute | solution.py:705
  92.3 33.0 %collective-permute-start.18 = (bf16[2,464,128]{2,1,0:T(8,128)(2,1)S(1)}, bf16[2,464,128]{2,1,0:T(8,128)(2,1)S(1)}, u32[]{:S(2)}, u32[]{:S(2)}) collective-permute-start(bf16[2,464,128]{2,1,0:T(8,128)(2,1)S(1)} %get-tuple-element.115), channel_id=1, source_target_pairs={{0,128},{64,192},{128,0},{192,64},{1,129},{65,193},{129,1},{193,65... | collective-permute-start | bytes 712712 | tf_op jit(solution)/shard_map/ppermute | solution.py:705
  98.0 27.2 %collective-permute-start.19 = (bf16[2,464,128]{2,1,0:T(8,128)(2,1)S(1)}, bf16[2,464,128]{2,1,0:T(8,128)(2,1)S(1)}, u32[]{:S(2)}, u32[]{:S(2)}) collective-permute-start(bf16[2,464,128]{2,1,0:T(8,128)(2,1)S(1)} %get-tuple-element.116), channel_id=1, source_target_pairs={{0,192},{64,0},{128,64},{192,128},{1,193},{65,1},{129,65},{193,129... | collective-permute-start | bytes 712712 | tf_op jit(solution)/shard_map/ppermute | solution.py:705
  104.9 6.2 %collective-permute-start.15 = (bf16[272,128]{1,0:T(8,128)(2,1)S(1)}, bf16[272,128]{1,0:T(8,128)(2,1)S(1)}, u32[]{:S(2)}, u32[]{:S(2)}) collective-permute-start(bf16[272,128]{1,0:T(8,128)(2,1)S(1)} %get-tuple-element.110), channel_id=1, source_target_pairs={{0,1},{1,0},{2,3},{3,2},{4,5},{5,4},{6,7},{7,6},{8,9},{9,8},{10,11... | collective-permute-start | bytes 208904 | tf_op jit(solution)/shard_map/ppermute | solution.py:347
  105.0 15.0 %collective-permute-start.16 = (bf16[272,128]{1,0:T(8,128)(2,1)S(1)}, bf16[272,128]{1,0:T(8,128)(2,1)S(1)}, u32[]{:S(2)}, u32[]{:S(2)}) collective-permute-start(bf16[272,128]{1,0:T(8,128)(2,1)S(1)} %get-tuple-element.111), channel_id=1, source_target_pairs={{1,2},{2,1},{3,4},{4,3},{5,6},{6,5},{7,8},{8,7},{9,10},{10,9},{11,... | collective-permute-start | bytes 208904 | tf_op jit(solution)/shard_map/ppermute | solution.py:347

commit v9 on v7

--- a/solution.py
+++ b/solution.py
@@ -19,7 +19,7 @@
 SMEM = pl.BlockSpec(memory_space=pltpu.SMEM)
 ANY = pl.BlockSpec(memory_space=pl.ANY)
 HBM = pl.BlockSpec(memory_space=pltpu.HBM)
-CHUNKS = (384, 576, 576)
+CHUNKS = (384, 640, 512)
 RIM_FOLD = 8
 NOTE = 16
 

time: 129 us -> 129 us (level)
  waiting for transfers between devices: 28 us -> 37.8 us
  starting transfers between devices: 47.8 us -> 38.1 us
    ppermute x12, waiting for transfers between devices: 4.16 us -> 11.8 us  [send(): return lax.ppermute(values, 'rcv', pairs) if offset else values]
    ppermute x8, starting transfers between devices: 31.5 us -> 26.4 us  [swap_edges(): got.append(lax.ppermute(edges, 'shot', pairs))]
    ppermute x12, starting transfers between devices: 16.3 us -> 11.7 us  [send(): return lax.ppermute(values, 'rcv', pairs) if offset else values]
    ppermute x8, waiting for transfers between devices: 23.9 us -> 26 us  [swap_edges(): got.append(lax.ppermute(edges, 'shot', pairs))]
  transfers between devices with their start and end apart: 20 -> 20, of which waited for: 5 -> 6; matrix products, arithmetic and copies ran while one was open for 0% -> 0% of each run, Pallas kernels for 27% -> 27%
where the time goes in v9:
time: 129 us; the launch traced here: 127 us
  Pallas kernels  44.8 us (35%)
  starting transfers between devices  38.1 us (30%)
  waiting for transfers between devices  37.8 us (29%)
  local copies, waits for them, and re-layouts  5.87 us (5%)
    ppermute x8, starting transfers between devices, swap_edges(): got.append(lax.ppermute(edges, 'shot', pairs))  26.4 us
    ppermute x8, waiting for transfers between devices, swap_edges(): got.append(lax.ppermute(edges, 'shot', pairs))  26 us
    pallas_call x2, Pallas kernels, first_pass(): pl.pallas_call(functools.partial(first_kernel, start, sizes, noted, owner...  15.8 us
    pallas_call x3, Pallas kernels, second_pass(): pl.pallas_call(functools.partial(second_kernel, at, past is not None), in...  13 us
    ppermute x12, waiting for transfers between devices, send(): return lax.ppermute(values, 'rcv', pairs) if offset else values  11.8 us
    ppermute x12, starting transfers between devices, send(): return lax.ppermute(values, 'rcv', pairs) if offset else values  11.7 us
    unnamed x18, local copies, waits for them, and re-layouts  5.87 us
    pallas_call x3, Pallas kernels, second_edges(): pl.pallas_call(second_edges_kernel, in_specs=[SMEM, SMEM, VMEM] + [ANY] *...  5.82 us
  transfers between devices with their start and end apart: 20, of which 6 were waited for; matrix products, arithmetic and copies ran while one was open for 0% of the time, Pallas kernels for 27%

profile of v9, /device:TPU:192, one launch (start us, length us, event | category | flops | bytes accessed | tf_op | source)
XLA Modules:
  0.0 127.0 jit_solution(4493492966822405160)
XLA Ops:
  0.0 0.0 copy-start.4
  0.0 1.6 %copy-done = bf16[4,2000,128]{2,1,0:T(8,128)(2,1)S(1)} copy-done((bf16[4,2000,128]{2,1,0:T(8,128)(2,1)S(1)}, bf16[4,2000,128]{2,1,0:T(8,128)(2,1)}, u32[]{:S(2)}) %copy-start) | copy-done | bytes 2048024
  1.6 1.6 %first_edges.1 = (bf16[512,128]{1,0:T(8,128)(2,1)}, bf16[512,128]{1,0:T(8,128)(2,1)S(1)}, bf16[2,256,256]{2,1,0:T(8,128)(2,1)S(1)}) custom-call(s32[1]{0:T(128)} %bitcast.even_ref, bf16[4,2000,128]{2,1,0:T(8,128)(2,1)S(1)} %copy-done), custom_call_target="tpu_custom_call" | custom-call | flops 1 | bytes 1 | tf_op jit(solution)/shard_map/first_edges/pallas_call | solution.py:253
  3.2 0.0 collective-permute-start
  3.2 7.2 %collective-permute-start.1 = (bf16[512,128]{1,0:T(8,128)(2,1)S(1)}, bf16[512,128]{1,0:T(8,128)(2,1)S(1)}, u32[]{:S(2)}, u32[]{:S(2)}) collective-permute-start(bf16[512,128]{1,0:T(8,128)(2,1)S(1)} %get-tuple-element.61), channel_id=1, source_target_pairs={{1,2},{2,1},{3,4},{4,3},{5,6},{6,5},{7,8},{8,7},{9,10},{10,9},{11,... | collective-permute-start | bytes 393224 | tf_op jit(solution)/shard_map/ppermute | solution.py:347
  10.4 0.0 copy-start.5
  10.4 0.7 copy-done.5
  11.1 0.7 copy-done.6
  11.8 0.6 weights.1
  12.4 0.0 copy-start.2
  12.4 1.3 %copy-done.2 = bf16[4,4,256,256]{3,2,1,0:T(8,128)(2,1)} copy-done((bf16[4,4,256,256]{3,2,1,0:T(8,128)(2,1)}, bf16[4,4,256,256]{3,2,1,0:T(8,128)(2,1)S(1)}, u32[]{:S(2)}) %copy-start.2) | copy-done | bytes 2097176
  13.7 0.0 collective-permute-done.edge_a
  13.7 5.3 %collective-permute-done.1.edge_b = bf16[512,128]{1,0:T(8,128)(2,1)S(1)} collective-permute-done((bf16[512,128]{1,0:T(8,128)(2,1)S(1)}, bf16[512,128]{1,0:T(8,128)(2,1)S(1)}, u32[]{:S(2)}, u32[]{:S(2)}) %collective-permute-start.1) | collective-permute-done | bytes 131104 | tf_op jit(solution)/shard_map/ppermute | solution.py:347
  19.0 0.0 copy-done.4
  19.0 0.0 copy-done.1
  19.0 1.6 %copy-done.3 = bf16[4,4,256,256]{3,2,1,0:T(8,128)(2,1)S(1)} copy-done((bf16[4,4,256,256]{3,2,1,0:T(8,128)(2,1)S(1)}, bf16[4,4,256,256]{3,2,1,0:T(8,128)(2,1)}, u32[]{:S(2)}) %copy-start.3) | copy-done | bytes 2097176
  20.6 3.6 %first_pass.2 = (bf16[2,400,128]{2,1,0:T(8,128)(2,1)S(1)}, bf16[2,400,128]{2,1,0:T(8,128)(2,1)S(1)}, bf16[2,400,128]{2,1,0:T(8,128)(2,1)S(1)}, bf16[2,400,128]{2,1,0:T(8,128)(2,1)S(1)}) custom-call(s32[1]{0:T(128)} %bitcast.1.me_ref, s32[4]{0:T(128)S(1)} %bitcast.3, bf16[4,2000,128]{2,1,0:T(8,128)(2,1)S(1)} %copy-done.1, ...), custom_call_target="tpu_custom_call" | custom-call | flops 1 | bytes 1 | tf_op jit(solution)/shard_map/first_pass/pallas_call | solution.py:514
  24.2 1.1 collective-permute-start.4
  25.3 1.1 collective-permute-start.3
  26.3 0.5 collective-permute-start.2
  26.8 12.2 %first_pass.3 = (bf16[2,640,128]{2,1,0:T(8,128)(2,1)S(1)}, bf16[2,640,128]{2,1,0:T(8,128)(2,1)S(1)}, bf16[2,640,128]{2,1,0:T(8,128)(2,1)S(1)}, bf16[2,640,128]{2...) custom-call(s32[1]{0:T(128)} %bitcast.1.me_ref, ...), custom_call_target="tpu_custom_call" | custom-call | flops 1 | bytes 1 | tf_op jit(solution)/shard_map/first_pass/pallas_call | solution.py:514
  39.1 0.0 collective-permute-done.4.refs_3_
  39.1 1.6 %collective-permute-start.10 = (bf16[2,640,128]{2,1,0:T(8,128)(2,1)S(1)}, bf16[2,640,128]{2,1,0:T(8,128)(2,1)S(1)}, u32[]{:S(2)}, u32[]{:S(2)}) collective-permute-start(bf16[2,640,128]{2,1,0:T(8,128)(2,1)S(1)} %get-tuple-element.90), channel_id=1, source_target_pairs={{0,192},{64,0},{128,64},{192,128},{1,193},{65,1},{129,65},{193,129... | collective-permute-start | bytes 983048 | tf_op jit(solution)/shard_map/ppermute | solution.py:705
  40.7 0.0 collective-permute-done.3.refs_2_
  40.7 3.6 %collective-permute-start.9 = (bf16[2,640,128]{2,1,0:T(8,128)(2,1)S(1)}, bf16[2,640,128]{2,1,0:T(8,128)(2,1)S(1)}, u32[]{:S(2)}, u32[]{:S(2)}) collective-permute-start(bf16[2,640,128]{2,1,0:T(8,128)(2,1)S(1)} %get-tuple-element.87), channel_id=1, source_target_pairs={{0,128},{64,192},{128,0},{192,64},{1,129},{65,193},{129,1},{193,65... | collective-permute-start | bytes 983048 | tf_op jit(solution)/shard_map/ppermute | solution.py:705
  44.3 8.7 %collective-permute-done.2.refs_1_ = bf16[2,400,128]{2,1,0:T(8,128)(2,1)S(1)} collective-permute-done((bf16[2,400,128]{2,1,0:T(8,128)(2,1)S(1)}, bf16[2,400,128]{2,1,0:T(8,128)(2,1)S(1)}, u32[]{:S(2)}, u32[]{:S(2)}) %collective-permute-start.2) | collective-permute-done | bytes 204832 | tf_op jit(solution)/shard_map/ppermute | solution.py:705
  53.1 0.0 collective-permute-start.5
  53.1 0.0 copy-done.7
  53.1 0.0 copy-done.8
  53.1 2.2 %late_weights.1 = (bf16[4,4,256,256]{3,2,1,0:T(8,128)(2,1)S(1)}, bf16[192,2048]{1,0:T(8,128)(2,1)S(1)}, s32[4]{0:T(128)S(1)}) custom-call(s32[1]{0:T(128)} %bitcast.even_ref, s32[1]{0:T(128)} %bitcast.1.me_ref, s32[4]{0:T(128)S(1)} %bitcast.5, bf16[8,16]{1,0:T(8,128)(2,1)S(1)} %copy-done.7, bf16[8,64]{1,0:T(8,128)(2,1)S(1)} %copy-done.8, ...), custom_call_target="tpu_custom_call" | custom-call | flops 1 | bytes 1 | tf_op jit(solution)/shard_map/late_weights/pallas_call | solution.py:165
  55.3 1.6 %second_edges.3 = (bf16[4,384,128]{2,1,0:T(8,128)(2,1)S(1)}, bf16[96,128]{1,0:T(8,128)(2,1)S(1)}, bf16[96,128]{1,0:T(8,128)(2,1)S(1)}) custom-call(s32[1]{0:T(128)} %bitcast.even_ref, s32[4]{0:T(128)S(1)} %get-tuple-element.69.slot_ref.refs_4_.refs_8_, bf16[2,256,256]{2,1,0:T(8,128)(2,1)S(1)} %get-tuple-element.70.picks_ref, ...), custom_call_target="tpu_custom_call" | custom-call | flops 1 | bytes 1 | tf_op jit(solution)/shard_map/second_edges/pallas_call | solution.py:324
  57.0 0.1 collective-permute-start.6
  57.1 1.9 %collective-permute-start.7 = (bf16[96,128]{1,0:T(8,128)(2,1)S(1)}, bf16[96,128]{1,0:T(8,128)(2,1)S(1)}, u32[]{:S(2)}, u32[]{:S(2)}) collective-permute-start(bf16[96,128]{1,0:T(8,128)(2,1)S(1)} %get-tuple-element.82), channel_id=1, source_target_pairs={{1,2},{2,1},{3,4},{4,3},{5,6},{6,5},{7,8},{8,7},{9,10},{10,9},{11,... | collective-permute-start | bytes 73736 | tf_op jit(solution)/shard_map/ppermute | solution.py:347
  59.0 0.0 collective-permute-done.6.refs_1_
  59.0 12.1 %collective-permute-done.7.refs_2_ = bf16[96,128]{1,0:T(8,128)(2,1)S(1)} collective-permute-done((bf16[96,128]{1,0:T(8,128)(2,1)S(1)}, bf16[96,128]{1,0:T(8,128)(2,1)S(1)}, u32[]{:S(2)}, u32[]{:S(2)}) %collective-permute-start.7) | collective-permute-done | bytes 24608 | tf_op jit(solution)/shard_map/ppermute | solution.py:347
  71.1 0.0 collective-permute-done.10.refs_3_
  71.1 1.7 %collective-permute-start.14 = (bf16[2,576,128]{2,1,0:T(8,128)(2,1)S(1)}, bf16[2,576,128]{2,1,0:T(8,128)(2,1)S(1)}, u32[]{:S(2)}, u32[]{:S(2)}) collective-permute-start(bf16[2,576,128]{2,1,0:T(8,128)(2,1)S(1)} %get-tuple-element.103), channel_id=1, source_target_pairs={{0,192},{64,0},{128,64},{192,128},{1,193},{65,1},{129,65},{193,129... | collective-permute-start | bytes 884744 | tf_op jit(solution)/shard_map/ppermute | solution.py:705
  72.8 0.0 collective-permute-done.9.refs_2_
  72.8 0.0 collective-permute-start.13
  72.8 3.1 %collective-permute-done.5.refs_1_ = bf16[2,640,128]{2,1,0:T(8,128)(2,1)S(1)} collective-permute-done((bf16[2,640,128]{2,1,0:T(8,128)(2,1)S(1)}, bf16[2,640,128]{2,1,0:T(8,128)(2,1)S(1)}, u32[]{:S(2)}, u32[]{:S(2)}) %collective-permute-start.5) | collective-permute-done | bytes 327712 | tf_op jit(solution)/shard_map/ppermute | solution.py:705
  75.9 0.0 collective-permute-start.8
  75.9 2.0 %second_edges.4 = (bf16[4,640,128]{2,1,0:T(8,128)(2,1)S(1)}, bf16[160,128]{1,0:T(8,128)(2,1)S(1)}, bf16[160,128]{1,0:T(8,128)(2,1)S(1)}) custom-call(s32[1]{0:T(128)} %bitcast.even_ref, s32[4]{0:T(128)S(1)} %get-tuple-element.69.slot_ref.refs_4_.refs_8_, bf16[2,256,256]{2,1,0:T(8,128)(2,1)S(1)} %get-tuple-element.70.picks_ref, ...), custom_call_target="tpu_custom_call" | custom-call | flops 1 | bytes 1 | tf_op jit(solution)/shard_map/second_edges/pallas_call | solution.py:324
  77.9 10.1 %collective-permute-start.12 = (bf16[160,128]{1,0:T(8,128)(2,1)S(1)}, bf16[160,128]{1,0:T(8,128)(2,1)S(1)}, u32[]{:S(2)}, u32[]{:S(2)}) collective-permute-start(bf16[160,128]{1,0:T(8,128)(2,1)S(1)} %get-tuple-element.93), channel_id=1, source_target_pairs={{1,2},{2,1},{3,4},{4,3},{5,6},{6,5},{7,8},{8,7},{9,10},{10,9},{11,... | collective-permute-start | bytes 122888 | tf_op jit(solution)/shard_map/ppermute | solution.py:347
  88.0 0.1 collective-permute-start.11
  88.1 2.9 %second_pass.3 = (f32[4,2000,128]{2,1,0:T(8,128)}, f32[8,128]{1,0:T(8,128)S(1)}) custom-call(bf16[4,384,128]{2,1,0:T(8,128)(2,1)S(1)} %get-tuple-element.94.refs_0_, bf16[96,128]{1,0:T(8,128)(2,1)S(1)} %collective-permute-done.6.refs_1_, bf16[96,128]{1,0:T(8,128)(2,1)S(1)} %collective-permute-done.7.refs_2_, ...), custom_call_target="tpu_custom_call" | custom-call | flops 1 | bytes 1 | tf_op jit(solution)/shard_map/second_pass/pallas_call | solution.py:594
  91.0 5.7 %collective-permute-done.12.refs_5_.refs_2_ = bf16[160,128]{1,0:T(8,128)(2,1)S(1)} collective-permute-done((bf16[160,128]{1,0:T(8,128)(2,1)S(1)}, bf16[160,128]{1,0:T(8,128)(2,1)S(1)}, u32[]{:S(2)}, u32[]{:S(2)}) %collective-permute-start.12) | collective-permute-done | bytes 40992 | tf_op jit(solution)/shard_map/ppermute | solution.py:347
  96.7 0.0 collective-permute-done.11.refs_4_.refs_1_
  96.7 0.0 collective-permute-done.14.refs_3_
  96.8 0.0 collective-permute-done.13.refs_2_
  96.8 0.0 collective-permute-done.8.refs_1_
  96.8 0.1 collective-permute-start.17
  96.9 1.3 collective-permute-start.18
  98.1 0.8 collective-permute-start.19
  98.9 2.1 %second_edges.5 = (bf16[4,512,128]{2,1,0:T(8,128)(2,1)S(1)}, bf16[256,128]{1,0:T(8,128)(2,1)S(1)}, bf16[256,128]{1,0:T(8,128)(2,1)S(1)}) custom-call(s32[1]{0:T(128)} %bitcast.even_ref, s32[4]{0:T(128)S(1)} %get-tuple-element.69.slot_ref.refs_4_.refs_8_, bf16[2,256,256]{2,1,0:T(8,128)(2,1)S(1)} %get-tuple-element.70.picks_ref, ...), custom_call_target="tpu_custom_call" | custom-call | flops 1 | bytes 1 | tf_op jit(solution)/shard_map/second_edges/pallas_call | solution.py:324
  101.0 6.7 %collective-permute-start.16 = (bf16[256,128]{1,0:T(8,128)(2,1)S(1)}, bf16[256,128]{1,0:T(8,128)(2,1)S(1)}, u32[]{:S(2)}, u32[]{:S(2)}) collective-permute-start(bf16[256,128]{1,0:T(8,128)(2,1)S(1)} %get-tuple-element.107), channel_id=1, source_target_pairs={{1,2},{2,1},{3,4},{4,3},{5,6},{6,5},{7,8},{8,7},{9,10},{10,9},{11,... | collective-permute-start | bytes 196616 | tf_op jit(solution)/shard_map/ppermute | solution.py:347
  107.7 0.3 collective-permute-start.15
  108.0 5.1 %second_pass.4 = (f32[4,2000,128]{2,1,0:T(8,128)}, f32[8,128]{1,0:T(8,128)}) custom-call(bf16[4,384,128]{2,1,0:T(8,128)(2,1)S(1)} %get-tuple-element.94.refs_0_, bf16[96,128]{1,0:T(8,128)(2,1)S(1)} %collective-permute-done.6.refs_1_, bf16[96,128]{1,0:T(8,128)(2,1)S(1)} %collective-permute-done.7.refs_2_, ...), custom_call_target="tpu_custom_call", output_to_operand_aliasing={{0}: (9, {})} | custom-call | flops 1 | bytes 1 | tf_op jit(solution)/shard_map/second_pass/pallas_call | solution.py:594
  113.2 2.9 %collective-permute-done.16.refs_5_.edge_b = bf16[256,128]{1,0:T(8,128)(2,1)S(1)} collective-permute-done((bf16[256,128]{1,0:T(8,128)(2,1)S(1)}, bf16[256,128]{1,0:T(8,128)(2,1)S(1)}, u32[]{:S(2)}, u32[]{:S(2)}) %collective-permute-start.16) | collective-permute-done | bytes 65568 | tf_op jit(solution)/shard_map/ppermute | solution.py:347
  116.1 0.0 collective-permute-done.15.refs_4_.edge_a
  116.1 5.0 %second_pass.5 = (f32[4,2000,128]{2,1,0:T(8,128)}, f32[8,128]{1,0:T(8,128)}) custom-call(bf16[4,640,128]{2,1,0:T(8,128)(2,1)S(1)} %get-tuple-element.108.refs_3_.refs_0_, bf16[160,128]{1,0:T(8,128)(2,1)S(1)} %collective-permute-done.11.refs_4_.refs_1_, bf16[160,128]{1,0:T(8,128)(2,1)S(1)} %collective-permute-done.12.refs_5_.refs_2_, ...), custom_call_target="tpu_custom_call", output_to_operand_aliasing={{0}: (9, {})} | custom-call | flops 1 | bytes 1 | tf_op jit(solution)/shard_map/second_pass/pallas_call | solution.py:594
  121.1 0.0 collective-permute-done.17.refs_1_
  121.1 0.0 collective-permute-done.18.refs_2_
  121.1 0.0 collective-permute-done.19.refs_3_
  121.1 5.7 %last_pass.1 = f32[4,2000,128]{2,1,0:T(8,128)} custom-call(s32[4]{0:T(128)S(1)} %get-tuple-element.69.slot_ref.refs_4_.refs_8_, bf16[4,512,128]{2,1,0:T(8,128)(2,1)S(1)} %get-tuple-element.105.refs_3_.past_ref, bf16[256,128]{1,0:T(8,128)(2,1)S(1)} %collective-permute-done.15.refs_4_.edge_a, ...), custom_call_target="tpu_custom_call", output_to_operand_aliasing={{}: (6, {})} | custom-call | flops 1 | bytes 1 | tf_op jit(solution)/shard_map/last_pass/pallas_call | solution.py:674
  (6 shorter events, 0.0 us)
Async XLA Ops:
  0.0 19.0 %copy-start.4 = (s32[4,1]{0,1:T(1,128)S(1)}, s32[4,1]{0,1:T(1,128)}, u32[]{:S(2)}) copy-start(s32[4,1]{0,1:T(1,128)} %param.11) | copy-start | bytes 52
  0.0 1.6 %copy-start = (bf16[4,2000,128]{2,1,0:T(8,128)(2,1)S(1)}, bf16[4,2000,128]{2,1,0:T(8,128)(2,1)}, u32[]{:S(2)}) copy-start(bf16[4,2000,128]{2,1,0:T(8,128)(2,1)} %x_ref.5) | copy-start | bytes 6144004
  1.6 17.4 %copy-start.1 = (bf16[4,2000,128]{2,1,0:T(8,128)(2,1)S(1)}, bf16[4,2000,128]{2,1,0:T(8,128)(2,1)}, u32[]{:S(2)}) copy-start(bf16[4,2000,128]{2,1,0:T(8,128)(2,1)} %x_ref.5) | copy-start | bytes 6144004
  3.2 10.5 %collective-permute-start = (bf16[512,128]{1,0:T(8,128)(2,1)}, bf16[512,128]{1,0:T(8,128)(2,1)S(1)}, u32[]{:S(2)}, u32[]{:S(2)}) collective-permute-start(bf16[512,128]{1,0:T(8,128)(2,1)} %get-tuple-element.60), channel_id=1, source_target_pairs={{0,1},{1,0},{2,3},{3,2},{4,5},{5,4},{6,7},{7,6},{8,9},{9,8},{10,11... | collective-permute-start | bytes 393224 | tf_op jit(solution)/shard_map/ppermute | solution.py:347
  3.2 15.8 %collective-permute-start.1 = (bf16[512,128]{1,0:T(8,128)(2,1)S(1)}, bf16[512,128]{1,0:T(8,128)(2,1)S(1)}, u32[]{:S(2)}, u32[]{:S(2)}) collective-permute-start(bf16[512,128]{1,0:T(8,128)(2,1)S(1)} %get-tuple-element.61), channel_id=1, source_target_pairs={{1,2},{2,1},{3,4},{4,3},{5,6},{6,5},{7,8},{8,7},{9,10},{10,9},{11,... | collective-permute-start | bytes 393224 | tf_op jit(solution)/shard_map/ppermute | solution.py:347
  10.4 0.7 copy-start.5
  11.1 0.7 copy-start.6
  12.4 1.3 %copy-start.2 = (bf16[4,4,256,256]{3,2,1,0:T(8,128)(2,1)}, bf16[4,4,256,256]{3,2,1,0:T(8,128)(2,1)S(1)}, u32[]{:S(2)}) copy-start(bf16[4,4,256,256]{3,2,1,0:T(8,128)(2,1)S(1)} %get-tuple-element.62.mats_ref) | copy-start | bytes 6291460
  19.0 1.6 %copy-start.3 = (bf16[4,4,256,256]{3,2,1,0:T(8,128)(2,1)S(1)}, bf16[4,4,256,256]{3,2,1,0:T(8,128)(2,1)}, u32[]{:S(2)}) copy-start(bf16[4,4,256,256]{3,2,1,0:T(8,128)(2,1)} %copy-done.2) | copy-start | bytes 6291460
  20.6 32.5 %copy-start.7 = (bf16[8,16]{1,0:T(8,128)(2,1)S(1)}, bf16[8,16]{1,0:T(8,128)(2,1)}, u32[]{:S(2)}) copy-start(bf16[8,16]{1,0:T(8,128)(2,1)} %trace_ref.3) | copy-start | bytes 772
  20.6 32.5 %copy-start.8 = (bf16[8,64]{1,0:T(8,128)(2,1)S(1)}, bf16[8,64]{1,0:T(8,128)(2,1)}, u32[]{:S(2)}) copy-start(bf16[8,64]{1,0:T(8,128)(2,1)} %time_ref.3) | copy-start | bytes 3076
  24.2 14.9 %collective-permute-start.4 = (bf16[2,400,128]{2,1,0:T(8,128)(2,1)S(1)}, bf16[2,400,128]{2,1,0:T(8,128)(2,1)S(1)}, u32[]{:S(2)}, u32[]{:S(2)}) collective-permute-start(bf16[2,400,128]{2,1,0:T(8,128)(2,1)S(1)} %get-tuple-element.67), channel_id=1, source_target_pairs={{0,192},{64,0},{128,64},{192,128},{1,193},{65,1},{129,65},{193,129... | collective-permute-start | bytes 614408 | tf_op jit(solution)/shard_map/ppermute | solution.py:705
  25.3 15.4 %collective-permute-start.3 = (bf16[2,400,128]{2,1,0:T(8,128)(2,1)S(1)}, bf16[2,400,128]{2,1,0:T(8,128)(2,1)S(1)}, u32[]{:S(2)}, u32[]{:S(2)}) collective-permute-start(bf16[2,400,128]{2,1,0:T(8,128)(2,1)S(1)} %get-tuple-element.66), channel_id=1, source_target_pairs={{0,128},{64,192},{128,0},{192,64},{1,129},{65,193},{129,1},{193,65... | collective-permute-start | bytes 614408 | tf_op jit(solution)/shard_map/ppermute | solution.py:705
  26.3 26.7 %collective-permute-start.2 = (bf16[2,400,128]{2,1,0:T(8,128)(2,1)S(1)}, bf16[2,400,128]{2,1,0:T(8,128)(2,1)S(1)}, u32[]{:S(2)}, u32[]{:S(2)}) collective-permute-start(bf16[2,400,128]{2,1,0:T(8,128)(2,1)S(1)} %get-tuple-element.65), channel_id=1, source_target_pairs={{0,64},{64,128},{128,192},{192,0},{1,65},{65,129},{129,193},{193,1... | collective-permute-start | bytes 614408 | tf_op jit(solution)/shard_map/ppermute | solution.py:705
  39.1 32.0 %collective-permute-start.10 = (bf16[2,640,128]{2,1,0:T(8,128)(2,1)S(1)}, bf16[2,640,128]{2,1,0:T(8,128)(2,1)S(1)}, u32[]{:S(2)}, u32[]{:S(2)}) collective-permute-start(bf16[2,640,128]{2,1,0:T(8,128)(2,1)S(1)} %get-tuple-element.90), channel_id=1, source_target_pairs={{0,192},{64,0},{128,64},{192,128},{1,193},{65,1},{129,65},{193,129... | collective-permute-start | bytes 983048 | tf_op jit(solution)/shard_map/ppermute | solution.py:705
  40.7 32.1 %collective-permute-start.9 = (bf16[2,640,128]{2,1,0:T(8,128)(2,1)S(1)}, bf16[2,640,128]{2,1,0:T(8,128)(2,1)S(1)}, u32[]{:S(2)}, u32[]{:S(2)}) collective-permute-start(bf16[2,640,128]{2,1,0:T(8,128)(2,1)S(1)} %get-tuple-element.87), channel_id=1, source_target_pairs={{0,128},{64,192},{128,0},{192,64},{1,129},{65,193},{129,1},{193,65... | collective-permute-start | bytes 983048 | tf_op jit(solution)/shard_map/ppermute | solution.py:705
  53.1 22.8 %collective-permute-start.5 = (bf16[2,640,128]{2,1,0:T(8,128)(2,1)S(1)}, bf16[2,640,128]{2,1,0:T(8,128)(2,1)S(1)}, u32[]{:S(2)}, u32[]{:S(2)}) collective-permute-start(bf16[2,640,128]{2,1,0:T(8,128)(2,1)S(1)} %get-tuple-element.75), channel_id=1, source_target_pairs={{0,64},{64,128},{128,192},{192,0},{1,65},{65,129},{129,193},{193,1... | collective-permute-start | bytes 983048 | tf_op jit(solution)/shard_map/ppermute | solution.py:705
  57.0 2.0 %collective-permute-start.6 = (bf16[96,128]{1,0:T(8,128)(2,1)S(1)}, bf16[96,128]{1,0:T(8,128)(2,1)S(1)}, u32[]{:S(2)}, u32[]{:S(2)}) collective-permute-start(bf16[96,128]{1,0:T(8,128)(2,1)S(1)} %get-tuple-element.81), channel_id=1, source_target_pairs={{0,1},{1,0},{2,3},{3,2},{4,5},{5,4},{6,7},{7,6},{8,9},{9,8},{10,11... | collective-permute-start | bytes 73736 | tf_op jit(solution)/shard_map/ppermute | solution.py:347
  57.1 14.0 %collective-permute-start.7 = (bf16[96,128]{1,0:T(8,128)(2,1)S(1)}, bf16[96,128]{1,0:T(8,128)(2,1)S(1)}, u32[]{:S(2)}, u32[]{:S(2)}) collective-permute-start(bf16[96,128]{1,0:T(8,128)(2,1)S(1)} %get-tuple-element.82), channel_id=1, source_target_pairs={{1,2},{2,1},{3,4},{4,3},{5,6},{6,5},{7,8},{8,7},{9,10},{10,9},{11,... | collective-permute-start | bytes 73736 | tf_op jit(solution)/shard_map/ppermute | solution.py:347
  71.1 25.6 %collective-permute-start.14 = (bf16[2,576,128]{2,1,0:T(8,128)(2,1)S(1)}, bf16[2,576,128]{2,1,0:T(8,128)(2,1)S(1)}, u32[]{:S(2)}, u32[]{:S(2)}) collective-permute-start(bf16[2,576,128]{2,1,0:T(8,128)(2,1)S(1)} %get-tuple-element.103), channel_id=1, source_target_pairs={{0,192},{64,0},{128,64},{192,128},{1,193},{65,1},{129,65},{193,129... | collective-permute-start | bytes 884744 | tf_op jit(solution)/shard_map/ppermute | solution.py:705
  72.8 23.9 %collective-permute-start.13 = (bf16[2,576,128]{2,1,0:T(8,128)(2,1)S(1)}, bf16[2,576,128]{2,1,0:T(8,128)(2,1)S(1)}, u32[]{:S(2)}, u32[]{:S(2)}) collective-permute-start(bf16[2,576,128]{2,1,0:T(8,128)(2,1)S(1)} %get-tuple-element.100), channel_id=1, source_target_pairs={{0,128},{64,192},{128,0},{192,64},{1,129},{65,193},{129,1},{193,65... | collective-permute-start | bytes 884744 | tf_op jit(solution)/shard_map/ppermute | solution.py:705
  75.9 20.9 %collective-permute-start.8 = (bf16[2,576,128]{2,1,0:T(8,128)(2,1)S(1)}, bf16[2,576,128]{2,1,0:T(8,128)(2,1)S(1)}, u32[]{:S(2)}, u32[]{:S(2)}) collective-permute-start(bf16[2,576,128]{2,1,0:T(8,128)(2,1)S(1)} %get-tuple-element.83), channel_id=1, source_target_pairs={{0,64},{64,128},{128,192},{192,0},{1,65},{65,129},{129,193},{193,1... | collective-permute-start | bytes 884744 | tf_op jit(solution)/shard_map/ppermute | solution.py:705
  77.9 18.8 %collective-permute-start.12 = (bf16[160,128]{1,0:T(8,128)(2,1)S(1)}, bf16[160,128]{1,0:T(8,128)(2,1)S(1)}, u32[]{:S(2)}, u32[]{:S(2)}) collective-permute-start(bf16[160,128]{1,0:T(8,128)(2,1)S(1)} %get-tuple-element.93), channel_id=1, source_target_pairs={{1,2},{2,1},{3,4},{4,3},{5,6},{6,5},{7,8},{8,7},{9,10},{10,9},{11,... | collective-permute-start | bytes 122888 | tf_op jit(solution)/shard_map/ppermute | solution.py:347
  88.0 8.7 %collective-permute-start.11 = (bf16[160,128]{1,0:T(8,128)(2,1)S(1)}, bf16[160,128]{1,0:T(8,128)(2,1)S(1)}, u32[]{:S(2)}, u32[]{:S(2)}) collective-permute-start(bf16[160,128]{1,0:T(8,128)(2,1)S(1)} %get-tuple-element.92.refs_5_), channel_id=1, source_target_pairs={{0,1},{1,0},{2,3},{3,2},{4,5},{5,4},{6,7},{7,6},{8,9},{9,8},{10,11... | collective-permute-start | bytes 122888 | tf_op jit(solution)/shard_map/ppermute | solution.py:347
  96.8 24.3 %collective-permute-start.17 = (bf16[2,464,128]{2,1,0:T(8,128)(2,1)S(1)}, bf16[2,464,128]{2,1,0:T(8,128)(2,1)S(1)}, u32[]{:S(2)}, u32[]{:S(2)}) collective-permute-start(bf16[2,464,128]{2,1,0:T(8,128)(2,1)S(1)} %get-tuple-element.112), channel_id=1, source_target_pairs={{0,64},{64,128},{128,192},{192,0},{1,65},{65,129},{129,193},{193,1... | collective-permute-start | bytes 712712 | tf_op jit(solution)/shard_map/ppermute | solution.py:705
  96.9 24.2 %collective-permute-start.18 = (bf16[2,464,128]{2,1,0:T(8,128)(2,1)S(1)}, bf16[2,464,128]{2,1,0:T(8,128)(2,1)S(1)}, u32[]{:S(2)}, u32[]{:S(2)}) collective-permute-start(bf16[2,464,128]{2,1,0:T(8,128)(2,1)S(1)} %get-tuple-element.113), channel_id=1, source_target_pairs={{0,128},{64,192},{128,0},{192,64},{1,129},{65,193},{129,1},{193,65... | collective-permute-start | bytes 712712 | tf_op jit(solution)/shard_map/ppermute | solution.py:705
  98.1 23.0 %collective-permute-start.19 = (bf16[2,464,128]{2,1,0:T(8,128)(2,1)S(1)}, bf16[2,464,128]{2,1,0:T(8,128)(2,1)S(1)}, u32[]{:S(2)}, u32[]{:S(2)}) collective-permute-start(bf16[2,464,128]{2,1,0:T(8,128)(2,1)S(1)} %get-tuple-element.114), channel_id=1, source_target_pairs={{0,192},{64,0},{128,64},{192,128},{1,193},{65,1},{129,65},{193,129... | collective-permute-start | bytes 712712 | tf_op jit(solution)/shard_map/ppermute | solution.py:705
  101.0 15.1 %collective-permute-start.16 = (bf16[256,128]{1,0:T(8,128)(2,1)S(1)}, bf16[256,128]{1,0:T(8,128)(2,1)S(1)}, u32[]{:S(2)}, u32[]{:S(2)}) collective-permute-start(bf16[256,128]{1,0:T(8,128)(2,1)S(1)} %get-tuple-element.107), channel_id=1, source_target_pairs={{1,2},{2,1},{3,4},{4,3},{5,6},{6,5},{7,8},{8,7},{9,10},{10,9},{11,... | collective-permute-start | bytes 196616 | tf_op jit(solution)/shard_map/ppermute | solution.py:347
  107.7 8.4 %collective-permute-start.15 = (bf16[256,128]{1,0:T(8,128)(2,1)S(1)}, bf16[256,128]{1,0:T(8,128)(2,1)S(1)}, u32[]{:S(2)}, u32[]{:S(2)}) collective-permute-start(bf16[256,128]{1,0:T(8,128)(2,1)S(1)} %get-tuple-element.106.refs_8_), channel_id=1, source_target_pairs={{0,1},{1,0},{2,3},{3,2},{4,5},{5,4},{6,7},{7,6},{8,9},{9,8},{10,11... | collective-permute-start | bytes 196616 | tf_op jit(solution)/shard_map/ppermute | solution.py:347
